TPU v7x, 32 devices: a whole 2x2x4 slice. The times are simulated.
32 devices in a mesh: front: 4 (over y, core), blk: 8 (over z, x).
Axes of the slice: x: 2, y: 2, z: 4, core: 2. Of those that a mesh axis runs over, the one named last changes fastest.
Arguments:
- front: float32 [12288, 3072], P('front', 'blk'), may hold values from -8 to 96, as said below
- parent_group: int32 [4, 8, 6, 1], P('front', 'blk'), may hold values from 0 to 3; in each aligned block of 6 rows (0 to 5, 6 to 11, ..., all dimensions but the last counted through in order) at most 2 rows name the same one
- row_block: int32 [4, 8, 6], P('front', 'blk'), may hold values from 0 to 7
- parent_base: float32 [4096, 3072], P('front', 'blk'), may hold values from -6 to 6
Outputs:
- factored: float32 [12288, 3072], P('front', 'blk')
- assembled: float32 [4096, 3072], P('front', 'blk')
Inputs may be any that keep to these rules, and one draw needn't show every extreme that they name: `parent_group`: in the 6 blocks of one device no group is named more than 2 times. `front`: diagonal entries at indices pivotal at some tick lie between 48 and 96; every other entry lies within 8 of zero.
All inputs are finite; a program needn't handle non-finite values.
Results may differ from a plain program's by a relative error of at most 0.003.
Values may be sent and summed in bfloat16 or wider, within the bound.
No kernel may reach another device: no remote copies, remote signals or barrier semaphores. Data moves between devices by JAX's collectives and lax.ppermute only.
A program may use at most 128 MiB of HBM per device.

v0:
```python
import jax
import jax.numpy as jnp
from jax import lax
from jax.sharding import PartitionSpec as P

P_SIZE = 256
TICKS = 5
NEWTON = 2
RB = 128
NB = 6
CAP = 2
ASM_BLOCKS = 8


def broadcast(value, axis, source):
    kept = jnp.where(lax.axis_index(axis) == source, value, 0).astype(value.dtype)
    return lax.psum(kept, axis)


def newton_inverse(block):
    inverse = jnp.diag(1.0 / jnp.diagonal(block))
    ident = jnp.eye(block.shape[0], dtype=block.dtype)
    for step in range(NEWTON):
        inverse = jnp.dot(
            inverse,
            2.0 * ident - jnp.dot(block, inverse, precision=lax.Precision.HIGHEST),
            precision=lax.Precision.HIGHEST,
        )
    return inverse


def local(front, parent_group, row_block, parent_base):
    order, width = front.shape
    member = lax.axis_index("blk")
    groups = lax.axis_size("front")
    index = jnp.arange(order)
    pivotal = index % width < P_SIZE
    left = front[:, :P_SIZE]
    right = front[:, P_SIZE:]
    for tick in range(TICKS):
        start = tick * width
        factor_left = left
        factor_start = tick * width
        live = jnp.logical_not(pivotal & (index // width <= tick))

        def owner_part(cols):
            inverse = newton_inverse(cols[factor_start : factor_start + P_SIZE, :])
            mult = jnp.dot(cols, inverse, precision=lax.Precision.HIGHEST)
            return mult * live[:, None].astype(cols.dtype)

        def other_part(cols):
            return jnp.zeros_like(cols)

        mult = lax.cond(member == tick, owner_part, other_part, factor_left)
        panel = broadcast(mult.astype(jnp.bfloat16), "blk", tick)
        factor_left = jnp.where((member == tick) & live[:, None], mult, factor_left)
        panel, left = (panel, factor_left)
        urows_left = left[start : start + P_SIZE, :].astype(jnp.bfloat16)
        urows_right = right[start : start + P_SIZE, :].astype(jnp.bfloat16)
        left_mask = (member > tick).astype(jnp.float32)
        left = left - jnp.dot(panel, urows_left, preferred_element_type=jnp.float32) * left_mask
        right = right - jnp.dot(panel, urows_right, preferred_element_type=jnp.float32)
    factored = jnp.concatenate([left, right], axis=1)
    tail_rows = order - NB * RB
    keep_left = (member >= TICKS).astype(jnp.float32)
    tail = jnp.concatenate([left[tail_rows:, :] * keep_left, right[tail_rows:, :]], axis=1)
    cont = tail.astype(jnp.bfloat16).reshape(NB, RB, width)
    dest = parent_group.reshape(NB)
    target_block = row_block.reshape(NB)
    offset_hot = (target_block[:, None] == jnp.arange(ASM_BLOCKS, dtype=jnp.int32)[None, :]).astype(
        jnp.bfloat16
    )
    number = jnp.arange(NB)
    earlier = (dest[None, :] == dest[:, None]) & (number[None, :] < number[:, None])
    slot = jnp.sum(earlier.astype(jnp.int32), axis=1)
    pick = (dest[None, None, :] == jnp.arange(groups, dtype=jnp.int32)[:, None, None]) & (
        slot[None, None, :] == jnp.arange(CAP, dtype=jnp.int32)[None, :, None]
    )
    pick = pick.astype(jnp.bfloat16)
    outgoing = jnp.einsum("gci,irk->gcrk", pick, cont, preferred_element_type=jnp.float32).astype(
        jnp.bfloat16
    )
    address = jnp.einsum(
        "gci,ia->gca", pick, offset_hot, preferred_element_type=jnp.float32
    ).astype(jnp.bfloat16)
    incoming, received_address = (
        lax.all_to_all(outgoing, "front", split_axis=0, concat_axis=0, tiled=True),
        lax.all_to_all(address, "front", split_axis=0, concat_axis=0, tiled=True),
    )
    added = jnp.einsum(
        "gca,gcrk->ark", received_address, incoming, preferred_element_type=jnp.float32
    )
    assembled = parent_base + added.reshape(ASM_BLOCKS * RB, width)
    return (factored, assembled)


def solution(mesh):
    placed = (
        P("front", "blk"),
        P("front", "blk", None, None),
        P("front", "blk", None),
        P("front", "blk"),
    )
    return jax.shard_map(
        local,
        mesh=mesh,
        in_specs=placed,
        out_specs=(P("front", "blk"), P("front", "blk")),
        check_vma=False,
    )
```

profile of v0, /device:TPU:0, one launch (start us, length us, event | category | flops | bytes accessed | tf_op | source)
XLA Modules:
  0.0 573.4 jit_solution(1360663287521132967)
XLA Ops:
  7.3 3.8 slice.69
  11.0 14.3 %conditional.5 = (f32[3072,256]{0,1:T(8,128)S(1)}) conditional(s32[]{:T(128)} %convert_element_type.106, () %tuple.42, (f32[3072,256]{1,0:T(8,128)}, s32[3072]{0:T(1024)S(1)}, pred[3072]{0:T(1024)(128)(4,1)S(1)}) %tuple.43), branch_computations={%region_0.1_spmd, %region_1.2_spmd} | conditional | flops 3222680832 | bytes 9748488 | solution.py:54
  18.1 7.2 %fusion = f32[3072,256]{0,1:T(8,128)S(1)} fusion(f32[256,256]{1,0:T(8,128)S(1)} %fusion.97, f32[3072,256]{1,0:T(8,128)} %get-tuple-element.70, f32[3072]{0:T(1024)S(1)} %not_convert_fusion), kind=kOutput, calls=%fused_computation.6 | convolution fusion | flops 2416705536 | bytes 6565888 | tf_op jit(solution)/shard_map/cond/branch_1_fun/dot_general | solution.py:48
  29.1 5.1 broadcast_select_fusion
  34.2 80.6 %all-reduce.6.cloned.1.call-done = bf16[3072,256]{0,1:T(8,128)(2,1)} async-done(((bf16[3072,256]{0,1:T(8,128)(2,1)}), bf16[3072,256]{0,1:T(8,128)(2,1)}) %all-reduce.6.cloned.1.call-update) | async-done | bytes 1572880 | tf_op jit(solution)/shard_map/psum | solution.py:17
  123.5 3.5 copy.30
  127.0 4.1 broadcast_select_fusion.1
  131.1 89.1 %all-reduce.8.cloned.1.call-done = bf16[3072,256]{0,1:T(8,128)(2,1)} async-done(((bf16[3072,256]{0,1:T(8,128)(2,1)}), bf16[3072,256]{0,1:T(8,128)(2,1)}) %all-reduce.8.cloned.1.call-update) | async-done | bytes 1572880 | tf_op jit(solution)/shard_map/psum | solution.py:17
  229.3 3.5 copy.31
  232.9 4.1 broadcast_select_fusion.2
  237.0 88.8 %all-reduce.10.cloned.1.call-done = bf16[3072,256]{0,1:T(8,128)(2,1)} async-done(((bf16[3072,256]{0,1:T(8,128)(2,1)}), bf16[3072,256]{0,1:T(8,128)(2,1)}) %all-reduce.10.cloned.1.call-update) | async-done | bytes 1572880 | tf_op jit(solution)/shard_map/psum | solution.py:17
  331.1 3.2 convert_select_fusion.1
  338.3 3.7 convolution_subtract_fusion.4
  342.0 3.5 copy.32
  345.6 4.1 broadcast_select_fusion.3
  349.7 82.2 %all-reduce.12.cloned.1.call-done = bf16[3072,256]{0,1:T(8,128)(2,1)} async-done(((bf16[3072,256]{0,1:T(8,128)(2,1)}), bf16[3072,256]{0,1:T(8,128)(2,1)}) %all-reduce.12.cloned.1.call-update) | async-done | bytes 1572880 | tf_op jit(solution)/shard_map/psum | solution.py:17
  435.0 8.2 %conditional.9 = (f32[3072,256]{0,1:T(8,128)}) conditional(s32[]{:T(128)} %convert_element_type.102, () %tuple.38, (f32[3072,256]{1,0:T(8,128)S(1)}, s32[3072]{0:T(1024)S(1)}, pred[3072]{0:T(1024)(128)(4,1)S(1)}) %tuple.47), branch_computations={%region_12.13_spmd, %region_13.14_spmd} | conditional | flops 3222680832 | bytes 9748488 | solution.py:54
  443.2 3.2 convert_select_fusion
  450.9 3.5 copy.33
  454.4 3.9 convolution_subtract_fusion.1
  461.0 76.7 %all-reduce.14.cloned.1.call-done = bf16[3072,256]{0,1:T(8,128)(2,1)} async-done(((bf16[3072,256]{0,1:T(8,128)(2,1)}), bf16[3072,256]{0,1:T(8,128)(2,1)}) %all-reduce.14.cloned.1.call-update) | async-done | bytes 1572880 | tf_op jit(solution)/shard_map/psum | solution.py:17
  546.6 4.2 all-to-all-start.1
  550.8 3.9 pad_maximum_fusion
  554.7 7.8 %all-to-all-done.1 = bf16[4,2,128,384]{3,1,2,0:T(2,128)(2,1)} async-done(((bf16[4,2,128,384]{3,1,2,0:T(2,128)(2,1)}), bf16[4,2,128,384]{3,1,2,0:T(2,128)(2,1)}, u32[]{:S(2)}, u32[]{:S(2)}) %all-to-all-start.1) | async-done | bytes 786464 | tf_op jit(solution)/shard_map/all_to_all | solution.py:87
  (76 shorter events, 68.8 us)
Async XLA Ops:
  7.2 107.7 %all-reduce.6.cloned.1.call-start = ((), (), s32[]{:S(2)}) async-start(), calls=%async_computation.2 | async-start | bytes 3145728 | tf_op jit(solution)/shard_map/psum | solution.py:17
  26.7 193.6 %all-reduce.8.cloned.1.call-start = ((), (), s32[]{:S(2)}) async-start(), calls=%async_computation.3 | async-start | bytes 3145728 | tf_op jit(solution)/shard_map/psum | solution.py:17
  123.4 202.3 %all-reduce.10.cloned.1.call-start = ((), (), s32[]{:S(2)}) async-start(), calls=%async_computation.4 | async-start | bytes 3145728 | tf_op jit(solution)/shard_map/psum | solution.py:17
  225.8 3.3 copy-start.5
  229.0 202.8 %all-reduce.12.cloned.1.call-start = ((), (), s32[]{:S(2)}) async-start(), calls=%async_computation.5 | async-start | bytes 3145728 | tf_op jit(solution)/shard_map/psum | solution.py:17
  331.0 3.2 copy-start.6
  335.0 211.6 %all-to-all-start = ((bf16[4,2,8]{2,1,0:T(2,128)(2,1)}), bf16[4,2,8]{2,1,0:T(2,128)(2,1)S(1)}, u32[]{:S(2)}, u32[]{:S(2)}) async-start(bf16[4,2,8]{2,1,0:T(2,128)(2,1)} %copy.34), calls=%async_computation | async-start | bytes 4096 | tf_op jit(solution)/shard_map/all_to_all | solution.py:88
  338.2 199.5 %all-reduce.14.cloned.1.call-start = ((), (), s32[]{:S(2)}) async-start(), calls=%async_computation.6 | async-start | bytes 3145728 | tf_op jit(solution)/shard_map/psum | solution.py:17
  446.4 2.7 copy-start.2
  454.4 3.9 copy-start
  537.7 4.0 copy-start.3
  540.4 1.1 copy-start.1
  546.6 15.9 %all-to-all-start.1 = ((bf16[4,2,128,384]{3,1,2,0:T(2,128)(2,1)}), bf16[4,2,128,384]{3,1,2,0:T(2,128)(2,1)}, u32[]{:S(2)}, u32[]{:S(2)}) async-start(bf16[4,2,128,384]{3,1,2,0:T(2,128)(2,1)} %copy.37), calls=%async_computation.1 | async-start | bytes 1572864 | tf_op jit(solution)/shard_map/all_to_all | solution.py:87
  554.7 10.4 %copy-start.4 = (f32[1024,384]{1,0:T(8,128)S(1)}, f32[1024,384]{1,0:T(8,128)}, u32[]{:S(2)}) copy-start(f32[1024,384]{1,0:T(8,128)} %param.17) | copy-start | bytes 4718596
Sparse Core Ops, SparseCore 0:
  26.8 88.0 all-reduce.5
  123.5 96.7 all-reduce.7
  229.2 96.5 all-reduce.9
  334.4 97.4 all-reduce.11
  446.5 91.1 all-reduce.13
where the time goes:
time: 582 us; the launch traced here: 573 us
  waiting for transfers between devices  425 us (73%)
  matrix products  43.6 us (7%)
  other arithmetic  39.9 us (7%)
  local copies, waits for them, and re-layouts  35.6 us (6%)
  between operations  14.5 us (2%)
  starting transfers between devices  7.56 us (1%)
  loops' own time  6.99 us (1%)
    psum x5, waiting for transfers between devices, broadcast(): return lax.psum(kept, axis)  417 us
    select_n x5, other arithmetic, local(): factor_left = jnp.where((member == tick) & live[:, None], mult, factor_left)  20.2 us
    cond x5, local copies, waits for them, and re-layouts, local(): mult = lax.cond(member == tick, owner_part, other_part, factor_left)  16.5 us
    dot_general x5, matrix products, local(): jnp.dot(panel, urows_left, preferred_element_type=jnp.float32) * left_mask  15 us
    dot_general x5, matrix products, local(): jnp.dot(panel, urows_right, preferred_element_type=jnp.float32)  14.7 us
    select_n x5, other arithmetic, broadcast(): jnp.where(lax.axis_index(axis) == source, value, 0).astype(value.dtype)  14.1 us
  transfers between devices with their start and end apart: 7, of which 6 were waited for; matrix products, arithmetic and copies ran while one was open for 12% of the time, Pallas kernels for 0%

commit v1 on v0

v1 whole, which is shorter than its diff:
```python
import functools

import jax
import jax.numpy as jnp
from jax import lax
from jax.experimental import pallas as pl
from jax.experimental.pallas import tpu as pltpu
from jax.sharding import PartitionSpec as P

P_SIZE = 256
TICKS = 5
NEWTON = 2
RB = 128
NB = 6
CAP = 2
ASM_BLOCKS = 8
ROW_TILE = 128
HIGH = lax.Precision.HIGHEST
ANY = pl.BlockSpec(memory_space=pl.ANY)
SMEM = pl.BlockSpec(memory_space=pltpu.SMEM)
VMEM = pl.BlockSpec(memory_space=pltpu.VMEM)


def after(values, done):
    return lax.optimization_barrier((values, done))[0]


def permute(value, pairs):
    return lax.ppermute(value, "blk", pairs)


def start_halves(own, member):
    half = own.shape[0] // 2
    moved = permute(own[half:], [(4, 5)])
    return jnp.where(member == 5, moved, own[:half])


def relay(segments, member):
    across = [(m, m ^ 1) for m in range(8)]
    near = [(m, m ^ 2) for m in range(8)]
    distant = [(m, m + 4) for m in range(4)]
    level = member // 2
    a, b, c = segments
    rest = jnp.concatenate([b, c], axis=0)

    first = permute(a, distant)
    half_a = start_halves(a, member)
    half_n = start_halves(rest, member)
    cur_a = jnp.where(member < 4, a, first)

    b1, ha, hn = after((b, half_a, half_n), first)
    cur_a = after(cur_a, half_a)
    far_a = permute(cur_a, near)
    over_a = permute(cur_a, across)
    back_a = permute(ha, [(4, 0), (5, 1)])
    first_b = permute(b1, distant)
    back_n = permute(hn, [(4, 0), (5, 1)])
    ha = jnp.where(level == 0, back_a, half_a)
    hn = jnp.where(level == 0, back_n, half_n)
    cur_b = jnp.where(member < 4, b, first_b)

    c1, cur_b, ha, hn, fa = after((c, cur_b, ha, hn, far_a), (far_a, over_a, first_b))
    spread = [(0, 2), (1, 3), (4, 6), (5, 7)]
    far_b = permute(cur_b, near)
    first_c = permute(c1, distant)
    overfar_a = permute(fa, across)
    spread_a = permute(ha, spread)
    over_b = permute(cur_b, across)
    spread_n = permute(hn, spread)
    ha = jnp.where(level % 2 == 1, spread_a, ha)
    hn = jnp.where(level % 2 == 1, spread_n, hn)
    cur_c = jnp.where(member < 4, c, first_c)

    cur_c, ha, hn, fb = after((cur_c, ha, hn, far_b), (far_b, first_c, overfar_a))
    overha = permute(ha, across)
    far_c = permute(cur_c, near)
    overfar_b = permute(fb, across)
    overhn = permute(hn, across)
    over_c = permute(cur_c, across)

    fc = after(far_c, (overfar_b, over_c))
    overfar_c = permute(fc, across)
    return (
        (cur_a, far_a, over_a, overfar_a, ha, overha),
        (cur_b, far_b, over_b, overfar_b, hn, overhn),
        (cur_c, far_c, over_c, overfar_c, hn, overhn),
    )


def fetch_relayed(member, refs, target, sems, first_row, total_rows, rows):
    cur, far, over, overfar, half, overhalf = refs
    x = lax.rem(member, 2)
    even = lax.rem(lax.div(member, 2), 2) == 0
    places = (
        (cur, jnp.where(even, x, 2 + x)),
        (far, jnp.where(even, 2 + x, x)),
        (over, jnp.where(even, 1 - x, 3 - x)),
        (overfar, jnp.where(even, 3 - x, 1 - x)),
    )
    copies = [
        pltpu.make_async_copy(ref, target.at[slab], sems.at[i]) for i, (ref, slab) in enumerate(places)
    ]
    for copy in copies:
        copy.start()
    split = total_rows // 2
    low = max(0, min(rows, split - first_row))
    pieces = []
    if low:
        pieces.append((0, first_row, 0, low))
    if rows - low:
        pieces.append((1, first_row + low - split, low, rows - low))
    for which in (0, 1):
        mine, other = (half, overhalf) if which == 0 else (overhalf, half)

        @pl.when(x == which)
        def _(mine=mine, other=other):
            for number, (part, source, to, count) in enumerate(pieces):
                ref = mine if part == 0 else other
                pltpu.make_async_copy(
                    ref.at[pl.ds(source, count)],
                    target.at[TICKS - 1, pl.ds(to, count)],
                    sems.at[4 + number],
                ).start()

    def wait():
        for copy in copies:
            copy.wait()
        for number, (part, source, to, count) in enumerate(pieces):
            pltpu.make_async_copy(
                half.at[pl.ds(source, count)],
                target.at[TICKS - 1, pl.ds(to, count)],
                sems.at[4 + number],
            ).wait()

    return wait


def fetch_gathered(member, refs, target, sems, first_row, total_rows, rows):
    copy = pltpu.make_async_copy(refs[0], target, sems.at[0])
    copy.start()
    return copy.wait


def diagonal_inverse(block):
    size = block.shape[0]
    row = lax.broadcasted_iota(jnp.int32, (size, size), 0)
    col = lax.broadcasted_iota(jnp.int32, (size, size), 1)
    on = row == col
    kept = jnp.where(on, block, 0.0)
    down = 1.0 / jnp.sum(kept, axis=1, keepdims=True)
    right = 1.0 / jnp.sum(kept, axis=0, keepdims=True)
    twice = jnp.where(on, 2.0, 0.0)
    inverse = down * (twice - block * right)
    for step in range(NEWTON - 1):
        inner = twice - jnp.dot(block, inverse, precision=HIGH, preferred_element_type=jnp.float32)
        inverse = jnp.dot(inverse, inner, precision=HIGH, preferred_element_type=jnp.float32)
    return inverse


def pivot_kernel(fetch, n_bufs, width, member_ref, front, *rest):
    bufs = rest[:n_bufs]
    out, w_out, raw, mat, own, inv, sems, own_sems = rest[n_bufs:]
    member = member_ref[0]
    p, rows = P_SIZE, TICKS * P_SIZE
    loads = [
        pltpu.make_async_copy(
            front.at[pl.ds(t * width, p), :], own.at[pl.ds(t * p, p), :], own_sems.at[t]
        )
        for t in range(TICKS)
    ]
    for load in loads:
        load.start()
    wait = fetch(member, bufs, raw, sems, 0, rows, rows)
    wait()
    for load in loads:
        load.wait()
    for s in range(TICKS):
        mat[s] = raw[s].astype(jnp.float32)
    for t in range(TICKS):
        lo, below = t * p, (t + 1) * p
        x = diagonal_inverse(mat[t, lo:below, :])
        inv[t] = x
        if below < rows:
            mult = jnp.dot(mat[t, below:, :], x, precision=HIGH, preferred_element_type=jnp.float32)
            panel = mult.astype(jnp.bfloat16)
            for s in range(t + 1, TICKS):
                mat[s, below:, :] = mat[s, below:, :] - jnp.dot(
                    panel, mat[s, lo:below, :].astype(jnp.bfloat16), preferred_element_type=jnp.float32
                )
            urows = own[lo:below, :].astype(jnp.bfloat16)
            own[below:, p:] = own[below:, p:] - jnp.dot(
                panel, urows[:, p:], preferred_element_type=jnp.float32
            )

            @pl.when((member >= TICKS) | (member > t))
            def _():
                own[below:, :p] = own[below:, :p] - jnp.dot(
                    panel, urows[:, :p], preferred_element_type=jnp.float32
                )

            @pl.when(member == t)
            def _():
                own[below:, :p] = jnp.dot(
                    own[below:, :p], x, precision=HIGH, preferred_element_type=jnp.float32
                )

    stores = [
        pltpu.make_async_copy(
            own.at[pl.ds(t * p, p), :], out.at[pl.ds(t * width, p), :], own_sems.at[t]
        )
        for t in range(TICKS)
    ]
    for store in stores:
        store.start()
    row = lax.broadcasted_iota(jnp.int32, (p, width), 0)
    col = lax.broadcasted_iota(jnp.int32, (p, width), 1)
    owner = (member < TICKS) & (col < p)
    for t in reversed(range(TICKS)):
        lo, hi = t * p, (t + 1) * p
        unit = jnp.where((row == col) & (member == t), -1.0, 0.0)
        side = jnp.where(owner, unit, own[lo:hi, :])
        for s in range(t + 1, TICKS):
            side = side - jnp.dot(
                mat[s, lo:hi, :].astype(jnp.bfloat16),
                w_out[s * p : (s + 1) * p, :],
                preferred_element_type=jnp.float32,
            )
        w_out[lo:hi, :] = jnp.dot(
            inv[t], side, precision=HIGH, preferred_element_type=jnp.float32
        ).astype(jnp.bfloat16)
    for store in stores:
        store.wait()


def pivot_rows(fetch, member, front, bufs):
    order, width = front.shape
    p, rows = P_SIZE, TICKS * P_SIZE
    return pl.pallas_call(
        functools.partial(pivot_kernel, fetch, len(bufs), width),
        name="pivot_rows",
        out_shape=(
            jax.ShapeDtypeStruct((order, width), jnp.float32),
            jax.ShapeDtypeStruct((rows, width), jnp.bfloat16),
        ),
        in_specs=[SMEM, ANY] + [ANY] * len(bufs),
        out_specs=(ANY, VMEM),
        scratch_shapes=[
            pltpu.VMEM((TICKS, rows, p), jnp.bfloat16),
            pltpu.VMEM((TICKS, rows, p), jnp.float32),
            pltpu.VMEM((rows, width), jnp.float32),
            pltpu.VMEM((TICKS, p, p), jnp.float32),
            pltpu.SemaphoreType.DMA((6,)),
            pltpu.SemaphoreType.DMA((TICKS,)),
        ],
    )(member, front, *bufs)


def other_kernel(fetch, n_bufs, ranges, first_row, total_rows, tail, member_ref, w, front, out_in, *rest):
    bufs = rest[:n_bufs]
    if tail:
        out, cont, raw, base, sems, base_sems = rest[n_bufs:]
    else:
        out, raw, base, sems, base_sems = rest[n_bufs:]
    member = member_ref[0]
    rows, width = base.shape
    loads = [
        pltpu.make_async_copy(front.at[pl.ds(src, n), :], base.at[pl.ds(dst, n), :], base_sems.at[i])
        for i, (src, dst, n) in enumerate(ranges)
    ]
    for load in loads:
        load.start()
    wait = fetch(member, bufs, raw, sems, first_row, total_rows, rows)
    wait()
    for load in loads:
        load.wait()
    keep = (member >= TICKS) | (lax.broadcasted_iota(jnp.int32, (ROW_TILE, width), 1) >= P_SIZE)

    def tile(i, carry):
        at = pl.ds(pl.multiple_of(i * ROW_TILE, ROW_TILE), ROW_TILE)
        total = jnp.where(keep, base[at, :], 0.0)
        for s in range(TICKS):
            total = total - jnp.dot(
                raw[s, at, :], w[s * P_SIZE : (s + 1) * P_SIZE, :], preferred_element_type=jnp.float32
            )
        base[at, :] = total
        if tail:
            cont[at, :] = jnp.where(keep, total, 0.0).astype(jnp.bfloat16)
        return carry

    lax.fori_loop(0, rows // ROW_TILE, tile, 0)
    stores = [
        pltpu.make_async_copy(base.at[pl.ds(dst, n), :], out.at[pl.ds(src, n), :], base_sems.at[i])
        for i, (src, dst, n) in enumerate(ranges)
    ]
    for store in stores:
        store.start()
    for store in stores:
        store.wait()


def other_rows(fetch, member, w, front, out, bufs, ranges, first_row, total_rows, tail):
    order, width = front.shape
    rows = sum(n for _, _, n in ranges)
    shapes = [jax.ShapeDtypeStruct((order, width), jnp.float32)]
    specs = [ANY]
    if tail:
        shapes.append(jax.ShapeDtypeStruct((rows, width), jnp.bfloat16))
        specs.append(VMEM)
    return pl.pallas_call(
        functools.partial(other_kernel, fetch, len(bufs), ranges, first_row, total_rows, tail),
        name="tail_rows" if tail else "middle_rows",
        out_shape=tuple(shapes),
        in_specs=[SMEM, VMEM, ANY, ANY] + [ANY] * len(bufs),
        out_specs=tuple(specs),
        input_output_aliases={3: 0},
        scratch_shapes=[
            pltpu.VMEM((TICKS, rows, P_SIZE), jnp.bfloat16),
            pltpu.VMEM((rows, width), jnp.float32),
            pltpu.SemaphoreType.DMA((6,)),
            pltpu.SemaphoreType.DMA((len(ranges),)),
        ],
    )(member, w, front, out, *bufs)


def assemble(cont, parent_group, row_block, parent_base):
    width = parent_base.shape[1]
    groups = lax.axis_size("front")
    cont = cont.reshape(NB, RB, width)
    dest = parent_group.reshape(NB)
    target_block = row_block.reshape(NB)
    offset_hot = (target_block[:, None] == jnp.arange(ASM_BLOCKS, dtype=jnp.int32)[None, :]).astype(
        jnp.bfloat16
    )
    number = jnp.arange(NB)
    earlier = (dest[None, :] == dest[:, None]) & (number[None, :] < number[:, None])
    slot = jnp.sum(earlier.astype(jnp.int32), axis=1)
    pick = (dest[None, None, :] == jnp.arange(groups, dtype=jnp.int32)[:, None, None]) & (
        slot[None, None, :] == jnp.arange(CAP, dtype=jnp.int32)[None, :, None]
    )
    pick = pick.astype(jnp.bfloat16)
    outgoing = jnp.einsum("gci,irk->gcrk", pick, cont, preferred_element_type=jnp.float32).astype(
        jnp.bfloat16
    )
    address = jnp.einsum(
        "gci,ia->gca", pick, offset_hot, preferred_element_type=jnp.float32
    ).astype(jnp.bfloat16)
    incoming = lax.all_to_all(outgoing, "front", split_axis=0, concat_axis=0, tiled=True)
    received_address = lax.all_to_all(address, "front", split_axis=0, concat_axis=0, tiled=True)
    added = jnp.einsum(
        "gca,gcrk->ark", received_address, incoming, preferred_element_type=jnp.float32
    )
    return parent_base + added.reshape(ASM_BLOCKS * RB, width)


def local(front, parent_group, row_block, parent_base):
    order, width = front.shape
    member = lax.axis_index("blk")
    holder = member.reshape(1).astype(jnp.int32)
    p, top = P_SIZE, TICKS * width
    tail_n = NB * RB
    tail_at = order - tail_n
    slabs = front[:top].reshape(TICKS, width, width)
    own_p = slabs[:, :p, :p].reshape(TICKS * p, p).astype(jnp.bfloat16)
    own_t = front[tail_at:, :p].astype(jnp.bfloat16)
    own_m = jnp.concatenate(
        [slabs[:, p:, :p].reshape(TICKS * (width - p), p), front[top:tail_at, :p]], axis=0
    ).astype(jnp.bfloat16)
    middle = [(t * width + p, t * (width - p), width - p) for t in range(TICKS)]
    if tail_at > top:
        middle.append((top, TICKS * (width - p), tail_at - top))
    segments = (own_p, own_t, own_m)
    if lax.axis_size("blk") == 8:
        fetch = fetch_relayed
        sets = relay(segments, member)
    else:
        fetch = fetch_gathered
        sets = tuple((lax.all_gather(s, "blk")[:TICKS],) for s in segments)
    rest = own_t.shape[0] + own_m.shape[0]
    out, w = pivot_rows(fetch, holder, front, sets[0])
    out, cont = other_rows(
        fetch, holder, w, front, out, sets[1], [(tail_at, 0, tail_n)], 0, rest, True
    )
    assembled = assemble(cont, parent_group, row_block, parent_base)
    (factored,) = other_rows(fetch, holder, w, front, out, sets[2], middle, tail_n, rest, False)
    return (factored, assembled)


def solution(mesh):
    placed = (
        P("front", "blk"),
        P("front", "blk", None, None),
        P("front", "blk", None),
        P("front", "blk"),
    )
    return jax.shard_map(
        local,
        mesh=mesh,
        in_specs=placed,
        out_specs=(P("front", "blk"), P("front", "blk")),
        check_vma=False,
    )
```

time: 582 us -> 223 us (0.38); the launches traced: 573 us -> 222 us
  waiting for transfers between devices: 425 us -> 98.3 us
  starting transfers between devices: 7.56 us -> 70.3 us
  matrix products: 43.6 us -> 2.95 us
  Pallas kernels: 0 us -> 35.4 us
  other arithmetic: 39.9 us -> 4.76 us
  local copies, waits for them, and re-layouts: 35.6 us -> 9.2 us
  between operations: 14.5 us -> 1.15 us
  loops' own time: 6.99 us -> 0 us
    psum x5 -> x0, waiting for transfers between devices: 417 us -> none  [broadcast(): return lax.psum(kept, axis)]
    ppermute x0 -> x20, waiting for transfers between devices: none -> 98.3 us  [permute(): return lax.ppermute(value, 'blk', pairs)]
    ppermute x0 -> x20, starting transfers between devices: none -> 63.6 us  [permute(): return lax.ppermute(value, 'blk', pairs)]
    dot_general x18 -> x3, matrix products: 43.6 us -> 2.95 us  [the longest x1 1.64 us: assemble(): jnp.einsum('gci,irk->gcrk', pick, cont, preferred_element_type=jnp.float32)]
    pallas_call x0 -> x3, Pallas kernels: none -> 35.4 us  [the longest x1 21.2 us: pivot_rows(): pl.pallas_call(functools.partial(pivot_kernel, fetch, len(bufs), width),...]
    select_n x11 -> x9, other arithmetic: 34.3 us -> 1.39 us  [the longest x1 0.81 us: relay(): cur_b = jnp.where(member < 4, b, first_b)]
    cond x5 -> x0, local copies, waits for them, and re-layouts: 16.5 us -> none  [local(): mult = lax.cond(member == tick, owner_part, other_part, factor_left)]
    another operation x4 -> x0, local copies, waits for them, and re-layouts: 8.13 us -> none
  transfers between devices with their start and end apart: 7 -> 22, of which waited for: 6 -> 9; matrix products, arithmetic and copies ran while one was open for 12% -> 5% of each run, Pallas kernels for 0% -> 13%
where the time goes in v1:
time: 223 us; the launch traced here: 222 us
  waiting for transfers between devices  98.3 us (44%)
  starting transfers between devices  70.3 us (32%)
  Pallas kernels  35.4 us (16%)
  local copies, waits for them, and re-layouts  9.2 us (4%)
  other arithmetic  4.76 us (2%)
  matrix products  2.95 us (1%)
    ppermute x20, waiting for transfers between devices, permute(): return lax.ppermute(value, 'blk', pairs)  98.3 us
    ppermute x20, starting transfers between devices, permute(): return lax.ppermute(value, 'blk', pairs)  63.6 us
    pallas_call x1, Pallas kernels, pivot_rows(): pl.pallas_call(functools.partial(pivot_kernel, fetch, len(bufs), width),...  21.2 us
    pallas_call x2, Pallas kernels, other_rows(): pl.pallas_call(functools.partial(other_kernel, fetch, len(bufs), ranges,...  14.2 us
  transfers between devices with their start and end apart: 22, of which 9 were waited for; matrix products, arithmetic and copies ran while one was open for 5% of the time, Pallas kernels for 13%

profile of v1, /device:TPU:0, one launch (start us, length us, event | category | flops | bytes accessed | tf_op | source)
XLA Modules:
  0.0 222.0 jit_solution(13030611968296313279)
XLA Ops:
  0.6 2.1 slice.58
  7.6 10.2 %collective-permute-start = (bf16[1280,256]{1,0:T(8,128)(2,1)S(1)}, bf16[1280,256]{1,0:T(8,128)(2,1)}, u32[]{:S(2)}, u32[]{:S(2)}) collective-permute-start(bf16[1280,256]{1,0:T(8,128)(2,1)S(1)} %bitcast.34), channel_id=1, source_target_pairs={{0,4},{1,5},{2,6},{3,7},{8,12},{9,13},{10,14},{11,15},{16,20},{17,... | collective-permute-start | bytes 1966088 | tf_op jit(solution)/shard_map/ppermute | solution.py:29
  19.8 10.8 %collective-permute-done = bf16[1280,256]{1,0:T(8,128)(2,1)} collective-permute-done((bf16[1280,256]{1,0:T(8,128)(2,1)S(1)}, bf16[1280,256]{1,0:T(8,128)(2,1)}, u32[]{:S(2)}, u32[]{:S(2)}) %collective-permute-start) | collective-permute-done | bytes 655392 | tf_op jit(solution)/shard_map/ppermute | solution.py:29
  30.6 5.5 %collective-permute-start.5 = (bf16[768,256]{1,0:T(8,128)(2,1)S(1)}, bf16[768,256]{1,0:T(8,128)(2,1)S(1)}, u32[]{:S(2)}, u32[]{:S(2)}) collective-permute-start(bf16[768,256]{1,0:T(8,128)(2,1)S(1)} %copy-done.5), channel_id=1, source_target_pairs={{0,4},{1,5},{2,6},{3,7},{8,12},{9,13},{10,14},{11,15},{16,20},{17,... | collective-permute-start | bytes 1179656 | tf_op jit(solution)/shard_map/ppermute | solution.py:29
  37.6 20.3 %collective-permute-start.2 = (bf16[1280,256]{1,0:T(8,128)(2,1)S(1)}, bf16[1280,256]{1,0:T(8,128)(2,1)S(1)}, u32[]{:S(2)}, u32[]{:S(2)}) collective-permute-start(bf16[1280,256]{1,0:T(8,128)(2,1)S(1)} %broadcast_select_fusion.rest_0_), channel_id=1, source_target_pairs={{0,2},{1,3},{2,0},{3,1},{4,6},{5,7},{6,4},{7,5},{8,10},{9,11},{10,... | collective-permute-start | bytes 1966088 | tf_op jit(solution)/shard_map/ppermute | solution.py:29
  61.1 12.3 %collective-permute-done.7 = bf16[896,256]{1,0:T(8,128)(2,1)S(1)} collective-permute-done((bf16[896,256]{1,0:T(8,128)(2,1)S(1)}, bf16[896,256]{1,0:T(8,128)(2,1)S(1)}, u32[]{:S(2)}, u32[]{:S(2)}) %collective-permute-start.7) | collective-permute-done | bytes 458784 | tf_op jit(solution)/shard_map/ppermute | solution.py:29
  73.5 7.8 %collective-permute-done.2.rest_1_ = bf16[1280,256]{1,0:T(8,128)(2,1)S(1)} collective-permute-done((bf16[1280,256]{1,0:T(8,128)(2,1)S(1)}, bf16[1280,256]{1,0:T(8,128)(2,1)S(1)}, u32[]{:S(2)}, u32[]{:S(2)}) %collective-permute-start.2) | collective-permute-done | bytes 655392 | tf_op jit(solution)/shard_map/ppermute | solution.py:29
  82.8 3.7 %collective-permute-start.9 = (bf16[1024,256]{1,0:T(8,128)(2,1)}, bf16[1024,256]{1,0:T(8,128)(2,1)}, u32[]{:S(2)}, u32[]{:S(2)}) collective-permute-start(bf16[1024,256]{1,0:T(8,128)(2,1)} %pad_maximum_fusion), channel_id=1, source_target_pairs={{0,4},{1,5},{2,6},{3,7},{8,12},{9,13},{10,14},{11,15},{16,20},{17,... | collective-permute-start | bytes 1572872 | tf_op jit(solution)/shard_map/ppermute | solution.py:29
  86.5 2.1 collective-permute-start.11
  88.6 2.1 collective-permute-start.8
  90.8 20.8 %collective-permute-done.11 = bf16[896,256]{1,0:T(8,128)(2,1)} collective-permute-done((bf16[896,256]{1,0:T(8,128)(2,1)S(1)}, bf16[896,256]{1,0:T(8,128)(2,1)}, u32[]{:S(2)}, u32[]{:S(2)}) %collective-permute-start.11) | collective-permute-done | bytes 458784 | tf_op jit(solution)/shard_map/ppermute | solution.py:29
  111.8 6.0 %collective-permute-done.12.rest_1_ = bf16[768,256]{1,0:T(8,128)(2,1)S(1)} collective-permute-done((bf16[768,256]{1,0:T(8,128)(2,1)}, bf16[768,256]{1,0:T(8,128)(2,1)S(1)}, u32[]{:S(2)}, u32[]{:S(2)}) %collective-permute-start.12) | collective-permute-done | bytes 393248 | tf_op jit(solution)/shard_map/ppermute | solution.py:29
  117.8 3.2 %collective-permute-start.16 = (bf16[896,256]{1,0:T(8,128)(2,1)S(1)}, bf16[896,256]{1,0:T(8,128)(2,1)S(1)}, u32[]{:S(2)}, u32[]{:S(2)}) collective-permute-start(bf16[896,256]{1,0:T(8,128)(2,1)S(1)} %broadcast_select_fusion.2.rest_4_), channel_id=1, source_target_pairs={{0,1},{1,0},{2,3},{3,2},{4,5},{5,4},{6,7},{7,6},{8,9},{9,8},{10,11... | collective-permute-start | bytes 1376264 | tf_op jit(solution)/shard_map/ppermute | solution.py:29
  121.2 2.0 collective-permute-start.13
  124.1 3.2 %all-to-all-start = ((bf16[4,2,8]{2,1,0:T(2,128)(2,1)}), bf16[4,2,8]{2,1,0:T(2,128)(2,1)S(1)}, u32[]{:S(2)}, u32[]{:S(2)}) async-start(bf16[4,2,8]{2,1,0:T(2,128)(2,1)} %copy.15), calls=%async_computation | async-start | bytes 4096 | tf_op jit(solution)/shard_map/all_to_all | solution.py:348
  127.3 20.6 %collective-permute-done.13.rest_5_ = bf16[640,256]{1,0:T(8,128)(2,1)} collective-permute-done((bf16[640,256]{1,0:T(8,128)(2,1)S(1)}, bf16[640,256]{1,0:T(8,128)(2,1)}, u32[]{:S(2)}, u32[]{:S(2)}) %collective-permute-start.13) | collective-permute-done | bytes 327712 | tf_op jit(solution)/shard_map/ppermute | solution.py:29
  147.9 21.2 %pivot_rows.1 = (f32[3072,384]{1,0:T(8,128)}, bf16[1280,384]{1,0:T(8,128)(2,1)}) custom-call(s32[1]{0:T(128)} %bitcast.member_ref, f32[3072,384]{1,0:T(8,128)} %front.5, bf16[1280,256]{1,0:T(8,128)(2,1)} %copy-done.2, bf16[1280,256]{1,0:T(8,128)(2,1)} %copy-done.8, bf16[1280,256]{1,0:T(8,128)(2,1)} %copy-done.9, bf16[1280,256]{1,0:T(8,128)(2,1)} %copy-done.10, ...), custom_call_target="tpu_custom_call" | custom-call | tf_op jit(solution)/shard_map/pivot_rows/pallas_call | solution.py:238
  170.0 6.9 %tail_rows.1 = (f32[3072,384]{1,0:T(8,128)}, bf16[768,384]{1,0:T(8,128)(2,1)}) custom-call(s32[1]{0:T(128)} %bitcast.member_ref, bf16[1280,384]{1,0:T(8,128)(2,1)} %get-tuple-element.30.w, f32[3072,384]{1,0:T(8,128)} %front.5, f32[3072,384]{1,0:T(8,128)} %get-tuple-element.31.out_in, ...), custom_call_target="tpu_custom_call", output_to_operand_aliasing={{0}: (3, {})} | custom-call | tf_op jit(solution)/shard_map/tail_rows/pallas_call | solution.py:309
  180.1 3.5 %all-to-all-start.1 = ((bf16[4,2,128,384]{3,1,2,0:T(2,128)(2,1)}), bf16[4,2,128,384]{3,1,2,0:T(2,128)(2,1)S(1)}, u32[]{:S(2)}, u32[]{:S(2)}) async-start(bf16[4,2,128,384]{3,1,2,0:T(2,128)(2,1)} %copy.17), calls=%async_computation.1 | async-start | bytes 1572864 | tf_op jit(solution)/shard_map/all_to_all | solution.py:347
  183.6 2.6 %collective-permute-start.17 = (bf16[1024,256]{1,0:T(8,128)(2,1)S(1)}, bf16[1024,256]{1,0:T(8,128)(2,1)S(1)}, u32[]{:S(2)}, u32[]{:S(2)}) collective-permute-start(bf16[1024,256]{1,0:T(8,128)(2,1)S(1)} %broadcast_select_fusion.1.rest_0_), channel_id=1, source_target_pairs={{0,2},{1,3},{2,0},{3,1},{4,6},{5,7},{6,4},{7,5},{8,10},{9,11},{10,... | collective-permute-start | bytes 1572872 | tf_op jit(solution)/shard_map/ppermute | solution.py:29
  186.2 2.0 collective-permute-start.18
  188.2 10.5 %collective-permute-done.17.rest_1_ = bf16[1024,256]{1,0:T(8,128)(2,1)S(1)} collective-permute-done((bf16[1024,256]{1,0:T(8,128)(2,1)S(1)}, bf16[1024,256]{1,0:T(8,128)(2,1)S(1)}, u32[]{:S(2)}, u32[]{:S(2)}) %collective-permute-start.17) | collective-permute-done | bytes 524320 | tf_op jit(solution)/shard_map/ppermute | solution.py:29
  206.0 7.8 %collective-permute-done.19.rest_3_ = bf16[1024,256]{1,0:T(8,128)(2,1)S(1)} collective-permute-done((bf16[1024,256]{1,0:T(8,128)(2,1)S(1)}, bf16[1024,256]{1,0:T(8,128)(2,1)S(1)}, u32[]{:S(2)}, u32[]{:S(2)}) %collective-permute-start.19) | collective-permute-done | bytes 524320 | tf_op jit(solution)/shard_map/ppermute | solution.py:29
  214.5 7.3 %middle_rows.1 = f32[3072,384]{1,0:T(8,128)} custom-call(s32[1]{0:T(128)} %bitcast.member_ref, bf16[1280,384]{1,0:T(8,128)(2,1)} %get-tuple-element.30.w, f32[3072,384]{1,0:T(8,128)} %front.5, f32[3072,384]{1,0:T(8,128)} %get-tuple-element.34.out_in, bf16[1024,256]{1,0:T(8,128)(2,1)} %copy-done.3, ...), custom_call_target="tpu_custom_call", output_to_operand_aliasing={{}: (3, {})} | custom-call | tf_op jit(solution)/shard_map/middle_rows/pallas_call | solution.py:309
  (87 shorter events, 26.4 us)
Async XLA Ops:
  3.6 15.8 %collective-permute-start.1 = (bf16[640,256]{1,0:T(8,128)(2,1)}, bf16[640,256]{1,0:T(8,128)(2,1)}, u32[]{:S(2)}, u32[]{:S(2)}) collective-permute-start(bf16[640,256]{1,0:T(8,128)(2,1)} %slice.42), channel_id=1, source_target_pairs={{4,5},{12,13},{20,21},{28,29}} | collective-permute-start | bytes 983048 | tf_op jit(solution)/shard_map/ppermute | solution.py:29
  6.1 13.3 %collective-permute-start.4 = (bf16[896,256]{1,0:T(8,128)(2,1)}, bf16[896,256]{1,0:T(8,128)(2,1)}, u32[]{:S(2)}, u32[]{:S(2)}) collective-permute-start(bf16[896,256]{1,0:T(8,128)(2,1)} %fusion.1), channel_id=1, source_target_pairs={{4,5},{12,13},{20,21},{28,29}} | collective-permute-start | bytes 1376264 | tf_op jit(solution)/shard_map/ppermute | solution.py:29
  7.6 23.1 %collective-permute-start = (bf16[1280,256]{1,0:T(8,128)(2,1)S(1)}, bf16[1280,256]{1,0:T(8,128)(2,1)}, u32[]{:S(2)}, u32[]{:S(2)}) collective-permute-start(bf16[1280,256]{1,0:T(8,128)(2,1)S(1)} %bitcast.34), channel_id=1, source_target_pairs={{0,4},{1,5},{2,6},{3,7},{8,12},{9,13},{10,14},{11,15},{16,20},{17,... | collective-permute-start | bytes 1966088 | tf_op jit(solution)/shard_map/ppermute | solution.py:29
  30.6 29.7 %collective-permute-start.5 = (bf16[768,256]{1,0:T(8,128)(2,1)S(1)}, bf16[768,256]{1,0:T(8,128)(2,1)S(1)}, u32[]{:S(2)}, u32[]{:S(2)}) collective-permute-start(bf16[768,256]{1,0:T(8,128)(2,1)S(1)} %copy-done.5), channel_id=1, source_target_pairs={{0,4},{1,5},{2,6},{3,7},{8,12},{9,13},{10,14},{11,15},{16,20},{17,... | collective-permute-start | bytes 1179656 | tf_op jit(solution)/shard_map/ppermute | solution.py:29
  36.1 24.2 %collective-permute-start.6 = (bf16[640,256]{1,0:T(8,128)(2,1)S(1)}, bf16[640,256]{1,0:T(8,128)(2,1)S(1)}, u32[]{:S(2)}, u32[]{:S(2)}) collective-permute-start(bf16[640,256]{1,0:T(8,128)(2,1)S(1)} %slice_select_fusion), channel_id=1, source_target_pairs={{4,0},{5,1},{12,8},{13,9},{20,16},{21,17},{28,24},{29,25}} | collective-permute-start | bytes 983048 | tf_op jit(solution)/shard_map/ppermute | solution.py:29
  37.6 43.7 %collective-permute-start.2 = (bf16[1280,256]{1,0:T(8,128)(2,1)S(1)}, bf16[1280,256]{1,0:T(8,128)(2,1)S(1)}, u32[]{:S(2)}, u32[]{:S(2)}) collective-permute-start(bf16[1280,256]{1,0:T(8,128)(2,1)S(1)} %broadcast_select_fusion.rest_0_), channel_id=1, source_target_pairs={{0,2},{1,3},{2,0},{3,1},{4,6},{5,7},{6,4},{7,5},{8,10},{9,11},{10,... | collective-permute-start | bytes 1966088 | tf_op jit(solution)/shard_map/ppermute | solution.py:29
  57.9 23.4 %collective-permute-start.3 = (bf16[1280,256]{1,0:T(8,128)(2,1)S(1)}, bf16[1280,256]{1,0:T(8,128)(2,1)S(1)}, u32[]{:S(2)}, u32[]{:S(2)}) collective-permute-start(bf16[1280,256]{1,0:T(8,128)(2,1)S(1)} %broadcast_select_fusion.rest_0_), channel_id=1, source_target_pairs={{0,1},{1,0},{2,3},{3,2},{4,5},{5,4},{6,7},{7,6},{8,9},{9,8},{10,11... | collective-permute-start | bytes 1966088 | tf_op jit(solution)/shard_map/ppermute | solution.py:29
  59.0 14.5 %collective-permute-start.7 = (bf16[896,256]{1,0:T(8,128)(2,1)S(1)}, bf16[896,256]{1,0:T(8,128)(2,1)S(1)}, u32[]{:S(2)}, u32[]{:S(2)}) collective-permute-start(bf16[896,256]{1,0:T(8,128)(2,1)S(1)} %fusion.2), channel_id=1, source_target_pairs={{4,0},{5,1},{12,8},{13,9},{20,16},{21,17},{28,24},{29,25}} | collective-permute-start | bytes 1376264 | tf_op jit(solution)/shard_map/ppermute | solution.py:29
  81.3 9.4 %collective-permute-start.10 = (bf16[640,256]{1,0:T(8,128)(2,1)S(1)}, bf16[640,256]{1,0:T(8,128)(2,1)S(1)}, u32[]{:S(2)}, u32[]{:S(2)}) collective-permute-start(bf16[640,256]{1,0:T(8,128)(2,1)S(1)} %broadcast_select_fusion.6), channel_id=1, source_target_pairs={{0,2},{1,3},{4,6},{5,7},{8,10},{9,11},{12,14},{13,15},{16,18},{17,... | collective-permute-start | bytes 983048 | tf_op jit(solution)/shard_map/ppermute | solution.py:29
  82.8 28.9 %collective-permute-start.9 = (bf16[1024,256]{1,0:T(8,128)(2,1)}, bf16[1024,256]{1,0:T(8,128)(2,1)}, u32[]{:S(2)}, u32[]{:S(2)}) collective-permute-start(bf16[1024,256]{1,0:T(8,128)(2,1)} %pad_maximum_fusion), channel_id=1, source_target_pairs={{0,4},{1,5},{2,6},{3,7},{8,12},{9,13},{10,14},{11,15},{16,20},{17,... | collective-permute-start | bytes 1572872 | tf_op jit(solution)/shard_map/ppermute | solution.py:29
  86.5 25.1 %collective-permute-start.11 = (bf16[896,256]{1,0:T(8,128)(2,1)S(1)}, bf16[896,256]{1,0:T(8,128)(2,1)}, u32[]{:S(2)}, u32[]{:S(2)}) collective-permute-start(bf16[896,256]{1,0:T(8,128)(2,1)S(1)} %broadcast_select_fusion.3), channel_id=1, source_target_pairs={{0,2},{1,3},{4,6},{5,7},{8,10},{9,11},{12,14},{13,15},{16,18},{17,... | collective-permute-start | bytes 1376264 | tf_op jit(solution)/shard_map/ppermute | solution.py:29
  88.6 29.2 %collective-permute-start.8 = (bf16[1280,256]{1,0:T(8,128)(2,1)}, bf16[1280,256]{1,0:T(8,128)(2,1)S(1)}, u32[]{:S(2)}, u32[]{:S(2)}) collective-permute-start(bf16[1280,256]{1,0:T(8,128)(2,1)} %copy-done.8), channel_id=1, source_target_pairs={{0,1},{1,0},{2,3},{3,2},{4,5},{5,4},{6,7},{7,6},{8,9},{9,8},{10,11... | collective-permute-start | bytes 1966088 | tf_op jit(solution)/shard_map/ppermute | solution.py:29
  90.7 27.0 %collective-permute-start.12 = (bf16[768,256]{1,0:T(8,128)(2,1)}, bf16[768,256]{1,0:T(8,128)(2,1)S(1)}, u32[]{:S(2)}, u32[]{:S(2)}) collective-permute-start(bf16[768,256]{1,0:T(8,128)(2,1)} %broadcast_select_fusion.4.rest_0_), channel_id=1, source_target_pairs={{0,2},{1,3},{2,0},{3,1},{4,6},{5,7},{6,4},{7,5},{8,10},{9,11},{10,... | collective-permute-start | bytes 1179656 | tf_op jit(solution)/shard_map/ppermute | solution.py:29
  111.6 57.4 %copy-start.1 = (bf16[896,256]{1,0:T(8,128)(2,1)}, bf16[896,256]{1,0:T(8,128)(2,1)S(1)}, u32[]{:S(2)}) copy-start(bf16[896,256]{1,0:T(8,128)(2,1)S(1)} %broadcast_select_fusion.2.rest_4_) | copy-start | bytes 1376260
  111.8 74.4 %copy-start.3 = (bf16[1024,256]{1,0:T(8,128)(2,1)}, bf16[1024,256]{1,0:T(8,128)(2,1)S(1)}, u32[]{:S(2)}) copy-start(bf16[1024,256]{1,0:T(8,128)(2,1)S(1)} %broadcast_select_fusion.1.rest_0_) | copy-start | bytes 1572868
  117.8 51.4 %collective-permute-start.16 = (bf16[896,256]{1,0:T(8,128)(2,1)S(1)}, bf16[896,256]{1,0:T(8,128)(2,1)S(1)}, u32[]{:S(2)}, u32[]{:S(2)}) collective-permute-start(bf16[896,256]{1,0:T(8,128)(2,1)S(1)} %broadcast_select_fusion.2.rest_4_), channel_id=1, source_target_pairs={{0,1},{1,0},{2,3},{3,2},{4,5},{5,4},{6,7},{7,6},{8,9},{9,8},{10,11... | collective-permute-start | bytes 1376264 | tf_op jit(solution)/shard_map/ppermute | solution.py:29
  121.1 48.0 %collective-permute-start.14 = (bf16[768,256]{1,0:T(8,128)(2,1)}, bf16[768,256]{1,0:T(8,128)(2,1)S(1)}, u32[]{:S(2)}, u32[]{:S(2)}) collective-permute-start(bf16[768,256]{1,0:T(8,128)(2,1)} %broadcast_select_fusion.4.rest_0_), channel_id=1, source_target_pairs={{0,1},{1,0},{2,3},{3,2},{4,5},{5,4},{6,7},{7,6},{8,9},{9,8},{10,11... | collective-permute-start | bytes 1179656 | tf_op jit(solution)/shard_map/ppermute | solution.py:29
  121.2 26.7 %collective-permute-start.13 = (bf16[640,256]{1,0:T(8,128)(2,1)S(1)}, bf16[640,256]{1,0:T(8,128)(2,1)}, u32[]{:S(2)}, u32[]{:S(2)}) collective-permute-start(bf16[640,256]{1,0:T(8,128)(2,1)S(1)} %broadcast_select_fusion.5.rest_4_), channel_id=1, source_target_pairs={{0,1},{1,0},{2,3},{3,2},{4,5},{5,4},{6,7},{7,6},{8,9},{9,8},{10,11... | collective-permute-start | bytes 983048 | tf_op jit(solution)/shard_map/ppermute | solution.py:29
  123.2 45.9 %collective-permute-start.15 = (bf16[768,256]{1,0:T(8,128)(2,1)S(1)}, bf16[768,256]{1,0:T(8,128)(2,1)}, u32[]{:S(2)}, u32[]{:S(2)}) collective-permute-start(bf16[768,256]{1,0:T(8,128)(2,1)S(1)} %collective-permute-done.12.rest_1_), channel_id=1, source_target_pairs={{0,1},{1,0},{2,3},{3,2},{4,5},{5,4},{6,7},{7,6},{8,9},{9,8},{10,11... | collective-permute-start | bytes 1179656 | tf_op jit(solution)/shard_map/ppermute | solution.py:29
  124.1 56.0 %all-to-all-start = ((bf16[4,2,8]{2,1,0:T(2,128)(2,1)}), bf16[4,2,8]{2,1,0:T(2,128)(2,1)S(1)}, u32[]{:S(2)}, u32[]{:S(2)}) async-start(bf16[4,2,8]{2,1,0:T(2,128)(2,1)} %copy.15), calls=%async_computation | async-start | bytes 4096 | tf_op jit(solution)/shard_map/all_to_all | solution.py:348
  180.1 22.1 %all-to-all-start.1 = ((bf16[4,2,128,384]{3,1,2,0:T(2,128)(2,1)}), bf16[4,2,128,384]{3,1,2,0:T(2,128)(2,1)S(1)}, u32[]{:S(2)}, u32[]{:S(2)}) async-start(bf16[4,2,128,384]{3,1,2,0:T(2,128)(2,1)} %copy.17), calls=%async_computation.1 | async-start | bytes 1572864 | tf_op jit(solution)/shard_map/all_to_all | solution.py:347
  183.6 15.1 %collective-permute-start.17 = (bf16[1024,256]{1,0:T(8,128)(2,1)S(1)}, bf16[1024,256]{1,0:T(8,128)(2,1)S(1)}, u32[]{:S(2)}, u32[]{:S(2)}) collective-permute-start(bf16[1024,256]{1,0:T(8,128)(2,1)S(1)} %broadcast_select_fusion.1.rest_0_), channel_id=1, source_target_pairs={{0,2},{1,3},{2,0},{3,1},{4,6},{5,7},{6,4},{7,5},{8,10},{9,11},{10,... | collective-permute-start | bytes 1572872 | tf_op jit(solution)/shard_map/ppermute | solution.py:29
  186.2 14.2 %collective-permute-start.18 = (bf16[1024,256]{1,0:T(8,128)(2,1)S(1)}, bf16[1024,256]{1,0:T(8,128)(2,1)S(1)}, u32[]{:S(2)}, u32[]{:S(2)}) collective-permute-start(bf16[1024,256]{1,0:T(8,128)(2,1)S(1)} %broadcast_select_fusion.1.rest_0_), channel_id=1, source_target_pairs={{0,1},{1,0},{2,3},{3,2},{4,5},{5,4},{6,7},{7,6},{8,9},{9,8},{10,11... | collective-permute-start | bytes 1572872 | tf_op jit(solution)/shard_map/ppermute | solution.py:29
  200.4 13.3 %collective-permute-start.19 = (bf16[1024,256]{1,0:T(8,128)(2,1)S(1)}, bf16[1024,256]{1,0:T(8,128)(2,1)S(1)}, u32[]{:S(2)}, u32[]{:S(2)}) collective-permute-start(bf16[1024,256]{1,0:T(8,128)(2,1)S(1)} %collective-permute-done.17.rest_1_), channel_id=1, source_target_pairs={{0,1},{1,0},{2,3},{3,2},{4,5},{5,4},{6,7},{7,6},{8,9},{9,8},{10,11... | collective-permute-start | bytes 1572872 | tf_op jit(solution)/shard_map/ppermute | solution.py:29
  (16 other events, 282.3 us)

commit v2 on v1

--- a/solution.py
+++ b/solution.py
@@ -6,6 +6,7 @@
 from jax.experimental import pallas as pl
 from jax.experimental.pallas import tpu as pltpu
 from jax.sharding import PartitionSpec as P
+
 
 P_SIZE = 256
 TICKS = 5
@@ -21,70 +22,35 @@
 VMEM = pl.BlockSpec(memory_space=pltpu.VMEM)
 
 
-def after(values, done):
-    return lax.optimization_barrier((values, done))[0]
-
-
 def permute(value, pairs):
     return lax.ppermute(value, "blk", pairs)
-
-
-def start_halves(own, member):
-    half = own.shape[0] // 2
-    moved = permute(own[half:], [(4, 5)])
-    return jnp.where(member == 5, moved, own[:half])
 
 
 def relay(segments, member):
     across = [(m, m ^ 1) for m in range(8)]
     near = [(m, m ^ 2) for m in range(8)]
     distant = [(m, m + 4) for m in range(4)]
+    beside, back = [(4, 5)], [(4, 0), (5, 1)]
+    spread = [(0, 2), (1, 3), (4, 6), (5, 7)]
     level = member // 2
+
+    def slabs(own):
+        cur = jnp.where(member < 4, own, permute(own, distant))
+        far = permute(cur, near)
+        over = permute(cur, across)
+        return cur, far, over, permute(far, across)
+
+    def halves(own):
+        n = own.shape[0] // 2
+        half = jnp.where(member == 5, permute(own[n:], beside), own[:n])
+        half = jnp.where(level == 0, permute(half, back), half)
+        half = jnp.where(level % 2 == 1, permute(half, spread), half)
+        return half, permute(half, across)
+
     a, b, c = segments
-    rest = jnp.concatenate([b, c], axis=0)
-
-    first = permute(a, distant)
-    half_a = start_halves(a, member)
-    half_n = start_halves(rest, member)
-    cur_a = jnp.where(member < 4, a, first)
-
-    b1, ha, hn = after((b, half_a, half_n), first)
-    cur_a = after(cur_a, half_a)
-    far_a = permute(cur_a, near)
-    over_a = permute(cur_a, across)
-    back_a = permute(ha, [(4, 0), (5, 1)])
-    first_b = permute(b1, distant)
-    back_n = permute(hn, [(4, 0), (5, 1)])
-    ha = jnp.where(level == 0, back_a, half_a)
-    hn = jnp.where(level == 0, back_n, half_n)
-    cur_b = jnp.where(member < 4, b, first_b)
-
-    c1, cur_b, ha, hn, fa = after((c, cur_b, ha, hn, far_a), (far_a, over_a, first_b))
-    spread = [(0, 2), (1, 3), (4, 6), (5, 7)]
-    far_b = permute(cur_b, near)
-    first_c = permute(c1, distant)
-    overfar_a = permute(fa, across)
-    spread_a = permute(ha, spread)
-    over_b = permute(cur_b, across)
-    spread_n = permute(hn, spread)
-    ha = jnp.where(level % 2 == 1, spread_a, ha)
-    hn = jnp.where(level % 2 == 1, spread_n, hn)
-    cur_c = jnp.where(member < 4, c, first_c)
-
-    cur_c, ha, hn, fb = after((cur_c, ha, hn, far_b), (far_b, first_c, overfar_a))
-    overha = permute(ha, across)
-    far_c = permute(cur_c, near)
-    overfar_b = permute(fb, across)
-    overhn = permute(hn, across)
-    over_c = permute(cur_c, across)
-
-    fc = after(far_c, (overfar_b, over_c))
-    overfar_c = permute(fc, across)
-    return (
-        (cur_a, far_a, over_a, overfar_a, ha, overha),
-        (cur_b, far_b, over_b, overfar_b, hn, overhn),
-        (cur_c, far_c, over_c, overfar_c, hn, overhn),
-    )
+    early = halves(jnp.concatenate([a, b], axis=0))
+    late = halves(c)
+    return slabs(a) + early, slabs(b) + early, slabs(c) + late
 
 
 def fetch_relayed(member, refs, target, sems, first_row, total_rows, rows):
@@ -151,13 +117,13 @@
     right = 1.0 / jnp.sum(kept, axis=0, keepdims=True)
     twice = jnp.where(on, 2.0, 0.0)
     inverse = down * (twice - block * right)
-    for step in range(NEWTON - 1):
+    for _ in range(NEWTON - 1):
         inner = twice - jnp.dot(block, inverse, precision=HIGH, preferred_element_type=jnp.float32)
         inverse = jnp.dot(inverse, inner, precision=HIGH, preferred_element_type=jnp.float32)
     return inverse
 
 
-def pivot_kernel(fetch, n_bufs, width, member_ref, front, *rest):
+def pivot_kernel(fetch, n_bufs, width, total_rows, member_ref, front, *rest):
     bufs = rest[:n_bufs]
     out, w_out, raw, mat, own, inv, sems, own_sems = rest[n_bufs:]
     member = member_ref[0]
@@ -170,7 +136,7 @@
     ]
     for load in loads:
         load.start()
-    wait = fetch(member, bufs, raw, sems, 0, rows, rows)
+    wait = fetch(member, bufs, raw, sems, 0, total_rows, rows)
     wait()
     for load in loads:
         load.wait()
@@ -232,11 +198,11 @@
         store.wait()
 
 
-def pivot_rows(fetch, member, front, bufs):
+def pivot_rows(fetch, member, front, bufs, total_rows):
     order, width = front.shape
     p, rows = P_SIZE, TICKS * P_SIZE
     return pl.pallas_call(
-        functools.partial(pivot_kernel, fetch, len(bufs), width),
+        functools.partial(pivot_kernel, fetch, len(bufs), width, total_rows),
         name="pivot_rows",
         out_shape=(
             jax.ShapeDtypeStruct((order, width), jnp.float32),
@@ -375,13 +341,13 @@
     else:
         fetch = fetch_gathered
         sets = tuple((lax.all_gather(s, "blk")[:TICKS],) for s in segments)
-    rest = own_t.shape[0] + own_m.shape[0]
-    out, w = pivot_rows(fetch, holder, front, sets[0])
+    early, late = TICKS * p + tail_n, own_m.shape[0]
+    out, w = pivot_rows(fetch, holder, front, sets[0], early)
     out, cont = other_rows(
-        fetch, holder, w, front, out, sets[1], [(tail_at, 0, tail_n)], 0, rest, True
+        fetch, holder, w, front, out, sets[1], [(tail_at, 0, tail_n)], TICKS * p, early, True
     )
     assembled = assemble(cont, parent_group, row_block, parent_base)
-    (factored,) = other_rows(fetch, holder, w, front, out, sets[2], middle, tail_n, rest, False)
+    (factored,) = other_rows(fetch, holder, w, front, out, sets[2], middle, 0, late, False)
     return (factored, assembled)
 
 

time: 223 us -> 212 us (0.951)
  the two profiles are of different devices: /device:TPU:0 before, /device:TPU:28 now
where the time goes in v2:
time: 212 us; the launch traced here: 211 us
  waiting for transfers between devices  119 us (56%)
  Pallas kernels  35 us (17%)
  starting transfers between devices  28.4 us (13%)
  other arithmetic  15 us (7%)
  local copies, waits for them, and re-layouts  9.77 us (5%)
  matrix products  2.95 us (1%)
    ppermute x20, waiting for transfers between devices, permute(): return lax.ppermute(value, 'blk', pairs)  119 us
    pallas_call x1, Pallas kernels, pivot_rows(): pl.pallas_call(functools.partial(pivot_kernel, fetch, len(bufs), width, t...  20.8 us
    ppermute x20, starting transfers between devices, permute(): return lax.ppermute(value, 'blk', pairs)  20.8 us
    pallas_call x2, Pallas kernels, other_rows(): pl.pallas_call(functools.partial(other_kernel, fetch, len(bufs), ranges,...  14.2 us
    select_n x3, other arithmetic, slabs(): cur = jnp.where(member < 4, own, permute(own, distant))  4.26 us
  transfers between devices with their start and end apart: 22, of which 7 were waited for; matrix products, arithmetic and copies ran while one was open for 9% of the time, Pallas kernels for 17%

profile of v2, /device:TPU:28, one launch (start us, length us, event | category | flops | bytes accessed | tf_op | source)
XLA Modules:
  0.0 211.0 jit_solution(14279646526201408551)
XLA Ops:
  0.6 2.0 slice.67
  4.0 2.6 %convert.12 = bf16[3072,384]{1,0:T(8,128)(2,1)S(1)} convert(f32[3072,384]{1,0:T(8,128)} %front.5) | non-fusion elementwise | flops 1179648 | bytes 7077888 | tf_op jit(solution)/shard_map/convert.5
  8.7 1.8 pad_maximum_fusion.1
  10.6 1.5 collective-permute-start.4
  17.4 38.3 %collective-permute-done = bf16[1280,256]{1,0:T(8,128)(2,1)} collective-permute-done((bf16[1280,256]{1,0:T(8,128)(2,1)S(1)}, bf16[1280,256]{1,0:T(8,128)(2,1)}, u32[]{:S(2)}, u32[]{:S(2)}) %collective-permute-start) | collective-permute-done | bytes 655392 | tf_op jit(solution)/shard_map/ppermute | solution.py:26
  60.9 3.3 %collective-permute-done.8 = bf16[768,256]{1,0:T(8,128)(2,1)} collective-permute-done((bf16[768,256]{1,0:T(8,128)(2,1)}, bf16[768,256]{1,0:T(8,128)(2,1)}, u32[]{:S(2)}, u32[]{:S(2)}) %collective-permute-start.8) | collective-permute-done | bytes 393248 | tf_op jit(solution)/shard_map/ppermute | solution.py:26
  64.3 1.9 broadcast_select_fusion.4.rest_0_
  67.0 22.5 %collective-permute-done.1.rest_1_ = bf16[1280,256]{1,0:T(8,128)(2,1)} collective-permute-done((bf16[1280,256]{1,0:T(8,128)(2,1)S(1)}, bf16[1280,256]{1,0:T(8,128)(2,1)}, u32[]{:S(2)}, u32[]{:S(2)}) %collective-permute-start.1) | collective-permute-done | bytes 655392 | tf_op jit(solution)/shard_map/ppermute | solution.py:26
  89.4 1.5 collective-permute-start.2
  90.9 9.7 %collective-permute-done.6 = bf16[1024,256]{1,0:T(8,128)(2,1)} collective-permute-done((bf16[1024,256]{1,0:T(8,128)(2,1)S(1)}, bf16[1024,256]{1,0:T(8,128)(2,1)}, u32[]{:S(2)}, u32[]{:S(2)}) %collective-permute-start.6) | collective-permute-done | bytes 524320 | tf_op jit(solution)/shard_map/ppermute | solution.py:26
  100.7 1.5 collective-permute-start.3
  105.4 3.7 %all-to-all-start = ((bf16[4,2,8]{2,1,0:T(2,128)(2,1)}), bf16[4,2,8]{2,1,0:T(2,128)(2,1)S(1)}, u32[]{:S(2)}, u32[]{:S(2)}) async-start(bf16[4,2,8]{2,1,0:T(2,128)(2,1)} %copy.15), calls=%async_computation | async-start | bytes 4096 | tf_op jit(solution)/shard_map/all_to_all | solution.py:314
  109.0 1.5 collective-permute-start.10
  112.4 8.8 %collective-permute-done.3.rest_3_ = bf16[1280,256]{1,0:T(8,128)(2,1)} collective-permute-done((bf16[1280,256]{1,0:T(8,128)(2,1)}, bf16[1280,256]{1,0:T(8,128)(2,1)}, u32[]{:S(2)}, u32[]{:S(2)}) %collective-permute-start.3) | collective-permute-done | bytes 655392 | tf_op jit(solution)/shard_map/ppermute | solution.py:26
  122.5 9.8 %collective-permute-done.7.rest_5_ = bf16[1024,256]{1,0:T(8,128)(2,1)S(1)} collective-permute-done((bf16[1024,256]{1,0:T(8,128)(2,1)S(1)}, bf16[1024,256]{1,0:T(8,128)(2,1)S(1)}, u32[]{:S(2)}, u32[]{:S(2)}) %collective-permute-start.7) | collective-permute-done | bytes 524320 | tf_op jit(solution)/shard_map/ppermute | solution.py:26
  133.1 20.8 %pivot_rows.1 = (f32[3072,384]{1,0:T(8,128)}, bf16[1280,384]{1,0:T(8,128)(2,1)}) custom-call(s32[1]{0:T(128)} %bitcast.member_ref, f32[3072,384]{1,0:T(8,128)} %front.5, bf16[1280,256]{1,0:T(8,128)(2,1)} %copy-done.2, bf16[1280,256]{1,0:T(8,128)(2,1)} %collective-permute-done.1.rest_1_, bf16[1280,256]{1,0:T(8,128)(2,1)} %collective-permute-done.2.rest_2_, ...), custom_call_target="tpu_custom_call" | custom-call | tf_op jit(solution)/shard_map/pivot_rows/pallas_call | solution.py:204
  154.0 6.9 %tail_rows.1 = (f32[3072,384]{1,0:T(8,128)}, bf16[768,384]{1,0:T(8,128)(2,1)}) custom-call(s32[1]{0:T(128)} %bitcast.member_ref, bf16[1280,384]{1,0:T(8,128)(2,1)} %get-tuple-element.6.w, f32[3072,384]{1,0:T(8,128)} %front.5, f32[3072,384]{1,0:T(8,128)} %get-tuple-element.7.out_in, ...), custom_call_target="tpu_custom_call", output_to_operand_aliasing={{0}: (3, {})} | custom-call | tf_op jit(solution)/shard_map/tail_rows/pallas_call | solution.py:275
  160.9 1.6 convolution_convert_fusion
  162.6 1.5 copy.17
  164.1 4.0 %all-to-all-start.1 = ((bf16[4,2,128,384]{3,1,2,0:T(2,128)(2,1)}), bf16[4,2,128,384]{3,1,2,0:T(2,128)(2,1)S(1)}, u32[]{:S(2)}, u32[]{:S(2)}) async-start(bf16[4,2,128,384]{3,1,2,0:T(2,128)(2,1)} %copy.17), calls=%async_computation.1 | async-start | bytes 1572864 | tf_op jit(solution)/shard_map/all_to_all | solution.py:313
  168.1 1.5 collective-permute-start.14
  171.1 1.5 collective-permute-start.19
  172.6 26.2 %collective-permute-done.19.rest_5_ = bf16[512,256]{1,0:T(8,128)(2,1)S(1)} collective-permute-done((bf16[512,256]{1,0:T(8,128)(2,1)S(1)}, bf16[512,256]{1,0:T(8,128)(2,1)S(1)}, u32[]{:S(2)}, u32[]{:S(2)}) %collective-permute-start.19) | collective-permute-done | bytes 262176 | tf_op jit(solution)/shard_map/ppermute | solution.py:26
  199.9 7.3 %middle_rows.1 = f32[3072,384]{1,0:T(8,128)} custom-call(s32[1]{0:T(128)} %bitcast.member_ref, bf16[1280,384]{1,0:T(8,128)(2,1)} %get-tuple-element.6.w, f32[3072,384]{1,0:T(8,128)} %front.5, f32[3072,384]{1,0:T(8,128)} %get-tuple-element.8.out_in, bf16[1024,256]{1,0:T(8,128)(2,1)} %copy-done.4, ...), custom_call_target="tpu_custom_call", output_to_operand_aliasing={{}: (3, {})} | custom-call | tf_op jit(solution)/shard_map/middle_rows/pallas_call | solution.py:275
  (87 shorter events, 28.1 us)
Async XLA Ops:
  2.7 53.1 %collective-permute-start = (bf16[1280,256]{1,0:T(8,128)(2,1)S(1)}, bf16[1280,256]{1,0:T(8,128)(2,1)}, u32[]{:S(2)}, u32[]{:S(2)}) collective-permute-start(bf16[1280,256]{1,0:T(8,128)(2,1)S(1)} %bitcast.37), channel_id=1, source_target_pairs={{0,4},{1,5},{2,6},{3,7},{8,12},{9,13},{10,14},{11,15},{16,20},{17,... | collective-permute-start | bytes 1966088 | tf_op jit(solution)/shard_map/ppermute | solution.py:26
  7.4 56.8 %collective-permute-start.8 = (bf16[768,256]{1,0:T(8,128)(2,1)}, bf16[768,256]{1,0:T(8,128)(2,1)}, u32[]{:S(2)}, u32[]{:S(2)}) collective-permute-start(bf16[768,256]{1,0:T(8,128)(2,1)} %slice.52), channel_id=1, source_target_pairs={{0,4},{1,5},{2,6},{3,7},{8,12},{9,13},{10,14},{11,15},{16,20},{17,... | collective-permute-start | bytes 1179656 | tf_op jit(solution)/shard_map/ppermute | solution.py:26
  10.6 6.0 %collective-permute-start.4 = (bf16[1024,256]{1,0:T(8,128)(2,1)}, bf16[1024,256]{1,0:T(8,128)(2,1)}, u32[]{:S(2)}, u32[]{:S(2)}) collective-permute-start(bf16[1024,256]{1,0:T(8,128)(2,1)} %pad_maximum_fusion.1), channel_id=1, source_target_pairs={{4,5},{12,13},{20,21},{28,29}} | collective-permute-start | bytes 1572872 | tf_op jit(solution)/shard_map/ppermute | solution.py:26
  12.8 46.3 %collective-permute-start.16 = (bf16[512,256]{1,0:T(8,128)(2,1)}, bf16[512,256]{1,0:T(8,128)(2,1)}, u32[]{:S(2)}, u32[]{:S(2)}) collective-permute-start(bf16[512,256]{1,0:T(8,128)(2,1)} %fusion.1), channel_id=1, source_target_pairs={{4,5},{12,13},{20,21},{28,29}} | collective-permute-start | bytes 786440 | tf_op jit(solution)/shard_map/ppermute | solution.py:26
  15.0 94.0 %collective-permute-start.12 = (bf16[1024,256]{1,0:T(8,128)(2,1)}, bf16[1024,256]{1,0:T(8,128)(2,1)}, u32[]{:S(2)}, u32[]{:S(2)}) collective-permute-start(bf16[1024,256]{1,0:T(8,128)(2,1)} %pad_maximum_fusion), channel_id=1, source_target_pairs={{0,4},{1,5},{2,6},{3,7},{8,12},{9,13},{10,14},{11,15},{16,20},{17,... | collective-permute-start | bytes 1572872 | tf_op jit(solution)/shard_map/ppermute | solution.py:26
  16.7 40.3 %collective-permute-start.5 = (bf16[1024,256]{1,0:T(8,128)(2,1)S(1)}, bf16[1024,256]{1,0:T(8,128)(2,1)S(1)}, u32[]{:S(2)}, u32[]{:S(2)}) collective-permute-start(bf16[1024,256]{1,0:T(8,128)(2,1)S(1)} %bitcast_select_fusion), channel_id=1, source_target_pairs={{4,0},{5,1},{12,8},{13,9},{20,16},{21,17},{28,24},{29,25}} | collective-permute-start | bytes 1572872 | tf_op jit(solution)/shard_map/ppermute | solution.py:26
  56.9 32.5 %collective-permute-start.1 = (bf16[1280,256]{1,0:T(8,128)(2,1)S(1)}, bf16[1280,256]{1,0:T(8,128)(2,1)}, u32[]{:S(2)}, u32[]{:S(2)}) collective-permute-start(bf16[1280,256]{1,0:T(8,128)(2,1)S(1)} %broadcast_select_fusion.rest_0_), channel_id=1, source_target_pairs={{0,2},{1,3},{2,0},{3,1},{4,6},{5,7},{6,4},{7,5},{8,10},{9,11},{10,... | collective-permute-start | bytes 1966088 | tf_op jit(solution)/shard_map/ppermute | solution.py:26
  57.1 43.6 %collective-permute-start.6 = (bf16[1024,256]{1,0:T(8,128)(2,1)S(1)}, bf16[1024,256]{1,0:T(8,128)(2,1)}, u32[]{:S(2)}, u32[]{:S(2)}) collective-permute-start(bf16[1024,256]{1,0:T(8,128)(2,1)S(1)} %broadcast_select_fusion.2), channel_id=1, source_target_pairs={{0,2},{1,3},{4,6},{5,7},{8,10},{9,11},{12,14},{13,15},{16,18},{17,... | collective-permute-start | bytes 1572872 | tf_op jit(solution)/shard_map/ppermute | solution.py:26
  60.1 44.5 %copy-start.16 = (s32[1,1,6]{2,1,0:T(1,128)S(1)}, s32[1,1,6]{2,1,0:T(1,128)}, u32[]{:S(2)}) copy-start(s32[1,1,6]{2,1,0:T(1,128)} %param.6) | copy-start | bytes 76
  60.1 43.2 %collective-permute-start.17 = (bf16[512,256]{1,0:T(8,128)(2,1)S(1)}, bf16[512,256]{1,0:T(8,128)(2,1)S(1)}, u32[]{:S(2)}, u32[]{:S(2)}) collective-permute-start(bf16[512,256]{1,0:T(8,128)(2,1)S(1)} %bitcast_select_fusion.1), channel_id=1, source_target_pairs={{4,0},{5,1},{12,8},{13,9},{20,16},{21,17},{28,24},{29,25}} | collective-permute-start | bytes 786440 | tf_op jit(solution)/shard_map/ppermute | solution.py:26
  66.2 44.3 %collective-permute-start.9 = (bf16[768,256]{1,0:T(8,128)(2,1)}, bf16[768,256]{1,0:T(8,128)(2,1)}, u32[]{:S(2)}, u32[]{:S(2)}) collective-permute-start(bf16[768,256]{1,0:T(8,128)(2,1)} %broadcast_select_fusion.4.rest_0_), channel_id=1, source_target_pairs={{0,2},{1,3},{2,0},{3,1},{4,6},{5,7},{6,4},{7,5},{8,10},{9,11},{10,... | collective-permute-start | bytes 1179656 | tf_op jit(solution)/shard_map/ppermute | solution.py:26
  89.4 22.8 %collective-permute-start.2 = (bf16[1280,256]{1,0:T(8,128)(2,1)S(1)}, bf16[1280,256]{1,0:T(8,128)(2,1)}, u32[]{:S(2)}, u32[]{:S(2)}) collective-permute-start(bf16[1280,256]{1,0:T(8,128)(2,1)S(1)} %broadcast_select_fusion.rest_0_), channel_id=1, source_target_pairs={{0,1},{1,0},{2,3},{3,2},{4,5},{5,4},{6,7},{7,6},{8,9},{9,8},{10,11... | collective-permute-start | bytes 1966088 | tf_op jit(solution)/shard_map/ppermute | solution.py:26
  100.7 20.5 %collective-permute-start.3 = (bf16[1280,256]{1,0:T(8,128)(2,1)}, bf16[1280,256]{1,0:T(8,128)(2,1)}, u32[]{:S(2)}, u32[]{:S(2)}) collective-permute-start(bf16[1280,256]{1,0:T(8,128)(2,1)} %collective-permute-done.1.rest_1_), channel_id=1, source_target_pairs={{0,1},{1,0},{2,3},{3,2},{4,5},{5,4},{6,7},{7,6},{8,9},{9,8},{10,11... | collective-permute-start | bytes 1966088 | tf_op jit(solution)/shard_map/ppermute | solution.py:26
  104.0 28.3 %collective-permute-start.7 = (bf16[1024,256]{1,0:T(8,128)(2,1)S(1)}, bf16[1024,256]{1,0:T(8,128)(2,1)S(1)}, u32[]{:S(2)}, u32[]{:S(2)}) collective-permute-start(bf16[1024,256]{1,0:T(8,128)(2,1)S(1)} %broadcast_select_fusion.3.rest_4_), channel_id=1, source_target_pairs={{0,1},{1,0},{2,3},{3,2},{4,5},{5,4},{6,7},{7,6},{8,9},{9,8},{10,11... | collective-permute-start | bytes 1572872 | tf_op jit(solution)/shard_map/ppermute | solution.py:26
  105.4 58.7 %all-to-all-start = ((bf16[4,2,8]{2,1,0:T(2,128)(2,1)}), bf16[4,2,8]{2,1,0:T(2,128)(2,1)S(1)}, u32[]{:S(2)}, u32[]{:S(2)}) async-start(bf16[4,2,8]{2,1,0:T(2,128)(2,1)} %copy.15), calls=%async_computation | async-start | bytes 4096 | tf_op jit(solution)/shard_map/all_to_all | solution.py:314
  109.0 44.9 %collective-permute-start.10 = (bf16[768,256]{1,0:T(8,128)(2,1)}, bf16[768,256]{1,0:T(8,128)(2,1)}, u32[]{:S(2)}, u32[]{:S(2)}) collective-permute-start(bf16[768,256]{1,0:T(8,128)(2,1)} %broadcast_select_fusion.4.rest_0_), channel_id=1, source_target_pairs={{0,1},{1,0},{2,3},{3,2},{4,5},{5,4},{6,7},{7,6},{8,9},{9,8},{10,11... | collective-permute-start | bytes 1179656 | tf_op jit(solution)/shard_map/ppermute | solution.py:26
  110.5 43.5 %collective-permute-start.11 = (bf16[768,256]{1,0:T(8,128)(2,1)}, bf16[768,256]{1,0:T(8,128)(2,1)}, u32[]{:S(2)}, u32[]{:S(2)}) collective-permute-start(bf16[768,256]{1,0:T(8,128)(2,1)} %collective-permute-done.9.rest_1_), channel_id=1, source_target_pairs={{0,1},{1,0},{2,3},{3,2},{4,5},{5,4},{6,7},{7,6},{8,9},{9,8},{10,11... | collective-permute-start | bytes 1179656 | tf_op jit(solution)/shard_map/ppermute | solution.py:26
  112.2 55.8 %copy-start.4 = (bf16[1024,256]{1,0:T(8,128)(2,1)}, bf16[1024,256]{1,0:T(8,128)(2,1)S(1)}, u32[]{:S(2)}) copy-start(bf16[1024,256]{1,0:T(8,128)(2,1)S(1)} %broadcast_select_fusion.1.rest_0_) | copy-start | bytes 1572868
  112.2 57.3 %collective-permute-start.13 = (bf16[1024,256]{1,0:T(8,128)(2,1)S(1)}, bf16[1024,256]{1,0:T(8,128)(2,1)S(1)}, u32[]{:S(2)}, u32[]{:S(2)}) collective-permute-start(bf16[1024,256]{1,0:T(8,128)(2,1)S(1)} %broadcast_select_fusion.1.rest_0_), channel_id=1, source_target_pairs={{0,2},{1,3},{2,0},{3,1},{4,6},{5,7},{6,4},{7,5},{8,10},{9,11},{10,... | collective-permute-start | bytes 1572872 | tf_op jit(solution)/shard_map/ppermute | solution.py:26
  121.2 48.9 %collective-permute-start.18 = (bf16[512,256]{1,0:T(8,128)(2,1)S(1)}, bf16[512,256]{1,0:T(8,128)(2,1)}, u32[]{:S(2)}, u32[]{:S(2)}) collective-permute-start(bf16[512,256]{1,0:T(8,128)(2,1)S(1)} %broadcast_select_fusion.5), channel_id=1, source_target_pairs={{0,2},{1,3},{4,6},{5,7},{8,10},{9,11},{12,14},{13,15},{16,18},{17,... | collective-permute-start | bytes 786440 | tf_op jit(solution)/shard_map/ppermute | solution.py:26
  164.1 43.1 %all-to-all-start.1 = ((bf16[4,2,128,384]{3,1,2,0:T(2,128)(2,1)}), bf16[4,2,128,384]{3,1,2,0:T(2,128)(2,1)S(1)}, u32[]{:S(2)}, u32[]{:S(2)}) async-start(bf16[4,2,128,384]{3,1,2,0:T(2,128)(2,1)} %copy.17), calls=%async_computation.1 | async-start | bytes 1572864 | tf_op jit(solution)/shard_map/all_to_all | solution.py:313
  168.1 30.8 %collective-permute-start.14 = (bf16[1024,256]{1,0:T(8,128)(2,1)S(1)}, bf16[1024,256]{1,0:T(8,128)(2,1)S(1)}, u32[]{:S(2)}, u32[]{:S(2)}) collective-permute-start(bf16[1024,256]{1,0:T(8,128)(2,1)S(1)} %broadcast_select_fusion.1.rest_0_), channel_id=1, source_target_pairs={{0,1},{1,0},{2,3},{3,2},{4,5},{5,4},{6,7},{7,6},{8,9},{9,8},{10,11... | collective-permute-start | bytes 1572872 | tf_op jit(solution)/shard_map/ppermute | solution.py:26
  169.5 29.3 %collective-permute-start.15 = (bf16[1024,256]{1,0:T(8,128)(2,1)S(1)}, bf16[1024,256]{1,0:T(8,128)(2,1)S(1)}, u32[]{:S(2)}, u32[]{:S(2)}) collective-permute-start(bf16[1024,256]{1,0:T(8,128)(2,1)S(1)} %collective-permute-done.13.rest_1_), channel_id=1, source_target_pairs={{0,1},{1,0},{2,3},{3,2},{4,5},{5,4},{6,7},{7,6},{8,9},{9,8},{10,11... | collective-permute-start | bytes 1572872 | tf_op jit(solution)/shard_map/ppermute | solution.py:26
  171.1 27.8 %collective-permute-start.19 = (bf16[512,256]{1,0:T(8,128)(2,1)S(1)}, bf16[512,256]{1,0:T(8,128)(2,1)S(1)}, u32[]{:S(2)}, u32[]{:S(2)}) collective-permute-start(bf16[512,256]{1,0:T(8,128)(2,1)S(1)} %broadcast_select_fusion.6.rest_4_), channel_id=1, source_target_pairs={{0,1},{1,0},{2,3},{3,2},{4,5},{5,4},{6,7},{7,6},{8,9},{9,8},{10,11... | collective-permute-start | bytes 786440 | tf_op jit(solution)/shard_map/ppermute | solution.py:26
  (15 other events, 189.0 us)

commit v3 on v2

v3 whole, which is shorter than its diff:
```python
import functools

import jax
import jax.numpy as jnp
from jax import lax
from jax.experimental import pallas as pl
from jax.experimental.pallas import tpu as pltpu
from jax.sharding import PartitionSpec as P


P_SIZE = 256
TICKS = 5
NEWTON = 2
RB = 128
NB = 6
CAP = 2
HIGH = lax.Precision.HIGHEST
ANY = pl.BlockSpec(memory_space=pl.ANY)
SMEM = pl.BlockSpec(memory_space=pltpu.SMEM)
VMEM = pl.BlockSpec(memory_space=pltpu.VMEM)


def permute(value, pairs):
    return lax.ppermute(value, "blk", pairs)


def relay(parts, member):
    across = [(m, m ^ 1) for m in range(8)]
    near = [(m, m ^ 2) for m in range(8)]
    distant = [(m, m + 4) for m in range(4)]
    pairs = [(0, 1), (1, 0), (2, 3), (3, 2)]
    beside, back = [(4, 5)], [(4, 0), (5, 1)]
    spread = [(0, 2), (1, 3), (4, 6), (5, 7)]
    level = member // 2
    a, b, c, e_low, e_high = parts

    def slabs(own):
        cur = jnp.where(member < 4, own, permute(own, distant))
        far = permute(cur, near)
        over = permute(cur, across)
        return cur, far, over, permute(far, across)

    def both_slabs(own):
        both = jnp.stack([own, permute(own, pairs)])
        cur = jnp.where(member < 4, both, permute(both, distant))
        return cur, permute(cur, near)

    def halves(low, high):
        half = jnp.where(member == 5, permute(high, beside), low)
        half = jnp.where(level == 0, permute(half, back), half)
        half = jnp.where(level % 2 == 1, permute(half, spread), half)
        return half, permute(half, across)

    early = halves(e_low, e_high)
    n = c.shape[0] // 2
    late = halves(c[:n], c[n:])
    return (slabs(a), early), (both_slabs(b), early), (slabs(c), late)


def placed_slabs(member, refs):
    x = lax.rem(member, 2)
    even = lax.rem(lax.div(member, 2), 2) == 0
    near, far = jnp.where(even, x, 2 + x), jnp.where(even, 2 + x, x)
    over, overfar = jnp.where(even, 1 - x, 3 - x), jnp.where(even, 3 - x, 1 - x)
    if len(refs) == 2:
        return ((refs[0].at[0], near), (refs[1].at[0], far), (refs[0].at[1], over), (refs[1].at[1], overfar))
    return tuple(zip(refs, (near, far, over, overfar)))


def start_first(member, refs, target, sems):
    if len(refs) == 1:
        copies = [pltpu.make_async_copy(refs[0].at[pl.ds(0, TICKS - 1)], target.at[pl.ds(0, TICKS - 1)], sems.at[0])]
    else:
        copies = [
            pltpu.make_async_copy(ref, target.at[slab], sems.at[i])
            for i, (ref, slab) in enumerate(placed_slabs(member, refs))
        ]
    for copy in copies:
        copy.start()
    return copies


def start_last(member, refs, target, sems, first_row, rows):
    if len(refs) == 1:
        copies = [pltpu.make_async_copy(refs[0].at[TICKS - 1], target, sems.at[0])]
        copies[0].start()
        return copies
    half, overhalf = refs
    x = lax.rem(member, 2)
    split = half.shape[0]
    low = max(0, min(rows, split - first_row))
    pieces = []
    if low:
        pieces.append((0, first_row, 0, low))
    if rows - low:
        pieces.append((1, first_row + low - split, low, rows - low))

    def copy(ref, number):
        _, source, to, count = pieces[number]
        return pltpu.make_async_copy(
            ref.at[pl.ds(source, count)], target.at[pl.ds(to, count)], sems.at[number]
        )

    for which in (0, 1):

        @pl.when(x == which)
        def _(which=which):
            for number, piece in enumerate(pieces):
                copy(half if piece[0] == which else overhalf, number).start()

    return [copy(half, number) for number in range(len(pieces))]


def wait_all(copies):
    for copy in copies:
        copy.wait()


def pack_kernel(pieces, front, *rest):
    outs, (held, sems) = rest[: len(pieces)], rest[len(pieces) :]
    copies, at = [], 0
    for ranges in pieces:
        for start, count in ranges:
            copies.append(
                pltpu.make_async_copy(
                    front.at[pl.ds(start, count), pl.ds(0, P_SIZE)], held.at[pl.ds(at, count), :], sems.at[len(copies)]
                )
            )
            copies[-1].start()
            at += count
    at, number = 0, 0
    for ranges, out in zip(pieces, outs):
        to = 0
        for _, count in ranges:
            copies[number].wait()
            out[pl.ds(to, count), :] = held[pl.ds(at, count), :].astype(jnp.bfloat16)
            at, to, number = at + count, to + count, number + 1


def pack(front, pieces):
    sizes = [sum(n for _, n in ranges) for ranges in pieces]
    return pl.pallas_call(
        functools.partial(pack_kernel, pieces),
        out_shape=tuple(jax.ShapeDtypeStruct((n, P_SIZE), jnp.bfloat16) for n in sizes),
        in_specs=[ANY],
        out_specs=(VMEM,) * len(sizes),
        scratch_shapes=[
            pltpu.VMEM((sum(sizes), P_SIZE), jnp.float32),
            pltpu.SemaphoreType.DMA((sum(len(r) for r in pieces),)),
        ],
    )(front)


def diagonal_inverse(block):
    size = block.shape[0]
    row = lax.broadcasted_iota(jnp.int32, (size, size), 0)
    col = lax.broadcasted_iota(jnp.int32, (size, size), 1)
    on = row == col
    kept = jnp.where(on, block, 0.0)
    down = 1.0 / jnp.sum(kept, axis=1, keepdims=True)
    right = 1.0 / jnp.sum(kept, axis=0, keepdims=True)
    twice = jnp.where(on, 2.0, 0.0)
    inverse = down * (twice - block * right)
    for _ in range(NEWTON - 1):
        inner = twice - jnp.dot(block, inverse, precision=HIGH, preferred_element_type=jnp.float32)
        inverse = jnp.dot(inverse, inner, precision=HIGH, preferred_element_type=jnp.float32)
    return inverse


def minus_dot(value, left, right):
    return value - jnp.dot(left, right, preferred_element_type=jnp.float32)


def pivot_kernel(n_bufs, width, member_ref, front, *rest):
    bufs = rest[:n_bufs]
    out, low_up, inv, own, raw, mat, sems, own_sems = rest[n_bufs:]
    member = member_ref[0]
    p = P_SIZE
    copies = start_first(member, bufs, raw, sems)
    loads = [
        pltpu.make_async_copy(
            front.at[pl.ds(t * width, p), :], own.at[pl.ds(t * p, p), :], own_sems.at[t]
        )
        for t in range(TICKS)
    ]
    for load in loads:
        load.start()
    wait_all(copies)
    for s in range(TICKS - 1):
        mat[s] = raw[s].astype(jnp.float32)
    wait_all(loads)
    for t in range(TICKS - 1):
        lo, below = t * p, (t + 1) * p
        x = diagonal_inverse(mat[t, lo:below, :])
        inv[t] = x
        mult = jnp.dot(mat[t, below:, :], x, precision=HIGH, preferred_element_type=jnp.float32)
        panel = mult.astype(jnp.bfloat16)
        low_up[t, below:, :] = panel
        for s in range(t + 1, TICKS - 1):
            urows = mat[s, lo:below, :].astype(jnp.bfloat16)
            low_up[s, lo:below, :] = urows
            mat[s, below:, :] = minus_dot(mat[s, below:, :], panel, urows)
        urows = own[lo:below, :].astype(jnp.bfloat16)
        own[below:, p:] = minus_dot(own[below:, p:], panel, urows[:, p:])

        @pl.when((member >= TICKS) | (member > t))
        def _():
            own[below:, :p] = minus_dot(own[below:, :p], panel, urows[:, :p])

        @pl.when(member == t)
        def _():
            own[below:, :p] = jnp.dot(
                own[below:, :p], x, precision=HIGH, preferred_element_type=jnp.float32
            )

    stores = [
        pltpu.make_async_copy(
            own.at[pl.ds(t * p, p), :], out.at[pl.ds(t * width, p), :], own_sems.at[t]
        )
        for t in range(TICKS)
    ]
    for store in stores:
        store.start()
    wait_all(stores)


def pivot_rows(member, front, bufs):
    order, width = front.shape
    p, rows = P_SIZE, TICKS * P_SIZE
    return pl.pallas_call(
        functools.partial(pivot_kernel, len(bufs), width),
        name="pivot_rows",
        out_shape=(
            jax.ShapeDtypeStruct((order, width), jnp.float32),
            jax.ShapeDtypeStruct((TICKS - 1, rows, p), jnp.bfloat16),
            jax.ShapeDtypeStruct((TICKS - 1, p, p), jnp.float32),
            jax.ShapeDtypeStruct((rows, width), jnp.float32),
        ),
        in_specs=[SMEM, ANY] + [ANY] * len(bufs),
        out_specs=(ANY, VMEM, VMEM, VMEM),
        scratch_shapes=[
            pltpu.VMEM((TICKS - 1, rows, p), jnp.bfloat16),
            pltpu.VMEM((TICKS - 1, rows, p), jnp.float32),
            pltpu.SemaphoreType.DMA((4,)),
            pltpu.SemaphoreType.DMA((TICKS,)),
        ],
    )(member, front, *bufs)


def solve_kernel(n_bufs, member_ref, low_up, inv, own, *rest):
    bufs = rest[:n_bufs]
    w_out, raw, mat, sems = rest[n_bufs:]
    member = member_ref[0]
    p, rows, width = P_SIZE, own.shape[0], own.shape[1]
    copies = start_last(member, bufs, raw, sems, 0, rows)
    wait_all(copies)
    mat[...] = raw[...].astype(jnp.float32)
    last = TICKS - 1
    for t in range(last):
        lo, below = t * p, (t + 1) * p
        mat[below:, :] = minus_dot(mat[below:, :], low_up[t, below:, :], mat[lo:below, :].astype(jnp.bfloat16))
    x_last = diagonal_inverse(mat[last * p :, :])
    row = lax.broadcasted_iota(jnp.int32, (p, width), 0)
    col = lax.broadcasted_iota(jnp.int32, (p, width), 1)
    owner = (member < TICKS) & (col < p)
    for t in reversed(range(TICKS)):
        lo, hi = t * p, (t + 1) * p
        unit = jnp.where((row == col) & (member == t), -1.0, 0.0)
        side = jnp.where(owner, unit, own[lo:hi, :])
        for s in range(t + 1, TICKS):
            urows = mat[lo:hi, :].astype(jnp.bfloat16) if s == last else low_up[s, lo:hi, :]
            side = minus_dot(side, urows, w_out[s * p : (s + 1) * p, :])
        x = x_last if t == last else inv[t]
        w_out[lo:hi, :] = jnp.dot(x, side, precision=HIGH, preferred_element_type=jnp.float32).astype(
            jnp.bfloat16
        )


def solve(member, low_up, inv, own, bufs):
    rows, width = own.shape
    return pl.pallas_call(
        functools.partial(solve_kernel, len(bufs)),
        name="solve",
        out_shape=jax.ShapeDtypeStruct((rows, width), jnp.bfloat16),
        in_specs=[SMEM, VMEM, VMEM, VMEM] + [ANY] * len(bufs),
        out_specs=VMEM,
        scratch_shapes=[
            pltpu.VMEM((rows, P_SIZE), jnp.bfloat16),
            pltpu.VMEM((rows, P_SIZE), jnp.float32),
            pltpu.SemaphoreType.DMA((2,)),
        ],
    )(member, low_up, inv, own, *bufs)


def other_kernel(counts, ranges, first_row, tail, member_ref, dest_ref, slot_ref, w, front, out_in, *rest):
    firsts, lasts = rest[: counts[0]], rest[counts[0] : sum(counts)]
    if tail:
        out, outgoing, raw, base, sems, last_sems, base_sems = rest[sum(counts) :]
    else:
        out, raw, base, sems, last_sems, base_sems = rest[sum(counts) :]
    member = member_ref[0]
    rows, width = base.shape
    copies = start_first(member, firsts, raw, sems)
    copies += start_last(member, lasts, raw.at[TICKS - 1], last_sems, first_row, rows)
    loads = [
        pltpu.make_async_copy(front.at[pl.ds(src, n), :], base.at[pl.ds(dst, n), :], base_sems.at[i])
        for i, (src, dst, n) in enumerate(ranges)
    ]
    for load in loads:
        load.start()
    wait_all(copies)
    wait_all(loads)
    keep = (member >= TICKS) | (lax.broadcasted_iota(jnp.int32, (RB, width), 1) >= P_SIZE)

    def tile(i, carry):
        at = pl.ds(pl.multiple_of(i * RB, RB), RB)
        total = jnp.where(keep, base[at, :], 0.0)
        for s in range(TICKS):
            total = minus_dot(total, raw[s, at, :], w[s * P_SIZE : (s + 1) * P_SIZE, :])
        base[at, :] = total
        if tail:
            outgoing[dest_ref[i], slot_ref[i]] = jnp.where(keep, total, 0.0).astype(jnp.bfloat16)
        return carry

    lax.fori_loop(0, rows // RB, tile, 0)
    stores = [
        pltpu.make_async_copy(base.at[pl.ds(dst, n), :], out.at[pl.ds(src, n), :], base_sems.at[i])
        for i, (src, dst, n) in enumerate(ranges)
    ]
    for store in stores:
        store.start()
    wait_all(stores)


def other_rows(member, dest, slot, w, front, out, bufs, ranges, first_row, groups=0):
    order, width = front.shape
    rows = sum(n for _, _, n in ranges)
    shapes = [jax.ShapeDtypeStruct((order, width), jnp.float32)]
    specs = [ANY]
    if groups:
        shapes.append(jax.ShapeDtypeStruct((groups, CAP, RB, width), jnp.bfloat16))
        specs.append(VMEM)
    counts = tuple(len(b) for b in bufs)
    return pl.pallas_call(
        functools.partial(other_kernel, counts, ranges, first_row, bool(groups)),
        name="tail_rows" if groups else "middle_rows",
        out_shape=tuple(shapes),
        in_specs=[SMEM, SMEM, SMEM, VMEM, ANY, ANY] + [ANY] * sum(counts),
        out_specs=tuple(specs),
        input_output_aliases={5: 0},
        scratch_shapes=[
            pltpu.VMEM((TICKS, rows, P_SIZE), jnp.bfloat16),
            pltpu.VMEM((rows, width), jnp.float32),
            pltpu.SemaphoreType.DMA((4,)),
            pltpu.SemaphoreType.DMA((2,)),
            pltpu.SemaphoreType.DMA((len(ranges),)),
        ],
    )(member, dest, slot, w, front, out, *bufs[0], *bufs[1])


def routes(parent_group, row_block):
    groups = lax.axis_size("front")
    dest = parent_group.reshape(NB)
    target = row_block.reshape(NB)
    number = jnp.arange(NB)
    earlier = (dest[None, :] == dest[:, None]) & (number[None, :] < number[:, None])
    slot = jnp.sum(earlier.astype(jnp.int32), axis=1)
    pick = (dest[None, None, :] == jnp.arange(groups, dtype=jnp.int32)[:, None, None]) & (
        slot[None, None, :] == jnp.arange(CAP, dtype=jnp.int32)[None, :, None]
    )
    address = jnp.sum(jnp.where(pick, target[None, None, :] + 1, 0), axis=2) - 1
    received = lax.all_to_all(address, "front", split_axis=0, concat_axis=0, tiled=True)
    return dest, slot, received.reshape(groups * CAP)


def add_kernel(address_ref, incoming, base, out):
    out[...] = base[...]
    for i in range(incoming.shape[0]):
        to = address_ref[i]

        @pl.when(to >= 0)
        def _(i=i, to=to):
            at = pl.ds(pl.multiple_of(to * RB, RB), RB)
            out[at, :] = out[at, :] + incoming[i].astype(jnp.float32)


def add_blocks(address, incoming, parent_base):
    groups, cap, rows, width = incoming.shape
    return pl.pallas_call(
        add_kernel,
        name="add_blocks",
        out_shape=jax.ShapeDtypeStruct(parent_base.shape, parent_base.dtype),
        in_specs=[SMEM, VMEM, VMEM],
        out_specs=VMEM,
    )(address, incoming.reshape(groups * cap, rows, width), parent_base)


def local(front, parent_group, row_block, parent_base):
    order, width = front.shape
    member = lax.axis_index("blk")
    holder = member.reshape(1).astype(jnp.int32)
    p, top = P_SIZE, TICKS * width
    tail_n = NB * RB
    tail_at = order - tail_n
    pivot_ranges = [(t * width, p) for t in range(TICKS)]
    tail_ranges = [(tail_at, tail_n)]
    middle_ranges = [(t * width + p, width - p) for t in range(TICKS)]
    if tail_at > top:
        middle_ranges.append((top, tail_at - top))
    middle, at = [], 0
    for start, count in middle_ranges:
        middle.append((start, at, count))
        at += count
    (own_p,) = pack(front, [pivot_ranges])
    if lax.axis_size("blk") == 8:
        own_t, e_high, own_m = pack(front, [tail_ranges, pivot_ranges[TICKS - 1 :] + tail_ranges, middle_ranges])
        sets = relay((own_p, own_t, own_m, own_p[: (TICKS - 1) * p], e_high), member)
    else:
        own_t, own_m = pack(front, [tail_ranges, middle_ranges])
        sets = tuple(((lax.all_gather(s, "blk")[:TICKS],),) * 2 for s in (own_p, own_t, own_m))
    dest, slot, address = routes(parent_group, row_block)
    out, low_up, inv, own = pivot_rows(holder, front, sets[0][0])
    w = solve(holder, low_up, inv, own, sets[0][1])
    out, outgoing = other_rows(
        holder, dest, slot, w, front, out, sets[1], [(tail_at, 0, tail_n)], TICKS * p, lax.axis_size("front")
    )
    incoming = lax.all_to_all(outgoing, "front", split_axis=0, concat_axis=0, tiled=True)
    (factored,) = other_rows(holder, dest, slot, w, front, out, sets[2], middle, 0)
    assembled = add_blocks(address, incoming, parent_base)
    return (factored, assembled)


def solution(mesh):
    placed = (
        P("front", "blk"),
        P("front", "blk", None, None),
        P("front", "blk", None),
        P("front", "blk"),
    )
    return jax.shard_map(
        local,
        mesh=mesh,
        in_specs=placed,
        out_specs=(P("front", "blk"), P("front", "blk")),
        check_vma=False,
    )
```

time: 212 us -> 220 us (1.038)
  Pallas kernels: 35 us -> 50.8 us
  waiting for transfers between devices: 119 us -> 126 us
  other arithmetic: 15 us -> 8.93 us
  matrix products: 2.95 us -> 0 us
  local copies, waits for them, and re-layouts: 9.77 us -> 6.95 us
  starting transfers between devices: 28.4 us -> 25.8 us
    pallas_call x3 -> x7, Pallas kernels: 35 us -> 50.8 us  [the longest x1 17.8 us: pivot_rows(): pl.pallas_call(functools.partial(pivot_kernel, len(bufs), width), name='p...]
    ppermute x20 -> x19, waiting for transfers between devices: 119 us -> 126 us  [permute(): return lax.ppermute(value, 'blk', pairs)]
    concatenate x3 -> x0, other arithmetic: 3.37 us -> none  [the longest x1 1.82 us: relay(): early = halves(jnp.concatenate([a, b], axis=0))]
    dot_general x3 -> x0, matrix products: 2.95 us -> none  [the longest x1 1.64 us: assemble(): jnp.einsum('gci,irk->gcrk', pick, cont, preferred_element_type=jnp.float32)]
    ppermute x20 -> x19, starting transfers between devices: 20.8 us -> 18.1 us  [permute(): return lax.ppermute(value, 'blk', pairs)]
  transfers between devices with their start and end apart: 22 -> 21, of which waited for: 7 -> 7; matrix products, arithmetic and copies ran while one was open for 9% -> 6% of each run, Pallas kernels for 17% -> 21%
where the time goes in v3:
time: 220 us; the launch traced here: 219 us
  waiting for transfers between devices  126 us (57%)
  Pallas kernels  50.8 us (23%)
  starting transfers between devices  25.8 us (12%)
  other arithmetic  8.93 us (4%)
  local copies, waits for them, and re-layouts  6.95 us (3%)
    ppermute x19, waiting for transfers between devices, permute(): return lax.ppermute(value, 'blk', pairs)  126 us
    ppermute x19, starting transfers between devices, permute(): return lax.ppermute(value, 'blk', pairs)  18.1 us
    pallas_call x1, Pallas kernels, pivot_rows(): pl.pallas_call(functools.partial(pivot_kernel, len(bufs), width), name='p...  17.8 us
    pallas_call x2, Pallas kernels, other_rows(): pl.pallas_call(functools.partial(other_kernel, counts, ranges, first_row,...  14.3 us
    pallas_call x1, Pallas kernels, solve(): pl.pallas_call(functools.partial(solve_kernel, len(bufs)), name='solve',...  10.7 us
    pallas_call x2, Pallas kernels, pack(): pl.pallas_call(functools.partial(pack_kernel, pieces), out_shape=tuple((j...  5.07 us
  transfers between devices with their start and end apart: 21, of which 7 were waited for; matrix products, arithmetic and copies ran while one was open for 6% of the time, Pallas kernels for 21%

profile of v3, /device:TPU:28, one launch (start us, length us, event | category | flops | bytes accessed | tf_op | source)
XLA Modules:
  0.0 219.1 jit_solution(9898897675858798954)
XLA Ops:
  0.7 2.2 shard_map.59
  2.8 1.4 collective-permute-start
  4.3 2.9 %shard_map.60 = (bf16[768,256]{1,0:T(8,128)(2,1)}, bf16[1024,256]{1,0:T(8,128)(2,1)}, bf16[1024,256]{1,0:T(8,128)(2,1)}) custom-call(f32[3072,384]{1,0:T(8,128)} %front.9), custom_call_target="tpu_custom_call" | custom-call | tf_op jit(solution)/shard_map/pallas_call | solution.py:142
  10.0 1.7 slice.10
  11.7 1.4 collective-permute-start.15
  13.3 2.1 pad_maximum_fusion
  17.5 47.2 %collective-permute-done = bf16[1280,256]{1,0:T(8,128)(2,1)} collective-permute-done((bf16[1280,256]{1,0:T(8,128)(2,1)}, bf16[1280,256]{1,0:T(8,128)(2,1)}, u32[]{:S(2)}, u32[]{:S(2)}) %collective-permute-start) | collective-permute-done | bytes 655392 | tf_op jit(solution)/shard_map/ppermute | solution.py:24
  68.2 24.5 %collective-permute-done.9 = bf16[2,768,256]{2,1,0:T(8,128)(2,1)} collective-permute-done((bf16[2,768,256]{2,1,0:T(8,128)(2,1)}, bf16[2,768,256]{2,1,0:T(8,128)(2,1)}, u32[]{:S(2)}, u32[]{:S(2)}) %collective-permute-start.9) | collective-permute-done | bytes 786464 | tf_op jit(solution)/shard_map/ppermute | solution.py:24
  92.8 1.5 collective-permute-start.2
  95.6 11.2 %collective-permute-done.1.rest_1_ = bf16[1280,256]{1,0:T(8,128)(2,1)} collective-permute-done((bf16[1280,256]{1,0:T(8,128)(2,1)S(1)}, bf16[1280,256]{1,0:T(8,128)(2,1)}, u32[]{:S(2)}, u32[]{:S(2)}) %collective-permute-start.1) | collective-permute-done | bytes 655392 | tf_op jit(solution)/shard_map/ppermute | solution.py:24
  106.8 11.2 %collective-permute-done.6 = bf16[1024,256]{1,0:T(8,128)(2,1)} collective-permute-done((bf16[1024,256]{1,0:T(8,128)(2,1)S(1)}, bf16[1024,256]{1,0:T(8,128)(2,1)}, u32[]{:S(2)}, u32[]{:S(2)}) %collective-permute-start.6) | collective-permute-done | bytes 524320 | tf_op jit(solution)/shard_map/ppermute | solution.py:24
  118.0 1.5 collective-permute-start.3
  125.4 3.6 %all-to-all-start = ((s32[4,1,2]{2,1,0:T(1,128)}), s32[4,1,2]{2,1,0:T(1,128)S(1)}, u32[]{:S(2)}, u32[]{:S(2)}) async-start(s32[4,1,2]{2,1,0:T(1,128)} %copy.11), calls=%async_computation | async-start | bytes 4096 | tf_op jit(solution)/shard_map/all_to_all | solution.py:372
  129.0 6.9 %collective-permute-done.3.rest_3_ = bf16[1280,256]{1,0:T(8,128)(2,1)} collective-permute-done((bf16[1280,256]{1,0:T(8,128)(2,1)}, bf16[1280,256]{1,0:T(8,128)(2,1)}, u32[]{:S(2)}, u32[]{:S(2)}) %collective-permute-start.3) | collective-permute-done | bytes 655392 | tf_op jit(solution)/shard_map/ppermute | solution.py:24
  136.0 17.8 %pivot_rows.1 = (f32[3072,384]{1,0:T(8,128)}, bf16[4,1280,256]{2,1,0:T(8,128)(2,1)}, f32[4,256,256]{2,1,0:T(8,128)}, f32[1280,384]{1,0:T(8,128)}) custom-call(s32[1]{0:T(128)} %bitcast.member_ref, f32[3072,384]{1,0:T(8,128)} %front.9, bf16[1280,256]{1,0:T(8,128)(2,1)} %copy-done.4, bf16[1280,256]{1,0:T(8,128)(2,1)} %collective-permute-done.1.rest_1_, ...), custom_call_target="tpu_custom_call" | custom-call | tf_op jit(solution)/shard_map/pivot_rows/pallas_call | solution.py:230
  154.6 10.7 %solve.1.w = bf16[1280,384]{1,0:T(8,128)(2,1)} custom-call(s32[1]{0:T(128)} %bitcast.member_ref, bf16[4,1280,256]{2,1,0:T(8,128)(2,1)} %get-tuple-element.11.low_up, f32[4,256,256]{2,1,0:T(8,128)} %get-tuple-element.12.inv, f32[1280,384]{1,0:T(8,128)} %get-tuple-element.13.own, bf16[1024,256]{1,0:T(8,128)(2,1)} %copy-done.1, bf16[1024,256]{1,0:T(8,128)(2,1)} %copy-done.6), custom_call_target="tpu_custom_call" | custom-call | tf_op jit(solution)/shard_map/solve/pallas_call | solution.py:281
  165.2 7.0 %tail_rows.1 = (f32[3072,384]{1,0:T(8,128)}, bf16[4,2,128,384]{3,2,1,0:T(8,128)(2,1)}) custom-call(s32[1]{0:T(128)} %bitcast.member_ref, s32[6]{0:T(128)} %bitcast.14, s32[6]{0:T(128)} %copy-done.16, bf16[1280,384]{1,0:T(8,128)(2,1)} %solve.1.w, f32[3072,384]{1,0:T(8,128)} %front.9, ...), custom_call_target="tpu_custom_call", output_to_operand_aliasing={{0}: (5, {})} | custom-call | tf_op jit(solution)/shard_map/tail_rows/pallas_call | solution.py:344
  172.2 4.0 %all-to-all-start.1 = ((bf16[4,2,128,384]{3,2,1,0:T(8,128)(2,1)}), bf16[4,2,128,384]{3,2,1,0:T(8,128)(2,1)S(1)}, u32[]{:S(2)}, u32[]{:S(2)}) async-start(bf16[4,2,128,384]{3,2,1,0:T(8,128)(2,1)} %get-tuple-element.19), calls=%async_computation.1 | async-start | bytes 1572864 | tf_op jit(solution)/shard_map/all_to_all | solution.py:427
  176.2 1.5 collective-permute-start.13
  179.3 1.5 collective-permute-start.18
  182.6 8.4 %collective-permute-done.13.rest_2_ = bf16[1024,256]{1,0:T(8,128)(2,1)S(1)} collective-permute-done((bf16[1024,256]{1,0:T(8,128)(2,1)S(1)}, bf16[1024,256]{1,0:T(8,128)(2,1)S(1)}, u32[]{:S(2)}, u32[]{:S(2)}) %collective-permute-start.13) | collective-permute-done | bytes 524320 | tf_op jit(solution)/shard_map/ppermute | solution.py:24
  191.0 16.0 %collective-permute-done.18.rest_5_ = bf16[512,256]{1,0:T(8,128)(2,1)S(1)} collective-permute-done((bf16[512,256]{1,0:T(8,128)(2,1)S(1)}, bf16[512,256]{1,0:T(8,128)(2,1)S(1)}, u32[]{:S(2)}, u32[]{:S(2)}) %collective-permute-start.18) | collective-permute-done | bytes 262176 | tf_op jit(solution)/shard_map/ppermute | solution.py:24
  207.9 7.3 %middle_rows.1 = f32[3072,384]{1,0:T(8,128)} custom-call(s32[1]{0:T(128)} %bitcast.member_ref, s32[6]{0:T(128)} %bitcast.15, s32[6]{0:T(128)} %copy-done.16, bf16[1280,384]{1,0:T(8,128)(2,1)} %solve.1.w, f32[3072,384]{1,0:T(8,128)} %front.9, f32[3072,384]{1,0:T(8,128)} %get-tuple-element.17.out_in, ...), custom_call_target="tpu_custom_call", output_to_operand_aliasing={{}: (5, {})} | custom-call | tf_op jit(solution)/shard_map/middle_rows/pallas_call | solution.py:344
  216.1 3.0 %add_blocks.1 = f32[1024,384]{1,0:T(8,128)} custom-call(s32[8]{0:T(128)} %reshape.81.address_ref, bf16[8,128,384]{2,1,0:T(8,128)(2,1)} %bitcast.9, f32[1024,384]{1,0:T(8,128)} %base.1), custom_call_target="tpu_custom_call" | custom-call | tf_op jit(solution)/shard_map/add_blocks/pallas_call | solution.py:389
  (82 shorter events, 21.5 us)
Async XLA Ops:
  2.8 61.8 %collective-permute-start = (bf16[1280,256]{1,0:T(8,128)(2,1)}, bf16[1280,256]{1,0:T(8,128)(2,1)}, u32[]{:S(2)}, u32[]{:S(2)}) collective-permute-start(bf16[1280,256]{1,0:T(8,128)(2,1)} %shard_map.59), channel_id=1, source_target_pairs={{0,4},{1,5},{2,6},{3,7},{8,12},{9,13},{10,14},{11,15},{16,20},{17,... | collective-permute-start | bytes 1966088 | tf_op jit(solution)/shard_map/ppermute | solution.py:24
  7.2 87.1 %copy-start.8 = (bf16[768,256]{1,0:T(8,128)(2,1)S(1)}, bf16[768,256]{1,0:T(8,128)(2,1)}, u32[]{:S(2)}) copy-start(bf16[768,256]{1,0:T(8,128)(2,1)} %get-tuple-element.16) | copy-start | bytes 1179652
  7.2 9.5 %collective-permute-start.4 = (bf16[1024,256]{1,0:T(8,128)(2,1)}, bf16[1024,256]{1,0:T(8,128)(2,1)S(1)}, u32[]{:S(2)}, u32[]{:S(2)}) collective-permute-start(bf16[1024,256]{1,0:T(8,128)(2,1)} %get-tuple-element.14), channel_id=1, source_target_pairs={{4,5},{12,13},{20,21},{28,29}} | collective-permute-start | bytes 1572872 | tf_op jit(solution)/shard_map/ppermute | solution.py:24
  8.0 5.3 %collective-permute-start.8 = (bf16[768,256]{1,0:T(8,128)(2,1)}, bf16[768,256]{1,0:T(8,128)(2,1)S(1)}, u32[]{:S(2)}, u32[]{:S(2)}) collective-permute-start(bf16[768,256]{1,0:T(8,128)(2,1)} %get-tuple-element.16), channel_id=1, source_target_pairs={{0,1},{1,0},{2,3},{3,2},{8,9},{9,8},{10,11},{11,10},{16,17},{17,16... | collective-permute-start | bytes 1179656 | tf_op jit(solution)/shard_map/ppermute | solution.py:24
  8.7 111.9 %collective-permute-start.11 = (bf16[1024,256]{1,0:T(8,128)(2,1)}, bf16[1024,256]{1,0:T(8,128)(2,1)}, u32[]{:S(2)}, u32[]{:S(2)}) collective-permute-start(bf16[1024,256]{1,0:T(8,128)(2,1)} %get-tuple-element.18), channel_id=1, source_target_pairs={{0,4},{1,5},{2,6},{3,7},{8,12},{9,13},{10,14},{11,15},{16,20},{17,... | collective-permute-start | bytes 1572872 | tf_op jit(solution)/shard_map/ppermute | solution.py:24
  11.7 55.8 %collective-permute-start.15 = (bf16[512,256]{1,0:T(8,128)(2,1)}, bf16[512,256]{1,0:T(8,128)(2,1)}, u32[]{:S(2)}, u32[]{:S(2)}) collective-permute-start(bf16[512,256]{1,0:T(8,128)(2,1)} %slice.10), channel_id=1, source_target_pairs={{4,5},{12,13},{20,21},{28,29}} | collective-permute-start | bytes 786440 | tf_op jit(solution)/shard_map/ppermute | solution.py:24
  13.3 82.3 %copy-start.16 = (s32[6]{0:T(128)}, s32[6]{0:T(128)S(1)}, u32[]{:S(2)}) copy-start(s32[6]{0:T(128)S(1)} %convert_reduce_fusion.slot_ref) | copy-start | bytes 76
  15.4 77.3 %collective-permute-start.9 = (bf16[2,768,256]{2,1,0:T(8,128)(2,1)}, bf16[2,768,256]{2,1,0:T(8,128)(2,1)}, u32[]{:S(2)}, u32[]{:S(2)}) collective-permute-start(bf16[2,768,256]{2,1,0:T(8,128)(2,1)} %pad_maximum_fusion), channel_id=1, source_target_pairs={{0,4},{1,5},{2,6},{3,7},{8,12},{9,13},{10,14},{11,15},{16,20},{17,... | collective-permute-start | bytes 2359304 | tf_op jit(solution)/shard_map/ppermute | solution.py:24
  16.8 49.1 %collective-permute-start.5 = (bf16[1024,256]{1,0:T(8,128)(2,1)S(1)}, bf16[1024,256]{1,0:T(8,128)(2,1)S(1)}, u32[]{:S(2)}, u32[]{:S(2)}) collective-permute-start(bf16[1024,256]{1,0:T(8,128)(2,1)S(1)} %slice_select_fusion), channel_id=1, source_target_pairs={{4,0},{5,1},{12,8},{13,9},{20,16},{21,17},{28,24},{29,25}} | collective-permute-start | bytes 1572872 | tf_op jit(solution)/shard_map/ppermute | solution.py:24
  65.8 70.1 %copy-start.4 = (bf16[1280,256]{1,0:T(8,128)(2,1)}, bf16[1280,256]{1,0:T(8,128)(2,1)S(1)}, u32[]{:S(2)}) copy-start(bf16[1280,256]{1,0:T(8,128)(2,1)S(1)} %broadcast_select_fusion.1.rest_0_) | copy-start | bytes 1966084
  65.8 41.0 %collective-permute-start.1 = (bf16[1280,256]{1,0:T(8,128)(2,1)S(1)}, bf16[1280,256]{1,0:T(8,128)(2,1)}, u32[]{:S(2)}, u32[]{:S(2)}) collective-permute-start(bf16[1280,256]{1,0:T(8,128)(2,1)S(1)} %broadcast_select_fusion.1.rest_0_), channel_id=1, source_target_pairs={{0,2},{1,3},{2,0},{3,1},{4,6},{5,7},{6,4},{7,5},{8,10},{9,11},{10,... | collective-permute-start | bytes 1966088 | tf_op jit(solution)/shard_map/ppermute | solution.py:24
  66.0 52.0 %collective-permute-start.6 = (bf16[1024,256]{1,0:T(8,128)(2,1)S(1)}, bf16[1024,256]{1,0:T(8,128)(2,1)}, u32[]{:S(2)}, u32[]{:S(2)}) collective-permute-start(bf16[1024,256]{1,0:T(8,128)(2,1)S(1)} %broadcast_select_fusion.3), channel_id=1, source_target_pairs={{0,2},{1,3},{4,6},{5,7},{8,10},{9,11},{12,14},{13,15},{16,18},{17,... | collective-permute-start | bytes 1572872 | tf_op jit(solution)/shard_map/ppermute | solution.py:24
  67.5 54.8 %collective-permute-start.16 = (bf16[512,256]{1,0:T(8,128)(2,1)S(1)}, bf16[512,256]{1,0:T(8,128)(2,1)S(1)}, u32[]{:S(2)}, u32[]{:S(2)}) collective-permute-start(bf16[512,256]{1,0:T(8,128)(2,1)S(1)} %slice_select_fusion.1), channel_id=1, source_target_pairs={{4,0},{5,1},{12,8},{13,9},{20,16},{21,17},{28,24},{29,25}} | collective-permute-start | bytes 786440 | tf_op jit(solution)/shard_map/ppermute | solution.py:24
  92.8 29.7 %collective-permute-start.2 = (bf16[1280,256]{1,0:T(8,128)(2,1)S(1)}, bf16[1280,256]{1,0:T(8,128)(2,1)S(1)}, u32[]{:S(2)}, u32[]{:S(2)}) collective-permute-start(bf16[1280,256]{1,0:T(8,128)(2,1)S(1)} %broadcast_select_fusion.1.rest_0_), channel_id=1, source_target_pairs={{0,1},{1,0},{2,3},{3,2},{4,5},{5,4},{6,7},{7,6},{8,9},{9,8},{10,11... | collective-permute-start | bytes 1966088 | tf_op jit(solution)/shard_map/ppermute | solution.py:24
  106.8 58.4 %collective-permute-start.10 = (bf16[2,768,256]{2,1,0:T(8,128)(2,1)S(1)}, bf16[2,768,256]{2,1,0:T(8,128)(2,1)}, u32[]{:S(2)}, u32[]{:S(2)}) collective-permute-start(bf16[2,768,256]{2,1,0:T(8,128)(2,1)S(1)} %broadcast_select_fusion.rest_0_), channel_id=1, source_target_pairs={{0,2},{1,3},{2,0},{3,1},{4,6},{5,7},{6,4},{7,5},{8,10},{9,11},{10,... | collective-permute-start | bytes 2359304 | tf_op jit(solution)/shard_map/ppermute | solution.py:24
  118.0 17.9 %collective-permute-start.3 = (bf16[1280,256]{1,0:T(8,128)(2,1)}, bf16[1280,256]{1,0:T(8,128)(2,1)}, u32[]{:S(2)}, u32[]{:S(2)}) collective-permute-start(bf16[1280,256]{1,0:T(8,128)(2,1)} %collective-permute-done.1.rest_1_), channel_id=1, source_target_pairs={{0,1},{1,0},{2,3},{3,2},{4,5},{5,4},{6,7},{7,6},{8,9},{9,8},{10,11... | collective-permute-start | bytes 1966088 | tf_op jit(solution)/shard_map/ppermute | solution.py:24
  120.6 33.1 %collective-permute-start.7 = (bf16[1024,256]{1,0:T(8,128)(2,1)S(1)}, bf16[1024,256]{1,0:T(8,128)(2,1)S(1)}, u32[]{:S(2)}, u32[]{:S(2)}) collective-permute-start(bf16[1024,256]{1,0:T(8,128)(2,1)S(1)} %broadcast_select_fusion.4.rest_0_.rest_2_), channel_id=1, source_target_pairs={{0,1},{1,0},{2,3},{3,2},{4,5},{5,4},{6,7},{7,6},{8,9},{9,8},{10,11... | collective-permute-start | bytes 1572872 | tf_op jit(solution)/shard_map/ppermute | solution.py:24
  122.4 55.4 %collective-permute-start.12 = (bf16[1024,256]{1,0:T(8,128)(2,1)S(1)}, bf16[1024,256]{1,0:T(8,128)(2,1)}, u32[]{:S(2)}, u32[]{:S(2)}) collective-permute-start(bf16[1024,256]{1,0:T(8,128)(2,1)S(1)} %broadcast_select_fusion.2.rest_0_), channel_id=1, source_target_pairs={{0,2},{1,3},{2,0},{3,1},{4,6},{5,7},{6,4},{7,5},{8,10},{9,11},{10,... | collective-permute-start | bytes 1572872 | tf_op jit(solution)/shard_map/ppermute | solution.py:24
  123.4 54.9 %collective-permute-start.17 = (bf16[512,256]{1,0:T(8,128)(2,1)S(1)}, bf16[512,256]{1,0:T(8,128)(2,1)}, u32[]{:S(2)}, u32[]{:S(2)}) collective-permute-start(bf16[512,256]{1,0:T(8,128)(2,1)S(1)} %broadcast_select_fusion.5), channel_id=1, source_target_pairs={{0,2},{1,3},{4,6},{5,7},{8,10},{9,11},{12,14},{13,15},{16,18},{17,... | collective-permute-start | bytes 786440 | tf_op jit(solution)/shard_map/ppermute | solution.py:24
  125.4 46.9 %all-to-all-start = ((s32[4,1,2]{2,1,0:T(1,128)}), s32[4,1,2]{2,1,0:T(1,128)S(1)}, u32[]{:S(2)}, u32[]{:S(2)}) async-start(s32[4,1,2]{2,1,0:T(1,128)} %copy.11), calls=%async_computation | async-start | bytes 4096 | tf_op jit(solution)/shard_map/all_to_all | solution.py:372
  172.2 43.0 %all-to-all-start.1 = ((bf16[4,2,128,384]{3,2,1,0:T(8,128)(2,1)}), bf16[4,2,128,384]{3,2,1,0:T(8,128)(2,1)S(1)}, u32[]{:S(2)}, u32[]{:S(2)}) async-start(bf16[4,2,128,384]{3,2,1,0:T(8,128)(2,1)} %get-tuple-element.19), calls=%async_computation.1 | async-start | bytes 1572864 | tf_op jit(solution)/shard_map/all_to_all | solution.py:427
  176.2 14.8 %collective-permute-start.13 = (bf16[1024,256]{1,0:T(8,128)(2,1)S(1)}, bf16[1024,256]{1,0:T(8,128)(2,1)S(1)}, u32[]{:S(2)}, u32[]{:S(2)}) collective-permute-start(bf16[1024,256]{1,0:T(8,128)(2,1)S(1)} %broadcast_select_fusion.2.rest_0_), channel_id=1, source_target_pairs={{0,1},{1,0},{2,3},{3,2},{4,5},{5,4},{6,7},{7,6},{8,9},{9,8},{10,11... | collective-permute-start | bytes 1572872 | tf_op jit(solution)/shard_map/ppermute | solution.py:24
  177.7 29.3 %collective-permute-start.14 = (bf16[1024,256]{1,0:T(8,128)(2,1)}, bf16[1024,256]{1,0:T(8,128)(2,1)S(1)}, u32[]{:S(2)}, u32[]{:S(2)}) collective-permute-start(bf16[1024,256]{1,0:T(8,128)(2,1)} %collective-permute-done.12.rest_1_), channel_id=1, source_target_pairs={{0,1},{1,0},{2,3},{3,2},{4,5},{5,4},{6,7},{7,6},{8,9},{9,8},{10,11... | collective-permute-start | bytes 1572872 | tf_op jit(solution)/shard_map/ppermute | solution.py:24
  179.3 27.8 %collective-permute-start.18 = (bf16[512,256]{1,0:T(8,128)(2,1)S(1)}, bf16[512,256]{1,0:T(8,128)(2,1)S(1)}, u32[]{:S(2)}, u32[]{:S(2)}) collective-permute-start(bf16[512,256]{1,0:T(8,128)(2,1)S(1)} %broadcast_select_fusion.6.rest_4_), channel_id=1, source_target_pairs={{0,1},{1,0},{2,3},{3,2},{4,5},{5,4},{6,7},{7,6},{8,9},{9,8},{10,11... | collective-permute-start | bytes 786440 | tf_op jit(solution)/shard_map/ppermute | solution.py:24
  (15 other events, 344.7 us)

commit v4 on v3

--- a/solution.py
+++ b/solution.py
@@ -28,7 +28,6 @@
     across = [(m, m ^ 1) for m in range(8)]
     near = [(m, m ^ 2) for m in range(8)]
     distant = [(m, m + 4) for m in range(4)]
-    pairs = [(0, 1), (1, 0), (2, 3), (3, 2)]
     beside, back = [(4, 5)], [(4, 0), (5, 1)]
     spread = [(0, 2), (1, 3), (4, 6), (5, 7)]
     level = member // 2
@@ -40,11 +39,6 @@
         over = permute(cur, across)
         return cur, far, over, permute(far, across)
 
-    def both_slabs(own):
-        both = jnp.stack([own, permute(own, pairs)])
-        cur = jnp.where(member < 4, both, permute(both, distant))
-        return cur, permute(cur, near)
-
     def halves(low, high):
         half = jnp.where(member == 5, permute(high, beside), low)
         half = jnp.where(level == 0, permute(half, back), half)
@@ -54,7 +48,7 @@
     early = halves(e_low, e_high)
     n = c.shape[0] // 2
     late = halves(c[:n], c[n:])
-    return (slabs(a), early), (both_slabs(b), early), (slabs(c), late)
+    return (slabs(a), early), (slabs(b), early), (slabs(c), late)
 
 
 def placed_slabs(member, refs):
@@ -62,8 +56,6 @@
     even = lax.rem(lax.div(member, 2), 2) == 0
     near, far = jnp.where(even, x, 2 + x), jnp.where(even, 2 + x, x)
     over, overfar = jnp.where(even, 1 - x, 3 - x), jnp.where(even, 3 - x, 1 - x)
-    if len(refs) == 2:
-        return ((refs[0].at[0], near), (refs[1].at[0], far), (refs[0].at[1], over), (refs[1].at[1], overfar))
     return tuple(zip(refs, (near, far, over, overfar)))
 
 
@@ -171,12 +163,17 @@
     return value - jnp.dot(left, right, preferred_element_type=jnp.float32)
 
 
-def pivot_kernel(n_bufs, width, member_ref, front, *rest):
-    bufs = rest[:n_bufs]
-    out, low_up, inv, own, raw, mat, sems, own_sems = rest[n_bufs:]
+def minus_dot(value, left, right):
+    return value - jnp.dot(left, right, preferred_element_type=jnp.float32)
+
+
+def pivot_kernel(counts, width, member_ref, front, *rest):
+    firsts, lasts = rest[: counts[0]], rest[counts[0] : sum(counts)]
+    out, w_out, raw, mat, own, inv, sems, last_sems, own_sems = rest[sum(counts) :]
     member = member_ref[0]
-    p = P_SIZE
-    copies = start_first(member, bufs, raw, sems)
+    p, rows = P_SIZE, TICKS * P_SIZE
+    copies = start_first(member, firsts, raw, sems)
+    copies += start_last(member, lasts, raw.at[TICKS - 1], last_sems, 0, rows)
     loads = [
         pltpu.make_async_copy(
             front.at[pl.ds(t * width, p), :], own.at[pl.ds(t * p, p), :], own_sems.at[t]
@@ -186,32 +183,32 @@
     for load in loads:
         load.start()
     wait_all(copies)
-    for s in range(TICKS - 1):
+    for s in range(TICKS):
         mat[s] = raw[s].astype(jnp.float32)
     wait_all(loads)
-    for t in range(TICKS - 1):
+    for t in range(TICKS):
         lo, below = t * p, (t + 1) * p
         x = diagonal_inverse(mat[t, lo:below, :])
         inv[t] = x
-        mult = jnp.dot(mat[t, below:, :], x, precision=HIGH, preferred_element_type=jnp.float32)
-        panel = mult.astype(jnp.bfloat16)
-        low_up[t, below:, :] = panel
-        for s in range(t + 1, TICKS - 1):
-            urows = mat[s, lo:below, :].astype(jnp.bfloat16)
-            low_up[s, lo:below, :] = urows
-            mat[s, below:, :] = minus_dot(mat[s, below:, :], panel, urows)
-        urows = own[lo:below, :].astype(jnp.bfloat16)
-        own[below:, p:] = minus_dot(own[below:, p:], panel, urows[:, p:])
-
-        @pl.when((member >= TICKS) | (member > t))
-        def _():
-            own[below:, :p] = minus_dot(own[below:, :p], panel, urows[:, :p])
-
-        @pl.when(member == t)
-        def _():
-            own[below:, :p] = jnp.dot(
-                own[below:, :p], x, precision=HIGH, preferred_element_type=jnp.float32
-            )
+        if below < rows:
+            mult = jnp.dot(mat[t, below:, :], x, precision=HIGH, preferred_element_type=jnp.float32)
+            panel = mult.astype(jnp.bfloat16)
+            for s in range(t + 1, TICKS):
+                mat[s, below:, :] = minus_dot(
+                    mat[s, below:, :], panel, mat[s, lo:below, :].astype(jnp.bfloat16)
+                )
+            urows = own[lo:below, :].astype(jnp.bfloat16)
+            own[below:, p:] = minus_dot(own[below:, p:], panel, urows[:, p:])
+
+            @pl.when((member >= TICKS) | (member > t))
+            def _():
+                own[below:, :p] = minus_dot(own[below:, :p], panel, urows[:, :p])
+
+            @pl.when(member == t)
+            def _():
+                own[below:, :p] = jnp.dot(
+                    own[below:, :p], x, precision=HIGH, preferred_element_type=jnp.float32
+                )
 
     stores = [
         pltpu.make_async_copy(
@@ -221,45 +218,6 @@
     ]
     for store in stores:
         store.start()
-    wait_all(stores)
-
-
-def pivot_rows(member, front, bufs):
-    order, width = front.shape
-    p, rows = P_SIZE, TICKS * P_SIZE
-    return pl.pallas_call(
-        functools.partial(pivot_kernel, len(bufs), width),
-        name="pivot_rows",
-        out_shape=(
-            jax.ShapeDtypeStruct((order, width), jnp.float32),
-            jax.ShapeDtypeStruct((TICKS - 1, rows, p), jnp.bfloat16),
-            jax.ShapeDtypeStruct((TICKS - 1, p, p), jnp.float32),
-            jax.ShapeDtypeStruct((rows, width), jnp.float32),
-        ),
-        in_specs=[SMEM, ANY] + [ANY] * len(bufs),
-        out_specs=(ANY, VMEM, VMEM, VMEM),
-        scratch_shapes=[
-            pltpu.VMEM((TICKS - 1, rows, p), jnp.bfloat16),
-            pltpu.VMEM((TICKS - 1, rows, p), jnp.float32),
-            pltpu.SemaphoreType.DMA((4,)),
-            pltpu.SemaphoreType.DMA((TICKS,)),
-        ],
-    )(member, front, *bufs)
-
-
-def solve_kernel(n_bufs, member_ref, low_up, inv, own, *rest):
-    bufs = rest[:n_bufs]
-    w_out, raw, mat, sems = rest[n_bufs:]
-    member = member_ref[0]
-    p, rows, width = P_SIZE, own.shape[0], own.shape[1]
-    copies = start_last(member, bufs, raw, sems, 0, rows)
-    wait_all(copies)
-    mat[...] = raw[...].astype(jnp.float32)
-    last = TICKS - 1
-    for t in range(last):
-        lo, below = t * p, (t + 1) * p
-        mat[below:, :] = minus_dot(mat[below:, :], low_up[t, below:, :], mat[lo:below, :].astype(jnp.bfloat16))
-    x_last = diagonal_inverse(mat[last * p :, :])
     row = lax.broadcasted_iota(jnp.int32, (p, width), 0)
     col = lax.broadcasted_iota(jnp.int32, (p, width), 1)
     owner = (member < TICKS) & (col < p)
@@ -268,28 +226,36 @@
         unit = jnp.where((row == col) & (member == t), -1.0, 0.0)
         side = jnp.where(owner, unit, own[lo:hi, :])
         for s in range(t + 1, TICKS):
-            urows = mat[lo:hi, :].astype(jnp.bfloat16) if s == last else low_up[s, lo:hi, :]
-            side = minus_dot(side, urows, w_out[s * p : (s + 1) * p, :])
-        x = x_last if t == last else inv[t]
-        w_out[lo:hi, :] = jnp.dot(x, side, precision=HIGH, preferred_element_type=jnp.float32).astype(
-            jnp.bfloat16
-        )
-
-
-def solve(member, low_up, inv, own, bufs):
-    rows, width = own.shape
+            side = minus_dot(side, mat[s, lo:hi, :].astype(jnp.bfloat16), w_out[s * p : (s + 1) * p, :])
+        w_out[lo:hi, :] = jnp.dot(
+            inv[t], side, precision=HIGH, preferred_element_type=jnp.float32
+        ).astype(jnp.bfloat16)
+    wait_all(stores)
+
+
+def pivot_rows(member, front, bufs):
+    order, width = front.shape
+    p, rows = P_SIZE, TICKS * P_SIZE
+    counts = tuple(len(b) for b in bufs)
     return pl.pallas_call(
-        functools.partial(solve_kernel, len(bufs)),
-        name="solve",
-        out_shape=jax.ShapeDtypeStruct((rows, width), jnp.bfloat16),
-        in_specs=[SMEM, VMEM, VMEM, VMEM] + [ANY] * len(bufs),
-        out_specs=VMEM,
+        functools.partial(pivot_kernel, counts, width),
+        name="pivot_rows",
+        out_shape=(
+            jax.ShapeDtypeStruct((order, width), jnp.float32),
+            jax.ShapeDtypeStruct((rows, width), jnp.bfloat16),
+        ),
+        in_specs=[SMEM, ANY] + [ANY] * sum(counts),
+        out_specs=(ANY, VMEM),
         scratch_shapes=[
-            pltpu.VMEM((rows, P_SIZE), jnp.bfloat16),
-            pltpu.VMEM((rows, P_SIZE), jnp.float32),
+            pltpu.VMEM((TICKS, rows, p), jnp.bfloat16),
+            pltpu.VMEM((TICKS, rows, p), jnp.float32),
+            pltpu.VMEM((rows, width), jnp.float32),
+            pltpu.VMEM((TICKS, p, p), jnp.float32),
+            pltpu.SemaphoreType.DMA((4,)),
             pltpu.SemaphoreType.DMA((2,)),
+            pltpu.SemaphoreType.DMA((TICKS,)),
         ],
-    )(member, low_up, inv, own, *bufs)
+    )(member, front, *bufs[0], *bufs[1])
 
 
 def other_kernel(counts, ranges, first_row, tail, member_ref, dest_ref, slot_ref, w, front, out_in, *rest):
@@ -419,8 +385,7 @@
         own_t, own_m = pack(front, [tail_ranges, middle_ranges])
         sets = tuple(((lax.all_gather(s, "blk")[:TICKS],),) * 2 for s in (own_p, own_t, own_m))
     dest, slot, address = routes(parent_group, row_block)
-    out, low_up, inv, own = pivot_rows(holder, front, sets[0][0])
-    w = solve(holder, low_up, inv, own, sets[0][1])
+    out, w = pivot_rows(holder, front, sets[0])
     out, outgoing = other_rows(
         holder, dest, slot, w, front, out, sets[1], [(tail_at, 0, tail_n)], TICKS * p, lax.axis_size("front")
     )

time: 220 us -> 211 us (0.959)
  the two profiles are of different devices: /device:TPU:28 before, /device:TPU:30 now
where the time goes in v4:
time: 211 us; the launch traced here: 210 us
  waiting for transfers between devices  131 us (62%)
  Pallas kernels  43.6 us (21%)
  starting transfers between devices  24.6 us (12%)
  local copies, waits for them, and re-layouts  5.75 us (3%)
  other arithmetic  4.53 us (2%)
    ppermute x20, waiting for transfers between devices, permute(): return lax.ppermute(value, 'blk', pairs)  131 us
    pallas_call x1, Pallas kernels, pivot_rows(): pl.pallas_call(functools.partial(pivot_kernel, counts, width), name='pivo...  21.2 us
    ppermute x20, starting transfers between devices, permute(): return lax.ppermute(value, 'blk', pairs)  16.9 us
    pallas_call x2, Pallas kernels, other_rows(): pl.pallas_call(functools.partial(other_kernel, counts, ranges, first_row,...  14.3 us
    pallas_call x2, Pallas kernels, pack(): pl.pallas_call(functools.partial(pack_kernel, pieces), out_shape=tuple((j...  5.09 us
  transfers between devices with their start and end apart: 22, of which 8 were waited for; matrix products, arithmetic and copies ran while one was open for 3% of the time, Pallas kernels for 18%

profile of v4, /device:TPU:30, one launch (start us, length us, event | category | flops | bytes accessed | tf_op | source)
XLA Modules:
  0.0 210.0 jit_solution(1799987666124203116)
XLA Ops:
  0.7 2.9 %shard_map.60 = (bf16[768,256]{1,0:T(8,128)(2,1)}, bf16[1024,256]{1,0:T(8,128)(2,1)}, bf16[1024,256]{1,0:T(8,128)(2,1)}) custom-call(f32[3072,384]{1,0:T(8,128)} %front.9), custom_call_target="tpu_custom_call" | custom-call | tf_op jit(solution)/shard_map/pallas_call | solution.py:134
  4.4 2.2 %shard_map.59 = bf16[1280,256]{1,0:T(8,128)(2,1)} custom-call(f32[3072,384]{1,0:T(8,128)} %front.9), custom_call_target="tpu_custom_call" | custom-call | tf_op jit(solution)/shard_map/pallas_call | solution.py:134
  6.6 1.3 collective-permute-start
  7.9 1.3 collective-permute-start.8
  9.2 1.3 collective-permute-start.12
  10.6 1.4 collective-permute-start.16
  14.0 46.4 %collective-permute-done = bf16[1280,256]{1,0:T(8,128)(2,1)S(1)} collective-permute-done((bf16[1280,256]{1,0:T(8,128)(2,1)}, bf16[1280,256]{1,0:T(8,128)(2,1)S(1)}, u32[]{:S(2)}, u32[]{:S(2)}) %collective-permute-start) | collective-permute-done | bytes 655392 | tf_op jit(solution)/shard_map/ppermute | solution.py:24
  60.6 1.3 collective-permute-start.6
  62.8 6.1 %collective-permute-done.8 = bf16[768,256]{1,0:T(8,128)(2,1)S(1)} collective-permute-done((bf16[768,256]{1,0:T(8,128)(2,1)S(1)}, bf16[768,256]{1,0:T(8,128)(2,1)S(1)}, u32[]{:S(2)}, u32[]{:S(2)}) %collective-permute-start.8) | collective-permute-done | bytes 393248 | tf_op jit(solution)/shard_map/ppermute | solution.py:24
  70.0 23.7 %collective-permute-done.1.rest_1_ = bf16[1280,256]{1,0:T(8,128)(2,1)} collective-permute-done((bf16[1280,256]{1,0:T(8,128)(2,1)S(1)}, bf16[1280,256]{1,0:T(8,128)(2,1)}, u32[]{:S(2)}, u32[]{:S(2)}) %collective-permute-start.1) | collective-permute-done | bytes 655392 | tf_op jit(solution)/shard_map/ppermute | solution.py:24
  93.7 11.1 %collective-permute-done.6 = bf16[1024,256]{1,0:T(8,128)(2,1)S(1)} collective-permute-done((bf16[1024,256]{1,0:T(8,128)(2,1)S(1)}, bf16[1024,256]{1,0:T(8,128)(2,1)S(1)}, u32[]{:S(2)}, u32[]{:S(2)}) %collective-permute-start.6) | collective-permute-done | bytes 524320 | tf_op jit(solution)/shard_map/ppermute | solution.py:24
  105.4 1.6 collective-permute-start.7
  108.7 4.4 %collective-permute-done.9.rest_1_ = bf16[768,256]{1,0:T(8,128)(2,1)S(1)} collective-permute-done((bf16[768,256]{1,0:T(8,128)(2,1)S(1)}, bf16[768,256]{1,0:T(8,128)(2,1)S(1)}, u32[]{:S(2)}, u32[]{:S(2)}) %collective-permute-start.9) | collective-permute-done | bytes 393248 | tf_op jit(solution)/shard_map/ppermute | solution.py:24
  114.0 8.6 %collective-permute-done.3.rest_3_ = bf16[1280,256]{1,0:T(8,128)(2,1)S(1)} collective-permute-done((bf16[1280,256]{1,0:T(8,128)(2,1)}, bf16[1280,256]{1,0:T(8,128)(2,1)S(1)}, u32[]{:S(2)}, u32[]{:S(2)}) %collective-permute-start.3) | collective-permute-done | bytes 655392 | tf_op jit(solution)/shard_map/ppermute | solution.py:24
  123.5 1.3 collective-permute-start.18
  125.5 3.7 %all-to-all-start = ((s32[4,1,2]{2,1,0:T(1,128)}), s32[4,1,2]{2,1,0:T(1,128)S(1)}, u32[]{:S(2)}, u32[]{:S(2)}) async-start(s32[4,1,2]{2,1,0:T(1,128)} %copy.11), calls=%async_computation | async-start | bytes 4096 | tf_op jit(solution)/shard_map/all_to_all | solution.py:338
  129.2 4.7 %collective-permute-done.7.rest_5_ = bf16[1024,256]{1,0:T(8,128)(2,1)S(1)} collective-permute-done((bf16[1024,256]{1,0:T(8,128)(2,1)S(1)}, bf16[1024,256]{1,0:T(8,128)(2,1)S(1)}, u32[]{:S(2)}, u32[]{:S(2)}) %collective-permute-start.7) | collective-permute-done | bytes 524320 | tf_op jit(solution)/shard_map/ppermute | solution.py:24
  134.7 21.2 %pivot_rows.1 = (f32[3072,384]{1,0:T(8,128)}, bf16[1280,384]{1,0:T(8,128)(2,1)}) custom-call(s32[1]{0:T(128)} %bitcast.member_ref, f32[3072,384]{1,0:T(8,128)} %front.9, bf16[1280,256]{1,0:T(8,128)(2,1)} %copy-done.2, bf16[1280,256]{1,0:T(8,128)(2,1)} %collective-permute-done.1.rest_1_, bf16[1280,256]{1,0:T(8,128)(2,1)} %copy-done.8, ...), custom_call_target="tpu_custom_call" | custom-call | tf_op jit(solution)/shard_map/pivot_rows/pallas_call | solution.py:240
  155.9 7.0 %tail_rows.1 = (f32[3072,384]{1,0:T(8,128)}, bf16[4,2,128,384]{3,2,1,0:T(8,128)(2,1)}) custom-call(s32[1]{0:T(128)} %bitcast.member_ref, s32[6]{0:T(128)} %bitcast.8, s32[6]{0:T(128)} %copy-done.16, bf16[1280,384]{1,0:T(8,128)(2,1)} %get-tuple-element.10.w, f32[3072,384]{1,0:T(8,128)} %front.9, ...), custom_call_target="tpu_custom_call", output_to_operand_aliasing={{0}: (5, {})} | custom-call | tf_op jit(solution)/shard_map/tail_rows/pallas_call | solution.py:310
  162.9 4.0 %all-to-all-start.1 = ((bf16[4,2,128,384]{3,2,1,0:T(8,128)(2,1)}), bf16[4,2,128,384]{3,2,1,0:T(8,128)(2,1)S(1)}, u32[]{:S(2)}, u32[]{:S(2)}) async-start(bf16[4,2,128,384]{3,2,1,0:T(8,128)(2,1)} %get-tuple-element.15), calls=%async_computation.1 | async-start | bytes 1572864 | tf_op jit(solution)/shard_map/all_to_all | solution.py:392
  167.2 1.7 collective-permute-start.15
  172.2 25.5 %collective-permute-done.19.rest_5_ = bf16[512,256]{1,0:T(8,128)(2,1)S(1)} collective-permute-done((bf16[512,256]{1,0:T(8,128)(2,1)S(1)}, bf16[512,256]{1,0:T(8,128)(2,1)S(1)}, u32[]{:S(2)}, u32[]{:S(2)}) %collective-permute-start.19) | collective-permute-done | bytes 262176 | tf_op jit(solution)/shard_map/ppermute | solution.py:24
  198.8 7.3 %middle_rows.1 = f32[3072,384]{1,0:T(8,128)} custom-call(s32[1]{0:T(128)} %bitcast.member_ref, s32[6]{0:T(128)} %bitcast.9, s32[6]{0:T(128)} %copy-done.16, bf16[1280,384]{1,0:T(8,128)(2,1)} %get-tuple-element.10.w, f32[3072,384]{1,0:T(8,128)} %front.9, f32[3072,384]{1,0:T(8,128)} %get-tuple-element.13.out_in, ...), custom_call_target="tpu_custom_call", output_to_operand_aliasing={{}: (5, {})} | custom-call | tf_op jit(solution)/shard_map/middle_rows/pallas_call | solution.py:310
  207.0 3.0 %add_blocks.1 = f32[1024,384]{1,0:T(8,128)} custom-call(s32[8]{0:T(128)} %reshape.81.address_ref, bf16[8,128,384]{2,1,0:T(8,128)(2,1)} %bitcast.7, f32[1024,384]{1,0:T(8,128)} %base.1), custom_call_target="tpu_custom_call" | custom-call | tf_op jit(solution)/shard_map/add_blocks/pallas_call | solution.py:355
  (82 shorter events, 16.1 us)
Async XLA Ops:
  3.6 8.5 %collective-permute-start.4 = (bf16[1024,256]{1,0:T(8,128)(2,1)}, bf16[1024,256]{1,0:T(8,128)(2,1)S(1)}, u32[]{:S(2)}, u32[]{:S(2)}) collective-permute-start(bf16[1024,256]{1,0:T(8,128)(2,1)} %get-tuple-element.9), channel_id=1, source_target_pairs={{4,5},{12,13},{20,21},{28,29}} | collective-permute-start | bytes 1572872 | tf_op jit(solution)/shard_map/ppermute | solution.py:24
  6.6 53.8 %collective-permute-start = (bf16[1280,256]{1,0:T(8,128)(2,1)}, bf16[1280,256]{1,0:T(8,128)(2,1)S(1)}, u32[]{:S(2)}, u32[]{:S(2)}) collective-permute-start(bf16[1280,256]{1,0:T(8,128)(2,1)} %shard_map.59), channel_id=1, source_target_pairs={{0,4},{1,5},{2,6},{3,7},{8,12},{9,13},{10,14},{11,15},{16,20},{17,... | collective-permute-start | bytes 1966088 | tf_op jit(solution)/shard_map/ppermute | solution.py:24
  7.9 61.0 %collective-permute-start.8 = (bf16[768,256]{1,0:T(8,128)(2,1)S(1)}, bf16[768,256]{1,0:T(8,128)(2,1)S(1)}, u32[]{:S(2)}, u32[]{:S(2)}) collective-permute-start(bf16[768,256]{1,0:T(8,128)(2,1)S(1)} %copy-done.12), channel_id=1, source_target_pairs={{0,4},{1,5},{2,6},{3,7},{8,12},{9,13},{10,14},{11,15},{16,20},{17,... | collective-permute-start | bytes 1179656 | tf_op jit(solution)/shard_map/ppermute | solution.py:24
  9.2 96.2 %collective-permute-start.12 = (bf16[1024,256]{1,0:T(8,128)(2,1)S(1)}, bf16[1024,256]{1,0:T(8,128)(2,1)}, u32[]{:S(2)}, u32[]{:S(2)}) collective-permute-start(bf16[1024,256]{1,0:T(8,128)(2,1)S(1)} %copy-done.3), channel_id=1, source_target_pairs={{0,4},{1,5},{2,6},{3,7},{8,12},{9,13},{10,14},{11,15},{16,20},{17,... | collective-permute-start | bytes 1572872 | tf_op jit(solution)/shard_map/ppermute | solution.py:24
  10.6 51.5 %collective-permute-start.16 = (bf16[512,256]{1,0:T(8,128)(2,1)S(1)}, bf16[512,256]{1,0:T(8,128)(2,1)}, u32[]{:S(2)}, u32[]{:S(2)}) collective-permute-start(bf16[512,256]{1,0:T(8,128)(2,1)S(1)} %slice.10), channel_id=1, source_target_pairs={{4,5},{12,13},{20,21},{28,29}} | collective-permute-start | bytes 786440 | tf_op jit(solution)/shard_map/ppermute | solution.py:24
  12.1 96.0 %copy-start.16 = (s32[6]{0:T(128)}, s32[6]{0:T(128)S(1)}, u32[]{:S(2)}) copy-start(s32[6]{0:T(128)S(1)} %convert_reduce_fusion.slot_ref) | copy-start | bytes 76
  13.3 47.3 %collective-permute-start.5 = (bf16[1024,256]{1,0:T(8,128)(2,1)S(1)}, bf16[1024,256]{1,0:T(8,128)(2,1)S(1)}, u32[]{:S(2)}, u32[]{:S(2)}) collective-permute-start(bf16[1024,256]{1,0:T(8,128)(2,1)S(1)} %slice_select_fusion), channel_id=1, source_target_pairs={{4,0},{5,1},{12,8},{13,9},{20,16},{21,17},{28,24},{29,25}} | collective-permute-start | bytes 1572872 | tf_op jit(solution)/shard_map/ppermute | solution.py:24
  60.5 33.2 %collective-permute-start.1 = (bf16[1280,256]{1,0:T(8,128)(2,1)S(1)}, bf16[1280,256]{1,0:T(8,128)(2,1)}, u32[]{:S(2)}, u32[]{:S(2)}) collective-permute-start(bf16[1280,256]{1,0:T(8,128)(2,1)S(1)} %broadcast_select_fusion.rest_0_), channel_id=1, source_target_pairs={{0,2},{1,3},{2,0},{3,1},{4,6},{5,7},{6,4},{7,5},{8,10},{9,11},{10,... | collective-permute-start | bytes 1966088 | tf_op jit(solution)/shard_map/ppermute | solution.py:24
  60.6 44.2 %collective-permute-start.6 = (bf16[1024,256]{1,0:T(8,128)(2,1)S(1)}, bf16[1024,256]{1,0:T(8,128)(2,1)S(1)}, u32[]{:S(2)}, u32[]{:S(2)}) collective-permute-start(bf16[1024,256]{1,0:T(8,128)(2,1)S(1)} %broadcast_select_fusion.2), channel_id=1, source_target_pairs={{0,2},{1,3},{4,6},{5,7},{8,10},{9,11},{12,14},{13,15},{16,18},{17,... | collective-permute-start | bytes 1572872 | tf_op jit(solution)/shard_map/ppermute | solution.py:24
  62.1 46.0 %collective-permute-start.17 = (bf16[512,256]{1,0:T(8,128)(2,1)S(1)}, bf16[512,256]{1,0:T(8,128)(2,1)S(1)}, u32[]{:S(2)}, u32[]{:S(2)}) collective-permute-start(bf16[512,256]{1,0:T(8,128)(2,1)S(1)} %slice_select_fusion.1), channel_id=1, source_target_pairs={{4,0},{5,1},{12,8},{13,9},{20,16},{21,17},{28,24},{29,25}} | collective-permute-start | bytes 786440 | tf_op jit(solution)/shard_map/ppermute | solution.py:24
  68.9 44.3 %collective-permute-start.2 = (bf16[1280,256]{1,0:T(8,128)(2,1)S(1)}, bf16[1280,256]{1,0:T(8,128)(2,1)S(1)}, u32[]{:S(2)}, u32[]{:S(2)}) collective-permute-start(bf16[1280,256]{1,0:T(8,128)(2,1)S(1)} %broadcast_select_fusion.rest_0_), channel_id=1, source_target_pairs={{0,1},{1,0},{2,3},{3,2},{4,5},{5,4},{6,7},{7,6},{8,9},{9,8},{10,11... | collective-permute-start | bytes 1966088 | tf_op jit(solution)/shard_map/ppermute | solution.py:24
  70.0 85.8 %copy-start.6 = (bf16[768,256]{1,0:T(8,128)(2,1)}, bf16[768,256]{1,0:T(8,128)(2,1)S(1)}, u32[]{:S(2)}) copy-start(bf16[768,256]{1,0:T(8,128)(2,1)S(1)} %broadcast_select_fusion.4.rest_0_) | copy-start | bytes 1179652
  93.7 19.5 %collective-permute-start.9 = (bf16[768,256]{1,0:T(8,128)(2,1)S(1)}, bf16[768,256]{1,0:T(8,128)(2,1)S(1)}, u32[]{:S(2)}, u32[]{:S(2)}) collective-permute-start(bf16[768,256]{1,0:T(8,128)(2,1)S(1)} %broadcast_select_fusion.4.rest_0_), channel_id=1, source_target_pairs={{0,2},{1,3},{2,0},{3,1},{4,6},{5,7},{6,4},{7,5},{8,10},{9,11},{10,... | collective-permute-start | bytes 1179656 | tf_op jit(solution)/shard_map/ppermute | solution.py:24
  104.8 17.8 %collective-permute-start.3 = (bf16[1280,256]{1,0:T(8,128)(2,1)}, bf16[1280,256]{1,0:T(8,128)(2,1)S(1)}, u32[]{:S(2)}, u32[]{:S(2)}) collective-permute-start(bf16[1280,256]{1,0:T(8,128)(2,1)} %collective-permute-done.1.rest_1_), channel_id=1, source_target_pairs={{0,1},{1,0},{2,3},{3,2},{4,5},{5,4},{6,7},{7,6},{8,9},{9,8},{10,11... | collective-permute-start | bytes 1966088 | tf_op jit(solution)/shard_map/ppermute | solution.py:24
  105.4 28.4 %collective-permute-start.7 = (bf16[1024,256]{1,0:T(8,128)(2,1)S(1)}, bf16[1024,256]{1,0:T(8,128)(2,1)S(1)}, u32[]{:S(2)}, u32[]{:S(2)}) collective-permute-start(bf16[1024,256]{1,0:T(8,128)(2,1)S(1)} %broadcast_select_fusion.3.rest_4_), channel_id=1, source_target_pairs={{0,1},{1,0},{2,3},{3,2},{4,5},{5,4},{6,7},{7,6},{8,9},{9,8},{10,11... | collective-permute-start | bytes 1572872 | tf_op jit(solution)/shard_map/ppermute | solution.py:24
  108.1 47.7 %collective-permute-start.10 = (bf16[768,256]{1,0:T(8,128)(2,1)S(1)}, bf16[768,256]{1,0:T(8,128)(2,1)}, u32[]{:S(2)}, u32[]{:S(2)}) collective-permute-start(bf16[768,256]{1,0:T(8,128)(2,1)S(1)} %broadcast_select_fusion.4.rest_0_), channel_id=1, source_target_pairs={{0,1},{1,0},{2,3},{3,2},{4,5},{5,4},{6,7},{7,6},{8,9},{9,8},{10,11... | collective-permute-start | bytes 1179656 | tf_op jit(solution)/shard_map/ppermute | solution.py:24
  113.2 54.1 %collective-permute-start.13 = (bf16[1024,256]{1,0:T(8,128)(2,1)S(1)}, bf16[1024,256]{1,0:T(8,128)(2,1)}, u32[]{:S(2)}, u32[]{:S(2)}) collective-permute-start(bf16[1024,256]{1,0:T(8,128)(2,1)S(1)} %broadcast_select_fusion.1.rest_0_), channel_id=1, source_target_pairs={{0,2},{1,3},{2,0},{3,1},{4,6},{5,7},{6,4},{7,5},{8,10},{9,11},{10,... | collective-permute-start | bytes 1572872 | tf_op jit(solution)/shard_map/ppermute | solution.py:24
  113.2 42.7 %collective-permute-start.11 = (bf16[768,256]{1,0:T(8,128)(2,1)S(1)}, bf16[768,256]{1,0:T(8,128)(2,1)}, u32[]{:S(2)}, u32[]{:S(2)}) collective-permute-start(bf16[768,256]{1,0:T(8,128)(2,1)S(1)} %collective-permute-done.9.rest_1_), channel_id=1, source_target_pairs={{0,1},{1,0},{2,3},{3,2},{4,5},{5,4},{6,7},{7,6},{8,9},{9,8},{10,11... | collective-permute-start | bytes 1179656 | tf_op jit(solution)/shard_map/ppermute | solution.py:24
  123.5 45.5 %collective-permute-start.18 = (bf16[512,256]{1,0:T(8,128)(2,1)S(1)}, bf16[512,256]{1,0:T(8,128)(2,1)}, u32[]{:S(2)}, u32[]{:S(2)}) collective-permute-start(bf16[512,256]{1,0:T(8,128)(2,1)S(1)} %broadcast_select_fusion.5), channel_id=1, source_target_pairs={{0,2},{1,3},{4,6},{5,7},{8,10},{9,11},{12,14},{13,15},{16,18},{17,... | collective-permute-start | bytes 786440 | tf_op jit(solution)/shard_map/ppermute | solution.py:24
  125.5 37.5 %all-to-all-start = ((s32[4,1,2]{2,1,0:T(1,128)}), s32[4,1,2]{2,1,0:T(1,128)S(1)}, u32[]{:S(2)}, u32[]{:S(2)}) async-start(s32[4,1,2]{2,1,0:T(1,128)} %copy.11), calls=%async_computation | async-start | bytes 4096 | tf_op jit(solution)/shard_map/all_to_all | solution.py:338
  162.9 43.1 %all-to-all-start.1 = ((bf16[4,2,128,384]{3,2,1,0:T(8,128)(2,1)}), bf16[4,2,128,384]{3,2,1,0:T(8,128)(2,1)S(1)}, u32[]{:S(2)}, u32[]{:S(2)}) async-start(bf16[4,2,128,384]{3,2,1,0:T(8,128)(2,1)} %get-tuple-element.15), calls=%async_computation.1 | async-start | bytes 1572864 | tf_op jit(solution)/shard_map/all_to_all | solution.py:392
  166.9 30.8 %collective-permute-start.14 = (bf16[1024,256]{1,0:T(8,128)(2,1)S(1)}, bf16[1024,256]{1,0:T(8,128)(2,1)S(1)}, u32[]{:S(2)}, u32[]{:S(2)}) collective-permute-start(bf16[1024,256]{1,0:T(8,128)(2,1)S(1)} %broadcast_select_fusion.1.rest_0_), channel_id=1, source_target_pairs={{0,1},{1,0},{2,3},{3,2},{4,5},{5,4},{6,7},{7,6},{8,9},{9,8},{10,11... | collective-permute-start | bytes 1572872 | tf_op jit(solution)/shard_map/ppermute | solution.py:24
  167.2 30.5 %collective-permute-start.15 = (bf16[1024,256]{1,0:T(8,128)(2,1)}, bf16[1024,256]{1,0:T(8,128)(2,1)S(1)}, u32[]{:S(2)}, u32[]{:S(2)}) collective-permute-start(bf16[1024,256]{1,0:T(8,128)(2,1)} %collective-permute-done.13.rest_1_), channel_id=1, source_target_pairs={{0,1},{1,0},{2,3},{3,2},{4,5},{5,4},{6,7},{7,6},{8,9},{9,8},{10,11... | collective-permute-start | bytes 1572872 | tf_op jit(solution)/shard_map/ppermute | solution.py:24
  169.9 27.8 %collective-permute-start.19 = (bf16[512,256]{1,0:T(8,128)(2,1)S(1)}, bf16[512,256]{1,0:T(8,128)(2,1)S(1)}, u32[]{:S(2)}, u32[]{:S(2)}) collective-permute-start(bf16[512,256]{1,0:T(8,128)(2,1)S(1)} %broadcast_select_fusion.6.rest_4_), channel_id=1, source_target_pairs={{0,1},{1,0},{2,3},{3,2},{4,5},{5,4},{6,7},{7,6},{8,9},{9,8},{10,11... | collective-permute-start | bytes 786440 | tf_op jit(solution)/shard_map/ppermute | solution.py:24
  (16 other events, 270.0 us)

commit v5 on v4

--- a/solution.py
+++ b/solution.py
@@ -14,7 +14,6 @@
 RB = 128
 NB = 6
 CAP = 2
-HIGH = lax.Precision.HIGHEST
 ANY = pl.BlockSpec(memory_space=pl.ANY)
 SMEM = pl.BlockSpec(memory_space=pltpu.SMEM)
 VMEM = pl.BlockSpec(memory_space=pltpu.VMEM)
@@ -28,10 +27,9 @@
     across = [(m, m ^ 1) for m in range(8)]
     near = [(m, m ^ 2) for m in range(8)]
     distant = [(m, m + 4) for m in range(4)]
-    beside, back = [(4, 5)], [(4, 0), (5, 1)]
-    spread = [(0, 2), (1, 3), (4, 6), (5, 7)]
+    beside, back, mid, up = [(4, 5)], [(4, 0), (5, 1)], [(4, 2), (5, 3)], [(4, 6), (5, 7)]
     level = member // 2
-    a, b, c, e_low, e_high = parts
+    a, b, c, e_halves, n_halves = parts
 
     def slabs(own):
         cur = jnp.where(member < 4, own, permute(own, distant))
@@ -41,14 +39,14 @@
 
     def halves(low, high):
         half = jnp.where(member == 5, permute(high, beside), low)
-        half = jnp.where(level == 0, permute(half, back), half)
-        half = jnp.where(level % 2 == 1, permute(half, spread), half)
+        to_up = permute(half, up)
+        to_back = permute(half, back)
+        to_mid = permute(half, mid)
+        half = jnp.where(level == 2, half, jnp.where(level == 3, to_up, jnp.where(level == 0, to_back, to_mid)))
         return half, permute(half, across)
 
-    early = halves(e_low, e_high)
-    n = c.shape[0] // 2
-    late = halves(c[:n], c[n:])
-    return (slabs(a), early), (slabs(b), early), (slabs(c), late)
+    early, late = halves(*e_halves), halves(*n_halves)
+    return (slabs(a), early), (slabs(b), late), (slabs(c), late)
 
 
 def placed_slabs(member, refs):
@@ -106,6 +104,19 @@
 def wait_all(copies):
     for copy in copies:
         copy.wait()
+
+
+def cut(ranges):
+    left = sum(n for _, n in ranges) // 2
+    low, high = [], []
+    for start, n in ranges:
+        take = min(left, n)
+        if take:
+            low.append((start, take))
+        if n - take:
+            high.append((start + take, n - take))
+        left -= take
+    return low, high
 
 
 def pack_kernel(pieces, front, *rest):
@@ -143,6 +154,22 @@
     )(front)
 
 
+def split(value):
+    high = value.astype(jnp.bfloat16)
+    return high, (value - high.astype(jnp.float32)).astype(jnp.bfloat16)
+
+
+def dot3(left, right):
+    (left_high, left_low), (right_high, right_low) = left, right
+    dot = functools.partial(jnp.dot, preferred_element_type=jnp.float32)
+    return dot(left_high, right_high) + (dot(left_low, right_high) + dot(left_high, right_low))
+
+
+def dot2(left, right):
+    dot = functools.partial(jnp.dot, preferred_element_type=jnp.float32)
+    return dot(left, right[0]) + dot(left, right[1])
+
+
 def diagonal_inverse(block):
     size = block.shape[0]
     row = lax.broadcasted_iota(jnp.int32, (size, size), 0)
@@ -152,11 +179,11 @@
     down = 1.0 / jnp.sum(kept, axis=1, keepdims=True)
     right = 1.0 / jnp.sum(kept, axis=0, keepdims=True)
     twice = jnp.where(on, 2.0, 0.0)
-    inverse = down * (twice - block * right)
+    parts = split(down * (twice - block * right))
+    block_parts = split(block)
     for _ in range(NEWTON - 1):
-        inner = twice - jnp.dot(block, inverse, precision=HIGH, preferred_element_type=jnp.float32)
-        inverse = jnp.dot(inverse, inner, precision=HIGH, preferred_element_type=jnp.float32)
-    return inverse
+        parts = split(dot3(parts, split(twice - dot3(block_parts, parts))))
+    return parts
 
 
 def minus_dot(value, left, right):
@@ -183,32 +210,33 @@
     for load in loads:
         load.start()
     wait_all(copies)
-    for s in range(TICKS):
-        mat[s] = raw[s].astype(jnp.float32)
+    x = diagonal_inverse(raw[0, :p, :].astype(jnp.float32))
     wait_all(loads)
     for t in range(TICKS):
         lo, below = t * p, (t + 1) * p
-        x = diagonal_inverse(mat[t, lo:below, :])
-        inv[t] = x
-        if below < rows:
-            mult = jnp.dot(mat[t, below:, :], x, precision=HIGH, preferred_element_type=jnp.float32)
-            panel = mult.astype(jnp.bfloat16)
-            for s in range(t + 1, TICKS):
-                mat[s, below:, :] = minus_dot(
-                    mat[s, below:, :], panel, mat[s, lo:below, :].astype(jnp.bfloat16)
-                )
-            urows = own[lo:below, :].astype(jnp.bfloat16)
-            own[below:, p:] = minus_dot(own[below:, p:], panel, urows[:, p:])
-
-            @pl.when((member >= TICKS) | (member > t))
-            def _():
-                own[below:, :p] = minus_dot(own[below:, :p], panel, urows[:, :p])
-
-            @pl.when(member == t)
-            def _():
-                own[below:, :p] = jnp.dot(
-                    own[below:, :p], x, precision=HIGH, preferred_element_type=jnp.float32
-                )
+        inv[0, t], inv[1, t] = x
+        if below == rows:
+            break
+        column = mat[t, below:, :] if t else raw[t, below:, :]
+        mult = dot3(split(column), x) if t else dot2(column, x)
+        panel = mult.astype(jnp.bfloat16)
+        for s in range(t + 1, TICKS):
+            if t:
+                urows = mat[s, lo:below, :].astype(jnp.bfloat16)
+                raw[s, lo:below, :] = urows
+                rest_rows = mat[s, below:, :]
+            else:
+                urows = raw[s, lo:below, :]
+                rest_rows = raw[s, below:, :].astype(jnp.float32)
+            mat[s, below:, :] = minus_dot(rest_rows, panel, urows)
+            if s == t + 1:
+                x = diagonal_inverse(mat[s, below : below + p, :])
+        urows = own[lo:below, :].astype(jnp.bfloat16)
+        own[below:, p:] = minus_dot(own[below:, p:], panel, urows[:, p:])
+        left = own[below:, :p]
+        live = (member >= TICKS) | (member > t)
+        changed = jnp.where(live, minus_dot(left, panel, urows[:, :p]), left)
+        own[below:, :p] = jnp.where(member == t, mult, changed)
 
     stores = [
         pltpu.make_async_copy(
@@ -226,10 +254,8 @@
         unit = jnp.where((row == col) & (member == t), -1.0, 0.0)
         side = jnp.where(owner, unit, own[lo:hi, :])
         for s in range(t + 1, TICKS):
-            side = minus_dot(side, mat[s, lo:hi, :].astype(jnp.bfloat16), w_out[s * p : (s + 1) * p, :])
-        w_out[lo:hi, :] = jnp.dot(
-            inv[t], side, precision=HIGH, preferred_element_type=jnp.float32
-        ).astype(jnp.bfloat16)
+            side = minus_dot(side, raw[s, lo:hi, :], w_out[s * p : (s + 1) * p, :])
+        w_out[lo:hi, :] = dot3((inv[0, t], inv[1, t]), split(side)).astype(jnp.bfloat16)
     wait_all(stores)
 
 
@@ -250,7 +276,7 @@
             pltpu.VMEM((TICKS, rows, p), jnp.bfloat16),
             pltpu.VMEM((TICKS, rows, p), jnp.float32),
             pltpu.VMEM((rows, width), jnp.float32),
-            pltpu.VMEM((TICKS, p, p), jnp.float32),
+            pltpu.VMEM((2, TICKS, p, p), jnp.bfloat16),
             pltpu.SemaphoreType.DMA((4,)),
             pltpu.SemaphoreType.DMA((2,)),
             pltpu.SemaphoreType.DMA((TICKS,)),
@@ -278,24 +304,25 @@
     wait_all(loads)
     keep = (member >= TICKS) | (lax.broadcasted_iota(jnp.int32, (RB, width), 1) >= P_SIZE)
 
-    def tile(i, carry):
-        at = pl.ds(pl.multiple_of(i * RB, RB), RB)
+    def tile(src, dst, sem, i, carry):
+        at = pl.ds(pl.multiple_of(dst + i * RB, RB), RB)
         total = jnp.where(keep, base[at, :], 0.0)
         for s in range(TICKS):
             total = minus_dot(total, raw[s, at, :], w[s * P_SIZE : (s + 1) * P_SIZE, :])
         base[at, :] = total
         if tail:
             outgoing[dest_ref[i], slot_ref[i]] = jnp.where(keep, total, 0.0).astype(jnp.bfloat16)
+        pltpu.make_async_copy(
+            base.at[at, :], out.at[pl.ds(pl.multiple_of(src + i * RB, RB), RB), :], sem
+        ).start()
         return carry
 
-    lax.fori_loop(0, rows // RB, tile, 0)
-    stores = [
-        pltpu.make_async_copy(base.at[pl.ds(dst, n), :], out.at[pl.ds(src, n), :], base_sems.at[i])
-        for i, (src, dst, n) in enumerate(ranges)
-    ]
-    for store in stores:
-        store.start()
-    wait_all(stores)
+    for number, (src, dst, n) in enumerate(ranges):
+        lax.fori_loop(0, n // RB, functools.partial(tile, src, dst, base_sems.at[number]), 0)
+    for number, (src, dst, n) in enumerate(ranges):
+        pltpu.make_async_copy(
+            base.at[pl.ds(dst, n), :], out.at[pl.ds(src, n), :], base_sems.at[number]
+        ).wait()
 
 
 def other_rows(member, dest, slot, w, front, out, bufs, ranges, first_row, groups=0):
@@ -377,20 +404,20 @@
     for start, count in middle_ranges:
         middle.append((start, at, count))
         at += count
-    (own_p,) = pack(front, [pivot_ranges])
     if lax.axis_size("blk") == 8:
-        own_t, e_high, own_m = pack(front, [tail_ranges, pivot_ranges[TICKS - 1 :] + tail_ranges, middle_ranges])
-        sets = relay((own_p, own_t, own_m, own_p[: (TICKS - 1) * p], e_high), member)
+        own_p, *e_halves = pack(front, [pivot_ranges, *cut(pivot_ranges)])
+        own_t, own_m, *n_halves = pack(front, [tail_ranges, middle_ranges, *cut(tail_ranges + middle_ranges)])
+        sets = relay((own_p, own_t, own_m, e_halves, n_halves), member)
     else:
-        own_t, own_m = pack(front, [tail_ranges, middle_ranges])
+        own_p, own_t, own_m = pack(front, [pivot_ranges, tail_ranges, middle_ranges])
         sets = tuple(((lax.all_gather(s, "blk")[:TICKS],),) * 2 for s in (own_p, own_t, own_m))
     dest, slot, address = routes(parent_group, row_block)
     out, w = pivot_rows(holder, front, sets[0])
     out, outgoing = other_rows(
-        holder, dest, slot, w, front, out, sets[1], [(tail_at, 0, tail_n)], TICKS * p, lax.axis_size("front")
+        holder, dest, slot, w, front, out, sets[1], [(tail_at, 0, tail_n)], 0, lax.axis_size("front")
     )
     incoming = lax.all_to_all(outgoing, "front", split_axis=0, concat_axis=0, tiled=True)
-    (factored,) = other_rows(holder, dest, slot, w, front, out, sets[2], middle, 0)
+    (factored,) = other_rows(holder, dest, slot, w, front, out, sets[2], middle, tail_n)
     assembled = add_blocks(address, incoming, parent_base)
     return (factored, assembled)
 

time: 211 us -> 198 us (0.938)
  the two profiles are of different devices: /device:TPU:30 before, /device:TPU:0 now
where the time goes in v5:
time: 198 us; the launch traced here: 197 us
  waiting for transfers between devices  83.5 us (42%)
  starting transfers between devices  68.7 us (35%)
  Pallas kernels  34.9 us (18%)
  local copies, waits for them, and re-layouts  5.18 us (3%)
  other arithmetic  3.48 us (2%)
    ppermute x22, waiting for transfers between devices, permute(): return lax.ppermute(value, 'blk', pairs)  83.5 us
    ppermute x22, starting transfers between devices, permute(): return lax.ppermute(value, 'blk', pairs)  62 us
    pallas_call x2, Pallas kernels, other_rows(): pl.pallas_call(functools.partial(other_kernel, counts, ranges, first_row,...  12.9 us
    pallas_call x1, Pallas kernels, pivot_rows(): pl.pallas_call(functools.partial(pivot_kernel, counts, width), name='pivo...  12.7 us
    pallas_call x2, Pallas kernels, pack(): pl.pallas_call(functools.partial(pack_kernel, pieces), out_shape=tuple((j...  6.32 us
  transfers between devices with their start and end apart: 24, of which 10 were waited for; matrix products, arithmetic and copies ran while one was open for 3% of the time, Pallas kernels for 14%

profile of v5, /device:TPU:0, one launch (start us, length us, event | category | flops | bytes accessed | tf_op | source)
XLA Modules:
  0.0 196.9 jit_solution(10923925349091769795)
XLA Ops:
  0.6 3.4 %shard_map.60 = (bf16[768,256]{1,0:T(8,128)(2,1)}, bf16[1024,256]{1,0:T(8,128)(2,1)}, bf16[896,256]{1,0:T(8,128)(2,1)}, bf16[896,256]{1,0:T(8,128)(2,1)}) custom-call(f32[3072,384]{1,0:T(8,128)} %front.9), custom_call_target="tpu_custom_call" | custom-call | tf_op jit(solution)/shard_map/pallas_call | solution.py:145
  4.9 2.9 %shard_map.59 = (bf16[1280,256]{1,0:T(8,128)(2,1)}, bf16[640,256]{1,0:T(8,128)(2,1)}, bf16[640,256]{1,0:T(8,128)(2,1)}) custom-call(f32[3072,384]{1,0:T(8,128)} %front.9), custom_call_target="tpu_custom_call" | custom-call | tf_op jit(solution)/shard_map/pallas_call | solution.py:145
  9.2 9.4 %collective-permute-start = (bf16[1280,256]{1,0:T(8,128)(2,1)}, bf16[1280,256]{1,0:T(8,128)(2,1)S(1)}, u32[]{:S(2)}, u32[]{:S(2)}) collective-permute-start(bf16[1280,256]{1,0:T(8,128)(2,1)} %get-tuple-element.13), channel_id=1, source_target_pairs={{0,4},{1,5},{2,6},{3,7},{8,12},{9,13},{10,14},{11,15},{16,20},{17,... | collective-permute-start | bytes 1966088 | tf_op jit(solution)/shard_map/ppermute | solution.py:23
  24.6 9.3 %collective-permute-done = bf16[1280,256]{1,0:T(8,128)(2,1)S(1)} collective-permute-done((bf16[1280,256]{1,0:T(8,128)(2,1)}, bf16[1280,256]{1,0:T(8,128)(2,1)S(1)}, u32[]{:S(2)}, u32[]{:S(2)}) %collective-permute-start) | collective-permute-done | bytes 655392 | tf_op jit(solution)/shard_map/ppermute | solution.py:23
  35.8 6.5 %collective-permute-done.9 = bf16[768,256]{1,0:T(8,128)(2,1)S(1)} collective-permute-done((bf16[768,256]{1,0:T(8,128)(2,1)S(1)}, bf16[768,256]{1,0:T(8,128)(2,1)S(1)}, u32[]{:S(2)}, u32[]{:S(2)}) %collective-permute-start.9) | collective-permute-done | bytes 393248 | tf_op jit(solution)/shard_map/ppermute | solution.py:23
  43.0 9.2 %collective-permute-done.18 = bf16[1024,256]{1,0:T(8,128)(2,1)S(1)} collective-permute-done((bf16[1024,256]{1,0:T(8,128)(2,1)S(1)}, bf16[1024,256]{1,0:T(8,128)(2,1)S(1)}, u32[]{:S(2)}, u32[]{:S(2)}) %collective-permute-start.18) | collective-permute-done | bytes 524320 | tf_op jit(solution)/shard_map/ppermute | solution.py:23
  53.5 31.7 %collective-permute-start.1 = (bf16[1280,256]{1,0:T(8,128)(2,1)S(1)}, bf16[1280,256]{1,0:T(8,128)(2,1)S(1)}, u32[]{:S(2)}, u32[]{:S(2)}) collective-permute-start(bf16[1280,256]{1,0:T(8,128)(2,1)S(1)} %broadcast_select_fusion.rest_0_), channel_id=1, source_target_pairs={{0,2},{1,3},{2,0},{3,1},{4,6},{5,7},{6,4},{7,5},{8,10},{9,11},{10,... | collective-permute-start | bytes 1966088 | tf_op jit(solution)/shard_map/ppermute | solution.py:23
  85.9 1.6 collective-permute-start.2
  89.2 2.1 %collective-permute-start.8 = (bf16[640,256]{1,0:T(8,128)(2,1)S(1)}, bf16[640,256]{1,0:T(8,128)(2,1)S(1)}, u32[]{:S(2)}, u32[]{:S(2)}) collective-permute-start(bf16[640,256]{1,0:T(8,128)(2,1)S(1)} %select_select_fusion.1.rest_4_), channel_id=1, source_target_pairs={{0,1},{1,0},{2,3},{3,2},{4,5},{5,4},{6,7},{7,6},{8,9},{9,8},{10,11... | collective-permute-start | bytes 983048 | tf_op jit(solution)/shard_map/ppermute | solution.py:23
  91.4 11.8 %collective-permute-done.1.rest_1_ = bf16[1280,256]{1,0:T(8,128)(2,1)S(1)} collective-permute-done((bf16[1280,256]{1,0:T(8,128)(2,1)S(1)}, bf16[1280,256]{1,0:T(8,128)(2,1)S(1)}, u32[]{:S(2)}, u32[]{:S(2)}) %collective-permute-start.1) | collective-permute-done | bytes 655392 | tf_op jit(solution)/shard_map/ppermute | solution.py:23
  103.2 2.1 %collective-permute-start.3 = (bf16[1280,256]{1,0:T(8,128)(2,1)S(1)}, bf16[1280,256]{1,0:T(8,128)(2,1)}, u32[]{:S(2)}, u32[]{:S(2)}) collective-permute-start(bf16[1280,256]{1,0:T(8,128)(2,1)S(1)} %collective-permute-done.1.rest_1_), channel_id=1, source_target_pairs={{0,1},{1,0},{2,3},{3,2},{4,5},{5,4},{6,7},{7,6},{8,9},{9,8},{10,11... | collective-permute-start | bytes 1966088 | tf_op jit(solution)/shard_map/ppermute | solution.py:23
  105.4 6.2 %collective-permute-done.10.rest_1_ = bf16[768,256]{1,0:T(8,128)(2,1)} collective-permute-done((bf16[768,256]{1,0:T(8,128)(2,1)S(1)}, bf16[768,256]{1,0:T(8,128)(2,1)}, u32[]{:S(2)}, u32[]{:S(2)}) %collective-permute-start.10) | collective-permute-done | bytes 393248 | tf_op jit(solution)/shard_map/ppermute | solution.py:23
  111.7 2.2 %collective-permute-start.12 = (bf16[768,256]{1,0:T(8,128)(2,1)}, bf16[768,256]{1,0:T(8,128)(2,1)}, u32[]{:S(2)}, u32[]{:S(2)}) collective-permute-start(bf16[768,256]{1,0:T(8,128)(2,1)} %collective-permute-done.10.rest_1_), channel_id=1, source_target_pairs={{0,1},{1,0},{2,3},{3,2},{4,5},{5,4},{6,7},{7,6},{8,9},{9,8},{10,11... | collective-permute-start | bytes 1179656 | tf_op jit(solution)/shard_map/ppermute | solution.py:23
  115.6 3.2 %all-to-all-start = ((s32[4,1,2]{2,1,0:T(1,128)}), s32[4,1,2]{2,1,0:T(1,128)S(1)}, u32[]{:S(2)}, u32[]{:S(2)}) async-start(s32[4,1,2]{2,1,0:T(1,128)} %copy.11), calls=%async_computation | async-start | bytes 4096 | tf_op jit(solution)/shard_map/all_to_all | solution.py:365
  118.8 14.4 %collective-permute-done.3.rest_3_ = bf16[1280,256]{1,0:T(8,128)(2,1)} collective-permute-done((bf16[1280,256]{1,0:T(8,128)(2,1)S(1)}, bf16[1280,256]{1,0:T(8,128)(2,1)}, u32[]{:S(2)}, u32[]{:S(2)}) %collective-permute-start.3) | collective-permute-done | bytes 655392 | tf_op jit(solution)/shard_map/ppermute | solution.py:23
  133.2 12.7 %pivot_rows.1 = (f32[3072,384]{1,0:T(8,128)}, bf16[1280,384]{1,0:T(8,128)(2,1)}) custom-call(s32[1]{0:T(128)} %bitcast.member_ref, f32[3072,384]{1,0:T(8,128)} %front.9, bf16[1280,256]{1,0:T(8,128)(2,1)} %copy-done.2, bf16[1280,256]{1,0:T(8,128)(2,1)} %copy-done.7, bf16[1280,256]{1,0:T(8,128)(2,1)} %copy-done.8, ...), custom_call_target="tpu_custom_call" | custom-call | tf_op jit(solution)/shard_map/pivot_rows/pallas_call | solution.py:266
  145.9 3.5 %collective-permute-done.17.rest_5_ = bf16[896,256]{1,0:T(8,128)(2,1)S(1)} collective-permute-done((bf16[896,256]{1,0:T(8,128)(2,1)S(1)}, bf16[896,256]{1,0:T(8,128)(2,1)S(1)}, u32[]{:S(2)}, u32[]{:S(2)}) %collective-permute-start.17) | collective-permute-done | bytes 458784 | tf_op jit(solution)/shard_map/ppermute | solution.py:23
  150.2 6.7 %tail_rows.1 = (f32[3072,384]{1,0:T(8,128)}, bf16[4,2,128,384]{3,2,1,0:T(8,128)(2,1)}) custom-call(s32[1]{0:T(128)} %bitcast.member_ref, s32[6]{0:T(128)} %bitcast.8, s32[6]{0:T(128)} %copy-done.17, bf16[1280,384]{1,0:T(8,128)(2,1)} %get-tuple-element.16.w, f32[3072,384]{1,0:T(8,128)} %front.9, ...), custom_call_target="tpu_custom_call", output_to_operand_aliasing={{0}: (5, {})} | custom-call | tf_op jit(solution)/shard_map/tail_rows/pallas_call | solution.py:337
  156.9 3.5 %all-to-all-start.1 = ((bf16[4,2,128,384]{3,2,1,0:T(8,128)(2,1)}), bf16[4,2,128,384]{3,2,1,0:T(8,128)(2,1)S(1)}, u32[]{:S(2)}, u32[]{:S(2)}) async-start(bf16[4,2,128,384]{3,2,1,0:T(8,128)(2,1)} %get-tuple-element.23), calls=%async_computation.1 | async-start | bytes 1572864 | tf_op jit(solution)/shard_map/all_to_all | solution.py:419
  160.4 1.8 collective-permute-start.20
  164.3 11.0 %collective-permute-done.20.rest_2_ = bf16[1024,256]{1,0:T(8,128)(2,1)S(1)} collective-permute-done((bf16[1024,256]{1,0:T(8,128)(2,1)S(1)}, bf16[1024,256]{1,0:T(8,128)(2,1)S(1)}, u32[]{:S(2)}, u32[]{:S(2)}) %collective-permute-start.20) | collective-permute-done | bytes 524320 | tf_op jit(solution)/shard_map/ppermute | solution.py:23
  175.3 10.7 %collective-permute-done.21.rest_3_ = bf16[1024,256]{1,0:T(8,128)(2,1)S(1)} collective-permute-done((bf16[1024,256]{1,0:T(8,128)(2,1)}, bf16[1024,256]{1,0:T(8,128)(2,1)S(1)}, u32[]{:S(2)}, u32[]{:S(2)}) %collective-permute-start.21) | collective-permute-done | bytes 524320 | tf_op jit(solution)/shard_map/ppermute | solution.py:23
  186.7 6.2 %middle_rows.1 = f32[3072,384]{1,0:T(8,128)} custom-call(s32[1]{0:T(128)} %bitcast.member_ref, s32[6]{0:T(128)} %bitcast.9, s32[6]{0:T(128)} %copy-done.17, bf16[1280,384]{1,0:T(8,128)(2,1)} %get-tuple-element.16.w, f32[3072,384]{1,0:T(8,128)} %front.9, f32[3072,384]{1,0:T(8,128)} %get-tuple-element.21.out_in, ...), custom_call_target="tpu_custom_call", output_to_operand_aliasing={{}: (5, {})} | custom-call | tf_op jit(solution)/shard_map/middle_rows/pallas_call | solution.py:337
  193.8 3.1 %add_blocks.1 = f32[1024,384]{1,0:T(8,128)} custom-call(s32[8]{0:T(128)} %reshape.81.address_ref, bf16[8,128,384]{2,1,0:T(8,128)(2,1)} %bitcast.7, f32[1024,384]{1,0:T(8,128)} %base.1), custom_call_target="tpu_custom_call" | custom-call | tf_op jit(solution)/shard_map/add_blocks/pallas_call | solution.py:382
  (85 shorter events, 20.9 us)
Async XLA Ops:
  4.1 19.2 %collective-permute-start.13 = (bf16[896,256]{1,0:T(8,128)(2,1)}, bf16[896,256]{1,0:T(8,128)(2,1)S(1)}, u32[]{:S(2)}, u32[]{:S(2)}) collective-permute-start(bf16[896,256]{1,0:T(8,128)(2,1)} %get-tuple-element.19), channel_id=1, source_target_pairs={{4,5},{12,13},{20,21},{28,29}} | collective-permute-start | bytes 1376264 | tf_op jit(solution)/shard_map/ppermute | solution.py:23
  7.8 13.7 %collective-permute-start.4 = (bf16[640,256]{1,0:T(8,128)(2,1)}, bf16[640,256]{1,0:T(8,128)(2,1)}, u32[]{:S(2)}, u32[]{:S(2)}) collective-permute-start(bf16[640,256]{1,0:T(8,128)(2,1)} %get-tuple-element.14), channel_id=1, source_target_pairs={{4,5},{12,13},{20,21},{28,29}} | collective-permute-start | bytes 983048 | tf_op jit(solution)/shard_map/ppermute | solution.py:23
  9.2 24.7 %collective-permute-start = (bf16[1280,256]{1,0:T(8,128)(2,1)}, bf16[1280,256]{1,0:T(8,128)(2,1)S(1)}, u32[]{:S(2)}, u32[]{:S(2)}) collective-permute-start(bf16[1280,256]{1,0:T(8,128)(2,1)} %get-tuple-element.13), channel_id=1, source_target_pairs={{0,4},{1,5},{2,6},{3,7},{8,12},{9,13},{10,14},{11,15},{16,20},{17,... | collective-permute-start | bytes 1966088 | tf_op jit(solution)/shard_map/ppermute | solution.py:23
  18.6 23.7 %collective-permute-start.9 = (bf16[768,256]{1,0:T(8,128)(2,1)S(1)}, bf16[768,256]{1,0:T(8,128)(2,1)S(1)}, u32[]{:S(2)}, u32[]{:S(2)}) collective-permute-start(bf16[768,256]{1,0:T(8,128)(2,1)S(1)} %copy-done.14), channel_id=1, source_target_pairs={{0,4},{1,5},{2,6},{3,7},{8,12},{9,13},{10,14},{11,15},{16,20},{17,... | collective-permute-start | bytes 1179656 | tf_op jit(solution)/shard_map/ppermute | solution.py:23
  19.9 32.2 %collective-permute-start.18 = (bf16[1024,256]{1,0:T(8,128)(2,1)S(1)}, bf16[1024,256]{1,0:T(8,128)(2,1)S(1)}, u32[]{:S(2)}, u32[]{:S(2)}) collective-permute-start(bf16[1024,256]{1,0:T(8,128)(2,1)S(1)} %copy-done.11), channel_id=1, source_target_pairs={{0,4},{1,5},{2,6},{3,7},{8,12},{9,13},{10,14},{11,15},{16,20},{17,... | collective-permute-start | bytes 1572872 | tf_op jit(solution)/shard_map/ppermute | solution.py:23
  22.5 30.9 %collective-permute-start.5 = (bf16[640,256]{1,0:T(8,128)(2,1)S(1)}, bf16[640,256]{1,0:T(8,128)(2,1)S(1)}, u32[]{:S(2)}, u32[]{:S(2)}) collective-permute-start(bf16[640,256]{1,0:T(8,128)(2,1)S(1)} %broadcast_select_fusion.4), channel_id=1, source_target_pairs={{4,6},{5,7},{12,14},{13,15},{20,22},{21,23},{28,30},{29,31}} | collective-permute-start | bytes 983048 | tf_op jit(solution)/shard_map/ppermute | solution.py:23
  23.2 61.9 %collective-permute-start.6 = (bf16[640,256]{1,0:T(8,128)(2,1)S(1)}, bf16[640,256]{1,0:T(8,128)(2,1)S(1)}, u32[]{:S(2)}, u32[]{:S(2)}) collective-permute-start(bf16[640,256]{1,0:T(8,128)(2,1)S(1)} %broadcast_select_fusion.4), channel_id=1, source_target_pairs={{4,0},{5,1},{12,8},{13,9},{20,16},{21,17},{28,24},{29,25}} | collective-permute-start | bytes 983048 | tf_op jit(solution)/shard_map/ppermute | solution.py:23
  34.0 51.9 %collective-permute-start.7 = (bf16[640,256]{1,0:T(8,128)(2,1)S(1)}, bf16[640,256]{1,0:T(8,128)(2,1)S(1)}, u32[]{:S(2)}, u32[]{:S(2)}) collective-permute-start(bf16[640,256]{1,0:T(8,128)(2,1)S(1)} %broadcast_select_fusion.4), channel_id=1, source_target_pairs={{4,2},{5,3},{12,10},{13,11},{20,18},{21,19},{28,26},{29,27}} | collective-permute-start | bytes 983048 | tf_op jit(solution)/shard_map/ppermute | solution.py:23
  42.3 45.2 %collective-permute-start.14 = (bf16[896,256]{1,0:T(8,128)(2,1)S(1)}, bf16[896,256]{1,0:T(8,128)(2,1)S(1)}, u32[]{:S(2)}, u32[]{:S(2)}) collective-permute-start(bf16[896,256]{1,0:T(8,128)(2,1)S(1)} %broadcast_select_fusion.2), channel_id=1, source_target_pairs={{4,6},{5,7},{12,14},{13,15},{20,22},{21,23},{28,30},{29,31}} | collective-permute-start | bytes 1376264 | tf_op jit(solution)/shard_map/ppermute | solution.py:23
  52.2 37.0 %collective-permute-start.15 = (bf16[896,256]{1,0:T(8,128)(2,1)S(1)}, bf16[896,256]{1,0:T(8,128)(2,1)S(1)}, u32[]{:S(2)}, u32[]{:S(2)}) collective-permute-start(bf16[896,256]{1,0:T(8,128)(2,1)S(1)} %broadcast_select_fusion.2), channel_id=1, source_target_pairs={{4,0},{5,1},{12,8},{13,9},{20,16},{21,17},{28,24},{29,25}} | collective-permute-start | bytes 1376264 | tf_op jit(solution)/shard_map/ppermute | solution.py:23
  53.5 49.7 %collective-permute-start.1 = (bf16[1280,256]{1,0:T(8,128)(2,1)S(1)}, bf16[1280,256]{1,0:T(8,128)(2,1)S(1)}, u32[]{:S(2)}, u32[]{:S(2)}) collective-permute-start(bf16[1280,256]{1,0:T(8,128)(2,1)S(1)} %broadcast_select_fusion.rest_0_), channel_id=1, source_target_pairs={{0,2},{1,3},{2,0},{3,1},{4,6},{5,7},{6,4},{7,5},{8,10},{9,11},{10,... | collective-permute-start | bytes 1966088 | tf_op jit(solution)/shard_map/ppermute | solution.py:23
  85.2 6.2 %collective-permute-start.16 = (bf16[896,256]{1,0:T(8,128)(2,1)S(1)}, bf16[896,256]{1,0:T(8,128)(2,1)S(1)}, u32[]{:S(2)}, u32[]{:S(2)}) collective-permute-start(bf16[896,256]{1,0:T(8,128)(2,1)S(1)} %broadcast_select_fusion.2), channel_id=1, source_target_pairs={{4,2},{5,3},{12,10},{13,11},{20,18},{21,19},{28,26},{29,27}} | collective-permute-start | bytes 1376264 | tf_op jit(solution)/shard_map/ppermute | solution.py:23
  85.9 27.9 %collective-permute-start.2 = (bf16[1280,256]{1,0:T(8,128)(2,1)S(1)}, bf16[1280,256]{1,0:T(8,128)(2,1)S(1)}, u32[]{:S(2)}, u32[]{:S(2)}) collective-permute-start(bf16[1280,256]{1,0:T(8,128)(2,1)S(1)} %broadcast_select_fusion.rest_0_), channel_id=1, source_target_pairs={{0,1},{1,0},{2,3},{3,2},{4,5},{5,4},{6,7},{7,6},{8,9},{9,8},{10,11... | collective-permute-start | bytes 1966088 | tf_op jit(solution)/shard_map/ppermute | solution.py:23
  87.5 24.1 %collective-permute-start.10 = (bf16[768,256]{1,0:T(8,128)(2,1)S(1)}, bf16[768,256]{1,0:T(8,128)(2,1)}, u32[]{:S(2)}, u32[]{:S(2)}) collective-permute-start(bf16[768,256]{1,0:T(8,128)(2,1)S(1)} %broadcast_select_fusion.3.rest_0_), channel_id=1, source_target_pairs={{0,2},{1,3},{2,0},{3,1},{4,6},{5,7},{6,4},{7,5},{8,10},{9,11},{10,... | collective-permute-start | bytes 1179656 | tf_op jit(solution)/shard_map/ppermute | solution.py:23
  89.2 22.5 %collective-permute-start.8 = (bf16[640,256]{1,0:T(8,128)(2,1)S(1)}, bf16[640,256]{1,0:T(8,128)(2,1)S(1)}, u32[]{:S(2)}, u32[]{:S(2)}) collective-permute-start(bf16[640,256]{1,0:T(8,128)(2,1)S(1)} %select_select_fusion.1.rest_4_), channel_id=1, source_target_pairs={{0,1},{1,0},{2,3},{3,2},{4,5},{5,4},{6,7},{7,6},{8,9},{9,8},{10,11... | collective-permute-start | bytes 983048 | tf_op jit(solution)/shard_map/ppermute | solution.py:23
  91.4 54.5 %collective-permute-start.11 = (bf16[768,256]{1,0:T(8,128)(2,1)S(1)}, bf16[768,256]{1,0:T(8,128)(2,1)}, u32[]{:S(2)}, u32[]{:S(2)}) collective-permute-start(bf16[768,256]{1,0:T(8,128)(2,1)S(1)} %broadcast_select_fusion.3.rest_0_), channel_id=1, source_target_pairs={{0,1},{1,0},{2,3},{3,2},{4,5},{5,4},{6,7},{7,6},{8,9},{9,8},{10,11... | collective-permute-start | bytes 1179656 | tf_op jit(solution)/shard_map/ppermute | solution.py:23
  103.2 30.0 %collective-permute-start.3 = (bf16[1280,256]{1,0:T(8,128)(2,1)S(1)}, bf16[1280,256]{1,0:T(8,128)(2,1)}, u32[]{:S(2)}, u32[]{:S(2)}) collective-permute-start(bf16[1280,256]{1,0:T(8,128)(2,1)S(1)} %collective-permute-done.1.rest_1_), channel_id=1, source_target_pairs={{0,1},{1,0},{2,3},{3,2},{4,5},{5,4},{6,7},{7,6},{8,9},{9,8},{10,11... | collective-permute-start | bytes 1966088 | tf_op jit(solution)/shard_map/ppermute | solution.py:23
  111.6 50.6 %collective-permute-start.19 = (bf16[1024,256]{1,0:T(8,128)(2,1)S(1)}, bf16[1024,256]{1,0:T(8,128)(2,1)}, u32[]{:S(2)}, u32[]{:S(2)}) collective-permute-start(bf16[1024,256]{1,0:T(8,128)(2,1)S(1)} %broadcast_select_fusion.1.rest_0_), channel_id=1, source_target_pairs={{0,2},{1,3},{2,0},{3,1},{4,6},{5,7},{6,4},{7,5},{8,10},{9,11},{10,... | collective-permute-start | bytes 1572872 | tf_op jit(solution)/shard_map/ppermute | solution.py:23
  111.7 34.2 %collective-permute-start.12 = (bf16[768,256]{1,0:T(8,128)(2,1)}, bf16[768,256]{1,0:T(8,128)(2,1)}, u32[]{:S(2)}, u32[]{:S(2)}) collective-permute-start(bf16[768,256]{1,0:T(8,128)(2,1)} %collective-permute-done.10.rest_1_), channel_id=1, source_target_pairs={{0,1},{1,0},{2,3},{3,2},{4,5},{5,4},{6,7},{7,6},{8,9},{9,8},{10,11... | collective-permute-start | bytes 1179656 | tf_op jit(solution)/shard_map/ppermute | solution.py:23
  114.7 34.7 %collective-permute-start.17 = (bf16[896,256]{1,0:T(8,128)(2,1)S(1)}, bf16[896,256]{1,0:T(8,128)(2,1)S(1)}, u32[]{:S(2)}, u32[]{:S(2)}) collective-permute-start(bf16[896,256]{1,0:T(8,128)(2,1)S(1)} %select_select_fusion.rest_4_), channel_id=1, source_target_pairs={{0,1},{1,0},{2,3},{3,2},{4,5},{5,4},{6,7},{7,6},{8,9},{9,8},{10,11... | collective-permute-start | bytes 1376264 | tf_op jit(solution)/shard_map/ppermute | solution.py:23
  115.6 41.3 %all-to-all-start = ((s32[4,1,2]{2,1,0:T(1,128)}), s32[4,1,2]{2,1,0:T(1,128)S(1)}, u32[]{:S(2)}, u32[]{:S(2)}) async-start(s32[4,1,2]{2,1,0:T(1,128)} %copy.11), calls=%async_computation | async-start | bytes 4096 | tf_op jit(solution)/shard_map/all_to_all | solution.py:365
  156.9 36.1 %all-to-all-start.1 = ((bf16[4,2,128,384]{3,2,1,0:T(8,128)(2,1)}), bf16[4,2,128,384]{3,2,1,0:T(8,128)(2,1)S(1)}, u32[]{:S(2)}, u32[]{:S(2)}) async-start(bf16[4,2,128,384]{3,2,1,0:T(8,128)(2,1)} %get-tuple-element.23), calls=%async_computation.1 | async-start | bytes 1572864 | tf_op jit(solution)/shard_map/all_to_all | solution.py:419
  160.4 14.9 %collective-permute-start.20 = (bf16[1024,256]{1,0:T(8,128)(2,1)S(1)}, bf16[1024,256]{1,0:T(8,128)(2,1)S(1)}, u32[]{:S(2)}, u32[]{:S(2)}) collective-permute-start(bf16[1024,256]{1,0:T(8,128)(2,1)S(1)} %broadcast_select_fusion.1.rest_0_), channel_id=1, source_target_pairs={{0,1},{1,0},{2,3},{3,2},{4,5},{5,4},{6,7},{7,6},{8,9},{9,8},{10,11... | collective-permute-start | bytes 1572872 | tf_op jit(solution)/shard_map/ppermute | solution.py:23
  162.2 23.7 %collective-permute-start.21 = (bf16[1024,256]{1,0:T(8,128)(2,1)}, bf16[1024,256]{1,0:T(8,128)(2,1)S(1)}, u32[]{:S(2)}, u32[]{:S(2)}) collective-permute-start(bf16[1024,256]{1,0:T(8,128)(2,1)} %collective-permute-done.19.rest_1_), channel_id=1, source_target_pairs={{0,1},{1,0},{2,3},{3,2},{4,5},{5,4},{6,7},{7,6},{8,9},{9,8},{10,11... | collective-permute-start | bytes 1572872 | tf_op jit(solution)/shard_map/ppermute | solution.py:23
  (19 other events, 646.5 us)

commit v6 on v5

--- a/solution.py
+++ b/solution.py
@@ -29,7 +29,7 @@
     distant = [(m, m + 4) for m in range(4)]
     beside, back, mid, up = [(4, 5)], [(4, 0), (5, 1)], [(4, 2), (5, 3)], [(4, 6), (5, 7)]
     level = member // 2
-    a, b, c, e_halves, n_halves = parts
+    a, b, c, e_halves, n = parts
 
     def slabs(own):
         cur = jnp.where(member < 4, own, permute(own, distant))
@@ -45,7 +45,16 @@
         half = jnp.where(level == 2, half, jnp.where(level == 3, to_up, jnp.where(level == 0, to_back, to_mid)))
         return half, permute(half, across)
 
-    early, late = halves(*e_halves), halves(*n_halves)
+    def whole(own):
+        rows = jnp.where(member == 5, permute(own, beside), own)
+        to_up = permute(rows, up)
+        to_back = permute(rows, back)
+        to_mid = permute(rows, mid)
+        return (
+            jnp.where(level == 2, rows, jnp.where(level == 3, to_up, jnp.where(level == 0, to_back, to_mid))),
+        )
+
+    early, late = halves(*e_halves), whole(n)
     return (slabs(a), early), (slabs(b), late), (slabs(c), late)
 
 
@@ -71,8 +80,12 @@
 
 
 def start_last(member, refs, target, sems, first_row, rows):
+    if len(refs) == 1 and len(refs[0].shape) == 3:
+        copies = [pltpu.make_async_copy(refs[0].at[TICKS - 1], target, sems.at[0])]
+        copies[0].start()
+        return copies
     if len(refs) == 1:
-        copies = [pltpu.make_async_copy(refs[0].at[TICKS - 1], target, sems.at[0])]
+        copies = [pltpu.make_async_copy(refs[0].at[pl.ds(first_row, rows)], target, sems.at[0])]
         copies[0].start()
         return copies
     half, overhalf = refs
@@ -406,8 +419,8 @@
         at += count
     if lax.axis_size("blk") == 8:
         own_p, *e_halves = pack(front, [pivot_ranges, *cut(pivot_ranges)])
-        own_t, own_m, *n_halves = pack(front, [tail_ranges, middle_ranges, *cut(tail_ranges + middle_ranges)])
-        sets = relay((own_p, own_t, own_m, e_halves, n_halves), member)
+        own_t, own_m, own_n = pack(front, [tail_ranges, middle_ranges, tail_ranges + middle_ranges])
+        sets = relay((own_p, own_t, own_m, e_halves, own_n), member)
     else:
         own_p, own_t, own_m = pack(front, [pivot_ranges, tail_ranges, middle_ranges])
         sets = tuple(((lax.all_gather(s, "blk")[:TICKS],),) * 2 for s in (own_p, own_t, own_m))

time: 198 us -> 199 us (level)
  waiting for transfers between devices: 83.5 us -> 73.1 us
  starting transfers between devices: 68.7 us -> 74.8 us
  other arithmetic: 3.48 us -> 7.75 us
    ppermute x22 -> x21, waiting for transfers between devices: 83.5 us -> 73.1 us  [permute(): return lax.ppermute(value, 'blk', pairs)]
    ppermute x22 -> x21, starting transfers between devices: 62 us -> 68.1 us  [permute(): return lax.ppermute(value, 'blk', pairs)]
    select_n x0 -> x2, other arithmetic: none -> 2.37 us  [the longest x1 2.27 us: whole(): jnp.where(level == 2, rows, jnp.where(level == 3, to_up, jnp.where(level...]
    unnamed x38 -> x42, local copies, waits for them, and re-layouts: 3.35 us -> 4.34 us
  transfers between devices with their start and end apart: 24 -> 23, of which waited for: 10 -> 7; matrix products, arithmetic and copies ran while one was open for 3% -> 5% of each run, Pallas kernels for 14% -> 14%
where the time goes in v6:
time: 199 us; the launch traced here: 198 us
  starting transfers between devices  74.8 us (38%)
  waiting for transfers between devices  73.1 us (37%)
  Pallas kernels  35.1 us (18%)
  other arithmetic  7.75 us (4%)
  local copies, waits for them, and re-layouts  6.21 us (3%)
    ppermute x21, waiting for transfers between devices, permute(): return lax.ppermute(value, 'blk', pairs)  73.1 us
    ppermute x21, starting transfers between devices, permute(): return lax.ppermute(value, 'blk', pairs)  68.1 us
    pallas_call x2, Pallas kernels, other_rows(): pl.pallas_call(functools.partial(other_kernel, counts, ranges, first_row,...  12.9 us
    pallas_call x1, Pallas kernels, pivot_rows(): pl.pallas_call(functools.partial(pivot_kernel, counts, width), name='pivo...  12.7 us
    pallas_call x2, Pallas kernels, pack(): pl.pallas_call(functools.partial(pack_kernel, pieces), out_shape=tuple((j...  6.42 us
    unnamed x42, local copies, waits for them, and re-layouts  4.34 us
  transfers between devices with their start and end apart: 23, of which 7 were waited for; matrix products, arithmetic and copies ran while one was open for 5% of the time, Pallas kernels for 14%

profile of v6, /device:TPU:0, one launch (start us, length us, event | category | flops | bytes accessed | tf_op | source)
XLA Modules:
  0.0 198.0 jit_solution(16129257838172639901)
XLA Ops:
  0.6 3.3 %shard_map.60 = (bf16[768,256]{1,0:T(8,128)(2,1)}, bf16[1024,256]{1,0:T(8,128)(2,1)}, bf16[1792,256]{1,0:T(8,128)(2,1)}) custom-call(f32[3072,384]{1,0:T(8,128)} %front.9), custom_call_target="tpu_custom_call" | custom-call | tf_op jit(solution)/shard_map/pallas_call | solution.py:158
  4.9 3.1 %shard_map.59 = (bf16[1280,256]{1,0:T(8,128)(2,1)}, bf16[640,256]{1,0:T(8,128)(2,1)}, bf16[640,256]{1,0:T(8,128)(2,1)}) custom-call(f32[3072,384]{1,0:T(8,128)} %front.9), custom_call_target="tpu_custom_call" | custom-call | tf_op jit(solution)/shard_map/pallas_call | solution.py:158
  8.7 10.2 %collective-permute-start = (bf16[1280,256]{1,0:T(8,128)(2,1)}, bf16[1280,256]{1,0:T(8,128)(2,1)}, u32[]{:S(2)}, u32[]{:S(2)}) collective-permute-start(bf16[1280,256]{1,0:T(8,128)(2,1)} %get-tuple-element.12), channel_id=1, source_target_pairs={{0,4},{1,5},{2,6},{3,7},{8,12},{9,13},{10,14},{11,15},{16,20},{17,... | collective-permute-start | bytes 1966088 | tf_op jit(solution)/shard_map/ppermute | solution.py:23
  20.2 2.1 %collective-permute-start.17 = (bf16[1024,256]{1,0:T(8,128)(2,1)}, bf16[1024,256]{1,0:T(8,128)(2,1)}, u32[]{:S(2)}, u32[]{:S(2)}) collective-permute-start(bf16[1024,256]{1,0:T(8,128)(2,1)} %get-tuple-element.20), channel_id=1, source_target_pairs={{0,4},{1,5},{2,6},{3,7},{8,12},{9,13},{10,14},{11,15},{16,20},{17,... | collective-permute-start | bytes 1572872 | tf_op jit(solution)/shard_map/ppermute | solution.py:23
  24.2 17.5 %collective-permute-done.9 = bf16[768,256]{1,0:T(8,128)(2,1)S(1)} collective-permute-done((bf16[768,256]{1,0:T(8,128)(2,1)S(1)}, bf16[768,256]{1,0:T(8,128)(2,1)S(1)}, u32[]{:S(2)}, u32[]{:S(2)}) %collective-permute-start.9) | collective-permute-done | bytes 393248 | tf_op jit(solution)/shard_map/ppermute | solution.py:23
  46.7 31.9 %collective-permute-start.10 = (bf16[768,256]{1,0:T(8,128)(2,1)S(1)}, bf16[768,256]{1,0:T(8,128)(2,1)}, u32[]{:S(2)}, u32[]{:S(2)}) collective-permute-start(bf16[768,256]{1,0:T(8,128)(2,1)S(1)} %broadcast_select_fusion.3.rest_0_), channel_id=1, source_target_pairs={{0,2},{1,3},{2,0},{3,1},{4,6},{5,7},{6,4},{7,5},{8,10},{9,11},{10,... | collective-permute-start | bytes 1179656 | tf_op jit(solution)/shard_map/ppermute | solution.py:23
  78.8 5.1 %collective-permute-start.1 = (bf16[1280,256]{1,0:T(8,128)(2,1)S(1)}, bf16[1280,256]{1,0:T(8,128)(2,1)S(1)}, u32[]{:S(2)}, u32[]{:S(2)}) collective-permute-start(bf16[1280,256]{1,0:T(8,128)(2,1)S(1)} %broadcast_select_fusion.1.rest_0_), channel_id=1, source_target_pairs={{0,2},{1,3},{2,0},{3,1},{4,6},{5,7},{6,4},{7,5},{8,10},{9,11},{10,... | collective-permute-start | bytes 1966088 | tf_op jit(solution)/shard_map/ppermute | solution.py:23
  83.9 1.6 collective-permute-start.14
  86.8 1.6 collective-permute-start.16
  89.5 1.6 collective-permute-start.8
  91.9 3.2 %all-to-all-start = ((s32[4,1,2]{2,1,0:T(1,128)}), s32[4,1,2]{2,1,0:T(1,128)S(1)}, u32[]{:S(2)}, u32[]{:S(2)}) async-start(s32[4,1,2]{2,1,0:T(1,128)} %copy.11), calls=%async_computation | async-start | bytes 4096 | tf_op jit(solution)/shard_map/all_to_all | solution.py:378
  95.1 2.9 %collective-permute-done.8.rest_5_ = bf16[640,256]{1,0:T(8,128)(2,1)S(1)} collective-permute-done((bf16[640,256]{1,0:T(8,128)(2,1)S(1)}, bf16[640,256]{1,0:T(8,128)(2,1)S(1)}, u32[]{:S(2)}, u32[]{:S(2)}) %collective-permute-start.8) | collective-permute-done | bytes 327712 | tf_op jit(solution)/shard_map/ppermute | solution.py:23
  99.4 20.0 %collective-permute-done.1.rest_1_ = bf16[1280,256]{1,0:T(8,128)(2,1)S(1)} collective-permute-done((bf16[1280,256]{1,0:T(8,128)(2,1)S(1)}, bf16[1280,256]{1,0:T(8,128)(2,1)S(1)}, u32[]{:S(2)}, u32[]{:S(2)}) %collective-permute-start.1) | collective-permute-done | bytes 655392 | tf_op jit(solution)/shard_map/ppermute | solution.py:23
  122.7 1.6 collective-permute-start.12
  124.3 2.3 %select_select_fusion.rest_4_ = bf16[1792,256]{1,0:T(8,128)(2,1)} fusion(bf16[1792,256]{1,0:T(8,128)(2,1)S(1)} %broadcast_select_fusion, bf16[1792,256]{1,0:T(8,128)(2,1)} %collective-permute-done.14, bf16[1792,256]{1,0:T(8,128)(2,1)} %collective-permute-done.15, bf16[1792,256]{1,0:T(8,128)(2,1)} %collective-permute-done.16, pred[]{:T(512)S(6)} %eq.71, ...), kind=kLoop, calls=%fused_computation | loop fusion | flops 1376256 | bytes 4587523 | tf_op jit(solution)/shard_map/jit(_where)/select_n | solution.py:54
  126.6 10.5 %collective-permute-done.3.rest_3_ = bf16[1280,256]{1,0:T(8,128)(2,1)S(1)} collective-permute-done((bf16[1280,256]{1,0:T(8,128)(2,1)S(1)}, bf16[1280,256]{1,0:T(8,128)(2,1)S(1)}, u32[]{:S(2)}, u32[]{:S(2)}) %collective-permute-start.3) | collective-permute-done | bytes 655392 | tf_op jit(solution)/shard_map/ppermute | solution.py:23
  138.0 12.7 %pivot_rows.1 = (f32[3072,384]{1,0:T(8,128)}, bf16[1280,384]{1,0:T(8,128)(2,1)}) custom-call(s32[1]{0:T(128)} %bitcast.member_ref, f32[3072,384]{1,0:T(8,128)} %front.9, bf16[1280,256]{1,0:T(8,128)(2,1)} %copy-done.1, bf16[1280,256]{1,0:T(8,128)(2,1)} %copy-done.7, bf16[1280,256]{1,0:T(8,128)(2,1)} %copy-done.8, bf16[1280,256]{1,0:T(8,128)(2,1)} %copy-done.9, ...), custom_call_target="tpu_custom_call" | custom-call | tf_op jit(solution)/shard_map/pivot_rows/pallas_call | solution.py:279
  151.2 6.7 %tail_rows.1 = (f32[3072,384]{1,0:T(8,128)}, bf16[4,2,128,384]{3,2,1,0:T(8,128)(2,1)}) custom-call(s32[1]{0:T(128)} %bitcast.member_ref, s32[6]{0:T(128)} %bitcast.8, s32[6]{0:T(128)} %copy-done.19, bf16[1280,384]{1,0:T(8,128)(2,1)} %get-tuple-element.15.w, f32[3072,384]{1,0:T(8,128)} %front.9, ...), custom_call_target="tpu_custom_call", output_to_operand_aliasing={{0}: (5, {})} | custom-call | tf_op jit(solution)/shard_map/tail_rows/pallas_call | solution.py:350
  157.9 3.5 %all-to-all-start.1 = ((bf16[4,2,128,384]{3,2,1,0:T(8,128)(2,1)}), bf16[4,2,128,384]{3,2,1,0:T(8,128)(2,1)S(1)}, u32[]{:S(2)}, u32[]{:S(2)}) async-start(bf16[4,2,128,384]{3,2,1,0:T(8,128)(2,1)} %get-tuple-element.21), calls=%async_computation.1 | async-start | bytes 1572864 | tf_op jit(solution)/shard_map/all_to_all | solution.py:432
  161.4 1.6 collective-permute-start.19
  165.4 10.9 %collective-permute-done.19.rest_2_ = bf16[1024,256]{1,0:T(8,128)(2,1)S(1)} collective-permute-done((bf16[1024,256]{1,0:T(8,128)(2,1)S(1)}, bf16[1024,256]{1,0:T(8,128)(2,1)S(1)}, u32[]{:S(2)}, u32[]{:S(2)}) %collective-permute-start.19) | collective-permute-done | bytes 524320 | tf_op jit(solution)/shard_map/ppermute | solution.py:23
  176.3 10.7 %collective-permute-done.20.rest_3_ = bf16[1024,256]{1,0:T(8,128)(2,1)S(1)} collective-permute-done((bf16[1024,256]{1,0:T(8,128)(2,1)}, bf16[1024,256]{1,0:T(8,128)(2,1)S(1)}, u32[]{:S(2)}, u32[]{:S(2)}) %collective-permute-start.20) | collective-permute-done | bytes 524320 | tf_op jit(solution)/shard_map/ppermute | solution.py:23
  187.7 6.3 %middle_rows.1 = f32[3072,384]{1,0:T(8,128)} custom-call(s32[1]{0:T(128)} %bitcast.member_ref, s32[6]{0:T(128)} %bitcast.9, s32[6]{0:T(128)} %copy-done.19, bf16[1280,384]{1,0:T(8,128)(2,1)} %get-tuple-element.15.w, f32[3072,384]{1,0:T(8,128)} %front.9, f32[3072,384]{1,0:T(8,128)} %get-tuple-element.19.out_in, ...), custom_call_target="tpu_custom_call", output_to_operand_aliasing={{}: (5, {})} | custom-call | tf_op jit(solution)/shard_map/middle_rows/pallas_call | solution.py:350
  194.9 3.1 %add_blocks.1 = f32[1024,384]{1,0:T(8,128)} custom-call(s32[8]{0:T(128)} %reshape.81.address_ref, bf16[8,128,384]{2,1,0:T(8,128)(2,1)} %bitcast.7, f32[1024,384]{1,0:T(8,128)} %base.1), custom_call_target="tpu_custom_call" | custom-call | tf_op jit(solution)/shard_map/add_blocks/pallas_call | solution.py:395
  (87 shorter events, 23.1 us)
Async XLA Ops:
  4.0 41.7 %collective-permute-start.13 = (bf16[1792,256]{1,0:T(8,128)(2,1)}, bf16[1792,256]{1,0:T(8,128)(2,1)S(1)}, u32[]{:S(2)}, u32[]{:S(2)}) collective-permute-start(bf16[1792,256]{1,0:T(8,128)(2,1)} %get-tuple-element.18), channel_id=1, source_target_pairs={{4,5},{12,13},{20,21},{28,29}} | collective-permute-start | bytes 2752520 | tf_op jit(solution)/shard_map/ppermute | solution.py:23
  8.0 14.5 %collective-permute-start.4 = (bf16[640,256]{1,0:T(8,128)(2,1)}, bf16[640,256]{1,0:T(8,128)(2,1)S(1)}, u32[]{:S(2)}, u32[]{:S(2)}) collective-permute-start(bf16[640,256]{1,0:T(8,128)(2,1)} %get-tuple-element.13), channel_id=1, source_target_pairs={{4,5},{12,13},{20,21},{28,29}} | collective-permute-start | bytes 983048 | tf_op jit(solution)/shard_map/ppermute | solution.py:23
  8.7 35.2 %collective-permute-start = (bf16[1280,256]{1,0:T(8,128)(2,1)}, bf16[1280,256]{1,0:T(8,128)(2,1)}, u32[]{:S(2)}, u32[]{:S(2)}) collective-permute-start(bf16[1280,256]{1,0:T(8,128)(2,1)} %get-tuple-element.12), channel_id=1, source_target_pairs={{0,4},{1,5},{2,6},{3,7},{8,12},{9,13},{10,14},{11,15},{16,20},{17,... | collective-permute-start | bytes 1966088 | tf_op jit(solution)/shard_map/ppermute | solution.py:23
  18.9 22.9 %collective-permute-start.9 = (bf16[768,256]{1,0:T(8,128)(2,1)S(1)}, bf16[768,256]{1,0:T(8,128)(2,1)S(1)}, u32[]{:S(2)}, u32[]{:S(2)}) collective-permute-start(bf16[768,256]{1,0:T(8,128)(2,1)S(1)} %copy-done.12), channel_id=1, source_target_pairs={{0,4},{1,5},{2,6},{3,7},{8,12},{9,13},{10,14},{11,15},{16,20},{17,... | collective-permute-start | bytes 1179656 | tf_op jit(solution)/shard_map/ppermute | solution.py:23
  20.2 58.6 %collective-permute-start.17 = (bf16[1024,256]{1,0:T(8,128)(2,1)}, bf16[1024,256]{1,0:T(8,128)(2,1)}, u32[]{:S(2)}, u32[]{:S(2)}) collective-permute-start(bf16[1024,256]{1,0:T(8,128)(2,1)} %get-tuple-element.20), channel_id=1, source_target_pairs={{0,4},{1,5},{2,6},{3,7},{8,12},{9,13},{10,14},{11,15},{16,20},{17,... | collective-permute-start | bytes 1572872 | tf_op jit(solution)/shard_map/ppermute | solution.py:23
  22.5 99.6 %copy-start.19 = (s32[6]{0:T(128)}, s32[6]{0:T(128)S(1)}, u32[]{:S(2)}) copy-start(s32[6]{0:T(128)S(1)} %convert_reduce_fusion.slot_ref) | copy-start | bytes 76
  23.5 60.4 %collective-permute-start.5 = (bf16[640,256]{1,0:T(8,128)(2,1)S(1)}, bf16[640,256]{1,0:T(8,128)(2,1)S(1)}, u32[]{:S(2)}, u32[]{:S(2)}) collective-permute-start(bf16[640,256]{1,0:T(8,128)(2,1)S(1)} %broadcast_select_fusion.4), channel_id=1, source_target_pairs={{4,6},{5,7},{12,14},{13,15},{20,22},{21,23},{28,30},{29,31}} | collective-permute-start | bytes 983048 | tf_op jit(solution)/shard_map/ppermute | solution.py:23
  42.5 43.0 %collective-permute-start.6 = (bf16[640,256]{1,0:T(8,128)(2,1)S(1)}, bf16[640,256]{1,0:T(8,128)(2,1)S(1)}, u32[]{:S(2)}, u32[]{:S(2)}) collective-permute-start(bf16[640,256]{1,0:T(8,128)(2,1)S(1)} %broadcast_select_fusion.4), channel_id=1, source_target_pairs={{4,0},{5,1},{12,8},{13,9},{20,16},{21,17},{28,24},{29,25}} | collective-permute-start | bytes 983048 | tf_op jit(solution)/shard_map/ppermute | solution.py:23
  43.9 42.9 %collective-permute-start.7 = (bf16[640,256]{1,0:T(8,128)(2,1)S(1)}, bf16[640,256]{1,0:T(8,128)(2,1)S(1)}, u32[]{:S(2)}, u32[]{:S(2)}) collective-permute-start(bf16[640,256]{1,0:T(8,128)(2,1)S(1)} %broadcast_select_fusion.4), channel_id=1, source_target_pairs={{4,2},{5,3},{12,10},{13,11},{20,18},{21,19},{28,26},{29,27}} | collective-permute-start | bytes 983048 | tf_op jit(solution)/shard_map/ppermute | solution.py:23
  46.7 42.8 %collective-permute-start.10 = (bf16[768,256]{1,0:T(8,128)(2,1)S(1)}, bf16[768,256]{1,0:T(8,128)(2,1)}, u32[]{:S(2)}, u32[]{:S(2)}) collective-permute-start(bf16[768,256]{1,0:T(8,128)(2,1)S(1)} %broadcast_select_fusion.3.rest_0_), channel_id=1, source_target_pairs={{0,2},{1,3},{2,0},{3,1},{4,6},{5,7},{6,4},{7,5},{8,10},{9,11},{10,... | collective-permute-start | bytes 1179656 | tf_op jit(solution)/shard_map/ppermute | solution.py:23
  78.8 40.7 %collective-permute-start.1 = (bf16[1280,256]{1,0:T(8,128)(2,1)S(1)}, bf16[1280,256]{1,0:T(8,128)(2,1)S(1)}, u32[]{:S(2)}, u32[]{:S(2)}) collective-permute-start(bf16[1280,256]{1,0:T(8,128)(2,1)S(1)} %broadcast_select_fusion.1.rest_0_), channel_id=1, source_target_pairs={{0,2},{1,3},{2,0},{3,1},{4,6},{5,7},{6,4},{7,5},{8,10},{9,11},{10,... | collective-permute-start | bytes 1966088 | tf_op jit(solution)/shard_map/ppermute | solution.py:23
  83.9 38.2 %collective-permute-start.14 = (bf16[1792,256]{1,0:T(8,128)(2,1)S(1)}, bf16[1792,256]{1,0:T(8,128)(2,1)}, u32[]{:S(2)}, u32[]{:S(2)}) collective-permute-start(bf16[1792,256]{1,0:T(8,128)(2,1)S(1)} %broadcast_select_fusion), channel_id=1, source_target_pairs={{4,6},{5,7},{12,14},{13,15},{20,22},{21,23},{28,30},{29,31}} | collective-permute-start | bytes 2752520 | tf_op jit(solution)/shard_map/ppermute | solution.py:23
  85.5 37.2 %collective-permute-start.15 = (bf16[1792,256]{1,0:T(8,128)(2,1)S(1)}, bf16[1792,256]{1,0:T(8,128)(2,1)}, u32[]{:S(2)}, u32[]{:S(2)}) collective-permute-start(bf16[1792,256]{1,0:T(8,128)(2,1)S(1)} %broadcast_select_fusion), channel_id=1, source_target_pairs={{4,0},{5,1},{12,8},{13,9},{20,16},{21,17},{28,24},{29,25}} | collective-permute-start | bytes 2752520 | tf_op jit(solution)/shard_map/ppermute | solution.py:23
  86.8 35.9 %collective-permute-start.16 = (bf16[1792,256]{1,0:T(8,128)(2,1)S(1)}, bf16[1792,256]{1,0:T(8,128)(2,1)}, u32[]{:S(2)}, u32[]{:S(2)}) collective-permute-start(bf16[1792,256]{1,0:T(8,128)(2,1)S(1)} %broadcast_select_fusion), channel_id=1, source_target_pairs={{4,2},{5,3},{12,10},{13,11},{20,18},{21,19},{28,26},{29,27}} | collective-permute-start | bytes 2752520 | tf_op jit(solution)/shard_map/ppermute | solution.py:23
  89.5 8.4 %collective-permute-start.8 = (bf16[640,256]{1,0:T(8,128)(2,1)S(1)}, bf16[640,256]{1,0:T(8,128)(2,1)S(1)}, u32[]{:S(2)}, u32[]{:S(2)}) collective-permute-start(bf16[640,256]{1,0:T(8,128)(2,1)S(1)} %select_select_fusion.1.rest_4_), channel_id=1, source_target_pairs={{0,1},{1,0},{2,3},{3,2},{4,5},{5,4},{6,7},{7,6},{8,9},{9,8},{10,11... | collective-permute-start | bytes 983048 | tf_op jit(solution)/shard_map/ppermute | solution.py:23
  91.9 66.0 %all-to-all-start = ((s32[4,1,2]{2,1,0:T(1,128)}), s32[4,1,2]{2,1,0:T(1,128)S(1)}, u32[]{:S(2)}, u32[]{:S(2)}) async-start(s32[4,1,2]{2,1,0:T(1,128)} %copy.11), calls=%async_computation | async-start | bytes 4096 | tf_op jit(solution)/shard_map/all_to_all | solution.py:378
  97.9 28.6 %collective-permute-start.2 = (bf16[1280,256]{1,0:T(8,128)(2,1)S(1)}, bf16[1280,256]{1,0:T(8,128)(2,1)S(1)}, u32[]{:S(2)}, u32[]{:S(2)}) collective-permute-start(bf16[1280,256]{1,0:T(8,128)(2,1)S(1)} %broadcast_select_fusion.1.rest_0_), channel_id=1, source_target_pairs={{0,1},{1,0},{2,3},{3,2},{4,5},{5,4},{6,7},{7,6},{8,9},{9,8},{10,11... | collective-permute-start | bytes 1966088 | tf_op jit(solution)/shard_map/ppermute | solution.py:23
  119.5 17.6 %collective-permute-start.3 = (bf16[1280,256]{1,0:T(8,128)(2,1)S(1)}, bf16[1280,256]{1,0:T(8,128)(2,1)S(1)}, u32[]{:S(2)}, u32[]{:S(2)}) collective-permute-start(bf16[1280,256]{1,0:T(8,128)(2,1)S(1)} %collective-permute-done.1.rest_1_), channel_id=1, source_target_pairs={{0,1},{1,0},{2,3},{3,2},{4,5},{5,4},{6,7},{7,6},{8,9},{9,8},{10,11... | collective-permute-start | bytes 1966088 | tf_op jit(solution)/shard_map/ppermute | solution.py:23
  122.1 28.5 %collective-permute-start.11 = (bf16[768,256]{1,0:T(8,128)(2,1)S(1)}, bf16[768,256]{1,0:T(8,128)(2,1)}, u32[]{:S(2)}, u32[]{:S(2)}) collective-permute-start(bf16[768,256]{1,0:T(8,128)(2,1)S(1)} %broadcast_select_fusion.3.rest_0_), channel_id=1, source_target_pairs={{0,1},{1,0},{2,3},{3,2},{4,5},{5,4},{6,7},{7,6},{8,9},{9,8},{10,11... | collective-permute-start | bytes 1179656 | tf_op jit(solution)/shard_map/ppermute | solution.py:23
  122.7 40.2 %collective-permute-start.18 = (bf16[1024,256]{1,0:T(8,128)(2,1)S(1)}, bf16[1024,256]{1,0:T(8,128)(2,1)}, u32[]{:S(2)}, u32[]{:S(2)}) collective-permute-start(bf16[1024,256]{1,0:T(8,128)(2,1)S(1)} %broadcast_select_fusion.2.rest_0_), channel_id=1, source_target_pairs={{0,2},{1,3},{2,0},{3,1},{4,6},{5,7},{6,4},{7,5},{8,10},{9,11},{10,... | collective-permute-start | bytes 1572872 | tf_op jit(solution)/shard_map/ppermute | solution.py:23
  122.7 28.4 %collective-permute-start.12 = (bf16[768,256]{1,0:T(8,128)(2,1)}, bf16[768,256]{1,0:T(8,128)(2,1)}, u32[]{:S(2)}, u32[]{:S(2)}) collective-permute-start(bf16[768,256]{1,0:T(8,128)(2,1)} %collective-permute-done.10.rest_1_), channel_id=1, source_target_pairs={{0,1},{1,0},{2,3},{3,2},{4,5},{5,4},{6,7},{7,6},{8,9},{9,8},{10,11... | collective-permute-start | bytes 1179656 | tf_op jit(solution)/shard_map/ppermute | solution.py:23
  157.9 36.1 %all-to-all-start.1 = ((bf16[4,2,128,384]{3,2,1,0:T(8,128)(2,1)}), bf16[4,2,128,384]{3,2,1,0:T(8,128)(2,1)S(1)}, u32[]{:S(2)}, u32[]{:S(2)}) async-start(bf16[4,2,128,384]{3,2,1,0:T(8,128)(2,1)} %get-tuple-element.21), calls=%async_computation.1 | async-start | bytes 1572864 | tf_op jit(solution)/shard_map/all_to_all | solution.py:432
  161.4 14.9 %collective-permute-start.19 = (bf16[1024,256]{1,0:T(8,128)(2,1)S(1)}, bf16[1024,256]{1,0:T(8,128)(2,1)S(1)}, u32[]{:S(2)}, u32[]{:S(2)}) collective-permute-start(bf16[1024,256]{1,0:T(8,128)(2,1)S(1)} %broadcast_select_fusion.2.rest_0_), channel_id=1, source_target_pairs={{0,1},{1,0},{2,3},{3,2},{4,5},{5,4},{6,7},{7,6},{8,9},{9,8},{10,11... | collective-permute-start | bytes 1572872 | tf_op jit(solution)/shard_map/ppermute | solution.py:23
  163.0 24.0 %collective-permute-start.20 = (bf16[1024,256]{1,0:T(8,128)(2,1)}, bf16[1024,256]{1,0:T(8,128)(2,1)S(1)}, u32[]{:S(2)}, u32[]{:S(2)}) collective-permute-start(bf16[1024,256]{1,0:T(8,128)(2,1)} %collective-permute-done.18.rest_1_), channel_id=1, source_target_pairs={{0,1},{1,0},{2,3},{3,2},{4,5},{5,4},{6,7},{7,6},{8,9},{9,8},{10,11... | collective-permute-start | bytes 1572872 | tf_op jit(solution)/shard_map/ppermute | solution.py:23
  (20 other events, 519.8 us)

commit v7 on v6

--- a/solution.py
+++ b/solution.py
@@ -29,7 +29,7 @@
     distant = [(m, m + 4) for m in range(4)]
     beside, back, mid, up = [(4, 5)], [(4, 0), (5, 1)], [(4, 2), (5, 3)], [(4, 6), (5, 7)]
     level = member // 2
-    a, b, c, e_halves, n = parts
+    a, b, c, e_halves = parts
 
     def slabs(own):
         cur = jnp.where(member < 4, own, permute(own, distant))
@@ -46,6 +46,7 @@
         return half, permute(half, across)
 
     def whole(own):
+        own = lax.optimization_barrier(own)
         rows = jnp.where(member == 5, permute(own, beside), own)
         to_up = permute(rows, up)
         to_back = permute(rows, back)
@@ -54,8 +55,7 @@
             jnp.where(level == 2, rows, jnp.where(level == 3, to_up, jnp.where(level == 0, to_back, to_mid))),
         )
 
-    early, late = halves(*e_halves), whole(n)
-    return (slabs(a), early), (slabs(b), late), (slabs(c), late)
+    return ((slabs(a), halves(*e_halves)), (slabs(b), whole(b)), (slabs(c), whole(c)))
 
 
 def placed_slabs(member, refs):
@@ -419,8 +419,8 @@
         at += count
     if lax.axis_size("blk") == 8:
         own_p, *e_halves = pack(front, [pivot_ranges, *cut(pivot_ranges)])
-        own_t, own_m, own_n = pack(front, [tail_ranges, middle_ranges, tail_ranges + middle_ranges])
-        sets = relay((own_p, own_t, own_m, e_halves, own_n), member)
+        own_t, own_m = pack(front, [tail_ranges, middle_ranges])
+        sets = relay((own_p, own_t, own_m, e_halves), member)
     else:
         own_p, own_t, own_m = pack(front, [pivot_ranges, tail_ranges, middle_ranges])
         sets = tuple(((lax.all_gather(s, "blk")[:TICKS],),) * 2 for s in (own_p, own_t, own_m))
@@ -430,7 +430,7 @@
         holder, dest, slot, w, front, out, sets[1], [(tail_at, 0, tail_n)], 0, lax.axis_size("front")
     )
     incoming = lax.all_to_all(outgoing, "front", split_axis=0, concat_axis=0, tiled=True)
-    (factored,) = other_rows(holder, dest, slot, w, front, out, sets[2], middle, tail_n)
+    (factored,) = other_rows(holder, dest, slot, w, front, out, sets[2], middle, 0)
     assembled = add_blocks(address, incoming, parent_base)
     return (factored, assembled)
 

time: 199 us -> 223 us (1.12)
  the two profiles are of different devices: /device:TPU:0 before, /device:TPU:22 now
where the time goes in v7:
time: 223 us; the launch traced here: 222 us
  starting transfers between devices  91.8 us (41%)
  waiting for transfers between devices  82.2 us (37%)
  Pallas kernels  34.3 us (15%)
  other arithmetic  8.19 us (4%)
  local copies, waits for them, and re-layouts  4.22 us (2%)
    ppermute x25, starting transfers between devices, permute(): return lax.ppermute(value, 'blk', pairs)  84.2 us
    ppermute x25, waiting for transfers between devices, permute(): return lax.ppermute(value, 'blk', pairs)  82.2 us
    pallas_call x2, Pallas kernels, other_rows(): pl.pallas_call(functools.partial(other_kernel, counts, ranges, first_row,...  13 us
    pallas_call x1, Pallas kernels, pivot_rows(): pl.pallas_call(functools.partial(pivot_kernel, counts, width), name='pivo...  12.9 us
    pallas_call x2, Pallas kernels, pack(): pl.pallas_call(functools.partial(pack_kernel, pieces), out_shape=tuple((j...  5.45 us
  transfers between devices with their start and end apart: 27, of which 9 were waited for; matrix products, arithmetic and copies ran while one was open for 4% of the time, Pallas kernels for 13%

profile of v7, /device:TPU:22, one launch (start us, length us, event | category | flops | bytes accessed | tf_op | source)
XLA Modules:
  0.0 221.9 jit_solution(18193182713270278408)
XLA Ops:
  0.7 3.0 %shard_map.59 = (bf16[1280,256]{1,0:T(8,128)(2,1)}, bf16[640,256]{1,0:T(8,128)(2,1)}, bf16[640,256]{1,0:T(8,128)(2,1)}) custom-call(f32[3072,384]{1,0:T(8,128)} %front.9), custom_call_target="tpu_custom_call" | custom-call | tf_op jit(solution)/shard_map/pallas_call | solution.py:158
  6.5 2.4 %shard_map.60 = (bf16[768,256]{1,0:T(8,128)(2,1)}, bf16[1024,256]{1,0:T(8,128)(2,1)}) custom-call(f32[3072,384]{1,0:T(8,128)} %front.9), custom_call_target="tpu_custom_call" | custom-call | tf_op jit(solution)/shard_map/pallas_call | solution.py:158
  13.3 2.6 %collective-permute-done.4 = bf16[640,256]{1,0:T(8,128)(2,1)S(1)} collective-permute-done((bf16[640,256]{1,0:T(8,128)(2,1)}, bf16[640,256]{1,0:T(8,128)(2,1)S(1)}, u32[]{:S(2)}, u32[]{:S(2)}) %collective-permute-start.4) | collective-permute-done | bytes 327712 | tf_op jit(solution)/shard_map/ppermute | solution.py:23
  17.3 8.5 %collective-permute-done = bf16[1280,256]{1,0:T(8,128)(2,1)S(1)} collective-permute-done((bf16[1280,256]{1,0:T(8,128)(2,1)}, bf16[1280,256]{1,0:T(8,128)(2,1)S(1)}, u32[]{:S(2)}, u32[]{:S(2)}) %collective-permute-start) | collective-permute-done | bytes 655392 | tf_op jit(solution)/shard_map/ppermute | solution.py:23
  25.8 36.0 %collective-permute-start.5 = (bf16[640,256]{1,0:T(8,128)(2,1)S(1)}, bf16[640,256]{1,0:T(8,128)(2,1)S(1)}, u32[]{:S(2)}, u32[]{:S(2)}) collective-permute-start(bf16[640,256]{1,0:T(8,128)(2,1)S(1)} %broadcast_select_fusion.5), channel_id=1, source_target_pairs={{4,6},{5,7},{12,14},{13,15},{20,22},{21,23},{28,30},{29,31}} | collective-permute-start | bytes 983048 | tf_op jit(solution)/shard_map/ppermute | solution.py:23
  64.0 5.2 %collective-permute-start.1 = (bf16[1280,256]{1,0:T(8,128)(2,1)S(1)}, bf16[1280,256]{1,0:T(8,128)(2,1)}, u32[]{:S(2)}, u32[]{:S(2)}) collective-permute-start(bf16[1280,256]{1,0:T(8,128)(2,1)S(1)} %broadcast_select_fusion.rest_0_), channel_id=1, source_target_pairs={{0,2},{1,3},{2,0},{3,1},{4,6},{5,7},{6,4},{7,5},{8,10},{9,11},{10,... | collective-permute-start | bytes 1966088 | tf_op jit(solution)/shard_map/ppermute | solution.py:23
  71.6 10.3 %collective-permute-start.14 = (bf16[768,256]{1,0:T(8,128)(2,1)S(1)}, bf16[768,256]{1,0:T(8,128)(2,1)}, u32[]{:S(2)}, u32[]{:S(2)}) collective-permute-start(bf16[768,256]{1,0:T(8,128)(2,1)S(1)} %broadcast_select_fusion.3), channel_id=1, source_target_pairs={{4,6},{5,7},{12,14},{13,15},{20,22},{21,23},{28,30},{29,31}} | collective-permute-start | bytes 1179656 | tf_op jit(solution)/shard_map/ppermute | solution.py:23
  81.8 1.8 collective-permute-done.5
  85.6 3.7 %all-to-all-start = ((s32[4,1,2]{2,1,0:T(1,128)}), s32[4,1,2]{2,1,0:T(1,128)S(1)}, u32[]{:S(2)}, u32[]{:S(2)}) async-start(s32[4,1,2]{2,1,0:T(1,128)} %copy.11), calls=%async_computation | async-start | bytes 4096 | tf_op jit(solution)/shard_map/all_to_all | solution.py:378
  93.2 12.9 %collective-permute-done.14 = bf16[768,256]{1,0:T(8,128)(2,1)} collective-permute-done((bf16[768,256]{1,0:T(8,128)(2,1)S(1)}, bf16[768,256]{1,0:T(8,128)(2,1)}, u32[]{:S(2)}, u32[]{:S(2)}) %collective-permute-start.14) | collective-permute-done | bytes 393248 | tf_op jit(solution)/shard_map/ppermute | solution.py:23
  112.5 1.9 collective-permute-done.10.rest_1_
  114.4 2.6 %collective-permute-start.18 = (bf16[1024,256]{1,0:T(8,128)(2,1)S(1)}, bf16[1024,256]{1,0:T(8,128)(2,1)}, u32[]{:S(2)}, u32[]{:S(2)}) collective-permute-start(bf16[1024,256]{1,0:T(8,128)(2,1)S(1)} %broadcast_select_fusion.2.rest_0_), channel_id=1, source_target_pairs={{0,2},{1,3},{2,0},{3,1},{4,6},{5,7},{6,4},{7,5},{8,10},{9,11},{10,... | collective-permute-start | bytes 1572872 | tf_op jit(solution)/shard_map/ppermute | solution.py:23
  119.4 33.7 %collective-permute-done.8.rest_5_ = bf16[640,256]{1,0:T(8,128)(2,1)S(1)} collective-permute-done((bf16[640,256]{1,0:T(8,128)(2,1)S(1)}, bf16[640,256]{1,0:T(8,128)(2,1)S(1)}, u32[]{:S(2)}, u32[]{:S(2)}) %collective-permute-start.8) | collective-permute-done | bytes 327712 | tf_op jit(solution)/shard_map/ppermute | solution.py:23
  153.2 4.5 %collective-permute-start.22 = (bf16[1024,256]{1,0:T(8,128)(2,1)S(1)}, bf16[1024,256]{1,0:T(8,128)(2,1)S(1)}, u32[]{:S(2)}, u32[]{:S(2)}) collective-permute-start(bf16[1024,256]{1,0:T(8,128)(2,1)S(1)} %broadcast_select_fusion.1), channel_id=1, source_target_pairs={{4,6},{5,7},{12,14},{13,15},{20,22},{21,23},{28,30},{29,31}} | collective-permute-start | bytes 1572872 | tf_op jit(solution)/shard_map/ppermute | solution.py:23
  157.7 2.1 collective-permute-start.23
  159.8 2.1 collective-permute-start.24
  162.7 12.9 %pivot_rows.1 = (f32[3072,384]{1,0:T(8,128)}, bf16[1280,384]{1,0:T(8,128)(2,1)}) custom-call(s32[1]{0:T(128)} %bitcast.member_ref, f32[3072,384]{1,0:T(8,128)} %front.9, bf16[1280,256]{1,0:T(8,128)(2,1)} %copy-done.1, bf16[1280,256]{1,0:T(8,128)(2,1)} %collective-permute-done.1.rest_1_, bf16[1280,256]{1,0:T(8,128)(2,1)} %copy-done.6, ...), custom_call_target="tpu_custom_call" | custom-call | tf_op jit(solution)/shard_map/pivot_rows/pallas_call | solution.py:279
  175.7 6.7 %tail_rows.1 = (f32[3072,384]{1,0:T(8,128)}, bf16[4,2,128,384]{3,2,1,0:T(8,128)(2,1)}) custom-call(s32[1]{0:T(128)} %bitcast.member_ref, s32[6]{0:T(128)} %bitcast.8, s32[6]{0:T(128)} %copy-done.21, bf16[1280,384]{1,0:T(8,128)(2,1)} %get-tuple-element.14.w, f32[3072,384]{1,0:T(8,128)} %front.9, ...), custom_call_target="tpu_custom_call", output_to_operand_aliasing={{0}: (5, {})} | custom-call | tf_op jit(solution)/shard_map/tail_rows/pallas_call | solution.py:350
  182.4 4.0 %all-to-all-start.1 = ((bf16[4,2,128,384]{3,2,1,0:T(8,128)(2,1)}), bf16[4,2,128,384]{3,2,1,0:T(8,128)(2,1)S(1)}, u32[]{:S(2)}, u32[]{:S(2)}) async-start(bf16[4,2,128,384]{3,2,1,0:T(8,128)(2,1)} %get-tuple-element.19), calls=%async_computation.1 | async-start | bytes 1572864 | tf_op jit(solution)/shard_map/all_to_all | solution.py:432
  190.1 1.9 select_select_fusion.rest_4_
  192.1 9.1 %collective-permute-done.19.rest_2_ = bf16[1024,256]{1,0:T(8,128)(2,1)S(1)} collective-permute-done((bf16[1024,256]{1,0:T(8,128)(2,1)S(1)}, bf16[1024,256]{1,0:T(8,128)(2,1)S(1)}, u32[]{:S(2)}, u32[]{:S(2)}) %collective-permute-start.19) | collective-permute-done | bytes 524320 | tf_op jit(solution)/shard_map/ppermute | solution.py:23
  201.2 10.5 %collective-permute-done.20.rest_3_ = bf16[1024,256]{1,0:T(8,128)(2,1)} collective-permute-done((bf16[1024,256]{1,0:T(8,128)(2,1)}, bf16[1024,256]{1,0:T(8,128)(2,1)}, u32[]{:S(2)}, u32[]{:S(2)}) %collective-permute-start.20) | collective-permute-done | bytes 524320 | tf_op jit(solution)/shard_map/ppermute | solution.py:23
  211.7 6.3 %middle_rows.1 = f32[3072,384]{1,0:T(8,128)} custom-call(s32[1]{0:T(128)} %bitcast.member_ref, s32[6]{0:T(128)} %bitcast.9, s32[6]{0:T(128)} %copy-done.21, bf16[1280,384]{1,0:T(8,128)(2,1)} %get-tuple-element.14.w, f32[3072,384]{1,0:T(8,128)} %front.9, f32[3072,384]{1,0:T(8,128)} %get-tuple-element.17.out_in, ...), custom_call_target="tpu_custom_call", output_to_operand_aliasing={{}: (5, {})} | custom-call | tf_op jit(solution)/shard_map/middle_rows/pallas_call | solution.py:350
  218.8 3.0 %add_blocks.1 = f32[1024,384]{1,0:T(8,128)} custom-call(s32[8]{0:T(128)} %reshape.81.address_ref, bf16[8,128,384]{2,1,0:T(8,128)(2,1)} %bitcast.7, f32[1024,384]{1,0:T(8,128)} %base.1), custom_call_target="tpu_custom_call" | custom-call | tf_op jit(solution)/shard_map/add_blocks/pallas_call | solution.py:395
  (101 shorter events, 33.0 us)
Async XLA Ops:
  5.2 20.7 %collective-permute-start = (bf16[1280,256]{1,0:T(8,128)(2,1)}, bf16[1280,256]{1,0:T(8,128)(2,1)S(1)}, u32[]{:S(2)}, u32[]{:S(2)}) collective-permute-start(bf16[1280,256]{1,0:T(8,128)(2,1)} %get-tuple-element.11), channel_id=1, source_target_pairs={{0,4},{1,5},{2,6},{3,7},{8,12},{9,13},{10,14},{11,15},{16,20},{17,... | collective-permute-start | bytes 1966088 | tf_op jit(solution)/shard_map/ppermute | solution.py:23
  8.9 54.4 %collective-permute-start.9 = (bf16[768,256]{1,0:T(8,128)(2,1)}, bf16[768,256]{1,0:T(8,128)(2,1)S(1)}, u32[]{:S(2)}, u32[]{:S(2)}) collective-permute-start(bf16[768,256]{1,0:T(8,128)(2,1)} %get-tuple-element.16), channel_id=1, source_target_pairs={{0,4},{1,5},{2,6},{3,7},{8,12},{9,13},{10,14},{11,15},{16,20},{17,... | collective-permute-start | bytes 1179656 | tf_op jit(solution)/shard_map/ppermute | solution.py:23
  10.3 51.6 %collective-permute-start.13 = (bf16[768,256]{1,0:T(8,128)(2,1)}, bf16[768,256]{1,0:T(8,128)(2,1)}, u32[]{:S(2)}, u32[]{:S(2)}) collective-permute-start(bf16[768,256]{1,0:T(8,128)(2,1)} %get-tuple-element.16), channel_id=1, source_target_pairs={{4,5},{12,13},{20,21},{28,29}} | collective-permute-start | bytes 1179656 | tf_op jit(solution)/shard_map/ppermute | solution.py:23
  11.6 59.9 %collective-permute-start.17 = (bf16[1024,256]{1,0:T(8,128)(2,1)}, bf16[1024,256]{1,0:T(8,128)(2,1)}, u32[]{:S(2)}, u32[]{:S(2)}) collective-permute-start(bf16[1024,256]{1,0:T(8,128)(2,1)} %get-tuple-element.18), channel_id=1, source_target_pairs={{0,4},{1,5},{2,6},{3,7},{8,12},{9,13},{10,14},{11,15},{16,20},{17,... | collective-permute-start | bytes 1572872 | tf_op jit(solution)/shard_map/ppermute | solution.py:23
  15.9 54.3 %collective-permute-start.21 = (bf16[1024,256]{1,0:T(8,128)(2,1)}, bf16[1024,256]{1,0:T(8,128)(2,1)S(1)}, u32[]{:S(2)}, u32[]{:S(2)}) collective-permute-start(bf16[1024,256]{1,0:T(8,128)(2,1)} %get-tuple-element.18), channel_id=1, source_target_pairs={{4,5},{12,13},{20,21},{28,29}} | collective-permute-start | bytes 1572872 | tf_op jit(solution)/shard_map/ppermute | solution.py:23
  25.8 57.8 %collective-permute-start.5 = (bf16[640,256]{1,0:T(8,128)(2,1)S(1)}, bf16[640,256]{1,0:T(8,128)(2,1)S(1)}, u32[]{:S(2)}, u32[]{:S(2)}) collective-permute-start(bf16[640,256]{1,0:T(8,128)(2,1)S(1)} %broadcast_select_fusion.5), channel_id=1, source_target_pairs={{4,6},{5,7},{12,14},{13,15},{20,22},{21,23},{28,30},{29,31}} | collective-permute-start | bytes 983048 | tf_op jit(solution)/shard_map/ppermute | solution.py:23
  61.9 27.4 %collective-permute-start.6 = (bf16[640,256]{1,0:T(8,128)(2,1)S(1)}, bf16[640,256]{1,0:T(8,128)(2,1)S(1)}, u32[]{:S(2)}, u32[]{:S(2)}) collective-permute-start(bf16[640,256]{1,0:T(8,128)(2,1)S(1)} %broadcast_select_fusion.5), channel_id=1, source_target_pairs={{4,0},{5,1},{12,8},{13,9},{20,16},{21,17},{28,24},{29,25}} | collective-permute-start | bytes 983048 | tf_op jit(solution)/shard_map/ppermute | solution.py:23
  64.0 44.1 %collective-permute-start.1 = (bf16[1280,256]{1,0:T(8,128)(2,1)S(1)}, bf16[1280,256]{1,0:T(8,128)(2,1)}, u32[]{:S(2)}, u32[]{:S(2)}) collective-permute-start(bf16[1280,256]{1,0:T(8,128)(2,1)S(1)} %broadcast_select_fusion.rest_0_), channel_id=1, source_target_pairs={{0,2},{1,3},{2,0},{3,1},{4,6},{5,7},{6,4},{7,5},{8,10},{9,11},{10,... | collective-permute-start | bytes 1966088 | tf_op jit(solution)/shard_map/ppermute | solution.py:23
  70.2 21.6 %collective-permute-start.7 = (bf16[640,256]{1,0:T(8,128)(2,1)S(1)}, bf16[640,256]{1,0:T(8,128)(2,1)S(1)}, u32[]{:S(2)}, u32[]{:S(2)}) collective-permute-start(bf16[640,256]{1,0:T(8,128)(2,1)S(1)} %broadcast_select_fusion.5), channel_id=1, source_target_pairs={{4,2},{5,3},{12,10},{13,11},{20,18},{21,19},{28,26},{29,27}} | collective-permute-start | bytes 983048 | tf_op jit(solution)/shard_map/ppermute | solution.py:23
  71.6 34.5 %collective-permute-start.14 = (bf16[768,256]{1,0:T(8,128)(2,1)S(1)}, bf16[768,256]{1,0:T(8,128)(2,1)}, u32[]{:S(2)}, u32[]{:S(2)}) collective-permute-start(bf16[768,256]{1,0:T(8,128)(2,1)S(1)} %broadcast_select_fusion.3), channel_id=1, source_target_pairs={{4,6},{5,7},{12,14},{13,15},{20,22},{21,23},{28,30},{29,31}} | collective-permute-start | bytes 1179656 | tf_op jit(solution)/shard_map/ppermute | solution.py:23
  83.6 23.0 %collective-permute-start.15 = (bf16[768,256]{1,0:T(8,128)(2,1)S(1)}, bf16[768,256]{1,0:T(8,128)(2,1)S(1)}, u32[]{:S(2)}, u32[]{:S(2)}) collective-permute-start(bf16[768,256]{1,0:T(8,128)(2,1)S(1)} %broadcast_select_fusion.3), channel_id=1, source_target_pairs={{4,0},{5,1},{12,8},{13,9},{20,16},{21,17},{28,24},{29,25}} | collective-permute-start | bytes 1179656 | tf_op jit(solution)/shard_map/ppermute | solution.py:23
  85.6 96.8 %all-to-all-start = ((s32[4,1,2]{2,1,0:T(1,128)}), s32[4,1,2]{2,1,0:T(1,128)S(1)}, u32[]{:S(2)}, u32[]{:S(2)}) async-start(s32[4,1,2]{2,1,0:T(1,128)} %copy.11), calls=%async_computation | async-start | bytes 4096 | tf_op jit(solution)/shard_map/all_to_all | solution.py:378
  89.3 20.6 %collective-permute-start.16 = (bf16[768,256]{1,0:T(8,128)(2,1)S(1)}, bf16[768,256]{1,0:T(8,128)(2,1)S(1)}, u32[]{:S(2)}, u32[]{:S(2)}) collective-permute-start(bf16[768,256]{1,0:T(8,128)(2,1)S(1)} %broadcast_select_fusion.3), channel_id=1, source_target_pairs={{4,2},{5,3},{12,10},{13,11},{20,18},{21,19},{28,26},{29,27}} | collective-permute-start | bytes 1179656 | tf_op jit(solution)/shard_map/ppermute | solution.py:23
  91.8 22.6 %collective-permute-start.10 = (bf16[768,256]{1,0:T(8,128)(2,1)S(1)}, bf16[768,256]{1,0:T(8,128)(2,1)}, u32[]{:S(2)}, u32[]{:S(2)}) collective-permute-start(bf16[768,256]{1,0:T(8,128)(2,1)S(1)} %broadcast_select_fusion.4.rest_0_), channel_id=1, source_target_pairs={{0,2},{1,3},{2,0},{3,1},{4,6},{5,7},{6,4},{7,5},{8,10},{9,11},{10,... | collective-permute-start | bytes 1179656 | tf_op jit(solution)/shard_map/ppermute | solution.py:23
  106.6 51.1 %collective-permute-start.2 = (bf16[1280,256]{1,0:T(8,128)(2,1)S(1)}, bf16[1280,256]{1,0:T(8,128)(2,1)S(1)}, u32[]{:S(2)}, u32[]{:S(2)}) collective-permute-start(bf16[1280,256]{1,0:T(8,128)(2,1)S(1)} %broadcast_select_fusion.rest_0_), channel_id=1, source_target_pairs={{0,1},{1,0},{2,3},{3,2},{4,5},{5,4},{6,7},{7,6},{8,9},{9,8},{10,11... | collective-permute-start | bytes 1966088 | tf_op jit(solution)/shard_map/ppermute | solution.py:23
  108.1 51.7 %collective-permute-start.3 = (bf16[1280,256]{1,0:T(8,128)(2,1)}, bf16[1280,256]{1,0:T(8,128)(2,1)S(1)}, u32[]{:S(2)}, u32[]{:S(2)}) collective-permute-start(bf16[1280,256]{1,0:T(8,128)(2,1)} %collective-permute-done.1.rest_1_), channel_id=1, source_target_pairs={{0,1},{1,0},{2,3},{3,2},{4,5},{5,4},{6,7},{7,6},{8,9},{9,8},{10,11... | collective-permute-start | bytes 1966088 | tf_op jit(solution)/shard_map/ppermute | solution.py:23
  110.0 43.2 %collective-permute-start.8 = (bf16[640,256]{1,0:T(8,128)(2,1)S(1)}, bf16[640,256]{1,0:T(8,128)(2,1)S(1)}, u32[]{:S(2)}, u32[]{:S(2)}) collective-permute-start(bf16[640,256]{1,0:T(8,128)(2,1)S(1)} %select_select_fusion.2.rest_4_), channel_id=1, source_target_pairs={{0,1},{1,0},{2,3},{3,2},{4,5},{5,4},{6,7},{7,6},{8,9},{9,8},{10,11... | collective-permute-start | bytes 983048 | tf_op jit(solution)/shard_map/ppermute | solution.py:23
  114.4 72.3 %collective-permute-start.18 = (bf16[1024,256]{1,0:T(8,128)(2,1)S(1)}, bf16[1024,256]{1,0:T(8,128)(2,1)}, u32[]{:S(2)}, u32[]{:S(2)}) collective-permute-start(bf16[1024,256]{1,0:T(8,128)(2,1)S(1)} %broadcast_select_fusion.2.rest_0_), channel_id=1, source_target_pairs={{0,2},{1,3},{2,0},{3,1},{4,6},{5,7},{6,4},{7,5},{8,10},{9,11},{10,... | collective-permute-start | bytes 1572872 | tf_op jit(solution)/shard_map/ppermute | solution.py:23
  118.8 56.9 %collective-permute-start.12 = (bf16[768,256]{1,0:T(8,128)(2,1)}, bf16[768,256]{1,0:T(8,128)(2,1)}, u32[]{:S(2)}, u32[]{:S(2)}) collective-permute-start(bf16[768,256]{1,0:T(8,128)(2,1)} %collective-permute-done.10.rest_1_), channel_id=1, source_target_pairs={{0,1},{1,0},{2,3},{3,2},{4,5},{5,4},{6,7},{7,6},{8,9},{9,8},{10,11... | collective-permute-start | bytes 1179656 | tf_op jit(solution)/shard_map/ppermute | solution.py:23
  153.2 37.0 %collective-permute-start.22 = (bf16[1024,256]{1,0:T(8,128)(2,1)S(1)}, bf16[1024,256]{1,0:T(8,128)(2,1)S(1)}, u32[]{:S(2)}, u32[]{:S(2)}) collective-permute-start(bf16[1024,256]{1,0:T(8,128)(2,1)S(1)} %broadcast_select_fusion.1), channel_id=1, source_target_pairs={{4,6},{5,7},{12,14},{13,15},{20,22},{21,23},{28,30},{29,31}} | collective-permute-start | bytes 1572872 | tf_op jit(solution)/shard_map/ppermute | solution.py:23
  157.7 32.4 %collective-permute-start.23 = (bf16[1024,256]{1,0:T(8,128)(2,1)S(1)}, bf16[1024,256]{1,0:T(8,128)(2,1)}, u32[]{:S(2)}, u32[]{:S(2)}) collective-permute-start(bf16[1024,256]{1,0:T(8,128)(2,1)S(1)} %broadcast_select_fusion.1), channel_id=1, source_target_pairs={{4,0},{5,1},{12,8},{13,9},{20,16},{21,17},{28,24},{29,25}} | collective-permute-start | bytes 1572872 | tf_op jit(solution)/shard_map/ppermute | solution.py:23
  159.8 30.3 %collective-permute-start.24 = (bf16[1024,256]{1,0:T(8,128)(2,1)S(1)}, bf16[1024,256]{1,0:T(8,128)(2,1)}, u32[]{:S(2)}, u32[]{:S(2)}) collective-permute-start(bf16[1024,256]{1,0:T(8,128)(2,1)S(1)} %broadcast_select_fusion.1), channel_id=1, source_target_pairs={{4,2},{5,3},{12,10},{13,11},{20,18},{21,19},{28,26},{29,27}} | collective-permute-start | bytes 1572872 | tf_op jit(solution)/shard_map/ppermute | solution.py:23
  182.4 35.5 %all-to-all-start.1 = ((bf16[4,2,128,384]{3,2,1,0:T(8,128)(2,1)}), bf16[4,2,128,384]{3,2,1,0:T(8,128)(2,1)S(1)}, u32[]{:S(2)}, u32[]{:S(2)}) async-start(bf16[4,2,128,384]{3,2,1,0:T(8,128)(2,1)} %get-tuple-element.19), calls=%async_computation.1 | async-start | bytes 1572864 | tf_op jit(solution)/shard_map/all_to_all | solution.py:432
  186.7 25.0 %collective-permute-start.20 = (bf16[1024,256]{1,0:T(8,128)(2,1)}, bf16[1024,256]{1,0:T(8,128)(2,1)}, u32[]{:S(2)}, u32[]{:S(2)}) collective-permute-start(bf16[1024,256]{1,0:T(8,128)(2,1)} %collective-permute-done.18.rest_1_), channel_id=1, source_target_pairs={{0,1},{1,0},{2,3},{3,2},{4,5},{5,4},{6,7},{7,6},{8,9},{9,8},{10,11... | collective-permute-start | bytes 1572872 | tf_op jit(solution)/shard_map/ppermute | solution.py:23
  (26 other events, 801.6 us)

commit v8 on v7

--- a/solution.py
+++ b/solution.py
@@ -51,9 +51,7 @@
         to_up = permute(rows, up)
         to_back = permute(rows, back)
         to_mid = permute(rows, mid)
-        return (
-            jnp.where(level == 2, rows, jnp.where(level == 3, to_up, jnp.where(level == 0, to_back, to_mid))),
-        )
+        return to_back, to_mid, rows, to_up
 
     return ((slabs(a), halves(*e_halves)), (slabs(b), whole(b)), (slabs(c), whole(c)))
 
@@ -84,10 +82,11 @@
         copies = [pltpu.make_async_copy(refs[0].at[TICKS - 1], target, sems.at[0])]
         copies[0].start()
         return copies
-    if len(refs) == 1:
-        copies = [pltpu.make_async_copy(refs[0].at[pl.ds(first_row, rows)], target, sems.at[0])]
-        copies[0].start()
-        return copies
+    if len(refs) == 4:
+        copies = [pltpu.make_async_copy(ref.at[pl.ds(0, rows)], target, sems.at[0]) for ref in refs]
+        for level, copy in enumerate(copies):
+            pl.when(lax.div(member, 2) == level)(copy.start)
+        return copies[:1]
     half, overhalf = refs
     x = lax.rem(member, 2)
     split = half.shape[0]
@@ -418,8 +417,8 @@
         middle.append((start, at, count))
         at += count
     if lax.axis_size("blk") == 8:
-        own_p, *e_halves = pack(front, [pivot_ranges, *cut(pivot_ranges)])
-        own_t, own_m = pack(front, [tail_ranges, middle_ranges])
+        (own_p,) = pack(front, [pivot_ranges])
+        *e_halves, own_t, own_m = pack(front, [*cut(pivot_ranges), tail_ranges, middle_ranges])
         sets = relay((own_p, own_t, own_m, e_halves), member)
     else:
         own_p, own_t, own_m = pack(front, [pivot_ranges, tail_ranges, middle_ranges])

time: 223 us -> 188 us (0.84)
  waiting for transfers between devices: 82.2 us -> 62.9 us
  starting transfers between devices: 91.8 us -> 82 us
  other arithmetic: 8.19 us -> 3.46 us
    ppermute x25, waiting for transfers between devices: 82.2 us -> 62.8 us  [permute(): return lax.ppermute(value, 'blk', pairs)]
    ppermute x25, starting transfers between devices: 84.2 us -> 74.4 us  [permute(): return lax.ppermute(value, 'blk', pairs)]
    select_n x2 -> x0, other arithmetic: 2.77 us -> none  [whole(): jnp.where(level == 2, rows, jnp.where(level == 3, to_up, jnp.where(level...]
  transfers between devices with their start and end apart: 27 -> 27, of which waited for: 9 -> 12; matrix products, arithmetic and copies ran while one was open for 4% -> 3% of each run, Pallas kernels for 13% -> 15%
where the time goes in v8:
time: 188 us
  starting transfers between devices  82 us (44%)
  waiting for transfers between devices  62.9 us (33%)
  Pallas kernels  34.1 us (18%)
  local copies, waits for them, and re-layouts  4.09 us (2%)
  other arithmetic  3.46 us (2%)
    ppermute x25, starting transfers between devices, permute(): return lax.ppermute(value, 'blk', pairs)  74.4 us
    ppermute x25, waiting for transfers between devices, permute(): return lax.ppermute(value, 'blk', pairs)  62.8 us
    pallas_call x1, Pallas kernels, pivot_rows(): pl.pallas_call(functools.partial(pivot_kernel, counts, width), name='pivo...  12.9 us
    pallas_call x2, Pallas kernels, other_rows(): pl.pallas_call(functools.partial(other_kernel, counts, ranges, first_row,...  12.9 us
    pallas_call x2, Pallas kernels, pack(): pl.pallas_call(functools.partial(pack_kernel, pieces), out_shape=tuple((j...  5.24 us
    all_to_all x1, starting transfers between devices, local(): lax.all_to_all(outgoing, 'front', split_axis=0, concat_axis=0, tiled=True)  3.98 us
  transfers between devices with their start and end apart: 27, of which 12 were waited for; matrix products, arithmetic and copies ran while one was open for 3% of the time, Pallas kernels for 15%

profile of v8, /device:TPU:22, one launch (start us, length us, event | category | flops | bytes accessed | tf_op | source)
XLA Modules:
  0.0 187.6 jit_solution(9491800024586395865)
XLA Ops:
  0.6 2.2 %shard_map.59 = bf16[1280,256]{1,0:T(8,128)(2,1)} custom-call(f32[3072,384]{1,0:T(8,128)} %front.9), custom_call_target="tpu_custom_call" | custom-call | tf_op jit(solution)/shard_map/pallas_call | solution.py:157
  4.3 3.1 %shard_map.60 = (bf16[640,256]{1,0:T(8,128)(2,1)}, bf16[640,256]{1,0:T(8,128)(2,1)}, bf16[768,256]{1,0:T(8,128)(2,1)}, bf16[1024,256]{1,0:T(8,128)(2,1)}) custom-call(f32[3072,384]{1,0:T(8,128)} %front.9), custom_call_target="tpu_custom_call" | custom-call | tf_op jit(solution)/shard_map/pallas_call | solution.py:157
  12.9 7.3 %collective-permute-done.4 = bf16[640,256]{1,0:T(8,128)(2,1)S(1)} collective-permute-done((bf16[640,256]{1,0:T(8,128)(2,1)}, bf16[640,256]{1,0:T(8,128)(2,1)S(1)}, u32[]{:S(2)}, u32[]{:S(2)}) %collective-permute-start.4) | collective-permute-done | bytes 327712 | tf_op jit(solution)/shard_map/ppermute | solution.py:23
  21.5 2.1 %collective-permute-done = bf16[1280,256]{1,0:T(8,128)(2,1)S(1)} collective-permute-done((bf16[1280,256]{1,0:T(8,128)(2,1)}, bf16[1280,256]{1,0:T(8,128)(2,1)S(1)}, u32[]{:S(2)}, u32[]{:S(2)}) %collective-permute-start) | collective-permute-done | bytes 655392 | tf_op jit(solution)/shard_map/ppermute | solution.py:23
  25.3 2.3 %collective-permute-done.13 = bf16[768,256]{1,0:T(8,128)(2,1)} collective-permute-done((bf16[768,256]{1,0:T(8,128)(2,1)}, bf16[768,256]{1,0:T(8,128)(2,1)}, u32[]{:S(2)}, u32[]{:S(2)}) %collective-permute-start.13) | collective-permute-done | bytes 393248 | tf_op jit(solution)/shard_map/ppermute | solution.py:23
  27.6 31.0 %collective-permute-start.7 = (bf16[640,256]{1,0:T(8,128)(2,1)S(1)}, bf16[640,256]{1,0:T(8,128)(2,1)S(1)}, u32[]{:S(2)}, u32[]{:S(2)}) collective-permute-start(bf16[640,256]{1,0:T(8,128)(2,1)S(1)} %broadcast_select_fusion.5), channel_id=1, source_target_pairs={{4,2},{5,3},{12,10},{13,11},{20,18},{21,19},{28,26},{29,27}} | collective-permute-start | bytes 983048 | tf_op jit(solution)/shard_map/ppermute | solution.py:23
  58.6 7.5 %collective-permute-start.1 = (bf16[1280,256]{1,0:T(8,128)(2,1)S(1)}, bf16[1280,256]{1,0:T(8,128)(2,1)S(1)}, u32[]{:S(2)}, u32[]{:S(2)}) collective-permute-start(bf16[1280,256]{1,0:T(8,128)(2,1)S(1)} %broadcast_select_fusion.rest_0_), channel_id=1, source_target_pairs={{0,2},{1,3},{2,0},{3,1},{4,6},{5,7},{6,4},{7,5},{8,10},{9,11},{10,... | collective-permute-start | bytes 1966088 | tf_op jit(solution)/shard_map/ppermute | solution.py:23
  70.9 6.5 %collective-permute-start.10 = (bf16[768,256]{1,0:T(8,128)(2,1)S(1)}, bf16[768,256]{1,0:T(8,128)(2,1)}, u32[]{:S(2)}, u32[]{:S(2)}) collective-permute-start(bf16[768,256]{1,0:T(8,128)(2,1)S(1)} %broadcast_select_fusion.4.rest_0_), channel_id=1, source_target_pairs={{0,2},{1,3},{2,0},{3,1},{4,6},{5,7},{6,4},{7,5},{8,10},{9,11},{10,... | collective-permute-start | bytes 1179656 | tf_op jit(solution)/shard_map/ppermute | solution.py:23
  79.0 9.9 %collective-permute-done.1.rest_1_ = bf16[1280,256]{1,0:T(8,128)(2,1)S(1)} collective-permute-done((bf16[1280,256]{1,0:T(8,128)(2,1)S(1)}, bf16[1280,256]{1,0:T(8,128)(2,1)S(1)}, u32[]{:S(2)}, u32[]{:S(2)}) %collective-permute-start.1) | collective-permute-done | bytes 655392 | tf_op jit(solution)/shard_map/ppermute | solution.py:23
  90.8 6.5 %collective-permute-done.10.rest_1_ = bf16[768,256]{1,0:T(8,128)(2,1)} collective-permute-done((bf16[768,256]{1,0:T(8,128)(2,1)S(1)}, bf16[768,256]{1,0:T(8,128)(2,1)}, u32[]{:S(2)}, u32[]{:S(2)}) %collective-permute-start.10) | collective-permute-done | bytes 393248 | tf_op jit(solution)/shard_map/ppermute | solution.py:23
  97.3 5.2 %collective-permute-start.16 = (bf16[768,256]{1,0:T(8,128)(2,1)S(1)}, bf16[768,256]{1,0:T(8,128)(2,1)}, u32[]{:S(2)}, u32[]{:S(2)}) collective-permute-start(bf16[768,256]{1,0:T(8,128)(2,1)S(1)} %broadcast_select_fusion.3.rest_6_), channel_id=1, source_target_pairs={{4,6},{5,7},{12,14},{13,15},{20,22},{21,23},{28,30},{29,31}} | collective-permute-start | bytes 1179656 | tf_op jit(solution)/shard_map/ppermute | solution.py:23
  104.7 4.2 %collective-permute-done.3.rest_3_ = bf16[1280,256]{1,0:T(8,128)(2,1)S(1)} collective-permute-done((bf16[1280,256]{1,0:T(8,128)(2,1)S(1)}, bf16[1280,256]{1,0:T(8,128)(2,1)S(1)}, u32[]{:S(2)}, u32[]{:S(2)}) %collective-permute-start.3) | collective-permute-done | bytes 655392 | tf_op jit(solution)/shard_map/ppermute | solution.py:23
  110.6 3.6 %all-to-all-start = ((s32[4,1,2]{2,1,0:T(1,128)}), s32[4,1,2]{2,1,0:T(1,128)S(1)}, u32[]{:S(2)}, u32[]{:S(2)}) async-start(s32[4,1,2]{2,1,0:T(1,128)} %copy.11), calls=%async_computation | async-start | bytes 4096 | tf_op jit(solution)/shard_map/all_to_all | solution.py:377
  114.2 12.9 %pivot_rows.1 = (f32[3072,384]{1,0:T(8,128)}, bf16[1280,384]{1,0:T(8,128)(2,1)}) custom-call(s32[1]{0:T(128)} %bitcast.member_ref, f32[3072,384]{1,0:T(8,128)} %front.9, bf16[1280,256]{1,0:T(8,128)(2,1)} %copy-done.1, bf16[1280,256]{1,0:T(8,128)(2,1)} %copy-done.9, bf16[1280,256]{1,0:T(8,128)(2,1)} %copy-done.10, bf16[1280,256]{1,0:T(8,128)(2,1)} %copy-done.11, ...), custom_call_target="tpu_custom_call" | custom-call | tf_op jit(solution)/shard_map/pivot_rows/pallas_call | solution.py:278
  128.7 6.8 %collective-permute-done.12.rest_3_ = bf16[768,256]{1,0:T(8,128)(2,1)} collective-permute-done((bf16[768,256]{1,0:T(8,128)(2,1)}, bf16[768,256]{1,0:T(8,128)(2,1)}, u32[]{:S(2)}, u32[]{:S(2)}) %collective-permute-start.12) | collective-permute-done | bytes 393248 | tf_op jit(solution)/shard_map/ppermute | solution.py:23
  135.5 6.7 %tail_rows.1 = (f32[3072,384]{1,0:T(8,128)}, bf16[4,2,128,384]{3,2,1,0:T(8,128)(2,1)}) custom-call(s32[1]{0:T(128)} %bitcast.member_ref, s32[6]{0:T(128)} %bitcast.8, s32[6]{0:T(128)} %copy-done.19, bf16[1280,384]{1,0:T(8,128)(2,1)} %get-tuple-element.12.w, f32[3072,384]{1,0:T(8,128)} %front.9, ...), custom_call_target="tpu_custom_call", output_to_operand_aliasing={{0}: (5, {})} | custom-call | tf_op jit(solution)/shard_map/tail_rows/pallas_call | solution.py:349
  142.2 4.0 %all-to-all-start.1 = ((bf16[4,2,128,384]{3,2,1,0:T(8,128)(2,1)}), bf16[4,2,128,384]{3,2,1,0:T(8,128)(2,1)S(1)}, u32[]{:S(2)}, u32[]{:S(2)}) async-start(bf16[4,2,128,384]{3,2,1,0:T(8,128)(2,1)} %get-tuple-element.17), calls=%async_computation.1 | async-start | bytes 1572864 | tf_op jit(solution)/shard_map/all_to_all | solution.py:431
  150.0 2.1 %collective-permute-start.24 = (bf16[1024,256]{1,0:T(8,128)(2,1)S(1)}, bf16[1024,256]{1,0:T(8,128)(2,1)}, u32[]{:S(2)}, u32[]{:S(2)}) collective-permute-start(bf16[1024,256]{1,0:T(8,128)(2,1)S(1)} %broadcast_select_fusion.1.rest_6_), channel_id=1, source_target_pairs={{4,6},{5,7},{12,14},{13,15},{20,22},{21,23},{28,30},{29,31}} | collective-permute-start | bytes 1572872 | tf_op jit(solution)/shard_map/ppermute | solution.py:23
  152.1 2.0 %collective-permute-start.20 = (bf16[1024,256]{1,0:T(8,128)(2,1)S(1)}, bf16[1024,256]{1,0:T(8,128)(2,1)}, u32[]{:S(2)}, u32[]{:S(2)}) collective-permute-start(bf16[1024,256]{1,0:T(8,128)(2,1)S(1)} %collective-permute-done.18.rest_1_), channel_id=1, source_target_pairs={{0,1},{1,0},{2,3},{3,2},{4,5},{5,4},{6,7},{7,6},{8,9},{9,8},{10,11... | collective-permute-start | bytes 1572872 | tf_op jit(solution)/shard_map/ppermute | solution.py:23
  156.1 4.9 %collective-permute-done.22.rest_4_ = bf16[1024,256]{1,0:T(8,128)(2,1)S(1)} collective-permute-done((bf16[1024,256]{1,0:T(8,128)(2,1)S(1)}, bf16[1024,256]{1,0:T(8,128)(2,1)S(1)}, u32[]{:S(2)}, u32[]{:S(2)}) %collective-permute-start.22) | collective-permute-done | bytes 524320 | tf_op jit(solution)/shard_map/ppermute | solution.py:23
  160.9 10.7 %collective-permute-done.23.rest_5_ = bf16[1024,256]{1,0:T(8,128)(2,1)S(1)} collective-permute-done((bf16[1024,256]{1,0:T(8,128)(2,1)S(1)}, bf16[1024,256]{1,0:T(8,128)(2,1)S(1)}, u32[]{:S(2)}, u32[]{:S(2)}) %collective-permute-start.23) | collective-permute-done | bytes 524320 | tf_op jit(solution)/shard_map/ppermute | solution.py:23
  171.6 5.8 %collective-permute-done.20.rest_3_ = bf16[1024,256]{1,0:T(8,128)(2,1)} collective-permute-done((bf16[1024,256]{1,0:T(8,128)(2,1)S(1)}, bf16[1024,256]{1,0:T(8,128)(2,1)}, u32[]{:S(2)}, u32[]{:S(2)}) %collective-permute-start.20) | collective-permute-done | bytes 524320 | tf_op jit(solution)/shard_map/ppermute | solution.py:23
  177.4 6.2 %middle_rows.1 = f32[3072,384]{1,0:T(8,128)} custom-call(s32[1]{0:T(128)} %bitcast.member_ref, s32[6]{0:T(128)} %bitcast.9, s32[6]{0:T(128)} %copy-done.19, bf16[1280,384]{1,0:T(8,128)(2,1)} %get-tuple-element.12.w, f32[3072,384]{1,0:T(8,128)} %front.9, f32[3072,384]{1,0:T(8,128)} %get-tuple-element.15.out_in, ...), custom_call_target="tpu_custom_call", output_to_operand_aliasing={{}: (5, {})} | custom-call | tf_op jit(solution)/shard_map/middle_rows/pallas_call | solution.py:349
  184.5 3.0 %add_blocks.1 = f32[1024,384]{1,0:T(8,128)} custom-call(s32[8]{0:T(128)} %reshape.81.address_ref, bf16[8,128,384]{2,1,0:T(8,128)(2,1)} %bitcast.7, f32[1024,384]{1,0:T(8,128)} %base.1), custom_call_target="tpu_custom_call" | custom-call | tf_op jit(solution)/shard_map/add_blocks/pallas_call | solution.py:394
  (95 shorter events, 30.0 us)
Async XLA Ops:
  2.8 20.8 %collective-permute-start = (bf16[1280,256]{1,0:T(8,128)(2,1)}, bf16[1280,256]{1,0:T(8,128)(2,1)S(1)}, u32[]{:S(2)}, u32[]{:S(2)}) collective-permute-start(bf16[1280,256]{1,0:T(8,128)(2,1)} %shard_map.59), channel_id=1, source_target_pairs={{0,4},{1,5},{2,6},{3,7},{8,12},{9,13},{10,14},{11,15},{16,20},{17,... | collective-permute-start | bytes 1966088 | tf_op jit(solution)/shard_map/ppermute | solution.py:23
  8.8 49.8 %collective-permute-start.9 = (bf16[768,256]{1,0:T(8,128)(2,1)}, bf16[768,256]{1,0:T(8,128)(2,1)S(1)}, u32[]{:S(2)}, u32[]{:S(2)}) collective-permute-start(bf16[768,256]{1,0:T(8,128)(2,1)} %get-tuple-element.14), channel_id=1, source_target_pairs={{0,4},{1,5},{2,6},{3,7},{8,12},{9,13},{10,14},{11,15},{16,20},{17,... | collective-permute-start | bytes 1179656 | tf_op jit(solution)/shard_map/ppermute | solution.py:23
  10.1 17.5 %collective-permute-start.13 = (bf16[768,256]{1,0:T(8,128)(2,1)}, bf16[768,256]{1,0:T(8,128)(2,1)}, u32[]{:S(2)}, u32[]{:S(2)}) collective-permute-start(bf16[768,256]{1,0:T(8,128)(2,1)} %get-tuple-element.14), channel_id=1, source_target_pairs={{4,5},{12,13},{20,21},{28,29}} | collective-permute-start | bytes 1179656 | tf_op jit(solution)/shard_map/ppermute | solution.py:23
  11.4 59.5 %collective-permute-start.17 = (bf16[1024,256]{1,0:T(8,128)(2,1)}, bf16[1024,256]{1,0:T(8,128)(2,1)S(1)}, u32[]{:S(2)}, u32[]{:S(2)}) collective-permute-start(bf16[1024,256]{1,0:T(8,128)(2,1)} %get-tuple-element.16), channel_id=1, source_target_pairs={{0,4},{1,5},{2,6},{3,7},{8,12},{9,13},{10,14},{11,15},{16,20},{17,... | collective-permute-start | bytes 1572872 | tf_op jit(solution)/shard_map/ppermute | solution.py:23
  20.2 47.0 %collective-permute-start.5 = (bf16[640,256]{1,0:T(8,128)(2,1)S(1)}, bf16[640,256]{1,0:T(8,128)(2,1)S(1)}, u32[]{:S(2)}, u32[]{:S(2)}) collective-permute-start(bf16[640,256]{1,0:T(8,128)(2,1)S(1)} %broadcast_select_fusion.5), channel_id=1, source_target_pairs={{4,6},{5,7},{12,14},{13,15},{20,22},{21,23},{28,30},{29,31}} | collective-permute-start | bytes 983048 | tf_op jit(solution)/shard_map/ppermute | solution.py:23
  23.7 45.2 %collective-permute-start.6 = (bf16[640,256]{1,0:T(8,128)(2,1)S(1)}, bf16[640,256]{1,0:T(8,128)(2,1)S(1)}, u32[]{:S(2)}, u32[]{:S(2)}) collective-permute-start(bf16[640,256]{1,0:T(8,128)(2,1)S(1)} %broadcast_select_fusion.5), channel_id=1, source_target_pairs={{4,0},{5,1},{12,8},{13,9},{20,16},{21,17},{28,24},{29,25}} | collective-permute-start | bytes 983048 | tf_op jit(solution)/shard_map/ppermute | solution.py:23
  27.6 42.6 %collective-permute-start.7 = (bf16[640,256]{1,0:T(8,128)(2,1)S(1)}, bf16[640,256]{1,0:T(8,128)(2,1)S(1)}, u32[]{:S(2)}, u32[]{:S(2)}) collective-permute-start(bf16[640,256]{1,0:T(8,128)(2,1)S(1)} %broadcast_select_fusion.5), channel_id=1, source_target_pairs={{4,2},{5,3},{12,10},{13,11},{20,18},{21,19},{28,26},{29,27}} | collective-permute-start | bytes 983048 | tf_op jit(solution)/shard_map/ppermute | solution.py:23
  58.6 30.3 %collective-permute-start.1 = (bf16[1280,256]{1,0:T(8,128)(2,1)S(1)}, bf16[1280,256]{1,0:T(8,128)(2,1)S(1)}, u32[]{:S(2)}, u32[]{:S(2)}) collective-permute-start(bf16[1280,256]{1,0:T(8,128)(2,1)S(1)} %broadcast_select_fusion.rest_0_), channel_id=1, source_target_pairs={{0,2},{1,3},{2,0},{3,1},{4,6},{5,7},{6,4},{7,5},{8,10},{9,11},{10,... | collective-permute-start | bytes 1966088 | tf_op jit(solution)/shard_map/ppermute | solution.py:23
  68.9 20.6 %collective-permute-start.15 = (bf16[768,256]{1,0:T(8,128)(2,1)S(1)}, bf16[768,256]{1,0:T(8,128)(2,1)S(1)}, u32[]{:S(2)}, u32[]{:S(2)}) collective-permute-start(bf16[768,256]{1,0:T(8,128)(2,1)S(1)} %broadcast_select_fusion.3.rest_6_), channel_id=1, source_target_pairs={{4,2},{5,3},{12,10},{13,11},{20,18},{21,19},{28,26},{29,27}} | collective-permute-start | bytes 1179656 | tf_op jit(solution)/shard_map/ppermute | solution.py:23
  70.2 32.9 %collective-permute-start.2 = (bf16[1280,256]{1,0:T(8,128)(2,1)S(1)}, bf16[1280,256]{1,0:T(8,128)(2,1)S(1)}, u32[]{:S(2)}, u32[]{:S(2)}) collective-permute-start(bf16[1280,256]{1,0:T(8,128)(2,1)S(1)} %broadcast_select_fusion.rest_0_), channel_id=1, source_target_pairs={{0,1},{1,0},{2,3},{3,2},{4,5},{5,4},{6,7},{7,6},{8,9},{9,8},{10,11... | collective-permute-start | bytes 1966088 | tf_op jit(solution)/shard_map/ppermute | solution.py:23
  70.9 26.4 %collective-permute-start.10 = (bf16[768,256]{1,0:T(8,128)(2,1)S(1)}, bf16[768,256]{1,0:T(8,128)(2,1)}, u32[]{:S(2)}, u32[]{:S(2)}) collective-permute-start(bf16[768,256]{1,0:T(8,128)(2,1)S(1)} %broadcast_select_fusion.4.rest_0_), channel_id=1, source_target_pairs={{0,2},{1,3},{2,0},{3,1},{4,6},{5,7},{6,4},{7,5},{8,10},{9,11},{10,... | collective-permute-start | bytes 1179656 | tf_op jit(solution)/shard_map/ppermute | solution.py:23
  78.2 24.3 %collective-permute-start.8 = (bf16[640,256]{1,0:T(8,128)(2,1)S(1)}, bf16[640,256]{1,0:T(8,128)(2,1)S(1)}, u32[]{:S(2)}, u32[]{:S(2)}) collective-permute-start(bf16[640,256]{1,0:T(8,128)(2,1)S(1)} %select_select_fusion.rest_4_), channel_id=1, source_target_pairs={{0,1},{1,0},{2,3},{3,2},{4,5},{5,4},{6,7},{7,6},{8,9},{9,8},{10,11... | collective-permute-start | bytes 983048 | tf_op jit(solution)/shard_map/ppermute | solution.py:23
  88.9 20.0 %collective-permute-start.3 = (bf16[1280,256]{1,0:T(8,128)(2,1)S(1)}, bf16[1280,256]{1,0:T(8,128)(2,1)S(1)}, u32[]{:S(2)}, u32[]{:S(2)}) collective-permute-start(bf16[1280,256]{1,0:T(8,128)(2,1)S(1)} %collective-permute-done.1.rest_1_), channel_id=1, source_target_pairs={{0,1},{1,0},{2,3},{3,2},{4,5},{5,4},{6,7},{7,6},{8,9},{9,8},{10,11... | collective-permute-start | bytes 1966088 | tf_op jit(solution)/shard_map/ppermute | solution.py:23
  89.5 56.7 %collective-permute-start.21 = (bf16[1024,256]{1,0:T(8,128)(2,1)S(1)}, bf16[1024,256]{1,0:T(8,128)(2,1)}, u32[]{:S(2)}, u32[]{:S(2)}) collective-permute-start(bf16[1024,256]{1,0:T(8,128)(2,1)S(1)} %copy-done.5), channel_id=1, source_target_pairs={{4,5},{12,13},{20,21},{28,29}} | collective-permute-start | bytes 1572872 | tf_op jit(solution)/shard_map/ppermute | solution.py:23
  97.3 29.9 %collective-permute-start.16 = (bf16[768,256]{1,0:T(8,128)(2,1)S(1)}, bf16[768,256]{1,0:T(8,128)(2,1)}, u32[]{:S(2)}, u32[]{:S(2)}) collective-permute-start(bf16[768,256]{1,0:T(8,128)(2,1)S(1)} %broadcast_select_fusion.3.rest_6_), channel_id=1, source_target_pairs={{4,6},{5,7},{12,14},{13,15},{20,22},{21,23},{28,30},{29,31}} | collective-permute-start | bytes 1179656 | tf_op jit(solution)/shard_map/ppermute | solution.py:23
  102.5 26.2 %collective-permute-start.11 = (bf16[768,256]{1,0:T(8,128)(2,1)S(1)}, bf16[768,256]{1,0:T(8,128)(2,1)}, u32[]{:S(2)}, u32[]{:S(2)}) collective-permute-start(bf16[768,256]{1,0:T(8,128)(2,1)S(1)} %broadcast_select_fusion.4.rest_0_), channel_id=1, source_target_pairs={{0,1},{1,0},{2,3},{3,2},{4,5},{5,4},{6,7},{7,6},{8,9},{9,8},{10,11... | collective-permute-start | bytes 1179656 | tf_op jit(solution)/shard_map/ppermute | solution.py:23
  103.3 32.3 %collective-permute-start.12 = (bf16[768,256]{1,0:T(8,128)(2,1)}, bf16[768,256]{1,0:T(8,128)(2,1)}, u32[]{:S(2)}, u32[]{:S(2)}) collective-permute-start(bf16[768,256]{1,0:T(8,128)(2,1)} %collective-permute-done.10.rest_1_), channel_id=1, source_target_pairs={{0,1},{1,0},{2,3},{3,2},{4,5},{5,4},{6,7},{7,6},{8,9},{9,8},{10,11... | collective-permute-start | bytes 1179656 | tf_op jit(solution)/shard_map/ppermute | solution.py:23
  108.9 43.2 %collective-permute-start.18 = (bf16[1024,256]{1,0:T(8,128)(2,1)S(1)}, bf16[1024,256]{1,0:T(8,128)(2,1)S(1)}, u32[]{:S(2)}, u32[]{:S(2)}) collective-permute-start(bf16[1024,256]{1,0:T(8,128)(2,1)S(1)} %broadcast_select_fusion.2.rest_0_), channel_id=1, source_target_pairs={{0,2},{1,3},{2,0},{3,1},{4,6},{5,7},{6,4},{7,5},{8,10},{9,11},{10,... | collective-permute-start | bytes 1572872 | tf_op jit(solution)/shard_map/ppermute | solution.py:23
  110.6 31.6 %all-to-all-start = ((s32[4,1,2]{2,1,0:T(1,128)}), s32[4,1,2]{2,1,0:T(1,128)S(1)}, u32[]{:S(2)}, u32[]{:S(2)}) async-start(s32[4,1,2]{2,1,0:T(1,128)} %copy.11), calls=%async_computation | async-start | bytes 4096 | tf_op jit(solution)/shard_map/all_to_all | solution.py:377
  142.2 41.4 %all-to-all-start.1 = ((bf16[4,2,128,384]{3,2,1,0:T(8,128)(2,1)}), bf16[4,2,128,384]{3,2,1,0:T(8,128)(2,1)S(1)}, u32[]{:S(2)}, u32[]{:S(2)}) async-start(bf16[4,2,128,384]{3,2,1,0:T(8,128)(2,1)} %get-tuple-element.17), calls=%async_computation.1 | async-start | bytes 1572864 | tf_op jit(solution)/shard_map/all_to_all | solution.py:431
  148.7 22.9 %collective-permute-start.23 = (bf16[1024,256]{1,0:T(8,128)(2,1)S(1)}, bf16[1024,256]{1,0:T(8,128)(2,1)S(1)}, u32[]{:S(2)}, u32[]{:S(2)}) collective-permute-start(bf16[1024,256]{1,0:T(8,128)(2,1)S(1)} %broadcast_select_fusion.1.rest_6_), channel_id=1, source_target_pairs={{4,2},{5,3},{12,10},{13,11},{20,18},{21,19},{28,26},{29,27}} | collective-permute-start | bytes 1572872 | tf_op jit(solution)/shard_map/ppermute | solution.py:23
  150.0 21.6 %collective-permute-start.24 = (bf16[1024,256]{1,0:T(8,128)(2,1)S(1)}, bf16[1024,256]{1,0:T(8,128)(2,1)}, u32[]{:S(2)}, u32[]{:S(2)}) collective-permute-start(bf16[1024,256]{1,0:T(8,128)(2,1)S(1)} %broadcast_select_fusion.1.rest_6_), channel_id=1, source_target_pairs={{4,6},{5,7},{12,14},{13,15},{20,22},{21,23},{28,30},{29,31}} | collective-permute-start | bytes 1572872 | tf_op jit(solution)/shard_map/ppermute | solution.py:23
  152.1 19.5 %collective-permute-start.19 = (bf16[1024,256]{1,0:T(8,128)(2,1)S(1)}, bf16[1024,256]{1,0:T(8,128)(2,1)}, u32[]{:S(2)}, u32[]{:S(2)}) collective-permute-start(bf16[1024,256]{1,0:T(8,128)(2,1)S(1)} %broadcast_select_fusion.2.rest_0_), channel_id=1, source_target_pairs={{0,1},{1,0},{2,3},{3,2},{4,5},{5,4},{6,7},{7,6},{8,9},{9,8},{10,11... | collective-permute-start | bytes 1572872 | tf_op jit(solution)/shard_map/ppermute | solution.py:23
  152.1 25.3 %collective-permute-start.20 = (bf16[1024,256]{1,0:T(8,128)(2,1)S(1)}, bf16[1024,256]{1,0:T(8,128)(2,1)}, u32[]{:S(2)}, u32[]{:S(2)}) collective-permute-start(bf16[1024,256]{1,0:T(8,128)(2,1)S(1)} %collective-permute-done.18.rest_1_), channel_id=1, source_target_pairs={{0,1},{1,0},{2,3},{3,2},{4,5},{5,4},{6,7},{7,6},{8,9},{9,8},{10,11... | collective-permute-start | bytes 1572872 | tf_op jit(solution)/shard_map/ppermute | solution.py:23
  (24 other events, 775.7 us)

commit v9 on v8

--- a/solution.py
+++ b/solution.py
@@ -14,6 +14,7 @@
 RB = 128
 NB = 6
 CAP = 2
+CHUNK = 256
 ANY = pl.BlockSpec(memory_space=pl.ANY)
 SMEM = pl.BlockSpec(memory_space=pltpu.SMEM)
 VMEM = pl.BlockSpec(memory_space=pltpu.VMEM)
@@ -64,12 +65,14 @@
     return tuple(zip(refs, (near, far, over, overfar)))
 
 
-def start_first(member, refs, target, sems):
+def start_first(member, refs, target, sems, lo, n):
+    at = pl.ds(lo, n)
     if len(refs) == 1:
-        copies = [pltpu.make_async_copy(refs[0].at[pl.ds(0, TICKS - 1)], target.at[pl.ds(0, TICKS - 1)], sems.at[0])]
+        most = pl.ds(0, TICKS - 1)
+        copies = [pltpu.make_async_copy(refs[0].at[most, at], target.at[most, at], sems.at[0])]
     else:
         copies = [
-            pltpu.make_async_copy(ref, target.at[slab], sems.at[i])
+            pltpu.make_async_copy(ref.at[at], target.at[slab, at], sems.at[i])
             for i, (ref, slab) in enumerate(placed_slabs(member, refs))
         ]
     for copy in copies:
@@ -77,40 +80,35 @@
     return copies
 
 
-def start_last(member, refs, target, sems, first_row, rows):
-    if len(refs) == 1 and len(refs[0].shape) == 3:
-        copies = [pltpu.make_async_copy(refs[0].at[TICKS - 1], target, sems.at[0])]
+def start_last(member, refs, target, sem, lo, n):
+    at = pl.ds(lo, n)
+    if len(refs) == 1:
+        copies = [pltpu.make_async_copy(refs[0].at[TICKS - 1, at], target.at[TICKS - 1, at], sem)]
         copies[0].start()
         return copies
-    if len(refs) == 4:
-        copies = [pltpu.make_async_copy(ref.at[pl.ds(0, rows)], target, sems.at[0]) for ref in refs]
-        for level, copy in enumerate(copies):
-            pl.when(lax.div(member, 2) == level)(copy.start)
-        return copies[:1]
+    copies = [pltpu.make_async_copy(ref.at[at], target.at[TICKS - 1, at], sem) for ref in refs]
+    for level, copy in enumerate(copies):
+        pl.when(lax.div(member, 2) == level)(copy.start)
+    return copies[:1]
+
+
+def start_halves(member, refs, target, sems, rows):
+    if len(refs) == 1:
+        return start_last(member, refs, target, sems.at[0], 0, rows)
     half, overhalf = refs
-    x = lax.rem(member, 2)
-    split = half.shape[0]
-    low = max(0, min(rows, split - first_row))
-    pieces = []
-    if low:
-        pieces.append((0, first_row, 0, low))
-    if rows - low:
-        pieces.append((1, first_row + low - split, low, rows - low))
+    x, n = lax.rem(member, 2), rows // 2
 
     def copy(ref, number):
-        _, source, to, count = pieces[number]
-        return pltpu.make_async_copy(
-            ref.at[pl.ds(source, count)], target.at[pl.ds(to, count)], sems.at[number]
-        )
+        return pltpu.make_async_copy(ref, target.at[TICKS - 1, pl.ds(number * n, n)], sems.at[number])
 
     for which in (0, 1):
 
         @pl.when(x == which)
         def _(which=which):
-            for number, piece in enumerate(pieces):
-                copy(half if piece[0] == which else overhalf, number).start()
-
-    return [copy(half, number) for number in range(len(pieces))]
+            copy(half, which).start()
+            copy(overhalf, 1 - which).start()
+
+    return [copy(half, 0), copy(half, 1)]
 
 
 def wait_all(copies):
@@ -211,8 +209,8 @@
     out, w_out, raw, mat, own, inv, sems, last_sems, own_sems = rest[sum(counts) :]
     member = member_ref[0]
     p, rows = P_SIZE, TICKS * P_SIZE
-    copies = start_first(member, firsts, raw, sems)
-    copies += start_last(member, lasts, raw.at[TICKS - 1], last_sems, 0, rows)
+    copies = start_first(member, firsts, raw, sems, 0, rows)
+    copies += start_halves(member, lasts, raw, last_sems, rows)
     loads = [
         pltpu.make_async_copy(
             front.at[pl.ds(t * width, p), :], own.at[pl.ds(t * p, p), :], own_sems.at[t]
@@ -296,48 +294,63 @@
     )(member, front, *bufs[0], *bufs[1])
 
 
-def other_kernel(counts, ranges, first_row, tail, member_ref, dest_ref, slot_ref, w, front, out_in, *rest):
+def windows(ranges, rows):
+    chunks = []
+    for lo in range(0, rows, CHUNK):
+        n = min(CHUNK, rows - lo)
+        pieces = []
+        for src, dst, count in ranges:
+            first, last = max(lo, dst), min(lo + n, dst + count)
+            if first < last:
+                pieces.append((src + first - dst, first, last - first))
+        chunks.append((lo, n, pieces))
+    return chunks
+
+
+def other_kernel(counts, chunks, tail, member_ref, dest_ref, slot_ref, w, front, out_in, *rest):
     firsts, lasts = rest[: counts[0]], rest[counts[0] : sum(counts)]
     if tail:
-        out, outgoing, raw, base, sems, last_sems, base_sems = rest[sum(counts) :]
+        out, outgoing, raw, base, sems, base_sems = rest[sum(counts) :]
     else:
-        out, raw, base, sems, last_sems, base_sems = rest[sum(counts) :]
+        out, raw, base, sems, base_sems = rest[sum(counts) :]
     member = member_ref[0]
-    rows, width = base.shape
-    copies = start_first(member, firsts, raw, sems)
-    copies += start_last(member, lasts, raw.at[TICKS - 1], last_sems, first_row, rows)
-    loads = [
-        pltpu.make_async_copy(front.at[pl.ds(src, n), :], base.at[pl.ds(dst, n), :], base_sems.at[i])
-        for i, (src, dst, n) in enumerate(ranges)
-    ]
-    for load in loads:
-        load.start()
-    wait_all(copies)
-    wait_all(loads)
+    width = base.shape[1]
+    waits = []
+    for number, (lo, n, pieces) in enumerate(chunks):
+        copies = start_first(member, firsts, raw, sems.at[number], lo, n)
+        copies += start_last(member, lasts, raw, sems.at[number, TICKS - 1], lo, n)
+        for i, (src, dst, count) in enumerate(pieces):
+            copies.append(
+                pltpu.make_async_copy(
+                    front.at[pl.ds(src, count), :], base.at[pl.ds(dst, count), :], base_sems.at[number, i]
+                )
+            )
+            copies[-1].start()
+        waits.append(copies)
     keep = (member >= TICKS) | (lax.broadcasted_iota(jnp.int32, (RB, width), 1) >= P_SIZE)
-
-    def tile(src, dst, sem, i, carry):
-        at = pl.ds(pl.multiple_of(dst + i * RB, RB), RB)
-        total = jnp.where(keep, base[at, :], 0.0)
-        for s in range(TICKS):
-            total = minus_dot(total, raw[s, at, :], w[s * P_SIZE : (s + 1) * P_SIZE, :])
-        base[at, :] = total
-        if tail:
-            outgoing[dest_ref[i], slot_ref[i]] = jnp.where(keep, total, 0.0).astype(jnp.bfloat16)
-        pltpu.make_async_copy(
-            base.at[at, :], out.at[pl.ds(pl.multiple_of(src + i * RB, RB), RB), :], sem
-        ).start()
-        return carry
-
-    for number, (src, dst, n) in enumerate(ranges):
-        lax.fori_loop(0, n // RB, functools.partial(tile, src, dst, base_sems.at[number]), 0)
-    for number, (src, dst, n) in enumerate(ranges):
-        pltpu.make_async_copy(
-            base.at[pl.ds(dst, n), :], out.at[pl.ds(src, n), :], base_sems.at[number]
-        ).wait()
-
-
-def other_rows(member, dest, slot, w, front, out, bufs, ranges, first_row, groups=0):
+    stores = []
+    for number, (lo, n, pieces) in enumerate(chunks):
+        wait_all(waits[number])
+        for first in range(lo, lo + n, RB):
+            at = pl.ds(first, RB)
+            total = jnp.where(keep, base[at, :], 0.0)
+            for s in range(TICKS):
+                total = minus_dot(total, raw[s, at, :], w[s * P_SIZE : (s + 1) * P_SIZE, :])
+            base[at, :] = total
+            if tail:
+                block = first // RB
+                outgoing[dest_ref[block], slot_ref[block]] = jnp.where(keep, total, 0.0).astype(jnp.bfloat16)
+        for i, (src, dst, count) in enumerate(pieces):
+            stores.append(
+                pltpu.make_async_copy(
+                    base.at[pl.ds(dst, count), :], out.at[pl.ds(src, count), :], base_sems.at[number, i]
+                )
+            )
+            stores[-1].start()
+    wait_all(stores)
+
+
+def other_rows(member, dest, slot, w, front, out, bufs, ranges, groups=0):
     order, width = front.shape
     rows = sum(n for _, _, n in ranges)
     shapes = [jax.ShapeDtypeStruct((order, width), jnp.float32)]
@@ -346,8 +359,9 @@
         shapes.append(jax.ShapeDtypeStruct((groups, CAP, RB, width), jnp.bfloat16))
         specs.append(VMEM)
     counts = tuple(len(b) for b in bufs)
+    chunks = windows(ranges, rows)
     return pl.pallas_call(
-        functools.partial(other_kernel, counts, ranges, first_row, bool(groups)),
+        functools.partial(other_kernel, counts, chunks, bool(groups)),
         name="tail_rows" if groups else "middle_rows",
         out_shape=tuple(shapes),
         in_specs=[SMEM, SMEM, SMEM, VMEM, ANY, ANY] + [ANY] * sum(counts),
@@ -356,9 +370,8 @@
         scratch_shapes=[
             pltpu.VMEM((TICKS, rows, P_SIZE), jnp.bfloat16),
             pltpu.VMEM((rows, width), jnp.float32),
-            pltpu.SemaphoreType.DMA((4,)),
-            pltpu.SemaphoreType.DMA((2,)),
-            pltpu.SemaphoreType.DMA((len(ranges),)),
+            pltpu.SemaphoreType.DMA((len(chunks), TICKS)),
+            pltpu.SemaphoreType.DMA((len(chunks), max(len(c[2]) for c in chunks))),
         ],
     )(member, dest, slot, w, front, out, *bufs[0], *bufs[1])
 
@@ -426,10 +439,10 @@
     dest, slot, address = routes(parent_group, row_block)
     out, w = pivot_rows(holder, front, sets[0])
     out, outgoing = other_rows(
-        holder, dest, slot, w, front, out, sets[1], [(tail_at, 0, tail_n)], 0, lax.axis_size("front")
+        holder, dest, slot, w, front, out, sets[1], [(tail_at, 0, tail_n)], lax.axis_size("front")
     )
     incoming = lax.all_to_all(outgoing, "front", split_axis=0, concat_axis=0, tiled=True)
-    (factored,) = other_rows(holder, dest, slot, w, front, out, sets[2], middle, 0)
+    (factored,) = other_rows(holder, dest, slot, w, front, out, sets[2], middle)
     assembled = add_blocks(address, incoming, parent_base)
     return (factored, assembled)
 

time: 188 us -> 188 us (level)
  no operation moved by 1% of the time
where the time goes in v9:
time: 188 us; the launch traced here: 187 us
  starting transfers between devices  82 us (44%)
  waiting for transfers between devices  62.9 us (33%)
  Pallas kernels  33.4 us (18%)
  local copies, waits for them, and re-layouts  4.09 us (2%)
  other arithmetic  3.46 us (2%)
    ppermute x25, starting transfers between devices, permute(): return lax.ppermute(value, 'blk', pairs)  74.4 us
    ppermute x25, waiting for transfers between devices, permute(): return lax.ppermute(value, 'blk', pairs)  62.9 us
    pallas_call x1, Pallas kernels, pivot_rows(): pl.pallas_call(functools.partial(pivot_kernel, counts, width), name='pivo...  12.9 us
    pallas_call x2, Pallas kernels, other_rows(): pl.pallas_call(functools.partial(other_kernel, counts, chunks, bool(group...  12.3 us
    pallas_call x2, Pallas kernels, pack(): pl.pallas_call(functools.partial(pack_kernel, pieces), out_shape=tuple((j...  5.24 us
    all_to_all x1, starting transfers between devices, local(): lax.all_to_all(outgoing, 'front', split_axis=0, concat_axis=0, tiled=True)  3.98 us
  transfers between devices with their start and end apart: 27, of which 12 were waited for; matrix products, arithmetic and copies ran while one was open for 3% of the time, Pallas kernels for 15%

profile of v9, /device:TPU:22, one launch (start us, length us, event | category | flops | bytes accessed | tf_op | source)
XLA Modules:
  0.0 187.0 jit_solution(14288979496698185887)
XLA Ops:
  0.6 2.2 %shard_map.59 = bf16[1280,256]{1,0:T(8,128)(2,1)} custom-call(f32[3072,384]{1,0:T(8,128)} %front.9), custom_call_target="tpu_custom_call" | custom-call | tf_op jit(solution)/shard_map/pallas_call | solution.py:155
  4.3 3.1 %shard_map.60 = (bf16[640,256]{1,0:T(8,128)(2,1)}, bf16[640,256]{1,0:T(8,128)(2,1)}, bf16[768,256]{1,0:T(8,128)(2,1)}, bf16[1024,256]{1,0:T(8,128)(2,1)}) custom-call(f32[3072,384]{1,0:T(8,128)} %front.9), custom_call_target="tpu_custom_call" | custom-call | tf_op jit(solution)/shard_map/pallas_call | solution.py:155
  12.9 7.3 %collective-permute-done.4 = bf16[640,256]{1,0:T(8,128)(2,1)S(1)} collective-permute-done((bf16[640,256]{1,0:T(8,128)(2,1)}, bf16[640,256]{1,0:T(8,128)(2,1)S(1)}, u32[]{:S(2)}, u32[]{:S(2)}) %collective-permute-start.4) | collective-permute-done | bytes 327712 | tf_op jit(solution)/shard_map/ppermute | solution.py:24
  21.5 2.1 %collective-permute-done = bf16[1280,256]{1,0:T(8,128)(2,1)S(1)} collective-permute-done((bf16[1280,256]{1,0:T(8,128)(2,1)}, bf16[1280,256]{1,0:T(8,128)(2,1)S(1)}, u32[]{:S(2)}, u32[]{:S(2)}) %collective-permute-start) | collective-permute-done | bytes 655392 | tf_op jit(solution)/shard_map/ppermute | solution.py:24
  25.3 2.3 %collective-permute-done.13 = bf16[768,256]{1,0:T(8,128)(2,1)} collective-permute-done((bf16[768,256]{1,0:T(8,128)(2,1)}, bf16[768,256]{1,0:T(8,128)(2,1)}, u32[]{:S(2)}, u32[]{:S(2)}) %collective-permute-start.13) | collective-permute-done | bytes 393248 | tf_op jit(solution)/shard_map/ppermute | solution.py:24
  27.6 31.0 %collective-permute-start.7 = (bf16[640,256]{1,0:T(8,128)(2,1)S(1)}, bf16[640,256]{1,0:T(8,128)(2,1)S(1)}, u32[]{:S(2)}, u32[]{:S(2)}) collective-permute-start(bf16[640,256]{1,0:T(8,128)(2,1)S(1)} %broadcast_select_fusion.5), channel_id=1, source_target_pairs={{4,2},{5,3},{12,10},{13,11},{20,18},{21,19},{28,26},{29,27}} | collective-permute-start | bytes 983048 | tf_op jit(solution)/shard_map/ppermute | solution.py:24
  58.6 7.5 %collective-permute-start.1 = (bf16[1280,256]{1,0:T(8,128)(2,1)S(1)}, bf16[1280,256]{1,0:T(8,128)(2,1)S(1)}, u32[]{:S(2)}, u32[]{:S(2)}) collective-permute-start(bf16[1280,256]{1,0:T(8,128)(2,1)S(1)} %broadcast_select_fusion.rest_0_), channel_id=1, source_target_pairs={{0,2},{1,3},{2,0},{3,1},{4,6},{5,7},{6,4},{7,5},{8,10},{9,11},{10,... | collective-permute-start | bytes 1966088 | tf_op jit(solution)/shard_map/ppermute | solution.py:24
  70.9 6.5 %collective-permute-start.10 = (bf16[768,256]{1,0:T(8,128)(2,1)S(1)}, bf16[768,256]{1,0:T(8,128)(2,1)}, u32[]{:S(2)}, u32[]{:S(2)}) collective-permute-start(bf16[768,256]{1,0:T(8,128)(2,1)S(1)} %broadcast_select_fusion.4.rest_0_), channel_id=1, source_target_pairs={{0,2},{1,3},{2,0},{3,1},{4,6},{5,7},{6,4},{7,5},{8,10},{9,11},{10,... | collective-permute-start | bytes 1179656 | tf_op jit(solution)/shard_map/ppermute | solution.py:24
  79.0 9.9 %collective-permute-done.1.rest_1_ = bf16[1280,256]{1,0:T(8,128)(2,1)S(1)} collective-permute-done((bf16[1280,256]{1,0:T(8,128)(2,1)S(1)}, bf16[1280,256]{1,0:T(8,128)(2,1)S(1)}, u32[]{:S(2)}, u32[]{:S(2)}) %collective-permute-start.1) | collective-permute-done | bytes 655392 | tf_op jit(solution)/shard_map/ppermute | solution.py:24
  90.8 6.5 %collective-permute-done.10.rest_1_ = bf16[768,256]{1,0:T(8,128)(2,1)} collective-permute-done((bf16[768,256]{1,0:T(8,128)(2,1)S(1)}, bf16[768,256]{1,0:T(8,128)(2,1)}, u32[]{:S(2)}, u32[]{:S(2)}) %collective-permute-start.10) | collective-permute-done | bytes 393248 | tf_op jit(solution)/shard_map/ppermute | solution.py:24
  97.3 5.2 %collective-permute-start.16 = (bf16[768,256]{1,0:T(8,128)(2,1)S(1)}, bf16[768,256]{1,0:T(8,128)(2,1)}, u32[]{:S(2)}, u32[]{:S(2)}) collective-permute-start(bf16[768,256]{1,0:T(8,128)(2,1)S(1)} %broadcast_select_fusion.3.rest_6_), channel_id=1, source_target_pairs={{4,6},{5,7},{12,14},{13,15},{20,22},{21,23},{28,30},{29,31}} | collective-permute-start | bytes 1179656 | tf_op jit(solution)/shard_map/ppermute | solution.py:24
  104.7 4.2 %collective-permute-done.3.rest_3_ = bf16[1280,256]{1,0:T(8,128)(2,1)S(1)} collective-permute-done((bf16[1280,256]{1,0:T(8,128)(2,1)S(1)}, bf16[1280,256]{1,0:T(8,128)(2,1)S(1)}, u32[]{:S(2)}, u32[]{:S(2)}) %collective-permute-start.3) | collective-permute-done | bytes 655392 | tf_op jit(solution)/shard_map/ppermute | solution.py:24
  110.6 3.6 %all-to-all-start = ((s32[4,1,2]{2,1,0:T(1,128)}), s32[4,1,2]{2,1,0:T(1,128)S(1)}, u32[]{:S(2)}, u32[]{:S(2)}) async-start(s32[4,1,2]{2,1,0:T(1,128)} %copy.11), calls=%async_computation | async-start | bytes 4096 | tf_op jit(solution)/shard_map/all_to_all | solution.py:390
  114.2 12.9 %pivot_rows.1 = (f32[3072,384]{1,0:T(8,128)}, bf16[1280,384]{1,0:T(8,128)(2,1)}) custom-call(s32[1]{0:T(128)} %bitcast.member_ref, f32[3072,384]{1,0:T(8,128)} %front.9, bf16[1280,256]{1,0:T(8,128)(2,1)} %copy-done.1, bf16[1280,256]{1,0:T(8,128)(2,1)} %copy-done.9, bf16[1280,256]{1,0:T(8,128)(2,1)} %copy-done.10, bf16[1280,256]{1,0:T(8,128)(2,1)} %copy-done.11, ...), custom_call_target="tpu_custom_call" | custom-call | tf_op jit(solution)/shard_map/pivot_rows/pallas_call | solution.py:276
  128.7 6.8 %collective-permute-done.12.rest_3_ = bf16[768,256]{1,0:T(8,128)(2,1)} collective-permute-done((bf16[768,256]{1,0:T(8,128)(2,1)}, bf16[768,256]{1,0:T(8,128)(2,1)}, u32[]{:S(2)}, u32[]{:S(2)}) %collective-permute-start.12) | collective-permute-done | bytes 393248 | tf_op jit(solution)/shard_map/ppermute | solution.py:24
  135.5 6.2 %tail_rows.1 = (f32[3072,384]{1,0:T(8,128)}, bf16[4,2,128,384]{3,2,1,0:T(8,128)(2,1)}) custom-call(s32[1]{0:T(128)} %bitcast.member_ref, s32[6]{0:T(128)} %bitcast.8, s32[6]{0:T(128)} %copy-done.19, bf16[1280,384]{1,0:T(8,128)(2,1)} %get-tuple-element.12.w, f32[3072,384]{1,0:T(8,128)} %front.9, ...), custom_call_target="tpu_custom_call", output_to_operand_aliasing={{0}: (5, {})} | custom-call | tf_op jit(solution)/shard_map/tail_rows/pallas_call | solution.py:363
  141.8 4.0 %all-to-all-start.1 = ((bf16[4,2,128,384]{3,2,1,0:T(8,128)(2,1)}), bf16[4,2,128,384]{3,2,1,0:T(8,128)(2,1)S(1)}, u32[]{:S(2)}, u32[]{:S(2)}) async-start(bf16[4,2,128,384]{3,2,1,0:T(8,128)(2,1)} %get-tuple-element.17), calls=%async_computation.1 | async-start | bytes 1572864 | tf_op jit(solution)/shard_map/all_to_all | solution.py:444
  149.5 2.1 %collective-permute-start.24 = (bf16[1024,256]{1,0:T(8,128)(2,1)S(1)}, bf16[1024,256]{1,0:T(8,128)(2,1)}, u32[]{:S(2)}, u32[]{:S(2)}) collective-permute-start(bf16[1024,256]{1,0:T(8,128)(2,1)S(1)} %broadcast_select_fusion.1.rest_6_), channel_id=1, source_target_pairs={{4,6},{5,7},{12,14},{13,15},{20,22},{21,23},{28,30},{29,31}} | collective-permute-start | bytes 1572872 | tf_op jit(solution)/shard_map/ppermute | solution.py:24
  151.7 2.0 %collective-permute-start.20 = (bf16[1024,256]{1,0:T(8,128)(2,1)S(1)}, bf16[1024,256]{1,0:T(8,128)(2,1)}, u32[]{:S(2)}, u32[]{:S(2)}) collective-permute-start(bf16[1024,256]{1,0:T(8,128)(2,1)S(1)} %collective-permute-done.18.rest_1_), channel_id=1, source_target_pairs={{0,1},{1,0},{2,3},{3,2},{4,5},{5,4},{6,7},{7,6},{8,9},{9,8},{10,11... | collective-permute-start | bytes 1572872 | tf_op jit(solution)/shard_map/ppermute | solution.py:24
  155.6 4.9 %collective-permute-done.22.rest_4_ = bf16[1024,256]{1,0:T(8,128)(2,1)S(1)} collective-permute-done((bf16[1024,256]{1,0:T(8,128)(2,1)S(1)}, bf16[1024,256]{1,0:T(8,128)(2,1)S(1)}, u32[]{:S(2)}, u32[]{:S(2)}) %collective-permute-start.22) | collective-permute-done | bytes 524320 | tf_op jit(solution)/shard_map/ppermute | solution.py:24
  160.5 10.7 %collective-permute-done.23.rest_5_ = bf16[1024,256]{1,0:T(8,128)(2,1)S(1)} collective-permute-done((bf16[1024,256]{1,0:T(8,128)(2,1)S(1)}, bf16[1024,256]{1,0:T(8,128)(2,1)S(1)}, u32[]{:S(2)}, u32[]{:S(2)}) %collective-permute-start.23) | collective-permute-done | bytes 524320 | tf_op jit(solution)/shard_map/ppermute | solution.py:24
  171.2 5.8 %collective-permute-done.20.rest_3_ = bf16[1024,256]{1,0:T(8,128)(2,1)} collective-permute-done((bf16[1024,256]{1,0:T(8,128)(2,1)S(1)}, bf16[1024,256]{1,0:T(8,128)(2,1)}, u32[]{:S(2)}, u32[]{:S(2)}) %collective-permute-start.20) | collective-permute-done | bytes 524320 | tf_op jit(solution)/shard_map/ppermute | solution.py:24
  177.0 6.1 %middle_rows.1 = f32[3072,384]{1,0:T(8,128)} custom-call(s32[1]{0:T(128)} %bitcast.member_ref, s32[6]{0:T(128)} %bitcast.9, s32[6]{0:T(128)} %copy-done.19, bf16[1280,384]{1,0:T(8,128)(2,1)} %get-tuple-element.12.w, f32[3072,384]{1,0:T(8,128)} %front.9, f32[3072,384]{1,0:T(8,128)} %get-tuple-element.15.out_in, ...), custom_call_target="tpu_custom_call", output_to_operand_aliasing={{}: (5, {})} | custom-call | tf_op jit(solution)/shard_map/middle_rows/pallas_call | solution.py:363
  183.9 3.0 %add_blocks.1 = f32[1024,384]{1,0:T(8,128)} custom-call(s32[8]{0:T(128)} %reshape.81.address_ref, bf16[8,128,384]{2,1,0:T(8,128)(2,1)} %bitcast.7, f32[1024,384]{1,0:T(8,128)} %base.1), custom_call_target="tpu_custom_call" | custom-call | tf_op jit(solution)/shard_map/add_blocks/pallas_call | solution.py:407
  (95 shorter events, 30.0 us)
Async XLA Ops:
  2.8 20.8 %collective-permute-start = (bf16[1280,256]{1,0:T(8,128)(2,1)}, bf16[1280,256]{1,0:T(8,128)(2,1)S(1)}, u32[]{:S(2)}, u32[]{:S(2)}) collective-permute-start(bf16[1280,256]{1,0:T(8,128)(2,1)} %shard_map.59), channel_id=1, source_target_pairs={{0,4},{1,5},{2,6},{3,7},{8,12},{9,13},{10,14},{11,15},{16,20},{17,... | collective-permute-start | bytes 1966088 | tf_op jit(solution)/shard_map/ppermute | solution.py:24
  8.8 49.8 %collective-permute-start.9 = (bf16[768,256]{1,0:T(8,128)(2,1)}, bf16[768,256]{1,0:T(8,128)(2,1)S(1)}, u32[]{:S(2)}, u32[]{:S(2)}) collective-permute-start(bf16[768,256]{1,0:T(8,128)(2,1)} %get-tuple-element.14), channel_id=1, source_target_pairs={{0,4},{1,5},{2,6},{3,7},{8,12},{9,13},{10,14},{11,15},{16,20},{17,... | collective-permute-start | bytes 1179656 | tf_op jit(solution)/shard_map/ppermute | solution.py:24
  10.1 17.5 %collective-permute-start.13 = (bf16[768,256]{1,0:T(8,128)(2,1)}, bf16[768,256]{1,0:T(8,128)(2,1)}, u32[]{:S(2)}, u32[]{:S(2)}) collective-permute-start(bf16[768,256]{1,0:T(8,128)(2,1)} %get-tuple-element.14), channel_id=1, source_target_pairs={{4,5},{12,13},{20,21},{28,29}} | collective-permute-start | bytes 1179656 | tf_op jit(solution)/shard_map/ppermute | solution.py:24
  11.4 59.5 %collective-permute-start.17 = (bf16[1024,256]{1,0:T(8,128)(2,1)}, bf16[1024,256]{1,0:T(8,128)(2,1)S(1)}, u32[]{:S(2)}, u32[]{:S(2)}) collective-permute-start(bf16[1024,256]{1,0:T(8,128)(2,1)} %get-tuple-element.16), channel_id=1, source_target_pairs={{0,4},{1,5},{2,6},{3,7},{8,12},{9,13},{10,14},{11,15},{16,20},{17,... | collective-permute-start | bytes 1572872 | tf_op jit(solution)/shard_map/ppermute | solution.py:24
  20.2 47.0 %collective-permute-start.5 = (bf16[640,256]{1,0:T(8,128)(2,1)S(1)}, bf16[640,256]{1,0:T(8,128)(2,1)S(1)}, u32[]{:S(2)}, u32[]{:S(2)}) collective-permute-start(bf16[640,256]{1,0:T(8,128)(2,1)S(1)} %broadcast_select_fusion.5), channel_id=1, source_target_pairs={{4,6},{5,7},{12,14},{13,15},{20,22},{21,23},{28,30},{29,31}} | collective-permute-start | bytes 983048 | tf_op jit(solution)/shard_map/ppermute | solution.py:24
  23.7 45.2 %collective-permute-start.6 = (bf16[640,256]{1,0:T(8,128)(2,1)S(1)}, bf16[640,256]{1,0:T(8,128)(2,1)S(1)}, u32[]{:S(2)}, u32[]{:S(2)}) collective-permute-start(bf16[640,256]{1,0:T(8,128)(2,1)S(1)} %broadcast_select_fusion.5), channel_id=1, source_target_pairs={{4,0},{5,1},{12,8},{13,9},{20,16},{21,17},{28,24},{29,25}} | collective-permute-start | bytes 983048 | tf_op jit(solution)/shard_map/ppermute | solution.py:24
  27.6 42.6 %collective-permute-start.7 = (bf16[640,256]{1,0:T(8,128)(2,1)S(1)}, bf16[640,256]{1,0:T(8,128)(2,1)S(1)}, u32[]{:S(2)}, u32[]{:S(2)}) collective-permute-start(bf16[640,256]{1,0:T(8,128)(2,1)S(1)} %broadcast_select_fusion.5), channel_id=1, source_target_pairs={{4,2},{5,3},{12,10},{13,11},{20,18},{21,19},{28,26},{29,27}} | collective-permute-start | bytes 983048 | tf_op jit(solution)/shard_map/ppermute | solution.py:24
  58.6 30.3 %collective-permute-start.1 = (bf16[1280,256]{1,0:T(8,128)(2,1)S(1)}, bf16[1280,256]{1,0:T(8,128)(2,1)S(1)}, u32[]{:S(2)}, u32[]{:S(2)}) collective-permute-start(bf16[1280,256]{1,0:T(8,128)(2,1)S(1)} %broadcast_select_fusion.rest_0_), channel_id=1, source_target_pairs={{0,2},{1,3},{2,0},{3,1},{4,6},{5,7},{6,4},{7,5},{8,10},{9,11},{10,... | collective-permute-start | bytes 1966088 | tf_op jit(solution)/shard_map/ppermute | solution.py:24
  68.9 20.6 %collective-permute-start.15 = (bf16[768,256]{1,0:T(8,128)(2,1)S(1)}, bf16[768,256]{1,0:T(8,128)(2,1)S(1)}, u32[]{:S(2)}, u32[]{:S(2)}) collective-permute-start(bf16[768,256]{1,0:T(8,128)(2,1)S(1)} %broadcast_select_fusion.3.rest_6_), channel_id=1, source_target_pairs={{4,2},{5,3},{12,10},{13,11},{20,18},{21,19},{28,26},{29,27}} | collective-permute-start | bytes 1179656 | tf_op jit(solution)/shard_map/ppermute | solution.py:24
  70.2 32.9 %collective-permute-start.2 = (bf16[1280,256]{1,0:T(8,128)(2,1)S(1)}, bf16[1280,256]{1,0:T(8,128)(2,1)S(1)}, u32[]{:S(2)}, u32[]{:S(2)}) collective-permute-start(bf16[1280,256]{1,0:T(8,128)(2,1)S(1)} %broadcast_select_fusion.rest_0_), channel_id=1, source_target_pairs={{0,1},{1,0},{2,3},{3,2},{4,5},{5,4},{6,7},{7,6},{8,9},{9,8},{10,11... | collective-permute-start | bytes 1966088 | tf_op jit(solution)/shard_map/ppermute | solution.py:24
  70.9 26.4 %collective-permute-start.10 = (bf16[768,256]{1,0:T(8,128)(2,1)S(1)}, bf16[768,256]{1,0:T(8,128)(2,1)}, u32[]{:S(2)}, u32[]{:S(2)}) collective-permute-start(bf16[768,256]{1,0:T(8,128)(2,1)S(1)} %broadcast_select_fusion.4.rest_0_), channel_id=1, source_target_pairs={{0,2},{1,3},{2,0},{3,1},{4,6},{5,7},{6,4},{7,5},{8,10},{9,11},{10,... | collective-permute-start | bytes 1179656 | tf_op jit(solution)/shard_map/ppermute | solution.py:24
  78.2 24.3 %collective-permute-start.8 = (bf16[640,256]{1,0:T(8,128)(2,1)S(1)}, bf16[640,256]{1,0:T(8,128)(2,1)S(1)}, u32[]{:S(2)}, u32[]{:S(2)}) collective-permute-start(bf16[640,256]{1,0:T(8,128)(2,1)S(1)} %select_select_fusion.rest_4_), channel_id=1, source_target_pairs={{0,1},{1,0},{2,3},{3,2},{4,5},{5,4},{6,7},{7,6},{8,9},{9,8},{10,11... | collective-permute-start | bytes 983048 | tf_op jit(solution)/shard_map/ppermute | solution.py:24
  88.9 20.0 %collective-permute-start.3 = (bf16[1280,256]{1,0:T(8,128)(2,1)S(1)}, bf16[1280,256]{1,0:T(8,128)(2,1)S(1)}, u32[]{:S(2)}, u32[]{:S(2)}) collective-permute-start(bf16[1280,256]{1,0:T(8,128)(2,1)S(1)} %collective-permute-done.1.rest_1_), channel_id=1, source_target_pairs={{0,1},{1,0},{2,3},{3,2},{4,5},{5,4},{6,7},{7,6},{8,9},{9,8},{10,11... | collective-permute-start | bytes 1966088 | tf_op jit(solution)/shard_map/ppermute | solution.py:24
  89.5 56.3 %collective-permute-start.21 = (bf16[1024,256]{1,0:T(8,128)(2,1)S(1)}, bf16[1024,256]{1,0:T(8,128)(2,1)}, u32[]{:S(2)}, u32[]{:S(2)}) collective-permute-start(bf16[1024,256]{1,0:T(8,128)(2,1)S(1)} %copy-done.5), channel_id=1, source_target_pairs={{4,5},{12,13},{20,21},{28,29}} | collective-permute-start | bytes 1572872 | tf_op jit(solution)/shard_map/ppermute | solution.py:24
  97.3 29.9 %collective-permute-start.16 = (bf16[768,256]{1,0:T(8,128)(2,1)S(1)}, bf16[768,256]{1,0:T(8,128)(2,1)}, u32[]{:S(2)}, u32[]{:S(2)}) collective-permute-start(bf16[768,256]{1,0:T(8,128)(2,1)S(1)} %broadcast_select_fusion.3.rest_6_), channel_id=1, source_target_pairs={{4,6},{5,7},{12,14},{13,15},{20,22},{21,23},{28,30},{29,31}} | collective-permute-start | bytes 1179656 | tf_op jit(solution)/shard_map/ppermute | solution.py:24
  102.5 26.2 %collective-permute-start.11 = (bf16[768,256]{1,0:T(8,128)(2,1)S(1)}, bf16[768,256]{1,0:T(8,128)(2,1)}, u32[]{:S(2)}, u32[]{:S(2)}) collective-permute-start(bf16[768,256]{1,0:T(8,128)(2,1)S(1)} %broadcast_select_fusion.4.rest_0_), channel_id=1, source_target_pairs={{0,1},{1,0},{2,3},{3,2},{4,5},{5,4},{6,7},{7,6},{8,9},{9,8},{10,11... | collective-permute-start | bytes 1179656 | tf_op jit(solution)/shard_map/ppermute | solution.py:24
  103.3 32.3 %collective-permute-start.12 = (bf16[768,256]{1,0:T(8,128)(2,1)}, bf16[768,256]{1,0:T(8,128)(2,1)}, u32[]{:S(2)}, u32[]{:S(2)}) collective-permute-start(bf16[768,256]{1,0:T(8,128)(2,1)} %collective-permute-done.10.rest_1_), channel_id=1, source_target_pairs={{0,1},{1,0},{2,3},{3,2},{4,5},{5,4},{6,7},{7,6},{8,9},{9,8},{10,11... | collective-permute-start | bytes 1179656 | tf_op jit(solution)/shard_map/ppermute | solution.py:24
  108.9 42.7 %collective-permute-start.18 = (bf16[1024,256]{1,0:T(8,128)(2,1)S(1)}, bf16[1024,256]{1,0:T(8,128)(2,1)S(1)}, u32[]{:S(2)}, u32[]{:S(2)}) collective-permute-start(bf16[1024,256]{1,0:T(8,128)(2,1)S(1)} %broadcast_select_fusion.2.rest_0_), channel_id=1, source_target_pairs={{0,2},{1,3},{2,0},{3,1},{4,6},{5,7},{6,4},{7,5},{8,10},{9,11},{10,... | collective-permute-start | bytes 1572872 | tf_op jit(solution)/shard_map/ppermute | solution.py:24
  110.6 31.2 %all-to-all-start = ((s32[4,1,2]{2,1,0:T(1,128)}), s32[4,1,2]{2,1,0:T(1,128)S(1)}, u32[]{:S(2)}, u32[]{:S(2)}) async-start(s32[4,1,2]{2,1,0:T(1,128)} %copy.11), calls=%async_computation | async-start | bytes 4096 | tf_op jit(solution)/shard_map/all_to_all | solution.py:390
  141.8 41.2 %all-to-all-start.1 = ((bf16[4,2,128,384]{3,2,1,0:T(8,128)(2,1)}), bf16[4,2,128,384]{3,2,1,0:T(8,128)(2,1)S(1)}, u32[]{:S(2)}, u32[]{:S(2)}) async-start(bf16[4,2,128,384]{3,2,1,0:T(8,128)(2,1)} %get-tuple-element.17), calls=%async_computation.1 | async-start | bytes 1572864 | tf_op jit(solution)/shard_map/all_to_all | solution.py:444
  148.2 22.9 %collective-permute-start.23 = (bf16[1024,256]{1,0:T(8,128)(2,1)S(1)}, bf16[1024,256]{1,0:T(8,128)(2,1)S(1)}, u32[]{:S(2)}, u32[]{:S(2)}) collective-permute-start(bf16[1024,256]{1,0:T(8,128)(2,1)S(1)} %broadcast_select_fusion.1.rest_6_), channel_id=1, source_target_pairs={{4,2},{5,3},{12,10},{13,11},{20,18},{21,19},{28,26},{29,27}} | collective-permute-start | bytes 1572872 | tf_op jit(solution)/shard_map/ppermute | solution.py:24
  149.5 21.6 %collective-permute-start.24 = (bf16[1024,256]{1,0:T(8,128)(2,1)S(1)}, bf16[1024,256]{1,0:T(8,128)(2,1)}, u32[]{:S(2)}, u32[]{:S(2)}) collective-permute-start(bf16[1024,256]{1,0:T(8,128)(2,1)S(1)} %broadcast_select_fusion.1.rest_6_), channel_id=1, source_target_pairs={{4,6},{5,7},{12,14},{13,15},{20,22},{21,23},{28,30},{29,31}} | collective-permute-start | bytes 1572872 | tf_op jit(solution)/shard_map/ppermute | solution.py:24
  151.6 19.5 %collective-permute-start.19 = (bf16[1024,256]{1,0:T(8,128)(2,1)S(1)}, bf16[1024,256]{1,0:T(8,128)(2,1)}, u32[]{:S(2)}, u32[]{:S(2)}) collective-permute-start(bf16[1024,256]{1,0:T(8,128)(2,1)S(1)} %broadcast_select_fusion.2.rest_0_), channel_id=1, source_target_pairs={{0,1},{1,0},{2,3},{3,2},{4,5},{5,4},{6,7},{7,6},{8,9},{9,8},{10,11... | collective-permute-start | bytes 1572872 | tf_op jit(solution)/shard_map/ppermute | solution.py:24
  151.7 25.3 %collective-permute-start.20 = (bf16[1024,256]{1,0:T(8,128)(2,1)S(1)}, bf16[1024,256]{1,0:T(8,128)(2,1)}, u32[]{:S(2)}, u32[]{:S(2)}) collective-permute-start(bf16[1024,256]{1,0:T(8,128)(2,1)S(1)} %collective-permute-done.18.rest_1_), channel_id=1, source_target_pairs={{0,1},{1,0},{2,3},{3,2},{4,5},{5,4},{6,7},{7,6},{8,9},{9,8},{10,11... | collective-permute-start | bytes 1572872 | tf_op jit(solution)/shard_map/ppermute | solution.py:24
  (24 other events, 775.2 us)

commit v10 on v9

--- a/solution.py
+++ b/solution.py
@@ -30,7 +30,7 @@
     distant = [(m, m + 4) for m in range(4)]
     beside, back, mid, up = [(4, 5)], [(4, 0), (5, 1)], [(4, 2), (5, 3)], [(4, 6), (5, 7)]
     level = member // 2
-    a, b, c, e_halves = parts
+    a, b, c = parts
 
     def slabs(own):
         cur = jnp.where(member < 4, own, permute(own, distant))
@@ -38,13 +38,14 @@
         over = permute(cur, across)
         return cur, far, over, permute(far, across)
 
-    def halves(low, high):
-        half = jnp.where(member == 5, permute(high, beside), low)
-        to_up = permute(half, up)
-        to_back = permute(half, back)
-        to_mid = permute(half, mid)
-        half = jnp.where(level == 2, half, jnp.where(level == 3, to_up, jnp.where(level == 0, to_back, to_mid)))
-        return half, permute(half, across)
+    def column(own):
+        to_beside = permute(own, beside)
+        to_up = permute(own, [(4, 6)])
+        to_back = permute(own, [(4, 0)])
+        to_mid = permute(own, [(4, 2)])
+        cross_up = permute(to_up, [(6, 7)])
+        cross_low = permute(jnp.where(level == 0, to_back, to_mid), [(0, 1), (2, 3)])
+        return to_back, cross_low, to_mid, cross_low, own, to_beside, to_up, cross_up
 
     def whole(own):
         own = lax.optimization_barrier(own)
@@ -54,7 +55,7 @@
         to_mid = permute(rows, mid)
         return to_back, to_mid, rows, to_up
 
-    return ((slabs(a), halves(*e_halves)), (slabs(b), whole(b)), (slabs(c), whole(c)))
+    return ((slabs(a), column(a)), (slabs(b), whole(b)), (slabs(c), whole(c)))
 
 
 def placed_slabs(member, refs):
@@ -86,47 +87,16 @@
         copies = [pltpu.make_async_copy(refs[0].at[TICKS - 1, at], target.at[TICKS - 1, at], sem)]
         copies[0].start()
         return copies
+    share = 8 // len(refs)
     copies = [pltpu.make_async_copy(ref.at[at], target.at[TICKS - 1, at], sem) for ref in refs]
-    for level, copy in enumerate(copies):
-        pl.when(lax.div(member, 2) == level)(copy.start)
+    for place, copy in enumerate(copies):
+        pl.when(lax.div(member, share) == place)(copy.start)
     return copies[:1]
-
-
-def start_halves(member, refs, target, sems, rows):
-    if len(refs) == 1:
-        return start_last(member, refs, target, sems.at[0], 0, rows)
-    half, overhalf = refs
-    x, n = lax.rem(member, 2), rows // 2
-
-    def copy(ref, number):
-        return pltpu.make_async_copy(ref, target.at[TICKS - 1, pl.ds(number * n, n)], sems.at[number])
-
-    for which in (0, 1):
-
-        @pl.when(x == which)
-        def _(which=which):
-            copy(half, which).start()
-            copy(overhalf, 1 - which).start()
-
-    return [copy(half, 0), copy(half, 1)]
 
 
 def wait_all(copies):
     for copy in copies:
         copy.wait()
-
-
-def cut(ranges):
-    left = sum(n for _, n in ranges) // 2
-    low, high = [], []
-    for start, n in ranges:
-        take = min(left, n)
-        if take:
-            low.append((start, take))
-        if n - take:
-            high.append((start + take, n - take))
-        left -= take
-    return low, high
 
 
 def pack_kernel(pieces, front, *rest):
@@ -210,7 +180,7 @@
     member = member_ref[0]
     p, rows = P_SIZE, TICKS * P_SIZE
     copies = start_first(member, firsts, raw, sems, 0, rows)
-    copies += start_halves(member, lasts, raw, last_sems, rows)
+    copies += start_last(member, lasts, raw, last_sems.at[0], 0, rows)
     loads = [
         pltpu.make_async_copy(
             front.at[pl.ds(t * width, p), :], own.at[pl.ds(t * p, p), :], own_sems.at[t]
@@ -288,7 +258,7 @@
             pltpu.VMEM((rows, width), jnp.float32),
             pltpu.VMEM((2, TICKS, p, p), jnp.bfloat16),
             pltpu.SemaphoreType.DMA((4,)),
-            pltpu.SemaphoreType.DMA((2,)),
+            pltpu.SemaphoreType.DMA((1,)),
             pltpu.SemaphoreType.DMA((TICKS,)),
         ],
     )(member, front, *bufs[0], *bufs[1])
@@ -327,19 +297,20 @@
             )
             copies[-1].start()
         waits.append(copies)
-    keep = (member >= TICKS) | (lax.broadcasted_iota(jnp.int32, (RB, width), 1) >= P_SIZE)
+    keep = (member >= TICKS) | (lax.broadcasted_iota(jnp.int32, (CHUNK, width), 1) >= P_SIZE)
     stores = []
     for number, (lo, n, pieces) in enumerate(chunks):
         wait_all(waits[number])
-        for first in range(lo, lo + n, RB):
-            at = pl.ds(first, RB)
-            total = jnp.where(keep, base[at, :], 0.0)
-            for s in range(TICKS):
-                total = minus_dot(total, raw[s, at, :], w[s * P_SIZE : (s + 1) * P_SIZE, :])
-            base[at, :] = total
-            if tail:
-                block = first // RB
-                outgoing[dest_ref[block], slot_ref[block]] = jnp.where(keep, total, 0.0).astype(jnp.bfloat16)
+        at = pl.ds(lo, n)
+        total = jnp.where(keep[:n], base[at, :], 0.0)
+        for s in range(TICKS):
+            total = minus_dot(total, raw[s, at, :], w[s * P_SIZE : (s + 1) * P_SIZE, :])
+        base[at, :] = total
+        if tail:
+            cont = jnp.where(keep[:n], total, 0.0).astype(jnp.bfloat16)
+            for first in range(0, n, RB):
+                block = (lo + first) // RB
+                outgoing[dest_ref[block], slot_ref[block]] = cont[first : first + RB]
         for i, (src, dst, count) in enumerate(pieces):
             stores.append(
                 pltpu.make_async_copy(
@@ -431,8 +402,8 @@
         at += count
     if lax.axis_size("blk") == 8:
         (own_p,) = pack(front, [pivot_ranges])
-        *e_halves, own_t, own_m = pack(front, [*cut(pivot_ranges), tail_ranges, middle_ranges])
-        sets = relay((own_p, own_t, own_m, e_halves), member)
+        own_t, own_m = pack(front, [tail_ranges, middle_ranges])
+        sets = relay((own_p, own_t, own_m), member)
     else:
         own_p, own_t, own_m = pack(front, [pivot_ranges, tail_ranges, middle_ranges])
         sets = tuple(((lax.all_gather(s, "blk")[:TICKS],),) * 2 for s in (own_p, own_t, own_m))

time: 188 us -> 202 us (1.074)
  the two profiles are of different devices: /device:TPU:22 before, /device:TPU:0 now
where the time goes in v10:
time: 202 us; the launch traced here: 200 us
  starting transfers between devices  92.1 us (46%)
  waiting for transfers between devices  64.2 us (32%)
  Pallas kernels  32.5 us (16%)
  other arithmetic  5.28 us (3%)
  local copies, waits for them, and re-layouts  4.4 us (2%)
    ppermute x26, starting transfers between devices, permute(): return lax.ppermute(value, 'blk', pairs)  85.3 us
    ppermute x26, waiting for transfers between devices, permute(): return lax.ppermute(value, 'blk', pairs)  64.2 us
    pallas_call x1, Pallas kernels, pivot_rows(): pl.pallas_call(functools.partial(pivot_kernel, counts, width), name='pivo...  12.4 us
    pallas_call x2, Pallas kernels, other_rows(): pl.pallas_call(functools.partial(other_kernel, counts, chunks, bool(group...  12.3 us
    pallas_call x2, Pallas kernels, pack(): pl.pallas_call(functools.partial(pack_kernel, pieces), out_shape=tuple((j...  4.62 us
  transfers between devices with their start and end apart: 28, of which 9 were waited for; matrix products, arithmetic and copies ran while one was open for 4% of the time, Pallas kernels for 14%

profile of v10, /device:TPU:0, one launch (start us, length us, event | category | flops | bytes accessed | tf_op | source)
XLA Modules:
  0.0 199.6 jit_solution(14742388668359031494)
XLA Ops:
  0.6 2.2 %shard_map.59.rest_8_ = bf16[1280,256]{1,0:T(8,128)(2,1)} custom-call(f32[3072,384]{1,0:T(8,128)} %front.9), custom_call_target="tpu_custom_call" | custom-call | tf_op jit(solution)/shard_map/pallas_call | solution.py:125
  2.8 7.0 %collective-permute-start = (bf16[1280,256]{1,0:T(8,128)(2,1)}, bf16[1280,256]{1,0:T(8,128)(2,1)}, u32[]{:S(2)}, u32[]{:S(2)}) collective-permute-start(bf16[1280,256]{1,0:T(8,128)(2,1)} %shard_map.59.rest_8_), channel_id=1, source_target_pairs={{0,4},{1,5},{2,6},{3,7},{8,12},{9,13},{10,14},{11,15},{16,20},{17,... | collective-permute-start | bytes 1966088 | tf_op jit(solution)/shard_map/ppermute | solution.py:24
  9.8 2.5 %shard_map.60 = (bf16[768,256]{1,0:T(8,128)(2,1)}, bf16[1024,256]{1,0:T(8,128)(2,1)}) custom-call(f32[3072,384]{1,0:T(8,128)} %front.9), custom_call_target="tpu_custom_call" | custom-call | tf_op jit(solution)/shard_map/pallas_call | solution.py:125
  15.1 6.9 %collective-permute-start.10 = (bf16[768,256]{1,0:T(8,128)(2,1)}, bf16[768,256]{1,0:T(8,128)(2,1)}, u32[]{:S(2)}, u32[]{:S(2)}) collective-permute-start(bf16[768,256]{1,0:T(8,128)(2,1)} %get-tuple-element.10), channel_id=1, source_target_pairs={{0,4},{1,5},{2,6},{3,7},{8,12},{9,13},{10,14},{11,15},{16,20},{17,... | collective-permute-start | bytes 1179656 | tf_op jit(solution)/shard_map/ppermute | solution.py:24
  24.0 7.7 %collective-permute-done.10 = bf16[768,256]{1,0:T(8,128)(2,1)} collective-permute-done((bf16[768,256]{1,0:T(8,128)(2,1)}, bf16[768,256]{1,0:T(8,128)(2,1)}, u32[]{:S(2)}, u32[]{:S(2)}) %collective-permute-start.10) | collective-permute-done | bytes 393248 | tf_op jit(solution)/shard_map/ppermute | solution.py:24
  32.4 8.1 %collective-permute-start.18 = (bf16[1024,256]{1,0:T(8,128)(2,1)}, bf16[1024,256]{1,0:T(8,128)(2,1)S(1)}, u32[]{:S(2)}, u32[]{:S(2)}) collective-permute-start(bf16[1024,256]{1,0:T(8,128)(2,1)} %get-tuple-element.12), channel_id=1, source_target_pairs={{0,4},{1,5},{2,6},{3,7},{8,12},{9,13},{10,14},{11,15},{16,20},{17,... | collective-permute-start | bytes 1572872 | tf_op jit(solution)/shard_map/ppermute | solution.py:24
  40.6 10.2 %collective-permute-done.18 = bf16[1024,256]{1,0:T(8,128)(2,1)S(1)} collective-permute-done((bf16[1024,256]{1,0:T(8,128)(2,1)}, bf16[1024,256]{1,0:T(8,128)(2,1)S(1)}, u32[]{:S(2)}, u32[]{:S(2)}) %collective-permute-start.18) | collective-permute-done | bytes 524320 | tf_op jit(solution)/shard_map/ppermute | solution.py:24
  52.9 33.8 %collective-permute-start.1 = (bf16[1280,256]{1,0:T(8,128)(2,1)S(1)}, bf16[1280,256]{1,0:T(8,128)(2,1)S(1)}, u32[]{:S(2)}, u32[]{:S(2)}) collective-permute-start(bf16[1280,256]{1,0:T(8,128)(2,1)S(1)} %broadcast_select_fusion.1.rest_0_), channel_id=1, source_target_pairs={{0,2},{1,3},{2,0},{3,1},{4,6},{5,7},{6,4},{7,5},{8,10},{9,11},{10,... | collective-permute-start | bytes 1966088 | tf_op jit(solution)/shard_map/ppermute | solution.py:24
  88.2 2.5 %collective-permute-start.6 = (bf16[1280,256]{1,0:T(8,128)(2,1)S(1)}, bf16[1280,256]{1,0:T(8,128)(2,1)S(1)}, u32[]{:S(2)}, u32[]{:S(2)}) collective-permute-start(bf16[1280,256]{1,0:T(8,128)(2,1)S(1)} %broadcast_select_fusion), channel_id=1, source_target_pairs={{0,1},{2,3},{8,9},{10,11},{16,17},{18,19},{24,25},{26,27}} | collective-permute-start | bytes 1966088 | tf_op jit(solution)/shard_map/ppermute | solution.py:24
  92.3 5.0 %collective-permute-start.11 = (bf16[768,256]{1,0:T(8,128)(2,1)}, bf16[768,256]{1,0:T(8,128)(2,1)}, u32[]{:S(2)}, u32[]{:S(2)}) collective-permute-start(bf16[768,256]{1,0:T(8,128)(2,1)} %broadcast_select_fusion.5.rest_0_), channel_id=1, source_target_pairs={{0,2},{1,3},{2,0},{3,1},{4,6},{5,7},{6,4},{7,5},{8,10},{9,11},{10,... | collective-permute-start | bytes 1179656 | tf_op jit(solution)/shard_map/ppermute | solution.py:24
  97.3 4.9 %collective-permute-done.1.rest_1_ = bf16[1280,256]{1,0:T(8,128)(2,1)S(1)} collective-permute-done((bf16[1280,256]{1,0:T(8,128)(2,1)S(1)}, bf16[1280,256]{1,0:T(8,128)(2,1)S(1)}, u32[]{:S(2)}, u32[]{:S(2)}) %collective-permute-start.1) | collective-permute-done | bytes 655392 | tf_op jit(solution)/shard_map/ppermute | solution.py:24
  103.7 5.5 %collective-permute-done.11.rest_1_ = bf16[768,256]{1,0:T(8,128)(2,1)} collective-permute-done((bf16[768,256]{1,0:T(8,128)(2,1)}, bf16[768,256]{1,0:T(8,128)(2,1)}, u32[]{:S(2)}, u32[]{:S(2)}) %collective-permute-start.11) | collective-permute-done | bytes 393248 | tf_op jit(solution)/shard_map/ppermute | solution.py:24
  110.7 6.7 %collective-permute-done.6.rest_5_.rest_7_ = bf16[1280,256]{1,0:T(8,128)(2,1)S(1)} collective-permute-done((bf16[1280,256]{1,0:T(8,128)(2,1)S(1)}, bf16[1280,256]{1,0:T(8,128)(2,1)S(1)}, u32[]{:S(2)}, u32[]{:S(2)}) %collective-permute-start.6) | collective-permute-done | bytes 655392 | tf_op jit(solution)/shard_map/ppermute | solution.py:24
  118.8 2.5 %collective-permute-start.12 = (bf16[768,256]{1,0:T(8,128)(2,1)}, bf16[768,256]{1,0:T(8,128)(2,1)}, u32[]{:S(2)}, u32[]{:S(2)}) collective-permute-start(bf16[768,256]{1,0:T(8,128)(2,1)} %broadcast_select_fusion.5.rest_0_), channel_id=1, source_target_pairs={{0,1},{1,0},{2,3},{3,2},{4,5},{5,4},{6,7},{7,6},{8,9},{9,8},{10,11... | collective-permute-start | bytes 1179656 | tf_op jit(solution)/shard_map/ppermute | solution.py:24
  124.1 7.3 %collective-permute-done.3.rest_3_ = bf16[1280,256]{1,0:T(8,128)(2,1)S(1)} collective-permute-done((bf16[1280,256]{1,0:T(8,128)(2,1)S(1)}, bf16[1280,256]{1,0:T(8,128)(2,1)S(1)}, u32[]{:S(2)}, u32[]{:S(2)}) %collective-permute-start.3) | collective-permute-done | bytes 655392 | tf_op jit(solution)/shard_map/ppermute | solution.py:24
  132.9 3.3 %all-to-all-start = ((s32[4,1,2]{2,1,0:T(1,128)}), s32[4,1,2]{2,1,0:T(1,128)S(1)}, u32[]{:S(2)}, u32[]{:S(2)}) async-start(s32[4,1,2]{2,1,0:T(1,128)} %copy.11), calls=%async_computation | async-start | bytes 4096 | tf_op jit(solution)/shard_map/all_to_all | solution.py:361
  136.3 12.4 %pivot_rows.1 = (f32[3072,384]{1,0:T(8,128)}, bf16[1280,384]{1,0:T(8,128)(2,1)}) custom-call(s32[1]{0:T(128)} %bitcast.member_ref, f32[3072,384]{1,0:T(8,128)} %front.9, bf16[1280,256]{1,0:T(8,128)(2,1)} %copy-done.5, bf16[1280,256]{1,0:T(8,128)(2,1)} %copy-done.12, bf16[1280,256]{1,0:T(8,128)(2,1)} %copy-done.13, bf16[1280,256]{1,0:T(8,128)(2,1)} %copy-done.15, ...), custom_call_target="tpu_custom_call" | custom-call | tf_op jit(solution)/shard_map/pivot_rows/pallas_call | solution.py:246
  148.8 6.3 %tail_rows.1 = (f32[3072,384]{1,0:T(8,128)}, bf16[4,2,128,384]{3,2,1,0:T(8,128)(2,1)}) custom-call(s32[1]{0:T(128)} %bitcast.member_ref, s32[6]{0:T(128)} %bitcast.8, s32[6]{0:T(128)} %copy-done.21, bf16[1280,384]{1,0:T(8,128)(2,1)} %get-tuple-element.8.w, f32[3072,384]{1,0:T(8,128)} %front.9, ...), custom_call_target="tpu_custom_call", output_to_operand_aliasing={{0}: (5, {})} | custom-call | tf_op jit(solution)/shard_map/tail_rows/pallas_call | solution.py:334
  155.1 3.5 %all-to-all-start.1 = ((bf16[4,2,128,384]{3,2,1,0:T(8,128)(2,1)}), bf16[4,2,128,384]{3,2,1,0:T(8,128)(2,1)S(1)}, u32[]{:S(2)}, u32[]{:S(2)}) async-start(bf16[4,2,128,384]{3,2,1,0:T(8,128)(2,1)} %get-tuple-element.13), calls=%async_computation.1 | async-start | bytes 1572864 | tf_op jit(solution)/shard_map/all_to_all | solution.py:415
  163.2 2.5 %collective-permute-start.20 = (bf16[1024,256]{1,0:T(8,128)(2,1)S(1)}, bf16[1024,256]{1,0:T(8,128)(2,1)}, u32[]{:S(2)}, u32[]{:S(2)}) collective-permute-start(bf16[1024,256]{1,0:T(8,128)(2,1)S(1)} %broadcast_select_fusion.3.rest_0_), channel_id=1, source_target_pairs={{0,1},{1,0},{2,3},{3,2},{4,5},{5,4},{6,7},{7,6},{8,9},{9,8},{10,11... | collective-permute-start | bytes 1572872 | tf_op jit(solution)/shard_map/ppermute | solution.py:24
  167.7 9.6 %collective-permute-done.23.rest_4_ = bf16[1024,256]{1,0:T(8,128)(2,1)S(1)} collective-permute-done((bf16[1024,256]{1,0:T(8,128)(2,1)S(1)}, bf16[1024,256]{1,0:T(8,128)(2,1)S(1)}, u32[]{:S(2)}, u32[]{:S(2)}) %collective-permute-start.23) | collective-permute-done | bytes 524320 | tf_op jit(solution)/shard_map/ppermute | solution.py:24
  178.6 11.0 %collective-permute-done.21.rest_3_ = bf16[1024,256]{1,0:T(8,128)(2,1)} collective-permute-done((bf16[1024,256]{1,0:T(8,128)(2,1)}, bf16[1024,256]{1,0:T(8,128)(2,1)}, u32[]{:S(2)}, u32[]{:S(2)}) %collective-permute-start.21) | collective-permute-done | bytes 524320 | tf_op jit(solution)/shard_map/ppermute | solution.py:24
  189.6 6.0 %middle_rows.1 = f32[3072,384]{1,0:T(8,128)} custom-call(s32[1]{0:T(128)} %bitcast.member_ref, s32[6]{0:T(128)} %bitcast.9, s32[6]{0:T(128)} %copy-done.21, bf16[1280,384]{1,0:T(8,128)(2,1)} %get-tuple-element.8.w, f32[3072,384]{1,0:T(8,128)} %front.9, f32[3072,384]{1,0:T(8,128)} %get-tuple-element.11.out_in, ...), custom_call_target="tpu_custom_call", output_to_operand_aliasing={{}: (5, {})} | custom-call | tf_op jit(solution)/shard_map/middle_rows/pallas_call | solution.py:334
  196.6 3.1 %add_blocks.1 = f32[1024,384]{1,0:T(8,128)} custom-call(s32[8]{0:T(128)} %reshape.81.address_ref, bf16[8,128,384]{2,1,0:T(8,128)(2,1)} %bitcast.7, f32[1024,384]{1,0:T(8,128)} %base.1), custom_call_target="tpu_custom_call" | custom-call | tf_op jit(solution)/shard_map/add_blocks/pallas_call | solution.py:378
  (100 shorter events, 28.0 us)
Async XLA Ops:
  2.8 29.6 %collective-permute-start = (bf16[1280,256]{1,0:T(8,128)(2,1)}, bf16[1280,256]{1,0:T(8,128)(2,1)}, u32[]{:S(2)}, u32[]{:S(2)}) collective-permute-start(bf16[1280,256]{1,0:T(8,128)(2,1)} %shard_map.59.rest_8_), channel_id=1, source_target_pairs={{0,4},{1,5},{2,6},{3,7},{8,12},{9,13},{10,14},{11,15},{16,20},{17,... | collective-permute-start | bytes 1966088 | tf_op jit(solution)/shard_map/ppermute | solution.py:24
  13.1 39.0 %collective-permute-start.4 = (bf16[1280,256]{1,0:T(8,128)(2,1)S(1)}, bf16[1280,256]{1,0:T(8,128)(2,1)S(1)}, u32[]{:S(2)}, u32[]{:S(2)}) collective-permute-start(bf16[1280,256]{1,0:T(8,128)(2,1)S(1)} %copy-done), channel_id=1, source_target_pairs={{4,0},{12,8},{20,16},{28,24}} | collective-permute-start | bytes 1966088 | tf_op jit(solution)/shard_map/ppermute | solution.py:24
  14.4 38.4 %collective-permute-start.5 = (bf16[1280,256]{1,0:T(8,128)(2,1)S(1)}, bf16[1280,256]{1,0:T(8,128)(2,1)S(1)}, u32[]{:S(2)}, u32[]{:S(2)}) collective-permute-start(bf16[1280,256]{1,0:T(8,128)(2,1)S(1)} %copy-done), channel_id=1, source_target_pairs={{4,2},{12,10},{20,18},{28,26}} | collective-permute-start | bytes 1966088 | tf_op jit(solution)/shard_map/ppermute | solution.py:24
  15.1 16.6 %collective-permute-start.10 = (bf16[768,256]{1,0:T(8,128)(2,1)}, bf16[768,256]{1,0:T(8,128)(2,1)}, u32[]{:S(2)}, u32[]{:S(2)}) collective-permute-start(bf16[768,256]{1,0:T(8,128)(2,1)} %get-tuple-element.10), channel_id=1, source_target_pairs={{0,4},{1,5},{2,6},{3,7},{8,12},{9,13},{10,14},{11,15},{16,20},{17,... | collective-permute-start | bytes 1179656 | tf_op jit(solution)/shard_map/ppermute | solution.py:24
  22.2 64.5 %collective-permute-start.8 = (bf16[1280,256]{1,0:T(8,128)(2,1)S(1)}, bf16[1280,256]{1,0:T(8,128)(2,1)S(1)}, u32[]{:S(2)}, u32[]{:S(2)}) collective-permute-start(bf16[1280,256]{1,0:T(8,128)(2,1)S(1)} %copy-done), channel_id=1, source_target_pairs={{4,6},{12,14},{20,22},{28,30}} | collective-permute-start | bytes 1966088 | tf_op jit(solution)/shard_map/ppermute | solution.py:24
  31.7 56.5 %collective-permute-start.7 = (bf16[1280,256]{1,0:T(8,128)(2,1)S(1)}, bf16[1280,256]{1,0:T(8,128)(2,1)S(1)}, u32[]{:S(2)}, u32[]{:S(2)}) collective-permute-start(bf16[1280,256]{1,0:T(8,128)(2,1)S(1)} %copy-done), channel_id=1, source_target_pairs={{4,5},{12,13},{20,21},{28,29}} | collective-permute-start | bytes 1966088 | tf_op jit(solution)/shard_map/ppermute | solution.py:24
  32.4 18.4 %collective-permute-start.18 = (bf16[1024,256]{1,0:T(8,128)(2,1)}, bf16[1024,256]{1,0:T(8,128)(2,1)S(1)}, u32[]{:S(2)}, u32[]{:S(2)}) collective-permute-start(bf16[1024,256]{1,0:T(8,128)(2,1)} %get-tuple-element.12), channel_id=1, source_target_pairs={{0,4},{1,5},{2,6},{3,7},{8,12},{9,13},{10,14},{11,15},{16,20},{17,... | collective-permute-start | bytes 1572872 | tf_op jit(solution)/shard_map/ppermute | solution.py:24
  50.8 39.9 %collective-permute-start.15 = (bf16[768,256]{1,0:T(8,128)(2,1)S(1)}, bf16[768,256]{1,0:T(8,128)(2,1)S(1)}, u32[]{:S(2)}, u32[]{:S(2)}) collective-permute-start(bf16[768,256]{1,0:T(8,128)(2,1)S(1)} %broadcast_select_fusion.4.rest_6_), channel_id=1, source_target_pairs={{4,0},{5,1},{12,8},{13,9},{20,16},{21,17},{28,24},{29,25}} | collective-permute-start | bytes 1179656 | tf_op jit(solution)/shard_map/ppermute | solution.py:24
  52.1 40.2 %collective-permute-start.16 = (bf16[768,256]{1,0:T(8,128)(2,1)S(1)}, bf16[768,256]{1,0:T(8,128)(2,1)S(1)}, u32[]{:S(2)}, u32[]{:S(2)}) collective-permute-start(bf16[768,256]{1,0:T(8,128)(2,1)S(1)} %broadcast_select_fusion.4.rest_6_), channel_id=1, source_target_pairs={{4,2},{5,3},{12,10},{13,11},{20,18},{21,19},{28,26},{29,27}} | collective-permute-start | bytes 1179656 | tf_op jit(solution)/shard_map/ppermute | solution.py:24
  52.9 49.4 %collective-permute-start.1 = (bf16[1280,256]{1,0:T(8,128)(2,1)S(1)}, bf16[1280,256]{1,0:T(8,128)(2,1)S(1)}, u32[]{:S(2)}, u32[]{:S(2)}) collective-permute-start(bf16[1280,256]{1,0:T(8,128)(2,1)S(1)} %broadcast_select_fusion.1.rest_0_), channel_id=1, source_target_pairs={{0,2},{1,3},{2,0},{3,1},{4,6},{5,7},{6,4},{7,5},{8,10},{9,11},{10,... | collective-permute-start | bytes 1966088 | tf_op jit(solution)/shard_map/ppermute | solution.py:24
  86.7 32.1 %collective-permute-start.2 = (bf16[1280,256]{1,0:T(8,128)(2,1)S(1)}, bf16[1280,256]{1,0:T(8,128)(2,1)S(1)}, u32[]{:S(2)}, u32[]{:S(2)}) collective-permute-start(bf16[1280,256]{1,0:T(8,128)(2,1)S(1)} %broadcast_select_fusion.1.rest_0_), channel_id=1, source_target_pairs={{0,1},{1,0},{2,3},{3,2},{4,5},{5,4},{6,7},{7,6},{8,9},{9,8},{10,11... | collective-permute-start | bytes 1966088 | tf_op jit(solution)/shard_map/ppermute | solution.py:24
  88.2 29.2 %collective-permute-start.6 = (bf16[1280,256]{1,0:T(8,128)(2,1)S(1)}, bf16[1280,256]{1,0:T(8,128)(2,1)S(1)}, u32[]{:S(2)}, u32[]{:S(2)}) collective-permute-start(bf16[1280,256]{1,0:T(8,128)(2,1)S(1)} %broadcast_select_fusion), channel_id=1, source_target_pairs={{0,1},{2,3},{8,9},{10,11},{16,17},{18,19},{24,25},{26,27}} | collective-permute-start | bytes 1966088 | tf_op jit(solution)/shard_map/ppermute | solution.py:24
  90.8 30.5 %collective-permute-start.9 = (bf16[1280,256]{1,0:T(8,128)(2,1)S(1)}, bf16[1280,256]{1,0:T(8,128)(2,1)S(1)}, u32[]{:S(2)}, u32[]{:S(2)}) collective-permute-start(bf16[1280,256]{1,0:T(8,128)(2,1)S(1)} %collective-permute-done.8.rest_10_), channel_id=1, source_target_pairs={{6,7},{14,15},{22,23},{30,31}} | collective-permute-start | bytes 1966088 | tf_op jit(solution)/shard_map/ppermute | solution.py:24
  92.3 16.9 %collective-permute-start.11 = (bf16[768,256]{1,0:T(8,128)(2,1)}, bf16[768,256]{1,0:T(8,128)(2,1)}, u32[]{:S(2)}, u32[]{:S(2)}) collective-permute-start(bf16[768,256]{1,0:T(8,128)(2,1)} %broadcast_select_fusion.5.rest_0_), channel_id=1, source_target_pairs={{0,2},{1,3},{2,0},{3,1},{4,6},{5,7},{6,4},{7,5},{8,10},{9,11},{10,... | collective-permute-start | bytes 1179656 | tf_op jit(solution)/shard_map/ppermute | solution.py:24
  102.2 29.2 %collective-permute-start.3 = (bf16[1280,256]{1,0:T(8,128)(2,1)S(1)}, bf16[1280,256]{1,0:T(8,128)(2,1)S(1)}, u32[]{:S(2)}, u32[]{:S(2)}) collective-permute-start(bf16[1280,256]{1,0:T(8,128)(2,1)S(1)} %collective-permute-done.1.rest_1_), channel_id=1, source_target_pairs={{0,1},{1,0},{2,3},{3,2},{4,5},{5,4},{6,7},{7,6},{8,9},{9,8},{10,11... | collective-permute-start | bytes 1966088 | tf_op jit(solution)/shard_map/ppermute | solution.py:24
  109.2 49.4 %collective-permute-start.22 = (bf16[1024,256]{1,0:T(8,128)(2,1)}, bf16[1024,256]{1,0:T(8,128)(2,1)}, u32[]{:S(2)}, u32[]{:S(2)}) collective-permute-start(bf16[1024,256]{1,0:T(8,128)(2,1)} %get-tuple-element.12), channel_id=1, source_target_pairs={{4,5},{12,13},{20,21},{28,29}} | collective-permute-start | bytes 1572872 | tf_op jit(solution)/shard_map/ppermute | solution.py:24
  117.4 31.4 %collective-permute-start.17 = (bf16[768,256]{1,0:T(8,128)(2,1)S(1)}, bf16[768,256]{1,0:T(8,128)(2,1)}, u32[]{:S(2)}, u32[]{:S(2)}) collective-permute-start(bf16[768,256]{1,0:T(8,128)(2,1)S(1)} %broadcast_select_fusion.4.rest_6_), channel_id=1, source_target_pairs={{4,6},{5,7},{12,14},{13,15},{20,22},{21,23},{28,30},{29,31}} | collective-permute-start | bytes 1179656 | tf_op jit(solution)/shard_map/ppermute | solution.py:24
  118.8 30.0 %collective-permute-start.12 = (bf16[768,256]{1,0:T(8,128)(2,1)}, bf16[768,256]{1,0:T(8,128)(2,1)}, u32[]{:S(2)}, u32[]{:S(2)}) collective-permute-start(bf16[768,256]{1,0:T(8,128)(2,1)} %broadcast_select_fusion.5.rest_0_), channel_id=1, source_target_pairs={{0,1},{1,0},{2,3},{3,2},{4,5},{5,4},{6,7},{7,6},{8,9},{9,8},{10,11... | collective-permute-start | bytes 1179656 | tf_op jit(solution)/shard_map/ppermute | solution.py:24
  122.1 26.7 %collective-permute-start.13 = (bf16[768,256]{1,0:T(8,128)(2,1)}, bf16[768,256]{1,0:T(8,128)(2,1)}, u32[]{:S(2)}, u32[]{:S(2)}) collective-permute-start(bf16[768,256]{1,0:T(8,128)(2,1)} %collective-permute-done.11.rest_1_), channel_id=1, source_target_pairs={{0,1},{1,0},{2,3},{3,2},{4,5},{5,4},{6,7},{7,6},{8,9},{9,8},{10,11... | collective-permute-start | bytes 1179656 | tf_op jit(solution)/shard_map/ppermute | solution.py:24
  131.4 34.3 %collective-permute-start.19 = (bf16[1024,256]{1,0:T(8,128)(2,1)S(1)}, bf16[1024,256]{1,0:T(8,128)(2,1)}, u32[]{:S(2)}, u32[]{:S(2)}) collective-permute-start(bf16[1024,256]{1,0:T(8,128)(2,1)S(1)} %broadcast_select_fusion.3.rest_0_), channel_id=1, source_target_pairs={{0,2},{1,3},{2,0},{3,1},{4,6},{5,7},{6,4},{7,5},{8,10},{9,11},{10,... | collective-permute-start | bytes 1572872 | tf_op jit(solution)/shard_map/ppermute | solution.py:24
  132.9 22.2 %all-to-all-start = ((s32[4,1,2]{2,1,0:T(1,128)}), s32[4,1,2]{2,1,0:T(1,128)S(1)}, u32[]{:S(2)}, u32[]{:S(2)}) async-start(s32[4,1,2]{2,1,0:T(1,128)} %copy.11), calls=%async_computation | async-start | bytes 4096 | tf_op jit(solution)/shard_map/all_to_all | solution.py:361
  155.1 40.5 %all-to-all-start.1 = ((bf16[4,2,128,384]{3,2,1,0:T(8,128)(2,1)}), bf16[4,2,128,384]{3,2,1,0:T(8,128)(2,1)S(1)}, u32[]{:S(2)}, u32[]{:S(2)}) async-start(bf16[4,2,128,384]{3,2,1,0:T(8,128)(2,1)} %get-tuple-element.13), calls=%async_computation.1 | async-start | bytes 1572864 | tf_op jit(solution)/shard_map/all_to_all | solution.py:415
  159.8 17.6 %collective-permute-start.23 = (bf16[1024,256]{1,0:T(8,128)(2,1)S(1)}, bf16[1024,256]{1,0:T(8,128)(2,1)S(1)}, u32[]{:S(2)}, u32[]{:S(2)}) collective-permute-start(bf16[1024,256]{1,0:T(8,128)(2,1)S(1)} %broadcast_select_fusion.2.rest_6_), channel_id=1, source_target_pairs={{4,0},{5,1},{12,8},{13,9},{20,16},{21,17},{28,24},{29,25}} | collective-permute-start | bytes 1572872 | tf_op jit(solution)/shard_map/ppermute | solution.py:24
  165.7 23.9 %collective-permute-start.21 = (bf16[1024,256]{1,0:T(8,128)(2,1)}, bf16[1024,256]{1,0:T(8,128)(2,1)}, u32[]{:S(2)}, u32[]{:S(2)}) collective-permute-start(bf16[1024,256]{1,0:T(8,128)(2,1)} %collective-permute-done.19.rest_1_), channel_id=1, source_target_pairs={{0,1},{1,0},{2,3},{3,2},{4,5},{5,4},{6,7},{7,6},{8,9},{9,8},{10,11... | collective-permute-start | bytes 1572872 | tf_op jit(solution)/shard_map/ppermute | solution.py:24
  (27 other events, 1090.9 us)

commit v11 on v9

--- a/solution.py
+++ b/solution.py
@@ -114,19 +114,6 @@
 def wait_all(copies):
     for copy in copies:
         copy.wait()
-
-
-def cut(ranges):
-    left = sum(n for _, n in ranges) // 2
-    low, high = [], []
-    for start, n in ranges:
-        take = min(left, n)
-        if take:
-            low.append((start, take))
-        if n - take:
-            high.append((start + take, n - take))
-        left -= take
-    return low, high
 
 
 def pack_kernel(pieces, front, *rest):
@@ -327,19 +314,20 @@
             )
             copies[-1].start()
         waits.append(copies)
-    keep = (member >= TICKS) | (lax.broadcasted_iota(jnp.int32, (RB, width), 1) >= P_SIZE)
+    keep = (member >= TICKS) | (lax.broadcasted_iota(jnp.int32, (CHUNK, width), 1) >= P_SIZE)
     stores = []
     for number, (lo, n, pieces) in enumerate(chunks):
         wait_all(waits[number])
-        for first in range(lo, lo + n, RB):
-            at = pl.ds(first, RB)
-            total = jnp.where(keep, base[at, :], 0.0)
-            for s in range(TICKS):
-                total = minus_dot(total, raw[s, at, :], w[s * P_SIZE : (s + 1) * P_SIZE, :])
-            base[at, :] = total
-            if tail:
-                block = first // RB
-                outgoing[dest_ref[block], slot_ref[block]] = jnp.where(keep, total, 0.0).astype(jnp.bfloat16)
+        at = pl.ds(lo, n)
+        total = jnp.where(keep[:n], base[at, :], 0.0)
+        for s in range(TICKS):
+            total = minus_dot(total, raw[s, at, :], w[s * P_SIZE : (s + 1) * P_SIZE, :])
+        base[at, :] = total
+        if tail:
+            cont = jnp.where(keep[:n], total, 0.0).astype(jnp.bfloat16)
+            for first in range(0, n, RB):
+                block = (lo + first) // RB
+                outgoing[dest_ref[block], slot_ref[block]] = cont[first : first + RB]
         for i, (src, dst, count) in enumerate(pieces):
             stores.append(
                 pltpu.make_async_copy(
@@ -431,8 +419,9 @@
         at += count
     if lax.axis_size("blk") == 8:
         (own_p,) = pack(front, [pivot_ranges])
-        *e_halves, own_t, own_m = pack(front, [*cut(pivot_ranges), tail_ranges, middle_ranges])
-        sets = relay((own_p, own_t, own_m, e_halves), member)
+        own_t, own_m = pack(front, [tail_ranges, middle_ranges])
+        half = own_p.shape[0] // 2
+        sets = relay((own_p, own_t, own_m, (own_p[:half], own_p[half:])), member)
     else:
         own_p, own_t, own_m = pack(front, [pivot_ranges, tail_ranges, middle_ranges])
         sets = tuple(((lax.all_gather(s, "blk")[:TICKS],),) * 2 for s in (own_p, own_t, own_m))

time: 188 us -> 188 us (level)
  waiting for transfers between devices: 62.9 us -> 60.2 us
  starting transfers between devices: 82 us -> 84.3 us
    ppermute x25, waiting for transfers between devices: 62.9 us -> 60.2 us  [permute(): return lax.ppermute(value, 'blk', pairs)]
    ppermute x25, starting transfers between devices: 74.4 us -> 76.7 us  [permute(): return lax.ppermute(value, 'blk', pairs)]
  transfers between devices with their start and end apart: 27 -> 27, of which waited for: 12 -> 11; matrix products, arithmetic and copies ran while one was open for 3% -> 3% of each run, Pallas kernels for 15% -> 15%
where the time goes in v11:
time: 188 us; the launch traced here: 187 us
  starting transfers between devices  84.3 us (45%)
  waiting for transfers between devices  60.2 us (32%)
  Pallas kernels  32.8 us (17%)
  local copies, waits for them, and re-layouts  5.09 us (3%)
  other arithmetic  3.45 us (2%)
    ppermute x25, starting transfers between devices, permute(): return lax.ppermute(value, 'blk', pairs)  76.7 us
    ppermute x25, waiting for transfers between devices, permute(): return lax.ppermute(value, 'blk', pairs)  60.2 us
    pallas_call x1, Pallas kernels, pivot_rows(): pl.pallas_call(functools.partial(pivot_kernel, counts, width), name='pivo...  12.9 us
    pallas_call x2, Pallas kernels, other_rows(): pl.pallas_call(functools.partial(other_kernel, counts, chunks, bool(group...  12.3 us
    pallas_call x2, Pallas kernels, pack(): pl.pallas_call(functools.partial(pack_kernel, pieces), out_shape=tuple((j...  4.58 us
    all_to_all x1, starting transfers between devices, local(): lax.all_to_all(outgoing, 'front', split_axis=0, concat_axis=0, tiled=True)  3.98 us
  transfers between devices with their start and end apart: 27, of which 11 were waited for; matrix products, arithmetic and copies ran while one was open for 3% of the time, Pallas kernels for 15%

profile of v11, /device:TPU:22, one launch (start us, length us, event | category | flops | bytes accessed | tf_op | source)
XLA Modules:
  0.0 186.9 jit_solution(15980429152531482778)
XLA Ops:
  0.6 2.2 %shard_map.59 = bf16[1280,256]{1,0:T(8,128)(2,1)} custom-call(f32[3072,384]{1,0:T(8,128)} %front.9), custom_call_target="tpu_custom_call" | custom-call | tf_op jit(solution)/shard_map/pallas_call | solution.py:142
  6.6 2.4 %shard_map.60 = (bf16[768,256]{1,0:T(8,128)(2,1)}, bf16[1024,256]{1,0:T(8,128)(2,1)}) custom-call(f32[3072,384]{1,0:T(8,128)} %front.9), custom_call_target="tpu_custom_call" | custom-call | tf_op jit(solution)/shard_map/pallas_call | solution.py:142
  13.3 4.5 %collective-permute-done.4 = bf16[640,256]{1,0:T(8,128)(2,1)S(1)} collective-permute-done((bf16[640,256]{1,0:T(8,128)(2,1)S(1)}, bf16[640,256]{1,0:T(8,128)(2,1)S(1)}, u32[]{:S(2)}, u32[]{:S(2)}) %collective-permute-start.4) | collective-permute-done | bytes 327712 | tf_op jit(solution)/shard_map/ppermute | solution.py:24
  19.1 4.6 %collective-permute-done = bf16[1280,256]{1,0:T(8,128)(2,1)S(1)} collective-permute-done((bf16[1280,256]{1,0:T(8,128)(2,1)}, bf16[1280,256]{1,0:T(8,128)(2,1)S(1)}, u32[]{:S(2)}, u32[]{:S(2)}) %collective-permute-start) | collective-permute-done | bytes 655392 | tf_op jit(solution)/shard_map/ppermute | solution.py:24
  25.3 33.3 %collective-permute-start.7 = (bf16[640,256]{1,0:T(8,128)(2,1)S(1)}, bf16[640,256]{1,0:T(8,128)(2,1)S(1)}, u32[]{:S(2)}, u32[]{:S(2)}) collective-permute-start(bf16[640,256]{1,0:T(8,128)(2,1)S(1)} %slice_select_fusion), channel_id=1, source_target_pairs={{4,2},{5,3},{12,10},{13,11},{20,18},{21,19},{28,26},{29,27}} | collective-permute-start | bytes 983048 | tf_op jit(solution)/shard_map/ppermute | solution.py:24
  58.6 7.5 %collective-permute-start.1 = (bf16[1280,256]{1,0:T(8,128)(2,1)S(1)}, bf16[1280,256]{1,0:T(8,128)(2,1)S(1)}, u32[]{:S(2)}, u32[]{:S(2)}) collective-permute-start(bf16[1280,256]{1,0:T(8,128)(2,1)S(1)} %broadcast_select_fusion.rest_0_), channel_id=1, source_target_pairs={{0,2},{1,3},{2,0},{3,1},{4,6},{5,7},{6,4},{7,5},{8,10},{9,11},{10,... | collective-permute-start | bytes 1966088 | tf_op jit(solution)/shard_map/ppermute | solution.py:24
  67.2 1.6 collective-permute-start.14
  70.9 6.5 %collective-permute-start.10 = (bf16[768,256]{1,0:T(8,128)(2,1)S(1)}, bf16[768,256]{1,0:T(8,128)(2,1)}, u32[]{:S(2)}, u32[]{:S(2)}) collective-permute-start(bf16[768,256]{1,0:T(8,128)(2,1)S(1)} %broadcast_select_fusion.4.rest_0_), channel_id=1, source_target_pairs={{0,2},{1,3},{2,0},{3,1},{4,6},{5,7},{6,4},{7,5},{8,10},{9,11},{10,... | collective-permute-start | bytes 1179656 | tf_op jit(solution)/shard_map/ppermute | solution.py:24
  79.0 9.9 %collective-permute-done.1.rest_1_ = bf16[1280,256]{1,0:T(8,128)(2,1)S(1)} collective-permute-done((bf16[1280,256]{1,0:T(8,128)(2,1)S(1)}, bf16[1280,256]{1,0:T(8,128)(2,1)S(1)}, u32[]{:S(2)}, u32[]{:S(2)}) %collective-permute-start.1) | collective-permute-done | bytes 655392 | tf_op jit(solution)/shard_map/ppermute | solution.py:24
  90.8 6.5 %collective-permute-done.10.rest_1_ = bf16[768,256]{1,0:T(8,128)(2,1)} collective-permute-done((bf16[768,256]{1,0:T(8,128)(2,1)S(1)}, bf16[768,256]{1,0:T(8,128)(2,1)}, u32[]{:S(2)}, u32[]{:S(2)}) %collective-permute-start.10) | collective-permute-done | bytes 393248 | tf_op jit(solution)/shard_map/ppermute | solution.py:24
  97.3 5.2 %collective-permute-start.16 = (bf16[768,256]{1,0:T(8,128)(2,1)S(1)}, bf16[768,256]{1,0:T(8,128)(2,1)}, u32[]{:S(2)}, u32[]{:S(2)}) collective-permute-start(bf16[768,256]{1,0:T(8,128)(2,1)S(1)} %broadcast_select_fusion.3.rest_6_), channel_id=1, source_target_pairs={{4,6},{5,7},{12,14},{13,15},{20,22},{21,23},{28,30},{29,31}} | collective-permute-start | bytes 1179656 | tf_op jit(solution)/shard_map/ppermute | solution.py:24
  104.7 4.2 %collective-permute-done.3.rest_3_ = bf16[1280,256]{1,0:T(8,128)(2,1)S(1)} collective-permute-done((bf16[1280,256]{1,0:T(8,128)(2,1)S(1)}, bf16[1280,256]{1,0:T(8,128)(2,1)S(1)}, u32[]{:S(2)}, u32[]{:S(2)}) %collective-permute-start.3) | collective-permute-done | bytes 655392 | tf_op jit(solution)/shard_map/ppermute | solution.py:24
  110.6 3.6 %all-to-all-start = ((s32[4,1,2]{2,1,0:T(1,128)}), s32[4,1,2]{2,1,0:T(1,128)S(1)}, u32[]{:S(2)}, u32[]{:S(2)}) async-start(s32[4,1,2]{2,1,0:T(1,128)} %copy.11), calls=%async_computation | async-start | bytes 4096 | tf_op jit(solution)/shard_map/all_to_all | solution.py:378
  114.2 12.9 %pivot_rows.1 = (f32[3072,384]{1,0:T(8,128)}, bf16[1280,384]{1,0:T(8,128)(2,1)}) custom-call(s32[1]{0:T(128)} %bitcast.member_ref, f32[3072,384]{1,0:T(8,128)} %front.9, bf16[1280,256]{1,0:T(8,128)(2,1)} %copy-done.2, bf16[1280,256]{1,0:T(8,128)(2,1)} %copy-done.9, bf16[1280,256]{1,0:T(8,128)(2,1)} %copy-done.10, bf16[1280,256]{1,0:T(8,128)(2,1)} %copy-done.11, ...), custom_call_target="tpu_custom_call" | custom-call | tf_op jit(solution)/shard_map/pivot_rows/pallas_call | solution.py:263
  128.7 6.8 %collective-permute-done.12.rest_3_ = bf16[768,256]{1,0:T(8,128)(2,1)} collective-permute-done((bf16[768,256]{1,0:T(8,128)(2,1)}, bf16[768,256]{1,0:T(8,128)(2,1)}, u32[]{:S(2)}, u32[]{:S(2)}) %collective-permute-start.12) | collective-permute-done | bytes 393248 | tf_op jit(solution)/shard_map/ppermute | solution.py:24
  135.5 6.2 %tail_rows.1 = (f32[3072,384]{1,0:T(8,128)}, bf16[4,2,128,384]{3,2,1,0:T(8,128)(2,1)}) custom-call(s32[1]{0:T(128)} %bitcast.member_ref, s32[6]{0:T(128)} %bitcast.8, s32[6]{0:T(128)} %copy-done.19, bf16[1280,384]{1,0:T(8,128)(2,1)} %get-tuple-element.8.w, f32[3072,384]{1,0:T(8,128)} %front.9, ...), custom_call_target="tpu_custom_call", output_to_operand_aliasing={{0}: (5, {})} | custom-call | tf_op jit(solution)/shard_map/tail_rows/pallas_call | solution.py:351
  141.8 4.0 %all-to-all-start.1 = ((bf16[4,2,128,384]{3,2,1,0:T(8,128)(2,1)}), bf16[4,2,128,384]{3,2,1,0:T(8,128)(2,1)S(1)}, u32[]{:S(2)}, u32[]{:S(2)}) async-start(bf16[4,2,128,384]{3,2,1,0:T(8,128)(2,1)} %get-tuple-element.13), calls=%async_computation.1 | async-start | bytes 1572864 | tf_op jit(solution)/shard_map/all_to_all | solution.py:433
  149.5 2.1 %collective-permute-start.24 = (bf16[1024,256]{1,0:T(8,128)(2,1)S(1)}, bf16[1024,256]{1,0:T(8,128)(2,1)}, u32[]{:S(2)}, u32[]{:S(2)}) collective-permute-start(bf16[1024,256]{1,0:T(8,128)(2,1)S(1)} %broadcast_select_fusion.1.rest_6_), channel_id=1, source_target_pairs={{4,6},{5,7},{12,14},{13,15},{20,22},{21,23},{28,30},{29,31}} | collective-permute-start | bytes 1572872 | tf_op jit(solution)/shard_map/ppermute | solution.py:24
  151.6 2.0 %collective-permute-start.20 = (bf16[1024,256]{1,0:T(8,128)(2,1)S(1)}, bf16[1024,256]{1,0:T(8,128)(2,1)}, u32[]{:S(2)}, u32[]{:S(2)}) collective-permute-start(bf16[1024,256]{1,0:T(8,128)(2,1)S(1)} %collective-permute-done.18.rest_1_), channel_id=1, source_target_pairs={{0,1},{1,0},{2,3},{3,2},{4,5},{5,4},{6,7},{7,6},{8,9},{9,8},{10,11... | collective-permute-start | bytes 1572872 | tf_op jit(solution)/shard_map/ppermute | solution.py:24
  155.6 4.9 %collective-permute-done.22.rest_4_ = bf16[1024,256]{1,0:T(8,128)(2,1)S(1)} collective-permute-done((bf16[1024,256]{1,0:T(8,128)(2,1)S(1)}, bf16[1024,256]{1,0:T(8,128)(2,1)S(1)}, u32[]{:S(2)}, u32[]{:S(2)}) %collective-permute-start.22) | collective-permute-done | bytes 524320 | tf_op jit(solution)/shard_map/ppermute | solution.py:24
  160.5 10.7 %collective-permute-done.23.rest_5_ = bf16[1024,256]{1,0:T(8,128)(2,1)S(1)} collective-permute-done((bf16[1024,256]{1,0:T(8,128)(2,1)S(1)}, bf16[1024,256]{1,0:T(8,128)(2,1)S(1)}, u32[]{:S(2)}, u32[]{:S(2)}) %collective-permute-start.23) | collective-permute-done | bytes 524320 | tf_op jit(solution)/shard_map/ppermute | solution.py:24
  171.1 5.8 %collective-permute-done.20.rest_3_ = bf16[1024,256]{1,0:T(8,128)(2,1)} collective-permute-done((bf16[1024,256]{1,0:T(8,128)(2,1)S(1)}, bf16[1024,256]{1,0:T(8,128)(2,1)}, u32[]{:S(2)}, u32[]{:S(2)}) %collective-permute-start.20) | collective-permute-done | bytes 524320 | tf_op jit(solution)/shard_map/ppermute | solution.py:24
  176.9 6.0 %middle_rows.1 = f32[3072,384]{1,0:T(8,128)} custom-call(s32[1]{0:T(128)} %bitcast.member_ref, s32[6]{0:T(128)} %bitcast.9, s32[6]{0:T(128)} %copy-done.19, bf16[1280,384]{1,0:T(8,128)(2,1)} %get-tuple-element.8.w, f32[3072,384]{1,0:T(8,128)} %front.9, f32[3072,384]{1,0:T(8,128)} %get-tuple-element.11.out_in, ...), custom_call_target="tpu_custom_call", output_to_operand_aliasing={{}: (5, {})} | custom-call | tf_op jit(solution)/shard_map/middle_rows/pallas_call | solution.py:351
  183.9 3.0 %add_blocks.1 = f32[1024,384]{1,0:T(8,128)} custom-call(s32[8]{0:T(128)} %reshape.81.address_ref, bf16[8,128,384]{2,1,0:T(8,128)(2,1)} %bitcast.7, f32[1024,384]{1,0:T(8,128)} %base.1), custom_call_target="tpu_custom_call" | custom-call | tf_op jit(solution)/shard_map/add_blocks/pallas_call | solution.py:395
  (96 shorter events, 29.4 us)
Async XLA Ops:
  2.8 20.8 %collective-permute-start = (bf16[1280,256]{1,0:T(8,128)(2,1)}, bf16[1280,256]{1,0:T(8,128)(2,1)S(1)}, u32[]{:S(2)}, u32[]{:S(2)}) collective-permute-start(bf16[1280,256]{1,0:T(8,128)(2,1)} %shard_map.59), channel_id=1, source_target_pairs={{0,4},{1,5},{2,6},{3,7},{8,12},{9,13},{10,14},{11,15},{16,20},{17,... | collective-permute-start | bytes 1966088 | tf_op jit(solution)/shard_map/ppermute | solution.py:24
  9.0 49.6 %collective-permute-start.9 = (bf16[768,256]{1,0:T(8,128)(2,1)}, bf16[768,256]{1,0:T(8,128)(2,1)S(1)}, u32[]{:S(2)}, u32[]{:S(2)}) collective-permute-start(bf16[768,256]{1,0:T(8,128)(2,1)} %get-tuple-element.10), channel_id=1, source_target_pairs={{0,4},{1,5},{2,6},{3,7},{8,12},{9,13},{10,14},{11,15},{16,20},{17,... | collective-permute-start | bytes 1179656 | tf_op jit(solution)/shard_map/ppermute | solution.py:24
  10.4 14.8 %collective-permute-start.13 = (bf16[768,256]{1,0:T(8,128)(2,1)}, bf16[768,256]{1,0:T(8,128)(2,1)}, u32[]{:S(2)}, u32[]{:S(2)}) collective-permute-start(bf16[768,256]{1,0:T(8,128)(2,1)} %get-tuple-element.10), channel_id=1, source_target_pairs={{4,5},{12,13},{20,21},{28,29}} | collective-permute-start | bytes 1179656 | tf_op jit(solution)/shard_map/ppermute | solution.py:24
  11.7 59.1 %collective-permute-start.17 = (bf16[1024,256]{1,0:T(8,128)(2,1)}, bf16[1024,256]{1,0:T(8,128)(2,1)S(1)}, u32[]{:S(2)}, u32[]{:S(2)}) collective-permute-start(bf16[1024,256]{1,0:T(8,128)(2,1)} %get-tuple-element.12), channel_id=1, source_target_pairs={{0,4},{1,5},{2,6},{3,7},{8,12},{9,13},{10,14},{11,15},{16,20},{17,... | collective-permute-start | bytes 1572872 | tf_op jit(solution)/shard_map/ppermute | solution.py:24
  17.8 49.4 %collective-permute-start.5 = (bf16[640,256]{1,0:T(8,128)(2,1)S(1)}, bf16[640,256]{1,0:T(8,128)(2,1)S(1)}, u32[]{:S(2)}, u32[]{:S(2)}) collective-permute-start(bf16[640,256]{1,0:T(8,128)(2,1)S(1)} %slice_select_fusion), channel_id=1, source_target_pairs={{4,6},{5,7},{12,14},{13,15},{20,22},{21,23},{28,30},{29,31}} | collective-permute-start | bytes 983048 | tf_op jit(solution)/shard_map/ppermute | solution.py:24
  23.7 45.2 %collective-permute-start.6 = (bf16[640,256]{1,0:T(8,128)(2,1)S(1)}, bf16[640,256]{1,0:T(8,128)(2,1)S(1)}, u32[]{:S(2)}, u32[]{:S(2)}) collective-permute-start(bf16[640,256]{1,0:T(8,128)(2,1)S(1)} %slice_select_fusion), channel_id=1, source_target_pairs={{4,0},{5,1},{12,8},{13,9},{20,16},{21,17},{28,24},{29,25}} | collective-permute-start | bytes 983048 | tf_op jit(solution)/shard_map/ppermute | solution.py:24
  25.3 44.9 %collective-permute-start.7 = (bf16[640,256]{1,0:T(8,128)(2,1)S(1)}, bf16[640,256]{1,0:T(8,128)(2,1)S(1)}, u32[]{:S(2)}, u32[]{:S(2)}) collective-permute-start(bf16[640,256]{1,0:T(8,128)(2,1)S(1)} %slice_select_fusion), channel_id=1, source_target_pairs={{4,2},{5,3},{12,10},{13,11},{20,18},{21,19},{28,26},{29,27}} | collective-permute-start | bytes 983048 | tf_op jit(solution)/shard_map/ppermute | solution.py:24
  58.6 30.3 %collective-permute-start.1 = (bf16[1280,256]{1,0:T(8,128)(2,1)S(1)}, bf16[1280,256]{1,0:T(8,128)(2,1)S(1)}, u32[]{:S(2)}, u32[]{:S(2)}) collective-permute-start(bf16[1280,256]{1,0:T(8,128)(2,1)S(1)} %broadcast_select_fusion.rest_0_), channel_id=1, source_target_pairs={{0,2},{1,3},{2,0},{3,1},{4,6},{5,7},{6,4},{7,5},{8,10},{9,11},{10,... | collective-permute-start | bytes 1966088 | tf_op jit(solution)/shard_map/ppermute | solution.py:24
  68.9 20.6 %collective-permute-start.15 = (bf16[768,256]{1,0:T(8,128)(2,1)S(1)}, bf16[768,256]{1,0:T(8,128)(2,1)S(1)}, u32[]{:S(2)}, u32[]{:S(2)}) collective-permute-start(bf16[768,256]{1,0:T(8,128)(2,1)S(1)} %broadcast_select_fusion.3.rest_6_), channel_id=1, source_target_pairs={{4,2},{5,3},{12,10},{13,11},{20,18},{21,19},{28,26},{29,27}} | collective-permute-start | bytes 1179656 | tf_op jit(solution)/shard_map/ppermute | solution.py:24
  70.2 32.9 %collective-permute-start.2 = (bf16[1280,256]{1,0:T(8,128)(2,1)S(1)}, bf16[1280,256]{1,0:T(8,128)(2,1)S(1)}, u32[]{:S(2)}, u32[]{:S(2)}) collective-permute-start(bf16[1280,256]{1,0:T(8,128)(2,1)S(1)} %broadcast_select_fusion.rest_0_), channel_id=1, source_target_pairs={{0,1},{1,0},{2,3},{3,2},{4,5},{5,4},{6,7},{7,6},{8,9},{9,8},{10,11... | collective-permute-start | bytes 1966088 | tf_op jit(solution)/shard_map/ppermute | solution.py:24
  70.9 26.4 %collective-permute-start.10 = (bf16[768,256]{1,0:T(8,128)(2,1)S(1)}, bf16[768,256]{1,0:T(8,128)(2,1)}, u32[]{:S(2)}, u32[]{:S(2)}) collective-permute-start(bf16[768,256]{1,0:T(8,128)(2,1)S(1)} %broadcast_select_fusion.4.rest_0_), channel_id=1, source_target_pairs={{0,2},{1,3},{2,0},{3,1},{4,6},{5,7},{6,4},{7,5},{8,10},{9,11},{10,... | collective-permute-start | bytes 1179656 | tf_op jit(solution)/shard_map/ppermute | solution.py:24
  78.2 24.3 %collective-permute-start.8 = (bf16[640,256]{1,0:T(8,128)(2,1)S(1)}, bf16[640,256]{1,0:T(8,128)(2,1)S(1)}, u32[]{:S(2)}, u32[]{:S(2)}) collective-permute-start(bf16[640,256]{1,0:T(8,128)(2,1)S(1)} %select_select_fusion.rest_4_), channel_id=1, source_target_pairs={{0,1},{1,0},{2,3},{3,2},{4,5},{5,4},{6,7},{7,6},{8,9},{9,8},{10,11... | collective-permute-start | bytes 983048 | tf_op jit(solution)/shard_map/ppermute | solution.py:24
  88.9 20.0 %collective-permute-start.3 = (bf16[1280,256]{1,0:T(8,128)(2,1)S(1)}, bf16[1280,256]{1,0:T(8,128)(2,1)S(1)}, u32[]{:S(2)}, u32[]{:S(2)}) collective-permute-start(bf16[1280,256]{1,0:T(8,128)(2,1)S(1)} %collective-permute-done.1.rest_1_), channel_id=1, source_target_pairs={{0,1},{1,0},{2,3},{3,2},{4,5},{5,4},{6,7},{7,6},{8,9},{9,8},{10,11... | collective-permute-start | bytes 1966088 | tf_op jit(solution)/shard_map/ppermute | solution.py:24
  89.5 56.2 %collective-permute-start.21 = (bf16[1024,256]{1,0:T(8,128)(2,1)S(1)}, bf16[1024,256]{1,0:T(8,128)(2,1)}, u32[]{:S(2)}, u32[]{:S(2)}) collective-permute-start(bf16[1024,256]{1,0:T(8,128)(2,1)S(1)} %copy-done.5), channel_id=1, source_target_pairs={{4,5},{12,13},{20,21},{28,29}} | collective-permute-start | bytes 1572872 | tf_op jit(solution)/shard_map/ppermute | solution.py:24
  97.3 29.9 %collective-permute-start.16 = (bf16[768,256]{1,0:T(8,128)(2,1)S(1)}, bf16[768,256]{1,0:T(8,128)(2,1)}, u32[]{:S(2)}, u32[]{:S(2)}) collective-permute-start(bf16[768,256]{1,0:T(8,128)(2,1)S(1)} %broadcast_select_fusion.3.rest_6_), channel_id=1, source_target_pairs={{4,6},{5,7},{12,14},{13,15},{20,22},{21,23},{28,30},{29,31}} | collective-permute-start | bytes 1179656 | tf_op jit(solution)/shard_map/ppermute | solution.py:24
  102.5 26.2 %collective-permute-start.11 = (bf16[768,256]{1,0:T(8,128)(2,1)S(1)}, bf16[768,256]{1,0:T(8,128)(2,1)}, u32[]{:S(2)}, u32[]{:S(2)}) collective-permute-start(bf16[768,256]{1,0:T(8,128)(2,1)S(1)} %broadcast_select_fusion.4.rest_0_), channel_id=1, source_target_pairs={{0,1},{1,0},{2,3},{3,2},{4,5},{5,4},{6,7},{7,6},{8,9},{9,8},{10,11... | collective-permute-start | bytes 1179656 | tf_op jit(solution)/shard_map/ppermute | solution.py:24
  103.2 32.3 %collective-permute-start.12 = (bf16[768,256]{1,0:T(8,128)(2,1)}, bf16[768,256]{1,0:T(8,128)(2,1)}, u32[]{:S(2)}, u32[]{:S(2)}) collective-permute-start(bf16[768,256]{1,0:T(8,128)(2,1)} %collective-permute-done.10.rest_1_), channel_id=1, source_target_pairs={{0,1},{1,0},{2,3},{3,2},{4,5},{5,4},{6,7},{7,6},{8,9},{9,8},{10,11... | collective-permute-start | bytes 1179656 | tf_op jit(solution)/shard_map/ppermute | solution.py:24
  108.9 42.7 %collective-permute-start.18 = (bf16[1024,256]{1,0:T(8,128)(2,1)S(1)}, bf16[1024,256]{1,0:T(8,128)(2,1)S(1)}, u32[]{:S(2)}, u32[]{:S(2)}) collective-permute-start(bf16[1024,256]{1,0:T(8,128)(2,1)S(1)} %broadcast_select_fusion.2.rest_0_), channel_id=1, source_target_pairs={{0,2},{1,3},{2,0},{3,1},{4,6},{5,7},{6,4},{7,5},{8,10},{9,11},{10,... | collective-permute-start | bytes 1572872 | tf_op jit(solution)/shard_map/ppermute | solution.py:24
  110.6 31.2 %all-to-all-start = ((s32[4,1,2]{2,1,0:T(1,128)}), s32[4,1,2]{2,1,0:T(1,128)S(1)}, u32[]{:S(2)}, u32[]{:S(2)}) async-start(s32[4,1,2]{2,1,0:T(1,128)} %copy.11), calls=%async_computation | async-start | bytes 4096 | tf_op jit(solution)/shard_map/all_to_all | solution.py:378
  141.8 41.2 %all-to-all-start.1 = ((bf16[4,2,128,384]{3,2,1,0:T(8,128)(2,1)}), bf16[4,2,128,384]{3,2,1,0:T(8,128)(2,1)S(1)}, u32[]{:S(2)}, u32[]{:S(2)}) async-start(bf16[4,2,128,384]{3,2,1,0:T(8,128)(2,1)} %get-tuple-element.13), calls=%async_computation.1 | async-start | bytes 1572864 | tf_op jit(solution)/shard_map/all_to_all | solution.py:433
  148.2 22.9 %collective-permute-start.23 = (bf16[1024,256]{1,0:T(8,128)(2,1)S(1)}, bf16[1024,256]{1,0:T(8,128)(2,1)S(1)}, u32[]{:S(2)}, u32[]{:S(2)}) collective-permute-start(bf16[1024,256]{1,0:T(8,128)(2,1)S(1)} %broadcast_select_fusion.1.rest_6_), channel_id=1, source_target_pairs={{4,2},{5,3},{12,10},{13,11},{20,18},{21,19},{28,26},{29,27}} | collective-permute-start | bytes 1572872 | tf_op jit(solution)/shard_map/ppermute | solution.py:24
  149.5 21.6 %collective-permute-start.24 = (bf16[1024,256]{1,0:T(8,128)(2,1)S(1)}, bf16[1024,256]{1,0:T(8,128)(2,1)}, u32[]{:S(2)}, u32[]{:S(2)}) collective-permute-start(bf16[1024,256]{1,0:T(8,128)(2,1)S(1)} %broadcast_select_fusion.1.rest_6_), channel_id=1, source_target_pairs={{4,6},{5,7},{12,14},{13,15},{20,22},{21,23},{28,30},{29,31}} | collective-permute-start | bytes 1572872 | tf_op jit(solution)/shard_map/ppermute | solution.py:24
  151.6 19.5 %collective-permute-start.19 = (bf16[1024,256]{1,0:T(8,128)(2,1)S(1)}, bf16[1024,256]{1,0:T(8,128)(2,1)}, u32[]{:S(2)}, u32[]{:S(2)}) collective-permute-start(bf16[1024,256]{1,0:T(8,128)(2,1)S(1)} %broadcast_select_fusion.2.rest_0_), channel_id=1, source_target_pairs={{0,1},{1,0},{2,3},{3,2},{4,5},{5,4},{6,7},{7,6},{8,9},{9,8},{10,11... | collective-permute-start | bytes 1572872 | tf_op jit(solution)/shard_map/ppermute | solution.py:24
  151.6 25.3 %collective-permute-start.20 = (bf16[1024,256]{1,0:T(8,128)(2,1)S(1)}, bf16[1024,256]{1,0:T(8,128)(2,1)}, u32[]{:S(2)}, u32[]{:S(2)}) collective-permute-start(bf16[1024,256]{1,0:T(8,128)(2,1)S(1)} %collective-permute-done.18.rest_1_), channel_id=1, source_target_pairs={{0,1},{1,0},{2,3},{3,2},{4,5},{5,4},{6,7},{7,6},{8,9},{9,8},{10,11... | collective-permute-start | bytes 1572872 | tf_op jit(solution)/shard_map/ppermute | solution.py:24
  (24 other events, 763.4 us)

commit v12 on v11

--- a/solution.py
+++ b/solution.py
@@ -57,12 +57,16 @@
     return ((slabs(a), halves(*e_halves)), (slabs(b), whole(b)), (slabs(c), whole(c)))
 
 
-def placed_slabs(member, refs):
+def places(member):
     x = lax.rem(member, 2)
     even = lax.rem(lax.div(member, 2), 2) == 0
     near, far = jnp.where(even, x, 2 + x), jnp.where(even, 2 + x, x)
     over, overfar = jnp.where(even, 1 - x, 3 - x), jnp.where(even, 3 - x, 1 - x)
-    return tuple(zip(refs, (near, far, over, overfar)))
+    return near, far, over, overfar
+
+
+def placed_slabs(member, refs):
+    return tuple(zip(refs, places(member)))
 
 
 def start_first(member, refs, target, sems, lo, n):
@@ -364,6 +368,115 @@
     )(member, dest, slot, w, front, out, *bufs[0], *bufs[1])
 
 
+def rows_of(slab):
+    return pl.ds(pl.multiple_of(slab * P_SIZE, P_SIZE), P_SIZE)
+
+
+def partial_kernel(n_bufs, chunks, member_ref, w, front, *rest):
+    bufs = rest[:n_bufs]
+    base, raw, sems, base_sems = rest[n_bufs:]
+    member = member_ref[0]
+    width = base.shape[1]
+    keep = (member >= TICKS) | (lax.broadcasted_iota(jnp.int32, (CHUNK, width), 1) >= P_SIZE)
+    waits = []
+    for number, (lo, n, pieces) in enumerate(chunks):
+        at = pl.ds(lo, n)
+        if n_bufs == 1:
+            slabs = tuple(range(TICKS - 2))
+            sources = [(bufs[0].at[slab], slab) for slab in slabs]
+        else:
+            sources = placed_slabs(member, bufs)
+            slabs = tuple(slab for _, slab in sources)
+        copies = [
+            pltpu.make_async_copy(ref.at[at], raw.at[slab, at], sems.at[number, i])
+            for i, (ref, slab) in enumerate(sources)
+        ]
+        copies += [
+            pltpu.make_async_copy(
+                front.at[pl.ds(src, count), :], base.at[pl.ds(dst, count), :], base_sems.at[number, i]
+            )
+            for i, (src, dst, count) in enumerate(pieces)
+        ]
+        for copy in copies:
+            copy.start()
+        waits.append(copies)
+    for number, (lo, n, pieces) in enumerate(chunks):
+        wait_all(waits[number])
+        at = pl.ds(lo, n)
+        total = jnp.where(keep[:n], base[at, :], 0.0)
+        for slab in slabs:
+            total = minus_dot(total, raw[slab, at, :], w[rows_of(slab), :])
+        base[at, :] = total
+
+
+def final_kernel(counts, chunks, gathered, member_ref, w, base, out_in, *rest):
+    firsts, lasts = rest[: counts[0]], rest[counts[0] : sum(counts)]
+    out, raw, held, sems, store_sems = rest[sum(counts) :]
+    member = member_ref[0]
+    waits = []
+    for number, (lo, n, pieces) in enumerate(chunks):
+        at = pl.ds(lo, n)
+        if gathered:
+            ref, slab = firsts[0].at[TICKS - 2], TICKS - 2
+        else:
+            ref, slab = firsts[0], places(member)[-1]
+        copy = pltpu.make_async_copy(ref.at[at], raw.at[slab, at], sems.at[number, 0])
+        copy.start()
+        waits.append([copy] + start_last(member, lasts, raw, sems.at[number, 1], lo, n))
+    stores = []
+    for number, (lo, n, pieces) in enumerate(chunks):
+        wait_all(waits[number])
+        at = pl.ds(lo, n)
+        total = base[at, :]
+        for s in (slab, TICKS - 1):
+            total = minus_dot(total, raw[s, at, :], w[rows_of(s), :])
+        held[at, :] = total
+        for i, (src, dst, count) in enumerate(pieces):
+            stores.append(
+                pltpu.make_async_copy(
+                    held.at[pl.ds(dst, count), :], out.at[pl.ds(src, count), :], store_sems.at[number, i]
+                )
+            )
+            stores[-1].start()
+    wait_all(stores)
+
+
+def middle_rows(member, w, front, out, bufs, ranges):
+    order, width = front.shape
+    rows = sum(n for _, _, n in ranges)
+    chunks = windows(ranges, rows)
+    pieces = max(len(c[2]) for c in chunks)
+    counts = tuple(len(b) for b in bufs)
+    early = bufs[0] if counts[0] == 1 else bufs[0][:-1]
+    base = pl.pallas_call(
+        functools.partial(partial_kernel, len(early), chunks),
+        name="partial_rows",
+        out_shape=jax.ShapeDtypeStruct((rows, width), jnp.float32),
+        in_specs=[SMEM, VMEM, ANY] + [ANY] * len(early),
+        out_specs=VMEM,
+        scratch_shapes=[
+            pltpu.VMEM((TICKS, rows, P_SIZE), jnp.bfloat16),
+            pltpu.SemaphoreType.DMA((len(chunks), TICKS)),
+            pltpu.SemaphoreType.DMA((len(chunks), pieces)),
+        ],
+    )(member, w, front, *early)
+    late = bufs[0] if counts[0] == 1 else bufs[0][-1:]
+    return pl.pallas_call(
+        functools.partial(final_kernel, (len(late), counts[1]), chunks, counts[0] == 1),
+        name="middle_rows",
+        out_shape=jax.ShapeDtypeStruct((order, width), jnp.float32),
+        in_specs=[SMEM, VMEM, VMEM, ANY] + [ANY] * (len(late) + counts[1]),
+        out_specs=ANY,
+        input_output_aliases={3: 0},
+        scratch_shapes=[
+            pltpu.VMEM((TICKS, rows, P_SIZE), jnp.bfloat16),
+            pltpu.VMEM((rows, width), jnp.float32),
+            pltpu.SemaphoreType.DMA((len(chunks), 2)),
+            pltpu.SemaphoreType.DMA((len(chunks), pieces)),
+        ],
+    )(member, w, base, out, *late, *bufs[1])
+
+
 def routes(parent_group, row_block):
     groups = lax.axis_size("front")
     dest = parent_group.reshape(NB)
@@ -431,7 +544,7 @@
         holder, dest, slot, w, front, out, sets[1], [(tail_at, 0, tail_n)], lax.axis_size("front")
     )
     incoming = lax.all_to_all(outgoing, "front", split_axis=0, concat_axis=0, tiled=True)
-    (factored,) = other_rows(holder, dest, slot, w, front, out, sets[2], middle)
+    factored = middle_rows(holder, w, front, out, sets[2], middle)
     assembled = add_blocks(address, incoming, parent_base)
     return (factored, assembled)
 

time: 188 us -> 184 us (0.979)
  the two profiles are of different devices: /device:TPU:22 before, /device:TPU:14 now
where the time goes in v12:
time: 184 us
  waiting for transfers between devices  102 us (55%)
  Pallas kernels  36.9 us (20%)
  starting transfers between devices  35.8 us (19%)
  local copies, waits for them, and re-layouts  4.72 us (3%)
  other arithmetic  3.38 us (2%)
    ppermute x25, waiting for transfers between devices, permute(): return lax.ppermute(value, 'blk', pairs)  102 us
    ppermute x25, starting transfers between devices, permute(): return lax.ppermute(value, 'blk', pairs)  28.4 us
    pallas_call x1, Pallas kernels, pivot_rows(): pl.pallas_call(functools.partial(pivot_kernel, counts, width), name='pivo...  12.9 us
    pallas_call x1, Pallas kernels, other_rows(): pl.pallas_call(functools.partial(other_kernel, counts, chunks, bool(group...  6.21 us
    pallas_call x1, Pallas kernels, middle_rows(): pl.pallas_call(functools.partial(partial_kernel, len(early), chunks), nam...  5.42 us
    pallas_call x1, Pallas kernels, middle_rows(): pl.pallas_call(functools.partial(final_kernel, (len(late), counts[1]), ch...  4.78 us
    pallas_call x2, Pallas kernels, pack(): pl.pallas_call(functools.partial(pack_kernel, pieces), out_shape=tuple((j...  4.58 us
    all_to_all x1, starting transfers between devices, local(): lax.all_to_all(outgoing, 'front', split_axis=0, concat_axis=0, tiled=True)  3.72 us
  transfers between devices with their start and end apart: 27, of which 7 were waited for; matrix products, arithmetic and copies ran while one was open for 3% of the time, Pallas kernels for 17%

profile of v12, /device:TPU:14, one launch (start us, length us, event | category | flops | bytes accessed | tf_op | source)
XLA Modules:
  0.0 183.6 jit_solution(10215132718646984932)
XLA Ops:
  0.6 2.2 %shard_map.59 = bf16[1280,256]{1,0:T(8,128)(2,1)} custom-call(f32[3072,384]{1,0:T(8,128)} %front.9), custom_call_target="tpu_custom_call" | custom-call | tf_op jit(solution)/shard_map/pallas_call | solution.py:146
  2.8 4.7 %collective-permute-start = (bf16[1280,256]{1,0:T(8,128)(2,1)}, bf16[1280,256]{1,0:T(8,128)(2,1)S(1)}, u32[]{:S(2)}, u32[]{:S(2)}) collective-permute-start(bf16[1280,256]{1,0:T(8,128)(2,1)} %shard_map.59), channel_id=1, source_target_pairs={{0,4},{1,5},{2,6},{3,7},{8,12},{9,13},{10,14},{11,15},{16,20},{17,... | collective-permute-start | bytes 1966088 | tf_op jit(solution)/shard_map/ppermute | solution.py:24
  9.2 2.4 %shard_map.60 = (bf16[768,256]{1,0:T(8,128)(2,1)}, bf16[1024,256]{1,0:T(8,128)(2,1)}) custom-call(f32[3072,384]{1,0:T(8,128)} %front.9), custom_call_target="tpu_custom_call" | custom-call | tf_op jit(solution)/shard_map/pallas_call | solution.py:146
  11.6 1.4 collective-permute-start.12
  13.8 2.1 %collective-permute-start.9 = (bf16[1024,256]{1,0:T(8,128)(2,1)}, bf16[1024,256]{1,0:T(8,128)(2,1)}, u32[]{:S(2)}, u32[]{:S(2)}) collective-permute-start(bf16[1024,256]{1,0:T(8,128)(2,1)} %get-tuple-element.9), channel_id=1, source_target_pairs={{0,4},{1,5},{2,6},{3,7},{8,12},{9,13},{10,14},{11,15},{16,20},{17,... | collective-permute-start | bytes 1572872 | tf_op jit(solution)/shard_map/ppermute | solution.py:24
  16.8 38.6 %collective-permute-done = bf16[1280,256]{1,0:T(8,128)(2,1)S(1)} collective-permute-done((bf16[1280,256]{1,0:T(8,128)(2,1)}, bf16[1280,256]{1,0:T(8,128)(2,1)S(1)}, u32[]{:S(2)}, u32[]{:S(2)}) %collective-permute-start) | collective-permute-done | bytes 655392 | tf_op jit(solution)/shard_map/ppermute | solution.py:24
  57.5 6.3 %collective-permute-done.12 = bf16[768,256]{1,0:T(8,128)(2,1)S(1)} collective-permute-done((bf16[768,256]{1,0:T(8,128)(2,1)}, bf16[768,256]{1,0:T(8,128)(2,1)S(1)}, u32[]{:S(2)}, u32[]{:S(2)}) %collective-permute-start.12) | collective-permute-done | bytes 393248 | tf_op jit(solution)/shard_map/ppermute | solution.py:24
  68.7 6.4 %collective-permute-done.9 = bf16[1024,256]{1,0:T(8,128)(2,1)} collective-permute-done((bf16[1024,256]{1,0:T(8,128)(2,1)}, bf16[1024,256]{1,0:T(8,128)(2,1)}, u32[]{:S(2)}, u32[]{:S(2)}) %collective-permute-start.9) | collective-permute-done | bytes 524320 | tf_op jit(solution)/shard_map/ppermute | solution.py:24
  75.8 11.6 %collective-permute-done.1.rest_1_ = bf16[1280,256]{1,0:T(8,128)(2,1)S(1)} collective-permute-done((bf16[1280,256]{1,0:T(8,128)(2,1)S(1)}, bf16[1280,256]{1,0:T(8,128)(2,1)S(1)}, u32[]{:S(2)}, u32[]{:S(2)}) %collective-permute-start.1) | collective-permute-done | bytes 655392 | tf_op jit(solution)/shard_map/ppermute | solution.py:24
  88.0 1.5 collective-permute-start.21
  89.5 5.6 %collective-permute-done.13.rest_1_ = bf16[768,256]{1,0:T(8,128)(2,1)} collective-permute-done((bf16[768,256]{1,0:T(8,128)(2,1)S(1)}, bf16[768,256]{1,0:T(8,128)(2,1)}, u32[]{:S(2)}, u32[]{:S(2)}) %collective-permute-start.13) | collective-permute-done | bytes 393248 | tf_op jit(solution)/shard_map/ppermute | solution.py:24
  97.0 1.5 collective-permute-start.15
  98.6 8.1 %collective-permute-done.3.rest_3_ = bf16[1280,256]{1,0:T(8,128)(2,1)S(1)} collective-permute-done((bf16[1280,256]{1,0:T(8,128)(2,1)S(1)}, bf16[1280,256]{1,0:T(8,128)(2,1)S(1)}, u32[]{:S(2)}, u32[]{:S(2)}) %collective-permute-start.3) | collective-permute-done | bytes 655392 | tf_op jit(solution)/shard_map/ppermute | solution.py:24
  106.7 2.0 %collective-permute-start.10 = (bf16[1024,256]{1,0:T(8,128)(2,1)S(1)}, bf16[1024,256]{1,0:T(8,128)(2,1)}, u32[]{:S(2)}, u32[]{:S(2)}) collective-permute-start(bf16[1024,256]{1,0:T(8,128)(2,1)S(1)} %broadcast_select_fusion.2.rest_0_), channel_id=1, source_target_pairs={{0,2},{1,3},{2,0},{3,1},{4,6},{5,7},{6,4},{7,5},{8,10},{9,11},{10,... | collective-permute-start | bytes 1572872 | tf_op jit(solution)/shard_map/ppermute | solution.py:24
  109.6 3.7 %all-to-all-start = ((s32[4,1,2]{2,1,0:T(1,128)}), s32[4,1,2]{2,1,0:T(1,128)S(1)}, u32[]{:S(2)}, u32[]{:S(2)}) async-start(s32[4,1,2]{2,1,0:T(1,128)} %copy.11), calls=%async_computation | async-start | bytes 4096 | tf_op jit(solution)/shard_map/all_to_all | solution.py:491
  113.3 12.9 %pivot_rows.1 = (f32[3072,384]{1,0:T(8,128)}, bf16[1280,384]{1,0:T(8,128)(2,1)}) custom-call(s32[1]{0:T(128)} %bitcast.member_ref, f32[3072,384]{1,0:T(8,128)} %front.9, bf16[1280,256]{1,0:T(8,128)(2,1)} %copy-done.2, bf16[1280,256]{1,0:T(8,128)(2,1)} %copy-done.9, bf16[1280,256]{1,0:T(8,128)(2,1)} %copy-done.10, bf16[1280,256]{1,0:T(8,128)(2,1)} %copy-done.11, ...), custom_call_target="tpu_custom_call" | custom-call | tf_op jit(solution)/shard_map/pivot_rows/pallas_call | solution.py:267
  126.7 6.2 %tail_rows.1 = (f32[3072,384]{1,0:T(8,128)}, bf16[4,2,128,384]{3,2,1,0:T(8,128)(2,1)}) custom-call(s32[1]{0:T(128)} %bitcast.member_ref, s32[6]{0:T(128)} %bitcast.8, s32[6]{0:T(128)} %copy-done.18, bf16[1280,384]{1,0:T(8,128)(2,1)} %get-tuple-element.8.w, f32[3072,384]{1,0:T(8,128)} %front.9, ...), custom_call_target="tpu_custom_call", output_to_operand_aliasing={{0}: (5, {})} | custom-call | tf_op jit(solution)/shard_map/tail_rows/pallas_call | solution.py:355
  132.9 3.7 %all-to-all-start.1 = ((bf16[4,2,128,384]{3,2,1,0:T(8,128)(2,1)}), bf16[4,2,128,384]{3,2,1,0:T(8,128)(2,1)S(1)}, u32[]{:S(2)}, u32[]{:S(2)}) async-start(bf16[4,2,128,384]{3,2,1,0:T(8,128)(2,1)} %get-tuple-element.13), calls=%async_computation.1 | async-start | bytes 1572864 | tf_op jit(solution)/shard_map/all_to_all | solution.py:546
  138.7 1.5 collective-permute-start.24
  140.2 1.7 collective-permute-start.20
  144.5 5.4 %partial_rows.1.base = f32[1024,384]{1,0:T(8,128)} custom-call(s32[1]{0:T(128)} %bitcast.member_ref, bf16[1280,384]{1,0:T(8,128)(2,1)} %get-tuple-element.8.w, f32[3072,384]{1,0:T(8,128)} %front.9, bf16[1024,256]{1,0:T(8,128)(2,1)} %copy-done.3, bf16[1024,256]{1,0:T(8,128)(2,1)} %collective-permute-done.10.rest_1_, bf16[1024,256]{1,0:T(8,128)(2,1)} %copy-done.12), custom_call_target="tpu_custom_call" | custom-call | tf_op jit(solution)/shard_map/partial_rows/pallas_call | solution.py:451
  149.9 24.9 %collective-permute-done.23.rest_2_ = bf16[1024,256]{1,0:T(8,128)(2,1)} collective-permute-done((bf16[1024,256]{1,0:T(8,128)(2,1)S(1)}, bf16[1024,256]{1,0:T(8,128)(2,1)}, u32[]{:S(2)}, u32[]{:S(2)}) %collective-permute-start.23) | collective-permute-done | bytes 524320 | tf_op jit(solution)/shard_map/ppermute | solution.py:24
  174.9 4.8 %middle_rows.1 = f32[3072,384]{1,0:T(8,128)} custom-call(s32[1]{0:T(128)} %bitcast.member_ref, bf16[1280,384]{1,0:T(8,128)(2,1)} %get-tuple-element.8.w, f32[1024,384]{1,0:T(8,128)} %partial_rows.1.base, f32[3072,384]{1,0:T(8,128)} %get-tuple-element.12.out_in, bf16[1024,256]{1,0:T(8,128)(2,1)} %collective-permute-done.20.rest_0_, ...), custom_call_target="tpu_custom_call", output_to_operand_aliasing={{}: (3, {})} | custom-call | tf_op jit(solution)/shard_map/middle_rows/pallas_call | solution.py:464
  180.6 3.0 %add_blocks.1 = f32[1024,384]{1,0:T(8,128)} custom-call(s32[8]{0:T(128)} %reshape.81.address_ref, bf16[8,128,384]{2,1,0:T(8,128)(2,1)} %bitcast.7, f32[1024,384]{1,0:T(8,128)} %base.1), custom_call_target="tpu_custom_call" | custom-call | tf_op jit(solution)/shard_map/add_blocks/pallas_call | solution.py:508
  (95 shorter events, 20.2 us)
Async XLA Ops:
  2.8 52.6 %collective-permute-start = (bf16[1280,256]{1,0:T(8,128)(2,1)}, bf16[1280,256]{1,0:T(8,128)(2,1)S(1)}, u32[]{:S(2)}, u32[]{:S(2)}) collective-permute-start(bf16[1280,256]{1,0:T(8,128)(2,1)} %shard_map.59), channel_id=1, source_target_pairs={{0,4},{1,5},{2,6},{3,7},{8,12},{9,13},{10,14},{11,15},{16,20},{17,... | collective-permute-start | bytes 1966088 | tf_op jit(solution)/shard_map/ppermute | solution.py:24
  11.6 52.2 %collective-permute-start.12 = (bf16[768,256]{1,0:T(8,128)(2,1)}, bf16[768,256]{1,0:T(8,128)(2,1)S(1)}, u32[]{:S(2)}, u32[]{:S(2)}) collective-permute-start(bf16[768,256]{1,0:T(8,128)(2,1)} %get-tuple-element.11), channel_id=1, source_target_pairs={{0,4},{1,5},{2,6},{3,7},{8,12},{9,13},{10,14},{11,15},{16,20},{17,... | collective-permute-start | bytes 1179656 | tf_op jit(solution)/shard_map/ppermute | solution.py:24
  13.1 43.1 %collective-permute-start.16 = (bf16[768,256]{1,0:T(8,128)(2,1)}, bf16[768,256]{1,0:T(8,128)(2,1)S(1)}, u32[]{:S(2)}, u32[]{:S(2)}) collective-permute-start(bf16[768,256]{1,0:T(8,128)(2,1)} %get-tuple-element.11), channel_id=1, source_target_pairs={{4,5},{12,13},{20,21},{28,29}} | collective-permute-start | bytes 1179656 | tf_op jit(solution)/shard_map/ppermute | solution.py:24
  13.8 61.3 %collective-permute-start.9 = (bf16[1024,256]{1,0:T(8,128)(2,1)}, bf16[1024,256]{1,0:T(8,128)(2,1)}, u32[]{:S(2)}, u32[]{:S(2)}) collective-permute-start(bf16[1024,256]{1,0:T(8,128)(2,1)} %get-tuple-element.9), channel_id=1, source_target_pairs={{0,4},{1,5},{2,6},{3,7},{8,12},{9,13},{10,14},{11,15},{16,20},{17,... | collective-permute-start | bytes 1572872 | tf_op jit(solution)/shard_map/ppermute | solution.py:24
  16.1 48.8 %collective-permute-start.5 = (bf16[640,256]{1,0:T(8,128)(2,1)S(1)}, bf16[640,256]{1,0:T(8,128)(2,1)S(1)}, u32[]{:S(2)}, u32[]{:S(2)}) collective-permute-start(bf16[640,256]{1,0:T(8,128)(2,1)S(1)} %slice_select_fusion), channel_id=1, source_target_pairs={{4,6},{5,7},{12,14},{13,15},{20,22},{21,23},{28,30},{29,31}} | collective-permute-start | bytes 983048 | tf_op jit(solution)/shard_map/ppermute | solution.py:24
  56.2 11.8 %collective-permute-start.7 = (bf16[640,256]{1,0:T(8,128)(2,1)S(1)}, bf16[640,256]{1,0:T(8,128)(2,1)S(1)}, u32[]{:S(2)}, u32[]{:S(2)}) collective-permute-start(bf16[640,256]{1,0:T(8,128)(2,1)S(1)} %slice_select_fusion), channel_id=1, source_target_pairs={{4,2},{5,3},{12,10},{13,11},{20,18},{21,19},{28,26},{29,27}} | collective-permute-start | bytes 983048 | tf_op jit(solution)/shard_map/ppermute | solution.py:24
  63.9 23.6 %collective-permute-start.1 = (bf16[1280,256]{1,0:T(8,128)(2,1)S(1)}, bf16[1280,256]{1,0:T(8,128)(2,1)S(1)}, u32[]{:S(2)}, u32[]{:S(2)}) collective-permute-start(bf16[1280,256]{1,0:T(8,128)(2,1)S(1)} %broadcast_select_fusion.rest_0_), channel_id=1, source_target_pairs={{0,2},{1,3},{2,0},{3,1},{4,6},{5,7},{6,4},{7,5},{8,10},{9,11},{10,... | collective-permute-start | bytes 1966088 | tf_op jit(solution)/shard_map/ppermute | solution.py:24
  66.7 21.3 %collective-permute-start.18 = (bf16[768,256]{1,0:T(8,128)(2,1)S(1)}, bf16[768,256]{1,0:T(8,128)(2,1)S(1)}, u32[]{:S(2)}, u32[]{:S(2)}) collective-permute-start(bf16[768,256]{1,0:T(8,128)(2,1)S(1)} %broadcast_select_fusion.3.rest_6_), channel_id=1, source_target_pairs={{4,2},{5,3},{12,10},{13,11},{20,18},{21,19},{28,26},{29,27}} | collective-permute-start | bytes 1179656 | tf_op jit(solution)/shard_map/ppermute | solution.py:24
  68.0 29.0 %collective-permute-start.2 = (bf16[1280,256]{1,0:T(8,128)(2,1)S(1)}, bf16[1280,256]{1,0:T(8,128)(2,1)S(1)}, u32[]{:S(2)}, u32[]{:S(2)}) collective-permute-start(bf16[1280,256]{1,0:T(8,128)(2,1)S(1)} %broadcast_select_fusion.rest_0_), channel_id=1, source_target_pairs={{0,1},{1,0},{2,3},{3,2},{4,5},{5,4},{6,7},{7,6},{8,9},{9,8},{10,11... | collective-permute-start | bytes 1966088 | tf_op jit(solution)/shard_map/ppermute | solution.py:24
  75.0 20.0 %collective-permute-start.13 = (bf16[768,256]{1,0:T(8,128)(2,1)S(1)}, bf16[768,256]{1,0:T(8,128)(2,1)}, u32[]{:S(2)}, u32[]{:S(2)}) collective-permute-start(bf16[768,256]{1,0:T(8,128)(2,1)S(1)} %broadcast_select_fusion.4.rest_0_), channel_id=1, source_target_pairs={{0,2},{1,3},{2,0},{3,1},{4,6},{5,7},{6,4},{7,5},{8,10},{9,11},{10,... | collective-permute-start | bytes 1179656 | tf_op jit(solution)/shard_map/ppermute | solution.py:24
  75.1 21.4 %collective-permute-start.8 = (bf16[640,256]{1,0:T(8,128)(2,1)S(1)}, bf16[640,256]{1,0:T(8,128)(2,1)S(1)}, u32[]{:S(2)}, u32[]{:S(2)}) collective-permute-start(bf16[640,256]{1,0:T(8,128)(2,1)S(1)} %select_select_fusion.rest_4_), channel_id=1, source_target_pairs={{0,1},{1,0},{2,3},{3,2},{4,5},{5,4},{6,7},{7,6},{8,9},{9,8},{10,11... | collective-permute-start | bytes 983048 | tf_op jit(solution)/shard_map/ppermute | solution.py:24
  87.4 19.3 %collective-permute-start.3 = (bf16[1280,256]{1,0:T(8,128)(2,1)S(1)}, bf16[1280,256]{1,0:T(8,128)(2,1)S(1)}, u32[]{:S(2)}, u32[]{:S(2)}) collective-permute-start(bf16[1280,256]{1,0:T(8,128)(2,1)S(1)} %collective-permute-done.1.rest_1_), channel_id=1, source_target_pairs={{0,1},{1,0},{2,3},{3,2},{4,5},{5,4},{6,7},{7,6},{8,9},{9,8},{10,11... | collective-permute-start | bytes 1966088 | tf_op jit(solution)/shard_map/ppermute | solution.py:24
  88.0 48.6 %collective-permute-start.21 = (bf16[1024,256]{1,0:T(8,128)(2,1)S(1)}, bf16[1024,256]{1,0:T(8,128)(2,1)}, u32[]{:S(2)}, u32[]{:S(2)}) collective-permute-start(bf16[1024,256]{1,0:T(8,128)(2,1)S(1)} %copy-done.5), channel_id=1, source_target_pairs={{4,5},{12,13},{20,21},{28,29}} | collective-permute-start | bytes 1572872 | tf_op jit(solution)/shard_map/ppermute | solution.py:24
  95.1 31.2 %collective-permute-start.19 = (bf16[768,256]{1,0:T(8,128)(2,1)S(1)}, bf16[768,256]{1,0:T(8,128)(2,1)}, u32[]{:S(2)}, u32[]{:S(2)}) collective-permute-start(bf16[768,256]{1,0:T(8,128)(2,1)S(1)} %broadcast_select_fusion.3.rest_6_), channel_id=1, source_target_pairs={{4,6},{5,7},{12,14},{13,15},{20,22},{21,23},{28,30},{29,31}} | collective-permute-start | bytes 1179656 | tf_op jit(solution)/shard_map/ppermute | solution.py:24
  96.5 30.2 %collective-permute-start.14 = (bf16[768,256]{1,0:T(8,128)(2,1)S(1)}, bf16[768,256]{1,0:T(8,128)(2,1)}, u32[]{:S(2)}, u32[]{:S(2)}) collective-permute-start(bf16[768,256]{1,0:T(8,128)(2,1)S(1)} %broadcast_select_fusion.4.rest_0_), channel_id=1, source_target_pairs={{0,1},{1,0},{2,3},{3,2},{4,5},{5,4},{6,7},{7,6},{8,9},{9,8},{10,11... | collective-permute-start | bytes 1179656 | tf_op jit(solution)/shard_map/ppermute | solution.py:24
  97.0 29.6 %collective-permute-start.15 = (bf16[768,256]{1,0:T(8,128)(2,1)}, bf16[768,256]{1,0:T(8,128)(2,1)}, u32[]{:S(2)}, u32[]{:S(2)}) collective-permute-start(bf16[768,256]{1,0:T(8,128)(2,1)} %collective-permute-done.13.rest_1_), channel_id=1, source_target_pairs={{0,1},{1,0},{2,3},{3,2},{4,5},{5,4},{6,7},{7,6},{8,9},{9,8},{10,11... | collective-permute-start | bytes 1179656 | tf_op jit(solution)/shard_map/ppermute | solution.py:24
  106.7 33.4 %collective-permute-start.10 = (bf16[1024,256]{1,0:T(8,128)(2,1)S(1)}, bf16[1024,256]{1,0:T(8,128)(2,1)}, u32[]{:S(2)}, u32[]{:S(2)}) collective-permute-start(bf16[1024,256]{1,0:T(8,128)(2,1)S(1)} %broadcast_select_fusion.2.rest_0_), channel_id=1, source_target_pairs={{0,2},{1,3},{2,0},{3,1},{4,6},{5,7},{6,4},{7,5},{8,10},{9,11},{10,... | collective-permute-start | bytes 1572872 | tf_op jit(solution)/shard_map/ppermute | solution.py:24
  109.6 23.3 %all-to-all-start = ((s32[4,1,2]{2,1,0:T(1,128)}), s32[4,1,2]{2,1,0:T(1,128)S(1)}, u32[]{:S(2)}, u32[]{:S(2)}) async-start(s32[4,1,2]{2,1,0:T(1,128)} %copy.11), calls=%async_computation | async-start | bytes 4096 | tf_op jit(solution)/shard_map/all_to_all | solution.py:491
  126.3 17.4 %collective-permute-start.11 = (bf16[1024,256]{1,0:T(8,128)(2,1)S(1)}, bf16[1024,256]{1,0:T(8,128)(2,1)S(1)}, u32[]{:S(2)}, u32[]{:S(2)}) collective-permute-start(bf16[1024,256]{1,0:T(8,128)(2,1)S(1)} %broadcast_select_fusion.2.rest_0_), channel_id=1, source_target_pairs={{0,1},{1,0},{2,3},{3,2},{4,5},{5,4},{6,7},{7,6},{8,9},{9,8},{10,11... | collective-permute-start | bytes 1572872 | tf_op jit(solution)/shard_map/ppermute | solution.py:24
  132.9 46.7 %all-to-all-start.1 = ((bf16[4,2,128,384]{3,2,1,0:T(8,128)(2,1)}), bf16[4,2,128,384]{3,2,1,0:T(8,128)(2,1)S(1)}, u32[]{:S(2)}, u32[]{:S(2)}) async-start(bf16[4,2,128,384]{3,2,1,0:T(8,128)(2,1)} %get-tuple-element.13), calls=%async_computation.1 | async-start | bytes 1572864 | tf_op jit(solution)/shard_map/all_to_all | solution.py:546
  136.7 13.2 %collective-permute-start.22 = (bf16[1024,256]{1,0:T(8,128)(2,1)S(1)}, bf16[1024,256]{1,0:T(8,128)(2,1)S(1)}, u32[]{:S(2)}, u32[]{:S(2)}) collective-permute-start(bf16[1024,256]{1,0:T(8,128)(2,1)S(1)} %broadcast_select_fusion.1.rest_3_), channel_id=1, source_target_pairs={{4,0},{5,1},{12,8},{13,9},{20,16},{21,17},{28,24},{29,25}} | collective-permute-start | bytes 1572872 | tf_op jit(solution)/shard_map/ppermute | solution.py:24
  137.4 37.4 %collective-permute-start.23 = (bf16[1024,256]{1,0:T(8,128)(2,1)S(1)}, bf16[1024,256]{1,0:T(8,128)(2,1)}, u32[]{:S(2)}, u32[]{:S(2)}) collective-permute-start(bf16[1024,256]{1,0:T(8,128)(2,1)S(1)} %broadcast_select_fusion.1.rest_3_), channel_id=1, source_target_pairs={{4,2},{5,3},{12,10},{13,11},{20,18},{21,19},{28,26},{29,27}} | collective-permute-start | bytes 1572872 | tf_op jit(solution)/shard_map/ppermute | solution.py:24
  138.7 36.1 %collective-permute-start.24 = (bf16[1024,256]{1,0:T(8,128)(2,1)S(1)}, bf16[1024,256]{1,0:T(8,128)(2,1)}, u32[]{:S(2)}, u32[]{:S(2)}) collective-permute-start(bf16[1024,256]{1,0:T(8,128)(2,1)S(1)} %broadcast_select_fusion.1.rest_3_), channel_id=1, source_target_pairs={{4,6},{5,7},{12,14},{13,15},{20,22},{21,23},{28,30},{29,31}} | collective-permute-start | bytes 1572872 | tf_op jit(solution)/shard_map/ppermute | solution.py:24
  140.2 34.7 %collective-permute-start.20 = (bf16[1024,256]{1,0:T(8,128)(2,1)}, bf16[1024,256]{1,0:T(8,128)(2,1)}, u32[]{:S(2)}, u32[]{:S(2)}) collective-permute-start(bf16[1024,256]{1,0:T(8,128)(2,1)} %collective-permute-done.10.rest_1_), channel_id=1, source_target_pairs={{0,1},{1,0},{2,3},{3,2},{4,5},{5,4},{6,7},{7,6},{8,9},{9,8},{10,11... | collective-permute-start | bytes 1572872 | tf_op jit(solution)/shard_map/ppermute | solution.py:24
  (23 other events, 706.8 us)

commit v13 on v12

--- a/solution.py
+++ b/solution.py
@@ -489,18 +489,24 @@
     )
     address = jnp.sum(jnp.where(pick, target[None, None, :] + 1, 0), axis=2) - 1
     received = lax.all_to_all(address, "front", split_axis=0, concat_axis=0, tiled=True)
-    return dest, slot, received.reshape(groups * CAP)
-
-
-def add_kernel(address_ref, incoming, base, out):
-    out[...] = base[...]
-    for i in range(incoming.shape[0]):
-        to = address_ref[i]
-
-        @pl.when(to >= 0)
-        def _(i=i, to=to):
-            at = pl.ds(pl.multiple_of(to * RB, RB), RB)
-            out[at, :] = out[at, :] + incoming[i].astype(jnp.float32)
+    return dest, slot, received.reshape(groups, CAP)
+
+
+def add_kernel(address_ref, incoming, base, out, held, sems):
+    rows = incoming.shape[1]
+    stores = []
+    for block in range(base.shape[0] // rows):
+        at = pl.ds(block * rows, rows)
+        held[at, :] = base[at, :]
+        for i in range(incoming.shape[0]):
+
+            @pl.when(address_ref[i // CAP, i % CAP] == block)
+            def _(i=i, at=at):
+                held[at, :] = held[at, :] + incoming[i].astype(jnp.float32)
+
+        stores.append(pltpu.make_async_copy(held.at[at, :], out.at[at, :], sems.at[block]))
+        stores[-1].start()
+    wait_all(stores)
 
 
 def add_blocks(address, incoming, parent_base):
@@ -510,7 +516,11 @@
         name="add_blocks",
         out_shape=jax.ShapeDtypeStruct(parent_base.shape, parent_base.dtype),
         in_specs=[SMEM, VMEM, VMEM],
-        out_specs=VMEM,
+        out_specs=ANY,
+        scratch_shapes=[
+            pltpu.VMEM(parent_base.shape, jnp.float32),
+            pltpu.SemaphoreType.DMA((parent_base.shape[0] // rows,)),
+        ],
     )(address, incoming.reshape(groups * cap, rows, width), parent_base)
 
 

time: 184 us -> 185 us (level)
  transfers between devices with their start and end apart: 27 -> 27, of which waited for: 7 -> 7; matrix products, arithmetic and copies ran while one was open for 3% -> 2% of each run, Pallas kernels for 17% -> 17%
where the time goes in v13:
time: 185 us; the launch traced here: 184 us
  waiting for transfers between devices  103 us (56%)
  Pallas kernels  36.9 us (20%)
  starting transfers between devices  35.9 us (19%)
  local copies, waits for them, and re-layouts  3.6 us (2%)
  other arithmetic  2.72 us (1%)
    ppermute x25, waiting for transfers between devices, permute(): return lax.ppermute(value, 'blk', pairs)  103 us
    ppermute x25, starting transfers between devices, permute(): return lax.ppermute(value, 'blk', pairs)  28.4 us
    pallas_call x1, Pallas kernels, pivot_rows(): pl.pallas_call(functools.partial(pivot_kernel, counts, width), name='pivo...  12.9 us
    pallas_call x1, Pallas kernels, other_rows(): pl.pallas_call(functools.partial(other_kernel, counts, chunks, bool(group...  6.19 us
    pallas_call x1, Pallas kernels, middle_rows(): pl.pallas_call(functools.partial(partial_kernel, len(early), chunks), nam...  5.42 us
    pallas_call x1, Pallas kernels, middle_rows(): pl.pallas_call(functools.partial(final_kernel, (len(late), counts[1]), ch...  4.78 us
    pallas_call x2, Pallas kernels, pack(): pl.pallas_call(functools.partial(pack_kernel, pieces), out_shape=tuple((j...  4.58 us
    all_to_all x1, starting transfers between devices, local(): lax.all_to_all(outgoing, 'front', split_axis=0, concat_axis=0, tiled=True)  3.71 us
  transfers between devices with their start and end apart: 27, of which 7 were waited for; matrix products, arithmetic and copies ran while one was open for 2% of the time, Pallas kernels for 17%

profile of v13, /device:TPU:14, one launch (start us, length us, event | category | flops | bytes accessed | tf_op | source)
XLA Modules:
  0.0 183.8 jit_solution(3964355884345074214)
XLA Ops:
  0.6 2.2 %shard_map.59 = bf16[1280,256]{1,0:T(8,128)(2,1)} custom-call(f32[3072,384]{1,0:T(8,128)} %front.9), custom_call_target="tpu_custom_call" | custom-call | tf_op jit(solution)/shard_map/pallas_call | solution.py:146
  2.8 4.7 %collective-permute-start = (bf16[1280,256]{1,0:T(8,128)(2,1)}, bf16[1280,256]{1,0:T(8,128)(2,1)S(1)}, u32[]{:S(2)}, u32[]{:S(2)}) collective-permute-start(bf16[1280,256]{1,0:T(8,128)(2,1)} %shard_map.59), channel_id=1, source_target_pairs={{0,4},{1,5},{2,6},{3,7},{8,12},{9,13},{10,14},{11,15},{16,20},{17,... | collective-permute-start | bytes 1966088 | tf_op jit(solution)/shard_map/ppermute | solution.py:24
  9.2 2.4 %shard_map.60 = (bf16[768,256]{1,0:T(8,128)(2,1)}, bf16[1024,256]{1,0:T(8,128)(2,1)}) custom-call(f32[3072,384]{1,0:T(8,128)} %front.9), custom_call_target="tpu_custom_call" | custom-call | tf_op jit(solution)/shard_map/pallas_call | solution.py:146
  11.6 1.4 collective-permute-start.12
  13.8 2.1 %collective-permute-start.9 = (bf16[1024,256]{1,0:T(8,128)(2,1)}, bf16[1024,256]{1,0:T(8,128)(2,1)}, u32[]{:S(2)}, u32[]{:S(2)}) collective-permute-start(bf16[1024,256]{1,0:T(8,128)(2,1)} %get-tuple-element.9), channel_id=1, source_target_pairs={{0,4},{1,5},{2,6},{3,7},{8,12},{9,13},{10,14},{11,15},{16,20},{17,... | collective-permute-start | bytes 1572872 | tf_op jit(solution)/shard_map/ppermute | solution.py:24
  16.8 38.6 %collective-permute-done = bf16[1280,256]{1,0:T(8,128)(2,1)S(1)} collective-permute-done((bf16[1280,256]{1,0:T(8,128)(2,1)}, bf16[1280,256]{1,0:T(8,128)(2,1)S(1)}, u32[]{:S(2)}, u32[]{:S(2)}) %collective-permute-start) | collective-permute-done | bytes 655392 | tf_op jit(solution)/shard_map/ppermute | solution.py:24
  57.5 6.3 %collective-permute-done.12 = bf16[768,256]{1,0:T(8,128)(2,1)S(1)} collective-permute-done((bf16[768,256]{1,0:T(8,128)(2,1)}, bf16[768,256]{1,0:T(8,128)(2,1)S(1)}, u32[]{:S(2)}, u32[]{:S(2)}) %collective-permute-start.12) | collective-permute-done | bytes 393248 | tf_op jit(solution)/shard_map/ppermute | solution.py:24
  68.7 6.4 %collective-permute-done.9 = bf16[1024,256]{1,0:T(8,128)(2,1)} collective-permute-done((bf16[1024,256]{1,0:T(8,128)(2,1)}, bf16[1024,256]{1,0:T(8,128)(2,1)}, u32[]{:S(2)}, u32[]{:S(2)}) %collective-permute-start.9) | collective-permute-done | bytes 524320 | tf_op jit(solution)/shard_map/ppermute | solution.py:24
  75.8 11.6 %collective-permute-done.1.rest_1_ = bf16[1280,256]{1,0:T(8,128)(2,1)S(1)} collective-permute-done((bf16[1280,256]{1,0:T(8,128)(2,1)S(1)}, bf16[1280,256]{1,0:T(8,128)(2,1)S(1)}, u32[]{:S(2)}, u32[]{:S(2)}) %collective-permute-start.1) | collective-permute-done | bytes 655392 | tf_op jit(solution)/shard_map/ppermute | solution.py:24
  88.0 1.5 collective-permute-start.21
  89.5 5.6 %collective-permute-done.13.rest_1_ = bf16[768,256]{1,0:T(8,128)(2,1)} collective-permute-done((bf16[768,256]{1,0:T(8,128)(2,1)S(1)}, bf16[768,256]{1,0:T(8,128)(2,1)}, u32[]{:S(2)}, u32[]{:S(2)}) %collective-permute-start.13) | collective-permute-done | bytes 393248 | tf_op jit(solution)/shard_map/ppermute | solution.py:24
  97.0 1.5 collective-permute-start.15
  98.6 8.1 %collective-permute-done.3.rest_3_ = bf16[1280,256]{1,0:T(8,128)(2,1)S(1)} collective-permute-done((bf16[1280,256]{1,0:T(8,128)(2,1)S(1)}, bf16[1280,256]{1,0:T(8,128)(2,1)S(1)}, u32[]{:S(2)}, u32[]{:S(2)}) %collective-permute-start.3) | collective-permute-done | bytes 655392 | tf_op jit(solution)/shard_map/ppermute | solution.py:24
  106.7 2.0 %collective-permute-start.10 = (bf16[1024,256]{1,0:T(8,128)(2,1)S(1)}, bf16[1024,256]{1,0:T(8,128)(2,1)}, u32[]{:S(2)}, u32[]{:S(2)}) collective-permute-start(bf16[1024,256]{1,0:T(8,128)(2,1)S(1)} %broadcast_select_fusion.2.rest_0_), channel_id=1, source_target_pairs={{0,2},{1,3},{2,0},{3,1},{4,6},{5,7},{6,4},{7,5},{8,10},{9,11},{10,... | collective-permute-start | bytes 1572872 | tf_op jit(solution)/shard_map/ppermute | solution.py:24
  109.6 3.7 %all-to-all-start = ((s32[4,1,2]{2,1,0:T(1,128)}), s32[4,1,2]{2,1,0:T(1,128)S(1)}, u32[]{:S(2)}, u32[]{:S(2)}) async-start(s32[4,1,2]{2,1,0:T(1,128)} %copy.12), calls=%async_computation | async-start | bytes 4096 | tf_op jit(solution)/shard_map/all_to_all | solution.py:491
  113.3 12.9 %pivot_rows.1 = (f32[3072,384]{1,0:T(8,128)}, bf16[1280,384]{1,0:T(8,128)(2,1)}) custom-call(s32[1]{0:T(128)} %bitcast.member_ref, f32[3072,384]{1,0:T(8,128)} %front.9, bf16[1280,256]{1,0:T(8,128)(2,1)} %copy-done.2, bf16[1280,256]{1,0:T(8,128)(2,1)} %copy-done.9, bf16[1280,256]{1,0:T(8,128)(2,1)} %copy-done.10, bf16[1280,256]{1,0:T(8,128)(2,1)} %copy-done.11, ...), custom_call_target="tpu_custom_call" | custom-call | tf_op jit(solution)/shard_map/pivot_rows/pallas_call | solution.py:267
  126.7 6.2 %tail_rows.1 = (f32[3072,384]{1,0:T(8,128)}, bf16[4,2,128,384]{3,2,1,0:T(8,128)(2,1)}) custom-call(s32[1]{0:T(128)} %bitcast.member_ref, s32[6]{0:T(128)} %bitcast.10, s32[6]{0:T(128)} %copy-done.19, bf16[1280,384]{1,0:T(8,128)(2,1)} %get-tuple-element.8.w, f32[3072,384]{1,0:T(8,128)} %front.9, ...), custom_call_target="tpu_custom_call", output_to_operand_aliasing={{0}: (5, {})} | custom-call | tf_op jit(solution)/shard_map/tail_rows/pallas_call | solution.py:355
  132.9 3.7 %all-to-all-start.1 = ((bf16[4,2,128,384]{3,2,1,0:T(8,128)(2,1)}), bf16[4,2,128,384]{3,2,1,0:T(8,128)(2,1)S(1)}, u32[]{:S(2)}, u32[]{:S(2)}) async-start(bf16[4,2,128,384]{3,2,1,0:T(8,128)(2,1)} %get-tuple-element.13), calls=%async_computation.1 | async-start | bytes 1572864 | tf_op jit(solution)/shard_map/all_to_all | solution.py:556
  138.7 1.5 collective-permute-start.24
  140.2 1.7 collective-permute-start.20
  142.7 5.4 %partial_rows.1.base = f32[1024,384]{1,0:T(8,128)} custom-call(s32[1]{0:T(128)} %bitcast.member_ref, bf16[1280,384]{1,0:T(8,128)(2,1)} %get-tuple-element.8.w, f32[3072,384]{1,0:T(8,128)} %front.9, bf16[1024,256]{1,0:T(8,128)(2,1)} %copy-done.3, bf16[1024,256]{1,0:T(8,128)(2,1)} %collective-permute-done.10.rest_1_, bf16[1024,256]{1,0:T(8,128)(2,1)} %copy-done.12), custom_call_target="tpu_custom_call" | custom-call | tf_op jit(solution)/shard_map/partial_rows/pallas_call | solution.py:451
  148.2 26.7 %collective-permute-done.23.rest_2_ = bf16[1024,256]{1,0:T(8,128)(2,1)} collective-permute-done((bf16[1024,256]{1,0:T(8,128)(2,1)S(1)}, bf16[1024,256]{1,0:T(8,128)(2,1)}, u32[]{:S(2)}, u32[]{:S(2)}) %collective-permute-start.23) | collective-permute-done | bytes 524320 | tf_op jit(solution)/shard_map/ppermute | solution.py:24
  174.9 4.8 %middle_rows.1 = f32[3072,384]{1,0:T(8,128)} custom-call(s32[1]{0:T(128)} %bitcast.member_ref, bf16[1280,384]{1,0:T(8,128)(2,1)} %get-tuple-element.8.w, f32[1024,384]{1,0:T(8,128)} %partial_rows.1.base, f32[3072,384]{1,0:T(8,128)} %get-tuple-element.12.out_in, bf16[1024,256]{1,0:T(8,128)(2,1)} %collective-permute-done.20.rest_0_, ...), custom_call_target="tpu_custom_call", output_to_operand_aliasing={{}: (3, {})} | custom-call | tf_op jit(solution)/shard_map/middle_rows/pallas_call | solution.py:464
  180.6 3.0 %add_blocks.1 = f32[1024,384]{1,0:T(8,128)} custom-call(s32[4,2]{1,0:T(4,128)} %bitcast.9, bf16[8,128,384]{2,1,0:T(8,128)(2,1)} %bitcast.8, f32[1024,384]{1,0:T(8,128)} %base.1), custom_call_target="tpu_custom_call" | custom-call | tf_op jit(solution)/shard_map/add_blocks/pallas_call | solution.py:514
  (94 shorter events, 18.4 us)
Async XLA Ops:
  2.8 52.6 %collective-permute-start = (bf16[1280,256]{1,0:T(8,128)(2,1)}, bf16[1280,256]{1,0:T(8,128)(2,1)S(1)}, u32[]{:S(2)}, u32[]{:S(2)}) collective-permute-start(bf16[1280,256]{1,0:T(8,128)(2,1)} %shard_map.59), channel_id=1, source_target_pairs={{0,4},{1,5},{2,6},{3,7},{8,12},{9,13},{10,14},{11,15},{16,20},{17,... | collective-permute-start | bytes 1966088 | tf_op jit(solution)/shard_map/ppermute | solution.py:24
  11.6 52.2 %collective-permute-start.12 = (bf16[768,256]{1,0:T(8,128)(2,1)}, bf16[768,256]{1,0:T(8,128)(2,1)S(1)}, u32[]{:S(2)}, u32[]{:S(2)}) collective-permute-start(bf16[768,256]{1,0:T(8,128)(2,1)} %get-tuple-element.11), channel_id=1, source_target_pairs={{0,4},{1,5},{2,6},{3,7},{8,12},{9,13},{10,14},{11,15},{16,20},{17,... | collective-permute-start | bytes 1179656 | tf_op jit(solution)/shard_map/ppermute | solution.py:24
  13.1 43.1 %collective-permute-start.16 = (bf16[768,256]{1,0:T(8,128)(2,1)}, bf16[768,256]{1,0:T(8,128)(2,1)S(1)}, u32[]{:S(2)}, u32[]{:S(2)}) collective-permute-start(bf16[768,256]{1,0:T(8,128)(2,1)} %get-tuple-element.11), channel_id=1, source_target_pairs={{4,5},{12,13},{20,21},{28,29}} | collective-permute-start | bytes 1179656 | tf_op jit(solution)/shard_map/ppermute | solution.py:24
  13.8 61.3 %collective-permute-start.9 = (bf16[1024,256]{1,0:T(8,128)(2,1)}, bf16[1024,256]{1,0:T(8,128)(2,1)}, u32[]{:S(2)}, u32[]{:S(2)}) collective-permute-start(bf16[1024,256]{1,0:T(8,128)(2,1)} %get-tuple-element.9), channel_id=1, source_target_pairs={{0,4},{1,5},{2,6},{3,7},{8,12},{9,13},{10,14},{11,15},{16,20},{17,... | collective-permute-start | bytes 1572872 | tf_op jit(solution)/shard_map/ppermute | solution.py:24
  16.2 48.8 %collective-permute-start.5 = (bf16[640,256]{1,0:T(8,128)(2,1)S(1)}, bf16[640,256]{1,0:T(8,128)(2,1)S(1)}, u32[]{:S(2)}, u32[]{:S(2)}) collective-permute-start(bf16[640,256]{1,0:T(8,128)(2,1)S(1)} %slice_select_fusion), channel_id=1, source_target_pairs={{4,6},{5,7},{12,14},{13,15},{20,22},{21,23},{28,30},{29,31}} | collective-permute-start | bytes 983048 | tf_op jit(solution)/shard_map/ppermute | solution.py:24
  56.2 11.8 %collective-permute-start.7 = (bf16[640,256]{1,0:T(8,128)(2,1)S(1)}, bf16[640,256]{1,0:T(8,128)(2,1)S(1)}, u32[]{:S(2)}, u32[]{:S(2)}) collective-permute-start(bf16[640,256]{1,0:T(8,128)(2,1)S(1)} %slice_select_fusion), channel_id=1, source_target_pairs={{4,2},{5,3},{12,10},{13,11},{20,18},{21,19},{28,26},{29,27}} | collective-permute-start | bytes 983048 | tf_op jit(solution)/shard_map/ppermute | solution.py:24
  63.9 23.6 %collective-permute-start.1 = (bf16[1280,256]{1,0:T(8,128)(2,1)S(1)}, bf16[1280,256]{1,0:T(8,128)(2,1)S(1)}, u32[]{:S(2)}, u32[]{:S(2)}) collective-permute-start(bf16[1280,256]{1,0:T(8,128)(2,1)S(1)} %broadcast_select_fusion.rest_0_), channel_id=1, source_target_pairs={{0,2},{1,3},{2,0},{3,1},{4,6},{5,7},{6,4},{7,5},{8,10},{9,11},{10,... | collective-permute-start | bytes 1966088 | tf_op jit(solution)/shard_map/ppermute | solution.py:24
  66.7 21.3 %collective-permute-start.18 = (bf16[768,256]{1,0:T(8,128)(2,1)S(1)}, bf16[768,256]{1,0:T(8,128)(2,1)S(1)}, u32[]{:S(2)}, u32[]{:S(2)}) collective-permute-start(bf16[768,256]{1,0:T(8,128)(2,1)S(1)} %broadcast_select_fusion.3.rest_6_), channel_id=1, source_target_pairs={{4,2},{5,3},{12,10},{13,11},{20,18},{21,19},{28,26},{29,27}} | collective-permute-start | bytes 1179656 | tf_op jit(solution)/shard_map/ppermute | solution.py:24
  68.0 29.0 %collective-permute-start.2 = (bf16[1280,256]{1,0:T(8,128)(2,1)S(1)}, bf16[1280,256]{1,0:T(8,128)(2,1)S(1)}, u32[]{:S(2)}, u32[]{:S(2)}) collective-permute-start(bf16[1280,256]{1,0:T(8,128)(2,1)S(1)} %broadcast_select_fusion.rest_0_), channel_id=1, source_target_pairs={{0,1},{1,0},{2,3},{3,2},{4,5},{5,4},{6,7},{7,6},{8,9},{9,8},{10,11... | collective-permute-start | bytes 1966088 | tf_op jit(solution)/shard_map/ppermute | solution.py:24
  75.0 20.0 %collective-permute-start.13 = (bf16[768,256]{1,0:T(8,128)(2,1)S(1)}, bf16[768,256]{1,0:T(8,128)(2,1)}, u32[]{:S(2)}, u32[]{:S(2)}) collective-permute-start(bf16[768,256]{1,0:T(8,128)(2,1)S(1)} %broadcast_select_fusion.4.rest_0_), channel_id=1, source_target_pairs={{0,2},{1,3},{2,0},{3,1},{4,6},{5,7},{6,4},{7,5},{8,10},{9,11},{10,... | collective-permute-start | bytes 1179656 | tf_op jit(solution)/shard_map/ppermute | solution.py:24
  75.1 21.4 %collective-permute-start.8 = (bf16[640,256]{1,0:T(8,128)(2,1)S(1)}, bf16[640,256]{1,0:T(8,128)(2,1)S(1)}, u32[]{:S(2)}, u32[]{:S(2)}) collective-permute-start(bf16[640,256]{1,0:T(8,128)(2,1)S(1)} %select_select_fusion.rest_4_), channel_id=1, source_target_pairs={{0,1},{1,0},{2,3},{3,2},{4,5},{5,4},{6,7},{7,6},{8,9},{9,8},{10,11... | collective-permute-start | bytes 983048 | tf_op jit(solution)/shard_map/ppermute | solution.py:24
  87.4 19.3 %collective-permute-start.3 = (bf16[1280,256]{1,0:T(8,128)(2,1)S(1)}, bf16[1280,256]{1,0:T(8,128)(2,1)S(1)}, u32[]{:S(2)}, u32[]{:S(2)}) collective-permute-start(bf16[1280,256]{1,0:T(8,128)(2,1)S(1)} %collective-permute-done.1.rest_1_), channel_id=1, source_target_pairs={{0,1},{1,0},{2,3},{3,2},{4,5},{5,4},{6,7},{7,6},{8,9},{9,8},{10,11... | collective-permute-start | bytes 1966088 | tf_op jit(solution)/shard_map/ppermute | solution.py:24
  88.0 48.6 %collective-permute-start.21 = (bf16[1024,256]{1,0:T(8,128)(2,1)S(1)}, bf16[1024,256]{1,0:T(8,128)(2,1)}, u32[]{:S(2)}, u32[]{:S(2)}) collective-permute-start(bf16[1024,256]{1,0:T(8,128)(2,1)S(1)} %copy-done.5), channel_id=1, source_target_pairs={{4,5},{12,13},{20,21},{28,29}} | collective-permute-start | bytes 1572872 | tf_op jit(solution)/shard_map/ppermute | solution.py:24
  95.1 31.2 %collective-permute-start.19 = (bf16[768,256]{1,0:T(8,128)(2,1)S(1)}, bf16[768,256]{1,0:T(8,128)(2,1)}, u32[]{:S(2)}, u32[]{:S(2)}) collective-permute-start(bf16[768,256]{1,0:T(8,128)(2,1)S(1)} %broadcast_select_fusion.3.rest_6_), channel_id=1, source_target_pairs={{4,6},{5,7},{12,14},{13,15},{20,22},{21,23},{28,30},{29,31}} | collective-permute-start | bytes 1179656 | tf_op jit(solution)/shard_map/ppermute | solution.py:24
  96.5 30.2 %collective-permute-start.14 = (bf16[768,256]{1,0:T(8,128)(2,1)S(1)}, bf16[768,256]{1,0:T(8,128)(2,1)}, u32[]{:S(2)}, u32[]{:S(2)}) collective-permute-start(bf16[768,256]{1,0:T(8,128)(2,1)S(1)} %broadcast_select_fusion.4.rest_0_), channel_id=1, source_target_pairs={{0,1},{1,0},{2,3},{3,2},{4,5},{5,4},{6,7},{7,6},{8,9},{9,8},{10,11... | collective-permute-start | bytes 1179656 | tf_op jit(solution)/shard_map/ppermute | solution.py:24
  97.0 29.6 %collective-permute-start.15 = (bf16[768,256]{1,0:T(8,128)(2,1)}, bf16[768,256]{1,0:T(8,128)(2,1)}, u32[]{:S(2)}, u32[]{:S(2)}) collective-permute-start(bf16[768,256]{1,0:T(8,128)(2,1)} %collective-permute-done.13.rest_1_), channel_id=1, source_target_pairs={{0,1},{1,0},{2,3},{3,2},{4,5},{5,4},{6,7},{7,6},{8,9},{9,8},{10,11... | collective-permute-start | bytes 1179656 | tf_op jit(solution)/shard_map/ppermute | solution.py:24
  106.7 33.4 %collective-permute-start.10 = (bf16[1024,256]{1,0:T(8,128)(2,1)S(1)}, bf16[1024,256]{1,0:T(8,128)(2,1)}, u32[]{:S(2)}, u32[]{:S(2)}) collective-permute-start(bf16[1024,256]{1,0:T(8,128)(2,1)S(1)} %broadcast_select_fusion.2.rest_0_), channel_id=1, source_target_pairs={{0,2},{1,3},{2,0},{3,1},{4,6},{5,7},{6,4},{7,5},{8,10},{9,11},{10,... | collective-permute-start | bytes 1572872 | tf_op jit(solution)/shard_map/ppermute | solution.py:24
  109.6 23.3 %all-to-all-start = ((s32[4,1,2]{2,1,0:T(1,128)}), s32[4,1,2]{2,1,0:T(1,128)S(1)}, u32[]{:S(2)}, u32[]{:S(2)}) async-start(s32[4,1,2]{2,1,0:T(1,128)} %copy.12), calls=%async_computation | async-start | bytes 4096 | tf_op jit(solution)/shard_map/all_to_all | solution.py:491
  126.3 15.6 %collective-permute-start.11 = (bf16[1024,256]{1,0:T(8,128)(2,1)S(1)}, bf16[1024,256]{1,0:T(8,128)(2,1)S(1)}, u32[]{:S(2)}, u32[]{:S(2)}) collective-permute-start(bf16[1024,256]{1,0:T(8,128)(2,1)S(1)} %broadcast_select_fusion.2.rest_0_), channel_id=1, source_target_pairs={{0,1},{1,0},{2,3},{3,2},{4,5},{5,4},{6,7},{7,6},{8,9},{9,8},{10,11... | collective-permute-start | bytes 1572872 | tf_op jit(solution)/shard_map/ppermute | solution.py:24
  132.9 46.8 %all-to-all-start.1 = ((bf16[4,2,128,384]{3,2,1,0:T(8,128)(2,1)}), bf16[4,2,128,384]{3,2,1,0:T(8,128)(2,1)S(1)}, u32[]{:S(2)}, u32[]{:S(2)}) async-start(bf16[4,2,128,384]{3,2,1,0:T(8,128)(2,1)} %get-tuple-element.13), calls=%async_computation.1 | async-start | bytes 1572864 | tf_op jit(solution)/shard_map/all_to_all | solution.py:556
  136.7 11.5 %collective-permute-start.22 = (bf16[1024,256]{1,0:T(8,128)(2,1)S(1)}, bf16[1024,256]{1,0:T(8,128)(2,1)S(1)}, u32[]{:S(2)}, u32[]{:S(2)}) collective-permute-start(bf16[1024,256]{1,0:T(8,128)(2,1)S(1)} %broadcast_select_fusion.1.rest_3_), channel_id=1, source_target_pairs={{4,0},{5,1},{12,8},{13,9},{20,16},{21,17},{28,24},{29,25}} | collective-permute-start | bytes 1572872 | tf_op jit(solution)/shard_map/ppermute | solution.py:24
  137.4 37.5 %collective-permute-start.23 = (bf16[1024,256]{1,0:T(8,128)(2,1)S(1)}, bf16[1024,256]{1,0:T(8,128)(2,1)}, u32[]{:S(2)}, u32[]{:S(2)}) collective-permute-start(bf16[1024,256]{1,0:T(8,128)(2,1)S(1)} %broadcast_select_fusion.1.rest_3_), channel_id=1, source_target_pairs={{4,2},{5,3},{12,10},{13,11},{20,18},{21,19},{28,26},{29,27}} | collective-permute-start | bytes 1572872 | tf_op jit(solution)/shard_map/ppermute | solution.py:24
  138.7 36.2 %collective-permute-start.24 = (bf16[1024,256]{1,0:T(8,128)(2,1)S(1)}, bf16[1024,256]{1,0:T(8,128)(2,1)}, u32[]{:S(2)}, u32[]{:S(2)}) collective-permute-start(bf16[1024,256]{1,0:T(8,128)(2,1)S(1)} %broadcast_select_fusion.1.rest_3_), channel_id=1, source_target_pairs={{4,6},{5,7},{12,14},{13,15},{20,22},{21,23},{28,30},{29,31}} | collective-permute-start | bytes 1572872 | tf_op jit(solution)/shard_map/ppermute | solution.py:24
  140.2 34.7 %collective-permute-start.20 = (bf16[1024,256]{1,0:T(8,128)(2,1)}, bf16[1024,256]{1,0:T(8,128)(2,1)}, u32[]{:S(2)}, u32[]{:S(2)}) collective-permute-start(bf16[1024,256]{1,0:T(8,128)(2,1)} %collective-permute-done.10.rest_1_), channel_id=1, source_target_pairs={{0,1},{1,0},{2,3},{3,2},{4,5},{5,4},{6,7},{7,6},{8,9},{9,8},{10,11... | collective-permute-start | bytes 1572872 | tf_op jit(solution)/shard_map/ppermute | solution.py:24
  (24 other events, 723.7 us)
